TPU v7x, 32 devices: a whole 2x2x4 slice. The times are simulated.
32 devices in a mesh: shot: 4 (over z), sub: 8 (over y, x, core).
Axes of the slice: x: 2, y: 2, z: 4, core: 2. Of those that a mesh axis runs over, the one named last changes fastest.
Arguments:
- electric: float32 [4, 3, 32, 32, 128], P('shot', None, 'sub'), may hold values from -6 to 6
- magnetic: float32 [4, 3, 32, 32, 128], P('shot', None, 'sub'), may hold values from -6 to 6
- polar: float32 [4, 3, 32, 32, 128], P('shot', None, 'sub'), may hold values from -4 to 4
- adj_electric: float32 [4, 3, 32, 32, 128], P('shot', None, 'sub'), may hold values from -6 to 6
- adj_magnetic: float32 [4, 3, 32, 32, 128], P('shot', None, 'sub'), may hold values from -6 to 6
- adj_polar: float32 [4, 3, 32, 32, 128], P('shot', None, 'sub'), may hold values from -4 to 4
- permittivity: float32 [32, 32, 128], P('sub'), may hold values from 3 to 25
- conductivity: float32 [32, 32, 128], P('sub'), may hold values from 0.02 to 2
- debye_class: int32 [32, 32, 128], P('sub'), may hold values from 0 to 7
- debye_rate: float32 [8], replicated, may hold values from 0.3 to 0.95
- debye_strength: float32 [8], replicated, may hold values from 0.3 to 3
- wavelet: float32 [6], replicated, may hold values from -4 to 4
- src_cell: int32 [4, 64], P('shot'), may hold values from 0 to 131071
- src_sign: int32 [4, 64], P('shot'), may hold values from 0 to 1
- rec_owner: int32 [4, 1024, 1], P('shot', 'sub'), may hold values from 0 to 7; in each aligned block of 128 rows (0 to 127, 128 to 255, ..., all dimensions but the last counted through in order) at most 16 rows name the same one
- rec_pos: int32 [4, 1024], P('shot', 'sub'), may hold values from 0 to 16383
- observed: float32 [4, 6, 1024], P('shot', None, 'sub'), may hold values from -6 to 6
Outputs:
- grad_eps: float32 [32, 32, 128], P('sub')
- grad_sigma: float32 [32, 32, 128], P('sub')
Inputs may be any that keep to these rules, and one draw needn't show every extreme that they name: Receiver r of a shot group lies in the x range of slab rec_owner; among the 128 receivers of each aligned block of the list at most 16 have the same owner.
All inputs are finite; a program needn't handle non-finite values.
Results may differ from a plain program's by a relative error of at most 0.0001.
Values sent between devices are 32-bit elements; how exact they have to be, the bound alone decides.
No kernel may reach another device: no remote copies, remote signals or barrier semaphores. Data moves between devices by JAX's collectives and lax.ppermute only.
A program may use at most 64 MiB of HBM per device.

v0:
```python
import jax
import jax.numpy as jnp
from jax import lax
from jax.sharding import PartitionSpec as P

CAP = 16


def from_behind(block, axis, distance):
    devices = range(lax.axis_size(axis))
    route = [(i - distance, i) for i in devices if i - distance in devices]
    return lax.ppermute(block, axis, route)


def diff_forward(u, axis):
    tail = lax.slice_in_dim(u, 1, u.shape[axis], axis=axis)
    edge = jnp.zeros_like(lax.slice_in_dim(u, 0, 1, axis=axis))
    return jnp.concatenate([tail, edge], axis) - u


def diff_backward(u, axis):
    head = lax.slice_in_dim(u, 0, u.shape[axis] - 1, axis=axis)
    edge = jnp.zeros_like(lax.slice_in_dim(u, 0, 1, axis=axis))
    return u - jnp.concatenate([edge, head], axis)


def forward_across(u, plane):
    return jnp.concatenate([u[1:], plane], 0) - u


def backward_across(u, plane):
    return u - jnp.concatenate([plane, u[:-1]], 0)


def advance(state, coefs, inject):
    e_field, h_field, p_field = state
    coef_a, coef_b, rate, strength = coefs
    east = from_behind(e_field[1:3, 0:1], "sub", -1)
    curl_e = jnp.stack(
        [
            diff_forward(e_field[2], 2) - diff_forward(e_field[1], 1),
            diff_forward(e_field[0], 1) - forward_across(e_field[2], east[1]),
            forward_across(e_field[1], east[0]) - diff_forward(e_field[0], 2),
        ]
    )
    h_new = h_field - 0.5 * curl_e
    west = from_behind(h_new[1:3, -1:], "sub", 1)
    curl_h = jnp.stack(
        [
            diff_backward(h_new[2], 2) - diff_backward(h_new[1], 1),
            diff_backward(h_new[0], 1) - backward_across(h_new[2], west[1]),
            backward_across(h_new[1], west[0]) - diff_backward(h_new[0], 2),
        ]
    )
    e_new = coef_a * e_field + coef_b * (curl_h - p_field)
    e_new = e_new.at[1].add(inject)
    p_new = rate * p_field + (1.0 - rate) * strength * e_new
    return (e_new, h_new, p_new)


def lookup(table, classes):
    picks = classes[None] == jnp.arange(table.shape[0], dtype=jnp.int32)[:, None, None, None]
    return jnp.sum(jnp.where(picks, table[:, None, None, None], 0.0), axis=0)


def per_device(
    electric,
    magnetic,
    polar,
    adj_electric,
    adj_magnetic,
    adj_polar,
    permittivity,
    conductivity,
    debye_class,
    debye_rate,
    debye_strength,
    wavelet,
    src_cell,
    src_sign,
    rec_owner,
    rec_pos,
    observed,
):
    width, depth, span = permittivity.shape
    steps = wavelet.shape[0]
    nsub = lax.axis_size("sub")
    nshot = lax.axis_size("shot")
    mine = lax.axis_index("sub")
    ratio = conductivity / (2.0 * permittivity)
    coefs = (
        (1.0 - ratio) / (1.0 + ratio),
        0.5 / (permittivity * (1.0 + ratio)),
        lookup(debye_rate, debye_class),
        lookup(debye_strength, debye_class),
    )
    full_x = width * nsub
    flat = src_cell[0]
    src_global = flat % full_x
    src_y = flat // full_x % span
    src_z = flat // (full_x * span)
    src_local = src_global - mine * width
    src_live = (src_local >= 0) & (src_local < width)
    src_x = jnp.clip(src_local, 0, width - 1)
    src_amp = jnp.where(src_live, (2 * src_sign[0] - 1).astype(jnp.float32), 0.0)
    owners = rec_owner[0, :, 0]
    cellpos = rec_pos[0]
    traces = observed[0]
    hits = (owners[:, None] == jnp.arange(nsub, dtype=jnp.int32)[None, :]).astype(jnp.int32)
    before = jnp.cumsum(hits, axis=0) - hits
    slots = jnp.sum(hits * before, axis=1)
    target = owners * CAP + slots
    send_trace = jnp.zeros((steps, nsub * CAP), jnp.float32).at[:, target].set(traces)
    send_pos = jnp.full((1, nsub * CAP), -1, jnp.int32).at[0, target].set(cellpos)
    got_trace, got_pos = (
        lax.all_to_all(send_trace, "sub", split_axis=1, concat_axis=1, tiled=True),
        lax.all_to_all(send_pos, "sub", split_axis=1, concat_axis=1, tiled=True),
    )
    positions = got_pos[0]
    live = positions >= 0
    positions = jnp.where(live, positions, 0)
    rec_x = positions % width
    rec_y = positions // width % span
    rec_z = positions // (width * span)
    state = (electric[0], magnetic[0], polar[0])
    history = [electric[0]]
    synth = []
    for step in range(steps):
        source = (
            jnp.zeros((width, depth, span), jnp.float32)
            .at[src_x, src_z, src_y]
            .add(src_amp * wavelet[step])
        )
        state = advance(state, coefs, source)
        history.append(state[0])
        synth.append(state[0][1][rec_x, rec_z, rec_y])
    resid = jnp.where(live[None], jnp.stack(synth) - got_trace, 0.0)
    state = (adj_electric[0], adj_magnetic[0], adj_polar[0])
    corr_eps = jnp.zeros((width, depth, span), jnp.float32)
    corr_sigma = jnp.zeros((width, depth, span), jnp.float32)
    for back in range(steps):
        later = steps - back
        source = (
            jnp.zeros((width, depth, span), jnp.float32)
            .at[rec_x, rec_z, rec_y]
            .add(resid[later - 1])
        )
        state = advance(state, coefs, source)
        adjoint = state[0]
        term_eps = jnp.sum(adjoint * (history[later] - history[later - 1]), axis=0)
        term_sigma = jnp.sum(adjoint * history[later], axis=0)
        corr_eps = corr_eps + term_eps
        corr_sigma = corr_sigma + term_sigma
    corr_eps, corr_sigma = lax.psum((corr_eps, corr_sigma), "shot")
    return (-(corr_eps / (steps * nshot)), -(corr_sigma / (steps * nshot)))


def solution(mesh):
    in_specs = (
        P("shot", None, "sub", None, None),
        P("shot", None, "sub", None, None),
        P("shot", None, "sub", None, None),
        P("shot", None, "sub", None, None),
        P("shot", None, "sub", None, None),
        P("shot", None, "sub", None, None),
        P("sub", None, None),
        P("sub", None, None),
        P("sub", None, None),
        P(),
        P(),
        P(),
        P("shot", None),
        P("shot", None),
        P("shot", "sub", None),
        P("shot", "sub"),
        P("shot", None, "sub"),
    )
    out_specs = (P("sub", None, None), P("sub", None, None))
    return jax.shard_map(
        per_device, mesh=mesh, in_specs=in_specs, out_specs=out_specs, check_vma=False
    )
```

profile of v0, /device:TPU:4, one launch (start us, length us, event | category | flops | bytes accessed | tf_op | source)
XLA Modules:
  0.0 286.7 jit_solution(6837316200168095393)
XLA Ops:
  8.0 2.8 collective-permute-start.2
  11.6 2.6 collective-permute-start
  14.6 1.1 scatter_custom_fusion
  16.4 3.3 %all-to-all-start = ((s32[1,8,16]{2,0,1:T(1,128)}), s32[1,8,16]{2,0,1:T(1,128)S(1)}, u32[]{:S(2)}, u32[]{:S(2)}) async-start(s32[1,8,16]{2,0,1:T(1,128)} %bitcast.28), calls=%async_computation | async-start | bytes 8192 | tf_op jit(solution)/shard_map/all_to_all | solution.py:117
  23.0 0.9 scatter_custom_fusion.7
  27.0 3.2 %broadcast_multiply_fusion.1 = (f32[64]{0:T(128)S(1)}, f32[64]{0:T(128)S(1)}, f32[64]{0:T(128)S(1)}, f32[64]{0:T(128)S(1)}, f32[64]{0:T(128)S(1)}) fusion(f32[64]{0:T(128)S(1)} %get-tuple-element.205, f32[]{:T(128)} %bitcast.150, f32[]{:T(128)} %bitcast.127, f32[]{:T(128)} %bitcast.104, f32[]{:T(128)} %bitcast.81, f32[]{:T(128)} %bitcast.57), kind=kLoop, calls=%fused_computation.540 | loop fusion | flops 320 | bytes 1556 | tf_op jit(solution)/shard_map/mul | solution.py:132
  30.2 4.5 %scatter_fusion = f32[4,32,128]{2,1,0:T(8,128)S(1)} fusion(f32[4,32,128]{2,1,0:T(8,128)S(1)} %broadcast.880.clone, s32[64]{0:T(128)S(1)} %fusion.152, f32[64]{0:T(128)S(1)} %get-tuple-element.440), kind=kCustom, calls=%fused_computation.7 | custom fusion | flops 64 | bytes 1536 | tf_op jit(solution)/shard_map/scatter-add | solution.py:132
  34.7 4.5 %scatter_fusion.1 = f32[4,32,128]{2,1,0:T(8,128)S(1)} fusion(f32[4,32,128]{2,1,0:T(8,128)S(1)} %broadcast.880.clone.1, s32[64]{0:T(128)S(1)} %fusion.152, f32[64]{0:T(128)S(1)} %get-tuple-element.439), kind=kCustom, calls=%fused_computation.8 | custom fusion | flops 64 | bytes 1536 | tf_op jit(solution)/shard_map/scatter-add | solution.py:132
  39.2 4.5 %scatter_fusion.2 = f32[4,32,128]{2,1,0:T(8,128)S(1)} fusion(f32[4,32,128]{2,1,0:T(8,128)S(1)} %broadcast.880.clone.2, s32[64]{0:T(128)S(1)} %fusion.152, f32[64]{0:T(128)S(1)} %get-tuple-element.438), kind=kCustom, calls=%fused_computation.9 | custom fusion | flops 64 | bytes 1536 | tf_op jit(solution)/shard_map/scatter-add | solution.py:132
  43.7 4.5 %scatter_fusion.3 = f32[4,32,128]{2,1,0:T(8,128)S(1)} fusion(f32[4,32,128]{2,1,0:T(8,128)S(1)} %broadcast.880.clone.3, s32[64]{0:T(128)S(1)} %fusion.152, f32[64]{0:T(128)S(1)} %get-tuple-element.437), kind=kCustom, calls=%fused_computation.10 | custom fusion | flops 64 | bytes 1536 | tf_op jit(solution)/shard_map/scatter-add | solution.py:132
  48.2 4.5 %scatter_fusion.4 = f32[4,32,128]{2,1,0:T(8,128)S(1)} fusion(f32[4,32,128]{2,1,0:T(8,128)S(1)} %broadcast.880.clone.4, s32[64]{0:T(128)S(1)} %fusion.152, f32[64]{0:T(128)S(1)} %get-tuple-element.436), kind=kCustom, calls=%fused_computation.11 | custom fusion | flops 64 | bytes 1536 | tf_op jit(solution)/shard_map/scatter-add | solution.py:132
  52.6 4.5 %scatter_fusion.5 = f32[4,32,128]{2,1,0:T(8,128)S(1)} fusion(f32[4,32,128]{2,1,0:T(8,128)S(1)} %broadcast.880.clone.6, s32[64]{0:T(128)S(1)} %fusion.152, f32[64]{0:T(128)S(1)} %get-tuple-element.204), kind=kCustom, calls=%fused_computation.12 | custom fusion | flops 64 | bytes 1536 | tf_op jit(solution)/shard_map/scatter-add | solution.py:132
  57.1 4.3 %all-to-all-start.1 = ((f32[6,8,16]{2,0,1:T(8,128)}), f32[6,8,16]{2,0,1:T(8,128)S(1)}, u32[]{:S(2)}, u32[]{:S(2)}) async-start(f32[6,8,16]{2,0,1:T(8,128)} %copy.45), calls=%async_computation.1 | async-start | bytes 65536 | tf_op jit(solution)/shard_map/all_to_all | solution.py:116
  63.3 1.5 all-to-all-done.1
  66.5 1.9 collective-permute-start.3
  69.5 2.6 collective-permute-start.1
  73.7 3.3 %collective-permute-start.4 = (f32[2,1,32,128]{3,2,1,0:T(8,128)S(1)}, f32[2,1,32,128]{3,2,1,0:T(8,128)S(1)}, u32[]{:S(2)}, u32[]{:S(2)}) collective-permute-start(f32[2,1,32,128]{3,2,1,0:T(8,128)S(1)} %slice.1942), channel_id=1, source_target_pairs={{1,0},{2,1},{3,2},{4,3},{5,4},{6,5},{7,6},{9,8},{10,9},{11,10},{12... | collective-permute-start | bytes 98312 | tf_op jit(solution)/shard_map/ppermute | solution.py:12
  78.0 1.5 gather_fusion
  79.7 1.9 collective-permute-start.5
  81.6 4.2 %collective-permute-done.5 = f32[2,1,32,128]{3,2,1,0:T(8,128)S(1)} collective-permute-done((f32[2,1,32,128]{3,2,1,0:T(8,128)S(1)}, f32[2,1,32,128]{3,2,1,0:T(8,128)S(1)}, u32[]{:S(2)}, u32[]{:S(2)}) %collective-permute-start.5) | collective-permute-done | bytes 32800 | tf_op jit(solution)/shard_map/ppermute | solution.py:12
  86.1 1.9 collective-permute-start.6
  88.2 1.5 gather_fusion.1
  89.9 2.4 collective-permute-start.7
  92.3 3.7 %collective-permute-done.7 = f32[2,1,32,128]{3,2,1,0:T(8,128)S(1)} collective-permute-done((f32[2,1,32,128]{3,2,1,0:T(8,128)S(1)}, f32[2,1,32,128]{3,2,1,0:T(8,128)S(1)}, u32[]{:S(2)}, u32[]{:S(2)}) %collective-permute-start.7) | collective-permute-done | bytes 32800 | tf_op jit(solution)/shard_map/ppermute | solution.py:12
  96.4 2.1 collective-permute-start.8
  98.6 2.0 gather_fusion.2
  101.4 2.4 collective-permute-start.9
  103.9 3.7 %collective-permute-done.9 = f32[2,1,32,128]{3,2,1,0:T(8,128)S(1)} collective-permute-done((f32[2,1,32,128]{3,2,1,0:T(8,128)S(1)}, f32[2,1,32,128]{3,2,1,0:T(8,128)S(1)}, u32[]{:S(2)}, u32[]{:S(2)}) %collective-permute-start.9) | collective-permute-done | bytes 32800 | tf_op jit(solution)/shard_map/ppermute | solution.py:12
  108.5 1.9 collective-permute-start.10
  111.8 2.0 gather_fusion.3
  115.8 2.4 collective-permute-start.11
  118.2 3.7 %collective-permute-done.11 = f32[2,1,32,128]{3,2,1,0:T(8,128)S(1)} collective-permute-done((f32[2,1,32,128]{3,2,1,0:T(8,128)S(1)}, f32[2,1,32,128]{3,2,1,0:T(8,128)S(1)}, u32[]{:S(2)}, u32[]{:S(2)}) %collective-permute-start.11) | collective-permute-done | bytes 32800 | tf_op jit(solution)/shard_map/ppermute | solution.py:12
  124.0 1.9 collective-permute-start.12
  127.3 2.1 gather_fusion.4
  131.4 2.4 collective-permute-start.13
  133.8 3.7 %collective-permute-done.13 = f32[2,1,32,128]{3,2,1,0:T(8,128)S(1)} collective-permute-done((f32[2,1,32,128]{3,2,1,0:T(8,128)S(1)}, f32[2,1,32,128]{3,2,1,0:T(8,128)S(1)}, u32[]{:S(2)}, u32[]{:S(2)}) %collective-permute-start.13) | collective-permute-done | bytes 32800 | tf_op jit(solution)/shard_map/ppermute | solution.py:12
  138.8 1.5 gather_fusion.5
  141.5 8.3 %scatter_fusion.6 = f32[4,32,128]{2,1,0:T(8,128)S(1)} fusion(f32[4,32,128]{2,1,0:T(8,128)S(1)} %broadcast.880.clone.5, s32[128]{0:T(128)S(1)} %get-tuple-element.216, f32[128]{0:T(128)S(1)} %get-tuple-element.185), kind=kCustom, calls=%fused_computation.14 | custom fusion | flops 128 | bytes 3072 | tf_op jit(solution)/shard_map/scatter-add | solution.py:146
  149.9 1.9 collective-permute-start.14
  152.1 8.3 %scatter_fusion.7 = f32[4,32,128]{2,1,0:T(8,128)S(1)} fusion(f32[4,32,128]{2,1,0:T(8,128)S(1)} %broadcast.880.clone.7, s32[128]{0:T(128)S(1)} %get-tuple-element.216, f32[128]{0:T(128)S(1)} %get-tuple-element.184), kind=kCustom, calls=%fused_computation.15 | custom fusion | flops 128 | bytes 3072 | tf_op jit(solution)/shard_map/scatter-add | solution.py:146
  160.4 8.3 %scatter_fusion.8 = f32[4,32,128]{2,1,0:T(8,128)S(1)} fusion(f32[4,32,128]{2,1,0:T(8,128)S(1)} %broadcast.880.clone.8, s32[128]{0:T(128)S(1)} %get-tuple-element.216, f32[128]{0:T(128)S(1)} %get-tuple-element.183), kind=kCustom, calls=%fused_computation.16 | custom fusion | flops 128 | bytes 3072 | tf_op jit(solution)/shard_map/scatter-add | solution.py:146
  168.8 8.3 %scatter_fusion.9 = f32[4,32,128]{2,1,0:T(8,128)S(1)} fusion(f32[4,32,128]{2,1,0:T(8,128)S(1)} %broadcast.880.clone.9, s32[128]{0:T(128)S(1)} %get-tuple-element.216, f32[128]{0:T(128)S(1)} %get-tuple-element.182), kind=kCustom, calls=%fused_computation.17 | custom fusion | flops 128 | bytes 3072 | tf_op jit(solution)/shard_map/scatter-add | solution.py:146
  177.1 8.3 %scatter_fusion.10 = f32[4,32,128]{2,1,0:T(8,128)S(1)} fusion(f32[4,32,128]{2,1,0:T(8,128)S(1)} %broadcast.880.clone.10, s32[128]{0:T(128)S(1)} %get-tuple-element.216, f32[128]{0:T(128)S(1)} %get-tuple-element.181), kind=kCustom, calls=%fused_computation.18 | custom fusion | flops 128 | bytes 3072 | tf_op jit(solution)/shard_map/scatter-add | solution.py:146
  185.5 8.3 %scatter_fusion.11 = f32[4,32,128]{2,1,0:T(8,128)S(1)} fusion(f32[4,32,128]{2,1,0:T(8,128)S(1)} %broadcast.880.clone.11, s32[128]{0:T(128)S(1)} %get-tuple-element.216, f32[128]{0:T(128)S(1)} %get-tuple-element.180), kind=kCustom, calls=%fused_computation.19 | custom fusion | flops 128 | bytes 3072 | tf_op jit(solution)/shard_map/scatter-add | solution.py:146
  194.0 2.3 collective-permute-start.15
  196.3 3.8 %collective-permute-done.15 = f32[2,1,32,128]{3,2,1,0:T(8,128)S(1)} collective-permute-done((f32[2,1,32,128]{3,2,1,0:T(8,128)S(1)}, f32[2,1,32,128]{3,2,1,0:T(8,128)S(1)}, u32[]{:S(2)}, u32[]{:S(2)}) %collective-permute-start.15) | collective-permute-done | bytes 32800 | tf_op jit(solution)/shard_map/ppermute | solution.py:12
  200.4 1.9 collective-permute-start.16
  202.6 1.4 collective-permute-done.16
  204.1 1.9 collective-permute-start.17
  206.1 4.2 %collective-permute-done.17 = f32[2,1,32,128]{3,2,1,0:T(8,128)S(1)} collective-permute-done((f32[2,1,32,128]{3,2,1,0:T(8,128)S(1)}, f32[2,1,32,128]{3,2,1,0:T(8,128)S(1)}, u32[]{:S(2)}, u32[]{:S(2)}) %collective-permute-start.17) | collective-permute-done | bytes 32800 | tf_op jit(solution)/shard_map/ppermute | solution.py:12
  210.6 1.9 collective-permute-start.18
  212.7 1.4 collective-permute-done.18
  214.3 1.9 collective-permute-start.19
  216.2 4.2 %collective-permute-done.19 = f32[2,1,32,128]{3,2,1,0:T(8,128)S(1)} collective-permute-done((f32[2,1,32,128]{3,2,1,0:T(8,128)S(1)}, f32[2,1,32,128]{3,2,1,0:T(8,128)S(1)}, u32[]{:S(2)}, u32[]{:S(2)}) %collective-permute-start.19) | collective-permute-done | bytes 32800 | tf_op jit(solution)/shard_map/ppermute | solution.py:12
  220.7 1.9 collective-permute-start.20
  222.9 1.4 collective-permute-done.20
  224.5 1.9 collective-permute-start.21
  226.4 4.2 %collective-permute-done.21 = f32[2,1,32,128]{3,2,1,0:T(8,128)S(1)} collective-permute-done((f32[2,1,32,128]{3,2,1,0:T(8,128)S(1)}, f32[2,1,32,128]{3,2,1,0:T(8,128)S(1)}, u32[]{:S(2)}, u32[]{:S(2)}) %collective-permute-start.21) | collective-permute-done | bytes 32800 | tf_op jit(solution)/shard_map/ppermute | solution.py:12
  230.9 1.9 collective-permute-start.22
  233.0 1.4 collective-permute-done.22
  234.7 1.9 collective-permute-start.23
  236.6 4.2 %collective-permute-done.23 = f32[2,1,32,128]{3,2,1,0:T(8,128)S(1)} collective-permute-done((f32[2,1,32,128]{3,2,1,0:T(8,128)S(1)}, f32[2,1,32,128]{3,2,1,0:T(8,128)S(1)}, u32[]{:S(2)}, u32[]{:S(2)}) %collective-permute-start.23) | collective-permute-done | bytes 32800 | tf_op jit(solution)/shard_map/ppermute | solution.py:12
  242.8 35.0 %all-reduce.100.cloned.1.call-done = (f32[4,32,128]{2,1,0:T(8,128)}, f32[4,32,128]{2,1,0:T(8,128)}) async-done(((f32[4,32,128]{2,1,0:T(8,128)}, f32[4,32,128]{2,1,0:T(8,128)}), (f32[4,32,128]{2,1,0:T(8,128)}, f32[4,32,128]{2,1,0:T(8,128)})) %all-reduce.100.cloned.1.call-update) | async-done | bytes 131088 | tf_op jit(solution)/shard_map/psum | solution.py:154
  277.7 1.5 multiply_negate_fusion.1
  (346 shorter events, 35.5 us)
Async XLA Ops:
  7.2 7.0 %copy-start.31 = (s32[1,128,1]{1,2,0:T(1,128)S(1)}, s32[1,128,1]{1,2,0:T(1,128)}, u32[]{:S(2)}) copy-start(s32[1,128,1]{1,2,0:T(1,128)} %param.55) | copy-start | bytes 1540
  7.2 12.5 %copy-start.2 = (f32[1,3,4,32,128]{4,3,2,1,0:T(8,128)S(1)}, f32[1,3,4,32,128]{4,3,2,1,0:T(8,128)}, u32[]{:S(2)}) copy-start(f32[1,3,4,32,128]{4,3,2,1,0:T(8,128)} %param.41) | copy-start | bytes 589828
  8.0 57.5 %collective-permute-start.2 = (f32[2,1,32,128]{3,2,1,0:T(8,128)S(1)}, f32[2,1,32,128]{3,2,1,0:T(8,128)S(1)}, u32[]{:S(2)}, u32[]{:S(2)}) collective-permute-start(f32[2,1,32,128]{3,2,1,0:T(8,128)S(1)} %slice.1919), channel_id=1, source_target_pairs={{1,0},{2,1},{3,2},{4,3},{5,4},{6,5},{7,6},{9,8},{10,9},{11,10},{12... | collective-permute-start | bytes 98312 | tf_op jit(solution)/shard_map/ppermute | solution.py:12
  11.6 56.9 %collective-permute-start = (f32[2,1,32,128]{3,2,1,0:T(8,128)S(1)}, f32[2,1,32,128]{3,2,1,0:T(8,128)S(1)}, u32[]{:S(2)}, u32[]{:S(2)}) collective-permute-start(f32[2,1,32,128]{3,2,1,0:T(8,128)S(1)} %slice.1899), channel_id=1, source_target_pairs={{1,0},{2,1},{3,2},{4,3},{5,4},{6,5},{7,6},{9,8},{10,9},{11,10},{12... | collective-permute-start | bytes 98312 | tf_op jit(solution)/shard_map/ppermute | solution.py:12
  16.4 40.7 %all-to-all-start = ((s32[1,8,16]{2,0,1:T(1,128)}), s32[1,8,16]{2,0,1:T(1,128)S(1)}, u32[]{:S(2)}, u32[]{:S(2)}) async-start(s32[1,8,16]{2,0,1:T(1,128)} %bitcast.28), calls=%async_computation | async-start | bytes 8192 | tf_op jit(solution)/shard_map/all_to_all | solution.py:117
  19.7 0.9 copy-start.5
  20.9 0.7 copy-start.29
  22.2 0.7 copy-start.30
  23.0 1.7 copy-start.28
  23.9 0.8 copy-start.27
  24.8 2.0 copy-start.25
  24.8 0.7 copy-start.38
  26.2 0.7 copy-start.35
  26.2 0.7 copy-start.36
  57.1 7.6 %all-to-all-start.1 = ((f32[6,8,16]{2,0,1:T(8,128)}), f32[6,8,16]{2,0,1:T(8,128)S(1)}, u32[]{:S(2)}, u32[]{:S(2)}) async-start(f32[6,8,16]{2,0,1:T(8,128)} %copy.45), calls=%async_computation.1 | async-start | bytes 65536 | tf_op jit(solution)/shard_map/all_to_all | solution.py:116
  61.4 216.4 %all-reduce.100.cloned.1.call-start = ((), (), s32[]{:S(2)}) async-start(), calls=%async_computation.2 | async-start | bytes 262144 | tf_op jit(solution)/shard_map/psum | solution.py:154
  65.5 0.9 copy-start
  66.5 6.1 %collective-permute-start.3 = (f32[2,1,32,128]{3,2,1,0:T(8,128)S(1)}, f32[2,1,32,128]{3,2,1,0:T(8,128)S(1)}, u32[]{:S(2)}, u32[]{:S(2)}) collective-permute-start(f32[2,1,32,128]{3,2,1,0:T(8,128)S(1)} %slice.1929), channel_id=1, source_target_pairs={{0,1},{1,2},{2,3},{3,4},{4,5},{5,6},{6,7},{8,9},{9,10},{10,11},{11... | collective-permute-start | bytes 98312 | tf_op jit(solution)/shard_map/ppermute | solution.py:12
  68.5 0.9 copy-start.1
  69.5 7.6 %collective-permute-start.1 = (f32[2,1,32,128]{3,2,1,0:T(8,128)S(1)}, f32[2,1,32,128]{3,2,1,0:T(8,128)S(1)}, u32[]{:S(2)}, u32[]{:S(2)}) collective-permute-start(f32[2,1,32,128]{3,2,1,0:T(8,128)S(1)} %slice.1909), channel_id=1, source_target_pairs={{0,1},{1,2},{2,3},{3,4},{4,5},{5,6},{6,7},{8,9},{9,10},{10,11},{11... | collective-permute-start | bytes 98312 | tf_op jit(solution)/shard_map/ppermute | solution.py:12
  72.6 0.9 copy-start.3
  73.7 5.8 %collective-permute-start.4 = (f32[2,1,32,128]{3,2,1,0:T(8,128)S(1)}, f32[2,1,32,128]{3,2,1,0:T(8,128)S(1)}, u32[]{:S(2)}, u32[]{:S(2)}) collective-permute-start(f32[2,1,32,128]{3,2,1,0:T(8,128)S(1)} %slice.1942), channel_id=1, source_target_pairs={{1,0},{2,1},{3,2},{4,3},{5,4},{6,5},{7,6},{9,8},{10,9},{11,10},{12... | collective-permute-start | bytes 98312 | tf_op jit(solution)/shard_map/ppermute | solution.py:12
  79.7 6.1 %collective-permute-start.5 = (f32[2,1,32,128]{3,2,1,0:T(8,128)S(1)}, f32[2,1,32,128]{3,2,1,0:T(8,128)S(1)}, u32[]{:S(2)}, u32[]{:S(2)}) collective-permute-start(f32[2,1,32,128]{3,2,1,0:T(8,128)S(1)} %slice.1953), channel_id=1, source_target_pairs={{0,1},{1,2},{2,3},{3,4},{4,5},{5,6},{6,7},{8,9},{9,10},{10,11},{11... | collective-permute-start | bytes 98312 | tf_op jit(solution)/shard_map/ppermute | solution.py:12
  86.1 3.6 %collective-permute-start.6 = (f32[2,1,32,128]{3,2,1,0:T(8,128)S(1)}, f32[2,1,32,128]{3,2,1,0:T(8,128)S(1)}, u32[]{:S(2)}, u32[]{:S(2)}) collective-permute-start(f32[2,1,32,128]{3,2,1,0:T(8,128)S(1)} %slice.1966), channel_id=1, source_target_pairs={{1,0},{2,1},{3,2},{4,3},{5,4},{6,5},{7,6},{9,8},{10,9},{11,10},{12... | collective-permute-start | bytes 98312 | tf_op jit(solution)/shard_map/ppermute | solution.py:12
  89.9 6.1 %collective-permute-start.7 = (f32[2,1,32,128]{3,2,1,0:T(8,128)S(1)}, f32[2,1,32,128]{3,2,1,0:T(8,128)S(1)}, u32[]{:S(2)}, u32[]{:S(2)}) collective-permute-start(f32[2,1,32,128]{3,2,1,0:T(8,128)S(1)} %slice.1977), channel_id=1, source_target_pairs={{0,1},{1,2},{2,3},{3,4},{4,5},{5,6},{6,7},{8,9},{9,10},{10,11},{11... | collective-permute-start | bytes 98312 | tf_op jit(solution)/shard_map/ppermute | solution.py:12
  96.4 4.3 %collective-permute-start.8 = (f32[2,1,32,128]{3,2,1,0:T(8,128)S(1)}, f32[2,1,32,128]{3,2,1,0:T(8,128)S(1)}, u32[]{:S(2)}, u32[]{:S(2)}) collective-permute-start(f32[2,1,32,128]{3,2,1,0:T(8,128)S(1)} %slice.1990), channel_id=1, source_target_pairs={{1,0},{2,1},{3,2},{4,3},{5,4},{6,5},{7,6},{9,8},{10,9},{11,10},{12... | collective-permute-start | bytes 98312 | tf_op jit(solution)/shard_map/ppermute | solution.py:12
  101.4 6.1 %collective-permute-start.9 = (f32[2,1,32,128]{3,2,1,0:T(8,128)S(1)}, f32[2,1,32,128]{3,2,1,0:T(8,128)S(1)}, u32[]{:S(2)}, u32[]{:S(2)}) collective-permute-start(f32[2,1,32,128]{3,2,1,0:T(8,128)S(1)} %slice.2001), channel_id=1, source_target_pairs={{0,1},{1,2},{2,3},{3,4},{4,5},{5,6},{6,7},{8,9},{9,10},{10,11},{11... | collective-permute-start | bytes 98312 | tf_op jit(solution)/shard_map/ppermute | solution.py:12
  108.5 5.4 %collective-permute-start.10 = (f32[2,1,32,128]{3,2,1,0:T(8,128)S(1)}, f32[2,1,32,128]{3,2,1,0:T(8,128)S(1)}, u32[]{:S(2)}, u32[]{:S(2)}) collective-permute-start(f32[2,1,32,128]{3,2,1,0:T(8,128)S(1)} %slice.2014), channel_id=1, source_target_pairs={{1,0},{2,1},{3,2},{4,3},{5,4},{6,5},{7,6},{9,8},{10,9},{11,10},{12... | collective-permute-start | bytes 98312 | tf_op jit(solution)/shard_map/ppermute | solution.py:12
  113.8 0.8 copy-start.21
  113.8 0.8 copy-start.23
  113.9 0.9 copy-start.18
  114.7 0.8 copy-start.7
  114.8 0.9 copy-start.10
  114.8 0.9 copy-start.12
  115.8 6.1 %collective-permute-start.11 = (f32[2,1,32,128]{3,2,1,0:T(8,128)S(1)}, f32[2,1,32,128]{3,2,1,0:T(8,128)S(1)}, u32[]{:S(2)}, u32[]{:S(2)}) collective-permute-start(f32[2,1,32,128]{3,2,1,0:T(8,128)S(1)} %slice.2025), channel_id=1, source_target_pairs={{0,1},{1,2},{2,3},{3,4},{4,5},{5,6},{6,7},{8,9},{9,10},{10,11},{11... | collective-permute-start | bytes 98312 | tf_op jit(solution)/shard_map/ppermute | solution.py:12
  124.0 5.4 %collective-permute-start.12 = (f32[2,1,32,128]{3,2,1,0:T(8,128)}, f32[2,1,32,128]{3,2,1,0:T(8,128)}, u32[]{:S(2)}, u32[]{:S(2)}) collective-permute-start(f32[2,1,32,128]{3,2,1,0:T(8,128)} %slice.2038), channel_id=1, source_target_pairs={{1,0},{2,1},{3,2},{4,3},{5,4},{6,5},{7,6},{9,8},{10,9},{11,10},{12... | collective-permute-start | bytes 98312 | tf_op jit(solution)/shard_map/ppermute | solution.py:12
  127.3 2.1 copy-start.20
  129.4 0.9 copy-start.22
  129.4 0.9 copy-start.24
  129.4 0.9 copy-start.19
  130.3 0.8 copy-start.9
  130.3 0.9 copy-start.11
  130.3 0.9 copy-start.13
  131.4 6.1 %collective-permute-start.13 = (f32[2,1,32,128]{3,2,1,0:T(8,128)S(1)}, f32[2,1,32,128]{3,2,1,0:T(8,128)S(1)}, u32[]{:S(2)}, u32[]{:S(2)}) collective-permute-start(f32[2,1,32,128]{3,2,1,0:T(8,128)S(1)} %slice.2049), channel_id=1, source_target_pairs={{0,1},{1,2},{2,3},{3,4},{4,5},{5,6},{6,7},{8,9},{9,10},{10,11},{11... | collective-permute-start | bytes 98312 | tf_op jit(solution)/shard_map/ppermute | solution.py:12
  137.5 0.9 copy-start.4
  137.5 0.9 copy-start.14
  137.5 1.0 copy-start.15
  137.5 1.0 copy-start.16
  138.7 1.5 copy-start.32
  138.7 1.5 copy-start.33
  138.7 1.5 copy-start.34
  140.2 0.8 copy-start.17
  140.3 0.8 copy-start.37
  149.9 43.9 %collective-permute-start.14 = (f32[2,1,32,128]{3,2,1,0:T(8,128)S(1)}, f32[2,1,32,128]{3,2,1,0:T(8,128)S(1)}, u32[]{:S(2)}, u32[]{:S(2)}) collective-permute-start(f32[2,1,32,128]{3,2,1,0:T(8,128)S(1)} %slice.2063), channel_id=1, source_target_pairs={{1,0},{2,1},{3,2},{4,3},{5,4},{6,5},{7,6},{9,8},{10,9},{11,10},{12... | collective-permute-start | bytes 98312 | tf_op jit(solution)/shard_map/ppermute | solution.py:12
  194.0 6.1 %collective-permute-start.15 = (f32[2,1,32,128]{3,2,1,0:T(8,128)S(1)}, f32[2,1,32,128]{3,2,1,0:T(8,128)S(1)}, u32[]{:S(2)}, u32[]{:S(2)}) collective-permute-start(f32[2,1,32,128]{3,2,1,0:T(8,128)S(1)} %slice.2074), channel_id=1, source_target_pairs={{0,1},{1,2},{2,3},{3,4},{4,5},{5,6},{6,7},{8,9},{9,10},{10,11},{11... | collective-permute-start | bytes 98312 | tf_op jit(solution)/shard_map/ppermute | solution.py:12
  200.4 3.5 %collective-permute-start.16 = (f32[2,1,32,128]{3,2,1,0:T(8,128)S(1)}, f32[2,1,32,128]{3,2,1,0:T(8,128)S(1)}, u32[]{:S(2)}, u32[]{:S(2)}) collective-permute-start(f32[2,1,32,128]{3,2,1,0:T(8,128)S(1)} %slice.2088), channel_id=1, source_target_pairs={{1,0},{2,1},{3,2},{4,3},{5,4},{6,5},{7,6},{9,8},{10,9},{11,10},{12... | collective-permute-start | bytes 98312 | tf_op jit(solution)/shard_map/ppermute | solution.py:12
  204.1 6.1 %collective-permute-start.17 = (f32[2,1,32,128]{3,2,1,0:T(8,128)S(1)}, f32[2,1,32,128]{3,2,1,0:T(8,128)S(1)}, u32[]{:S(2)}, u32[]{:S(2)}) collective-permute-start(f32[2,1,32,128]{3,2,1,0:T(8,128)S(1)} %slice.2099), channel_id=1, source_target_pairs={{0,1},{1,2},{2,3},{3,4},{4,5},{5,6},{6,7},{8,9},{9,10},{10,11},{11... | collective-permute-start | bytes 98312 | tf_op jit(solution)/shard_map/ppermute | solution.py:12
  210.6 3.5 %collective-permute-start.18 = (f32[2,1,32,128]{3,2,1,0:T(8,128)S(1)}, f32[2,1,32,128]{3,2,1,0:T(8,128)S(1)}, u32[]{:S(2)}, u32[]{:S(2)}) collective-permute-start(f32[2,1,32,128]{3,2,1,0:T(8,128)S(1)} %slice.2113), channel_id=1, source_target_pairs={{1,0},{2,1},{3,2},{4,3},{5,4},{6,5},{7,6},{9,8},{10,9},{11,10},{12... | collective-permute-start | bytes 98312 | tf_op jit(solution)/shard_map/ppermute | solution.py:12
  214.3 6.1 %collective-permute-start.19 = (f32[2,1,32,128]{3,2,1,0:T(8,128)S(1)}, f32[2,1,32,128]{3,2,1,0:T(8,128)S(1)}, u32[]{:S(2)}, u32[]{:S(2)}) collective-permute-start(f32[2,1,32,128]{3,2,1,0:T(8,128)S(1)} %slice.2124), channel_id=1, source_target_pairs={{0,1},{1,2},{2,3},{3,4},{4,5},{5,6},{6,7},{8,9},{9,10},{10,11},{11... | collective-permute-start | bytes 98312 | tf_op jit(solution)/shard_map/ppermute | solution.py:12
  220.7 3.5 %collective-permute-start.20 = (f32[2,1,32,128]{3,2,1,0:T(8,128)S(1)}, f32[2,1,32,128]{3,2,1,0:T(8,128)S(1)}, u32[]{:S(2)}, u32[]{:S(2)}) collective-permute-start(f32[2,1,32,128]{3,2,1,0:T(8,128)S(1)} %slice.2138), channel_id=1, source_target_pairs={{1,0},{2,1},{3,2},{4,3},{5,4},{6,5},{7,6},{9,8},{10,9},{11,10},{12... | collective-permute-start | bytes 98312 | tf_op jit(solution)/shard_map/ppermute | solution.py:12
  224.5 6.1 %collective-permute-start.21 = (f32[2,1,32,128]{3,2,1,0:T(8,128)S(1)}, f32[2,1,32,128]{3,2,1,0:T(8,128)S(1)}, u32[]{:S(2)}, u32[]{:S(2)}) collective-permute-start(f32[2,1,32,128]{3,2,1,0:T(8,128)S(1)} %slice.2149), channel_id=1, source_target_pairs={{0,1},{1,2},{2,3},{3,4},{4,5},{5,6},{6,7},{8,9},{9,10},{10,11},{11... | collective-permute-start | bytes 98312 | tf_op jit(solution)/shard_map/ppermute | solution.py:12
  230.9 3.5 %collective-permute-start.22 = (f32[2,1,32,128]{3,2,1,0:T(8,128)S(1)}, f32[2,1,32,128]{3,2,1,0:T(8,128)S(1)}, u32[]{:S(2)}, u32[]{:S(2)}) collective-permute-start(f32[2,1,32,128]{3,2,1,0:T(8,128)S(1)} %slice.2163), channel_id=1, source_target_pairs={{1,0},{2,1},{3,2},{4,3},{5,4},{6,5},{7,6},{9,8},{10,9},{11,10},{12... | collective-permute-start | bytes 98312 | tf_op jit(solution)/shard_map/ppermute | solution.py:12
  234.7 6.1 %collective-permute-start.23 = (f32[2,1,32,128]{3,2,1,0:T(8,128)S(1)}, f32[2,1,32,128]{3,2,1,0:T(8,128)S(1)}, u32[]{:S(2)}, u32[]{:S(2)}) collective-permute-start(f32[2,1,32,128]{3,2,1,0:T(8,128)S(1)} %slice.2174), channel_id=1, source_target_pairs={{0,1},{1,2},{2,3},{3,4},{4,5},{5,6},{6,7},{8,9},{9,10},{10,11},{11... | collective-permute-start | bytes 98312 | tf_op jit(solution)/shard_map/ppermute | solution.py:12
  277.7 1.5 copy-start.26
  (3 other events, 1.9 us)
Sparse Core Ops, SparseCore 0:
  242.9 34.7 all-reduce.99
where the time goes:
time: 290 us; the launch traced here: 287 us
  other arithmetic  91 us (31%)
  waiting for transfers between devices  82.1 us (28%)
  starting transfers between devices  59.7 us (21%)
  local copies, waits for them, and re-layouts  37.9 us (13%)
  between operations  15.9 us (5%)
    ppermute x24, starting transfers between devices, from_behind(): return lax.ppermute(block, axis, route)  52.1 us
    scatter-add x6, other arithmetic, per_device(): source = jnp.zeros((width, depth, span), jnp.float32).at[rec_x, rec_z, re...  50 us
    ppermute x24, waiting for transfers between devices, from_behind(): return lax.ppermute(block, axis, route)  45.7 us
    psum x1, waiting for transfers between devices, per_device(): corr_eps, corr_sigma = lax.psum((corr_eps, corr_sigma), 'shot')  35 us
    scatter-add x6, other arithmetic, per_device(): source = jnp.zeros((width, depth, span), jnp.float32).at[src_x, src_z, sr...  26.7 us
    unnamed x80, local copies, waits for them, and re-layouts  10.6 us
    gather x6, local copies, waits for them, and re-layouts, per_device(): synth.append(state[0][1][rec_x, rec_z, rec_y])  10.6 us
  transfers between devices with their start and end apart: 27, of which 17 were waited for; matrix products, arithmetic and copies ran while one was open for 33% of the time, Pallas kernels for 0%

commit v1 on v0

v1 whole, which is shorter than its diff:
```python
import jax
import jax.numpy as jnp
from jax import lax
from jax.experimental import pallas as pl
from jax.experimental.pallas import tpu as pltpu
from jax.sharding import PartitionSpec as P

ROUND = 3
F32 = jnp.float32


def pair_swap(block, axis, first):
    route = []
    for i in range(first, lax.axis_size(axis) - 1, 2):
        route += [(i, i + 1), (i + 1, i)]
    return lax.ppermute(block, axis, route)


def exchange(inner, outer):
    got_outer = pair_swap(outer, "sub", 1)
    got_inner = pair_swap(inner, "sub", 0)
    return got_inner, got_outer


def shot_sum(x):
    n = lax.axis_size("shot")
    if n & (n - 1):
        return lax.psum(x, "shot")
    flip = 1
    while flip < n:
        x = x + lax.ppermute(x, "shot", [(i, i ^ flip) for i in range(n)])
        flip = 2 * flip + 1
    return x


def split_index(v, n):
    if n & (n - 1) == 0:
        return v & (n - 1), v >> (n.bit_length() - 1)
    return v % n, v // n


def ahead(u, axis):
    n = u.shape[axis]
    edge = lax.broadcasted_iota(jnp.int32, u.shape, axis) == n - 1
    return jnp.where(edge, 0.0, pltpu.roll(u, n - 1, axis))


def behind(u, axis):
    edge = lax.broadcasted_iota(jnp.int32, u.shape, axis) == 0
    return jnp.where(edge, 0.0, pltpu.roll(u, 1, axis))


def dfy(u):
    return ahead(u, 1) - u


def dfz(u):
    return ahead(u, 0) - u


def dby(u):
    return u - behind(u, 1)


def dbz(u):
    return u - behind(u, 0)


def h_step(h, e, e_next, keep=None, parts=(0, 1, 2)):
    ex, ey, ez = e
    new = {}
    if 0 in parts:
        new[0] = h[0] - 0.5 * (dfy(ez) - dfz(ey))
    ny, nz = e_next[1], e_next[2]
    if keep is not None:
        ny, nz = ny * keep, nz * keep
    new[1] = h[1] - 0.5 * (dfz(ex) - (nz - ez))
    new[2] = h[2] - 0.5 * ((ny - ey) - dfy(ex))
    return new


def e_step(e, h, h_prev, p, coef, inject, parts=(0, 1, 2)):
    ca, cb = coef[0], coef[1]
    new = {}
    for c in parts:
        if c == 0:
            curl = dby(h[2]) - dbz(h[1])
        elif c == 1:
            curl = dbz(h[0]) - (h[2] - h_prev[2])
        else:
            curl = (h[1] - h_prev[1]) - dby(h[0])
        new[c] = ca * e[c] + cb * (curl - p[c])
        if c == 1:
            new[c] = new[c] + inject
    return new


def p_step(p, e_new, coef):
    return {c: coef[2] * p[c] + coef[3] * e_new[c] for c in e_new}


class Planes:
    def __init__(self):
        self.at = {}

    def put(self, key, ref, *idx):
        self.at[key] = (ref, idx)

    def get(self, kind, c, i):
        ref, idx = self.at[kind, c, i]
        return ref[idx]

    def triple(self, kind, i, parts=(0, 1, 2)):
        return {c: self.get(kind, c, i) for c in parts}


def pick(even, a_ref, b_ref, k, low):
    a, b = a_ref[k], b_ref[k]
    return jnp.where(even, b, a) if low else jnp.where(even, a, b)


def emit(even, a_ref, b_ref, k, right, left):
    if right is None:
        right = left
    if left is None:
        left = right
    a_ref[k] = jnp.where(even, right, left)
    b_ref[k] = jnp.where(even, left, right)


def pre_steps(planes, coef_of, inject):
    h1, e1 = {}, {}
    last = planes.last
    sides = (0, 1, 2) if last <= 3 else (0, 1, last - 2, last - 1)
    for i in sides:
        e = [planes.get("E", c, i) for c in range(3)]
        nxt = {c: planes.get("E", c, i + 1) for c in (1, 2)}
        h1[i] = h_step(planes.triple("H", i), e, nxt)
    for i in (1, last - 1):
        parts = (0, 1, 2) if i == last - 1 else (1, 2)
        e1[i] = e_step(planes.triple("E", i), h1[i], h1[i - 1], planes.triple("P", i), coef_of(i), inject(i), parts)
    return h1, e1


def emit_state(even, planes, h1, e1, a_ref, b_ref, full):
    last = planes.last
    right = [planes.get("E", c, last) for c in range(3)]
    right += [h1[last - 1][1], h1[last - 1][2]] + [e1[last - 1][c] for c in range(3)]
    left = [planes.get("E", c, 0) for c in range(3)]
    left += [h1[0][c] for c in range(3)] + [e1[1][1], e1[1][2]]
    if full:
        right += [planes.get("P", c, last) for c in range(3)] + [planes.get("H", c, last) for c in range(3)]
        left += [planes.get("P", c, 0) for c in range(3)] + [None] * 3
    for k, (r, l) in enumerate(zip(right, left)):
        emit(even, a_ref, b_ref, k, r, l)


def own_planes(e_ref, h_ref, p_ref, h_at=0, p_at=0):
    planes = Planes()
    width = e_ref.shape[1]
    planes.last = width - 1
    for i in range(width):
        for c in range(3):
            planes.put(("E", c, i), e_ref, c, i)
            planes.put(("H", c, i), h_ref, c, i + h_at)
            planes.put(("P", c, i), p_ref, c, i + p_at)
    return planes


def source_map(cell_ref, sign_ref, mine, width, depth, span, full_x):
    flat = cell_ref[...]
    x, rest = split_index(flat, full_x)
    y, z = split_index(rest, span)
    row = (x - (mine * width - 1)) * depth + z
    rows = (width + 2) * depth
    n = flat.shape[1]
    hot = lax.broadcasted_iota(jnp.int32, (rows, n), 0) == row
    amp = (2 * sign_ref[...] - 1).astype(F32)
    where_y = lax.broadcasted_iota(jnp.int32, (span, n), 0) == y
    left = jnp.where(hot, 1.0, 0.0).astype(jnp.bfloat16)
    right = jnp.where(where_y, amp, 0.0).astype(jnp.bfloat16)
    return lax.dot_general(left, right, (((1,), (1,)), ((), ())), preferred_element_type=F32)


def first_kernel(full_x, meta, rate_t, strength_t, wavelet, e_ref, h_ref, p_ref, perm, cond, cls, cells, signs,
                 coef_ref, src_ref, a_ref, b_ref):
    even = meta[1] == 0
    width, depth, span = perm.shape
    src = source_map(cells, signs, meta[0], width, depth, span, full_x)
    src_ref[...] = src.reshape(width + 2, depth, span)
    for i in range(width):
        ratio = cond[i] / (2.0 * perm[i])
        coef_ref[0, i] = (1.0 - ratio) / (1.0 + ratio)
        coef_ref[1, i] = 0.5 / (perm[i] * (1.0 + ratio))
        kind = cls[i]
        rate = jnp.zeros((depth, span), F32)
        gain = jnp.zeros((depth, span), F32)
        for k in range(rate_t.shape[0]):
            rate = jnp.where(kind == k, rate_t[k], rate)
            gain = jnp.where(kind == k, (1.0 - rate_t[k]) * strength_t[k], gain)
        coef_ref[2, i] = rate
        coef_ref[3, i] = gain
    planes = own_planes(e_ref, h_ref, p_ref)
    h1, e1 = pre_steps(planes, lambda i: [coef_ref[k, i] for k in range(4)], lambda i: src_ref[i + 1] * wavelet[0])
    emit_state(even, planes, h1, e1, a_ref, b_ref, True)
    last = width - 1
    emit(even, a_ref, b_ref, 14, coef_ref[0, last], coef_ref[0, 0])
    emit(even, a_ref, b_ref, 15, coef_ref[1, last], coef_ref[1, 0])
    emit(even, a_ref, b_ref, 16, cls[last].astype(F32), cls[0].astype(F32))


def adjoint_first_kernel(meta, e_ref, h_ref, p_ref, coef_ref, a_ref, b_ref):
    planes = own_planes(e_ref, h_ref, p_ref)
    h1, e1 = pre_steps(planes, lambda i: [coef_ref[k, i] for k in range(4)], lambda i: 0.0)
    emit_state(meta[1] == 0, planes, h1, e1, a_ref, b_ref, True)


def receiver_kernel(meta, width, depth, got, maps_ref, acc):
    mine = meta[0]
    rows = (width + 2) * depth
    span = acc.shape[2]
    blocks, lists, n = got.shape
    steps = lists - 2
    acc[...] = jnp.zeros(acc.shape, F32)

    def block(b, carry):
        row = got[b, 0:1, :] - ((mine * width - 1) * depth).astype(F32)
        y = got[b, 1:2, :]
        hot = lax.broadcasted_iota(jnp.int32, (rows, n), 0).astype(F32) == row
        left = jnp.where(hot, 1.0, 0.0).astype(jnp.bfloat16)
        left3 = jnp.concatenate([left, left, left], axis=1)
        at_y = lax.broadcasted_iota(jnp.int32, (span, n), 0).astype(F32) == y
        one = jnp.where(at_y, 1.0, 0.0).astype(jnp.bfloat16)
        dims = (((1,), (1,)), ((), ()))
        acc[0] += lax.dot_general(left, one, dims, preferred_element_type=F32)
        for s in range(steps):
            v = got[b, 2 + s:3 + s, :]
            high = v.astype(jnp.bfloat16).astype(F32)
            mid = (v - high).astype(jnp.bfloat16).astype(F32)
            low = (v - high) - mid
            parts = [jnp.where(at_y, u, 0.0).astype(jnp.bfloat16) for u in (high, mid, low)]
            right = jnp.concatenate(parts, axis=1)
            acc[1 + s] += lax.dot_general(left3, right, dims, preferred_element_type=F32)
        return carry

    lax.fori_loop(0, blocks, block, 0)
    maps_ref[...] = acc[...].reshape(maps_ref.shape)


def round_body(planes, meta, coef_ref, coefh_ref, a_ref, b_ref, full, inject, first_extra, dest, prestep, seen):
    even = meta[1] == 0
    keep = jnp.where(meta[0] > 0, 1.0, 0.0).astype(F32)
    last = planes.last
    w = last + 1

    def low(k):
        return pick(even, a_ref, b_ref, k, True)

    def high(k):
        return pick(even, a_ref, b_ref, k, False)

    def coef_of(i):
        if i == -1:
            return [coefh_ref[0, k] for k in range(4)]
        if i == w:
            return [coefh_ref[1, k] for k in range(4)]
        return [coef_ref[k, i] for k in range(4)]

    held = {}
    for c in range(3):
        held["E", c, -1] = low(c)
        held["E", c, w] = high(c)
        held["H", c, w] = high(3 + c)
    held["H", 1, -2], held["H", 2, -2] = low(3), low(4)
    if full:
        for c in range(3):
            held["P", c, -1] = low(8 + c)
            held["H", c, -1] = low(11 + c)
            held["P", c, w] = high(8 + c)
    else:
        for i in (-1, w):
            cf = coef_of(i)
            for c in range(3):
                held["P", c, i] = cf[2] * planes.get("P", c, i) + cf[3] * held["E", c, i]

    def get(kind, c, i):
        if (kind, c, i) in held:
            return held[kind, c, i]
        return planes.get(kind, c, i)

    def store(kind, c, i, level, value):
        held.pop((kind, c, i), None)
        ref, idx = dest(kind, c, i, level)
        ref[idx] = value
        planes.put((kind, c, i), ref, *idx)

    for level in (1, 2, 3):
        if level == 2:
            for c in range(3):
                v = low(5 + c)
                if c == 1 and first_extra is not None:
                    v = v + first_extra(-2)
                held["E", c, -2] = v
            for c in (1, 2):
                v = high(5 + c)
                if c == 1 and first_extra is not None:
                    v = v + first_extra(w + 1)
                held["E", c, w + 1] = v
        h_lo = {1: -1, 2: -2, 3: -1}[level]
        h_hi = {1: last, 2: w, 3: last}[level]
        e_lo, e_hi = (0, last) if level == 3 else (-1, w)
        h_prev = None
        if h_lo > e_lo - 1:
            h_prev = {c: get("H", c, e_lo - 1) for c in (1, 2)}
        for i in range(h_lo, max(h_hi, e_hi) + 1):
            e = [get("E", c, i) for c in range(3)]
            if i <= h_hi:
                parts = (1, 2) if i == -2 else (0, 1, 2)
                h = h_step({c: get("H", c, i) for c in parts}, e, {c: get("E", c, i + 1) for c in (1, 2)},
                           keep if i == -1 else None, parts)
                for c in parts:
                    store("H", c, i, level, h[c])
            else:
                h = {c: get("H", c, i) for c in range(3)}
            if e_lo <= i <= e_hi:
                p = {c: get("P", c, i) for c in range(3)}
                cf = coef_of(i)
                new = e_step(e, h, h_prev, p, cf, inject(level, i))
                pn = p_step(p, new, cf)
                for c in range(3):
                    store("E", c, i, level, new[c])
                    store("P", c, i, level, pn[c])
                if seen is not None:
                    seen(level, i, new)
            h_prev = h
    if prestep is None:
        return
    h1, e1 = pre_steps(planes, coef_of, lambda i: inject(4, i))
    emit_state(even, planes, h1, e1, prestep[0], prestep[1], False)


def scratch_dest(es, hs, ps, own_e=None, width=4):
    def dest(kind, c, i, level):
        if kind == "E":
            if own_e is not None and 0 <= i < width:
                return own_e, (level - 1, c, i)
            return es, (c, i + 1)
        if kind == "H":
            return hs, (c, i + 2)
        return ps, (c, i + 1)

    return dest


def forward_one_kernel(meta, rate_t, strength_t, wavelet, e_ref, h_ref, p_ref, coef_ref, src_ref, a_ref, b_ref,
                       hist_ref, hs_ref, ps_ref, coefh_ref, eyh_ref, oa_ref, ob_ref, es_ref):
    even = meta[1] == 0
    width = e_ref.shape[1]
    for side in (0, 1):
        coefh_ref[side, 0] = pick(even, a_ref, b_ref, 14, side == 0)
        coefh_ref[side, 1] = pick(even, a_ref, b_ref, 15, side == 0)
        kind = pick(even, a_ref, b_ref, 16, side == 0)
        rate = jnp.zeros(kind.shape, F32)
        gain = jnp.zeros(kind.shape, F32)
        for k in range(rate_t.shape[0]):
            rate = jnp.where(kind == float(k), rate_t[k], rate)
            gain = jnp.where(kind == float(k), (1.0 - rate_t[k]) * strength_t[k], gain)
        coefh_ref[side, 2] = rate
        coefh_ref[side, 3] = gain
    planes = own_planes(e_ref, h_ref, p_ref)

    def seen(level, i, e):
        if level == 2 and i in (-1, width):
            eyh_ref[0 if i < 0 else 1] = e[1]

    round_body(planes, meta, coef_ref, coefh_ref, a_ref, b_ref, True,
               lambda level, i: src_ref[i + 1] * wavelet[level - 1], None,
               scratch_dest(es_ref, hs_ref, ps_ref, hist_ref, width), (oa_ref, ob_ref), seen)


def state_planes(e_ref, hs_ref, ps_ref, level=None):
    planes = Planes()
    width = e_ref.shape[-3]
    planes.last = width - 1
    for c in range(3):
        for i in range(width):
            if level is None:
                planes.put(("E", c, i), e_ref, c, i + 0)
            else:
                planes.put(("E", c, i), e_ref, level, c, i)
        for i in range(-1, width):
            planes.put(("H", c, i), hs_ref, c, i + 2)
        for i in range(-1, width + 1):
            planes.put(("P", c, i), ps_ref, c, i + 1)
    return planes


def forward_two_kernel(meta, wavelet, hist_in, hs_in, ps_in, coef_ref, coefh_ref, src_ref, maps_ref, a_ref, b_ref,
                       hist_ref, eyh_ref, oa_ref, ob_ref, es_ref, hs_ref, ps_ref):
    even = meta[1] == 0
    width = hist_in.shape[2]
    planes = state_planes(hist_in, hs_in, ps_in, 2)
    eyh_ref[0] = pick(even, a_ref, b_ref, 1, True)
    eyh_ref[1] = pick(even, a_ref, b_ref, 1, False)

    def seen(level, i, e):
        if level == 2 and i in (-1, width):
            eyh_ref[2 if i < 0 else 3] = e[1]

    round_body(planes, meta, coef_ref, coefh_ref, a_ref, b_ref, False,
               lambda level, i: src_ref[i + 1] * wavelet[ROUND + level - 1], None,
               scratch_dest(es_ref, hs_ref, ps_ref, hist_ref, width), None, seen)
    steps = 2 * ROUND

    def resid(i):
        return maps_ref[0, i + 1] * hist_ref[2, 1, i] - maps_ref[steps, i + 1]

    last = width - 1
    emit(even, oa_ref, ob_ref, 0, resid(last), resid(0))
    emit(even, oa_ref, ob_ref, 1, resid(last - 1), resid(1))


def correlate(corr_ref, i, b, now, prev, add):
    eps = b[0] * (now[0] - prev[0]) + b[1] * (now[1] - prev[1]) + b[2] * (now[2] - prev[2])
    sig = b[0] * now[0] + b[1] * now[1] + b[2] * now[2]
    if add is not None:
        eps, sig = eps + add[0, i], sig + add[1, i]
    corr_ref[0, i] = eps
    corr_ref[1, i] = sig


def adjoint_one_kernel(meta, e_ref, h_ref, p_ref, coef_ref, coefh_ref, maps_ref, hist1_ref, hist2_ref, eyh_ref,
                       a_ref, b_ref, ra_ref, rb_ref, e_out, hs_ref, ps_ref, corr_ref, oa_ref, ob_ref, es_ref):
    even = meta[1] == 0
    width = e_ref.shape[1]
    steps = 2 * ROUND
    planes = own_planes(e_ref, h_ref, p_ref)

    def ey(n, i):
        if 0 <= i < width:
            return hist1_ref[n - 1, 1, i] if n <= ROUND else hist2_ref[n - 1 - ROUND, 1, i]
        at = {3: 0, 5: 2}[n]
        return eyh_ref[at if i < 0 else at + 1]

    def extra(i):
        if i < 0:
            return pick(even, ra_ref, rb_ref, -1 - i, True)
        return pick(even, ra_ref, rb_ref, i - width, False)

    def inject(level, i):
        n = steps + 1 - level
        if n == steps and not 0 <= i < width:
            return extra(i)
        return maps_ref[0, i + 1] * ey(n, i) - maps_ref[n, i + 1]

    def seen(level, i, e):
        if not 0 <= i < width:
            return
        n = steps + 1 - level
        now = [hist2_ref[n - 1 - ROUND, c, i] for c in range(3)]
        prev = [hist2_ref[n - 2 - ROUND, c, i] if n - 1 > ROUND else hist1_ref[n - 2, c, i] for c in range(3)]
        correlate(corr_ref, i, e, now, prev, corr_ref if level > 1 else None)

    def dest(kind, c, i, level):
        if kind == "E":
            if 0 <= i < width:
                return e_out, (c, i)
            return es_ref, (c, i + 1)
        if kind == "H":
            return hs_ref, (c, i + 2)
        return ps_ref, (c, i + 1)

    round_body(planes, meta, coef_ref, coefh_ref, a_ref, b_ref, True, inject, extra, dest, (oa_ref, ob_ref), seen)


def adjoint_two_kernel(meta, e_ref, hs_in, ps_in, coef_ref, coefh_ref, maps_ref, e0_ref, hist1_ref, ey2_ref, eyh_ref,
                       corr_in, a_ref, b_ref, corr_ref, es_ref, hs_ref, ps_ref):
    width = e_ref.shape[1]
    steps = 2 * ROUND
    planes = state_planes(e_ref, hs_in, ps_in)

    def ey(n, i):
        if 0 <= i < width:
            return hist1_ref[n - 1, 1, i]
        if n == 3:
            return eyh_ref[0 if i < 0 else 1]
        return ey2_ref[0 if i < 0 else 1]

    def inject(level, i):
        n = steps + 1 - ROUND - level
        return maps_ref[0, i + 1] * ey(n, i) - maps_ref[n, i + 1]

    def seen(level, i, e):
        if not 0 <= i < width:
            return
        n = steps + 1 - ROUND - level
        now = [hist1_ref[n - 1, c, i] for c in range(3)]
        prev = [hist1_ref[n - 2, c, i] if n > 1 else e0_ref[c, i] for c in range(3)]
        correlate(corr_ref, i, e, now, prev, corr_ref if level > 1 else corr_in)

    round_body(planes, meta, coef_ref, coefh_ref, a_ref, b_ref, False, inject, None,
               scratch_dest(es_ref, hs_ref, ps_ref), None, seen)


def call(body, name, inputs, scalars, outs, scratch=()):
    smem = pl.BlockSpec(memory_space=pltpu.SMEM)
    vmem = pl.BlockSpec(memory_space=pltpu.VMEM)
    return pl.pallas_call(
        body,
        name=name,
        out_shape=[jax.ShapeDtypeStruct(s, F32) for s in outs],
        in_specs=[smem] * len(scalars) + [vmem] * len(inputs),
        out_specs=[vmem] * len(outs),
        scratch_shapes=[pltpu.VMEM(s, F32) for s in scratch],
        compiler_params=pltpu.CompilerParams(vmem_limit_bytes=48 * 1024 * 1024),
    )(*scalars, *inputs)


def per_device(
    electric,
    magnetic,
    polar,
    adj_electric,
    adj_magnetic,
    adj_polar,
    permittivity,
    conductivity,
    debye_class,
    debye_rate,
    debye_strength,
    wavelet,
    src_cell,
    src_sign,
    rec_owner,
    rec_pos,
    observed,
):
    width, depth, span = permittivity.shape
    steps = wavelet.shape[0]
    nsub = lax.axis_size("sub")
    nshot = lax.axis_size("shot")
    mine = lax.axis_index("sub")
    meta = jnp.stack([mine, mine % 2]).astype(jnp.int32)
    plane = (depth, span)

    in_x, rest = split_index(rec_pos[0], width)
    rec_y, rec_z = split_index(rest, span)
    rec_row = (rec_owner[0, :, 0] * width + in_x) * depth + rec_z
    listed = jnp.concatenate([rec_row[None].astype(F32), rec_y[None].astype(F32), observed[0]], axis=0)
    got = lax.all_gather(listed, "sub")

    fields = (electric[0], magnetic[0], polar[0])
    adjoint = (adj_electric[0], adj_magnetic[0], adj_polar[0])

    coef, src, a1, b1 = call(
        lambda *refs: first_kernel(width * nsub, *refs),
        "first",
        [*fields, permittivity, conductivity, debye_class, src_cell, src_sign],
        [meta, debye_rate, debye_strength, wavelet],
        [(4, width, *plane), (width + 2, *plane), (17, *plane), (17, *plane)],
    )
    got_a1, got_b1 = exchange(a1, b1)
    a3, b3 = call(adjoint_first_kernel, "adjoint_first", [*adjoint, coef], [meta], [(14, *plane), (14, *plane)])
    (maps,) = call(
        lambda meta_ref, *refs: receiver_kernel(meta_ref, width, depth, *refs),
        "receivers",
        [got],
        [meta],
        [(steps + 1, width + 2, *plane)],
        [(steps + 1, (width + 2) * depth, span)],
    )
    e_sh, h_sh, p_sh = (3, width + 2, *plane), (3, width + 3, *plane), (3, width + 2, *plane)
    hist1, hs, ps, coefh, ey2, a2, b2 = call(
        forward_one_kernel,
        "forward_one",
        [*fields, coef, src, got_a1, got_b1],
        [meta, debye_rate, debye_strength, wavelet],
        [(ROUND, 3, width, *plane), h_sh, p_sh, (2, 4, *plane), (2, *plane), (8, *plane), (8, *plane)],
        [e_sh],
    )
    got_a2, got_b2 = exchange(a2, b2)
    got_a3, got_b3 = exchange(a3, b3)
    hist2, eyh, a4, b4 = call(
        forward_two_kernel,
        "forward_two",
        [hist1, hs, ps, coef, coefh, src, maps, got_a2, got_b2],
        [meta, wavelet],
        [(ROUND, 3, width, *plane), (4, *plane), (2, *plane), (2, *plane)],
        [e_sh, h_sh, p_sh],
    )
    got_a4, got_b4 = exchange(a4, b4)
    e_adj, hs, ps, corr, a5, b5 = call(
        adjoint_one_kernel,
        "adjoint_one",
        [*adjoint, coef, coefh, maps, hist1, hist2, eyh, got_a3, got_b3, got_a4, got_b4],
        [meta],
        [(3, width, *plane), h_sh, p_sh, (2, width, *plane), (8, *plane), (8, *plane)],
        [e_sh],
    )
    got_a5, got_b5 = exchange(a5, b5)
    (corr,) = call(
        adjoint_two_kernel,
        "adjoint_two",
        [e_adj, hs, ps, coef, coefh, maps, fields[0], hist1, ey2, eyh, corr, got_a5, got_b5],
        [meta],
        [(2, width, *plane)],
        [e_sh, h_sh, p_sh],
    )
    total = shot_sum(corr)
    return (-(total[0] / (steps * nshot)), -(total[1] / (steps * nshot)))


def solution(mesh):
    in_specs = (
        P("shot", None, "sub", None, None),
        P("shot", None, "sub", None, None),
        P("shot", None, "sub", None, None),
        P("shot", None, "sub", None, None),
        P("shot", None, "sub", None, None),
        P("shot", None, "sub", None, None),
        P("sub", None, None),
        P("sub", None, None),
        P("sub", None, None),
        P(),
        P(),
        P(),
        P("shot", None),
        P("shot", None),
        P("shot", "sub", None),
        P("shot", "sub"),
        P("shot", None, "sub"),
    )
    out_specs = (P("sub", None, None), P("sub", None, None))
    return jax.shard_map(
        per_device, mesh=mesh, in_specs=in_specs, out_specs=out_specs, check_vma=False
    )
```

time: 290 us -> 70.1 us (0.24)
  the two profiles are of different devices: /device:TPU:4 before, /device:TPU:18 now
where the time goes in v1:
time: 70.1 us; the launch traced here: 69.6 us
  waiting for transfers between devices  21.9 us (31%)
  starting transfers between devices  19.4 us (28%)
  Pallas kernels  11.3 us (16%)
  blocking collectives  9.29 us (13%)
  local copies, waits for them, and re-layouts  6.03 us (9%)
  between operations  0.9 us (1%)
  other arithmetic  0.79 us (1%)
    ppermute x10, starting transfers between devices, pair_swap(): return lax.ppermute(block, axis, route)  17.3 us
    ppermute x2, waiting for transfers between devices, shot_sum(): x = x + lax.ppermute(x, 'shot', [(i, i ^ flip) for i in range(n)])  12.7 us
    pallas_call x7, Pallas kernels, call(): pl.pallas_call(body, name=name, out_shape=[jax.ShapeDtypeStruct(s, F32) f...  11.3 us
    all_gather x1, blocking collectives, per_device(): got = lax.all_gather(listed, 'sub')  9.29 us
    ppermute x10, waiting for transfers between devices, pair_swap(): return lax.ppermute(block, axis, route)  9.19 us
    unnamed x37, local copies, waits for them, and re-layouts  6.03 us
    ppermute x2, starting transfers between devices, shot_sum(): x = x + lax.ppermute(x, 'shot', [(i, i ^ flip) for i in range(n)])  2.15 us
  transfers between devices with their start and end apart: 12, of which 5 were waited for; matrix products, arithmetic and copies ran while one was open for 0% of the time, Pallas kernels for 11%

profile of v1, /device:TPU:18, one launch (start us, length us, event | category | flops | bytes accessed | tf_op | source)
XLA Modules:
  0.0 69.6 jit_solution(5192528497718988761)
XLA Ops:
  0.6 0.1 pad_add_fusion.refs_0_.meta.meta_ref
  0.7 0.0 copy-start.13
  0.7 0.0 copy-start.14
  0.7 0.0 copy-start.10
  0.7 0.0 copy-start.11
  0.7 0.0 copy-start.12
  0.7 0.6 copy-done.13
  1.4 0.0 copy-done.14
  1.4 0.0 copy-done.10
  1.4 0.0 copy-done.11
  1.4 0.0 copy-done.12
  1.4 0.0 copy-start
  1.4 0.9 %copy-done = f32[1,3,4,32,128]{4,3,2,1,0:T(8,128)S(1)} copy-done((f32[1,3,4,32,128]{4,3,2,1,0:T(8,128)S(1)}, f32[1,3,4,32,128]{4,3,2,1,0:T(8,128)}, u32[]{:S(2)}) %copy-start) | copy-done | bytes 196632
  2.4 0.0 copy-start.5
  2.4 0.9 %copy-done.5 = f32[1,3,4,32,128]{4,3,2,1,0:T(8,128)S(1)} copy-done((f32[1,3,4,32,128]{4,3,2,1,0:T(8,128)S(1)}, f32[1,3,4,32,128]{4,3,2,1,0:T(8,128)}, u32[]{:S(2)}) %copy-start.5) | copy-done | bytes 196632
  3.3 0.0 copy-start.6
  3.3 0.9 %copy-done.6 = f32[1,3,4,32,128]{4,3,2,1,0:T(8,128)S(1)} copy-done((f32[1,3,4,32,128]{4,3,2,1,0:T(8,128)S(1)}, f32[1,3,4,32,128]{4,3,2,1,0:T(8,128)}, u32[]{:S(2)}) %copy-start.6) | copy-done | bytes 196632
  4.2 0.0 copy-start.7
  4.2 0.8 %copy-done.7 = f32[4,32,128]{2,1,0:T(8,128)S(1)} copy-done((f32[4,32,128]{2,1,0:T(8,128)S(1)}, f32[4,32,128]{2,1,0:T(8,128)}, u32[]{:S(2)}) %copy-start.7) | copy-done | bytes 65560
  5.1 0.0 copy-start.8
  5.1 0.8 %copy-done.8 = f32[4,32,128]{2,1,0:T(8,128)S(1)} copy-done((f32[4,32,128]{2,1,0:T(8,128)S(1)}, f32[4,32,128]{2,1,0:T(8,128)}, u32[]{:S(2)}) %copy-start.8) | copy-done | bytes 65560
  5.9 0.8 %copy-done.9 = s32[4,32,128]{2,1,0:T(8,128)S(1)} copy-done((s32[4,32,128]{2,1,0:T(8,128)S(1)}, s32[4,32,128]{2,1,0:T(8,128)}, u32[]{:S(2)}) %copy-start.9) | copy-done | bytes 65560
  6.7 0.8 %first.1 = (f32[4,4,32,128]{3,2,1,0:T(8,128)S(1)}, f32[6,32,128]{2,1,0:T(8,128)S(1)}, f32[17,32,128]{2,1,0:T(8,128)S(1)}, f32[17,32,128]{2,1,0:T(8,128)S(1)}) custom-call(s32[2]{0:T(128)S(1)} %pad_add_fusion.refs_0_.meta.meta_ref, f32[8]{0:T(128)S(1)} %copy-done.11, f32[8]{0:T(128)S(1)} %copy-done.12, f32[6]{0:T(128)S(1)} %copy-done.10, ...), custom_call_target="tpu_custom_call" | custom-call | tf_op jit(solution)/shard_map/first/pallas_call | solution.py:508
  7.5 0.1 collective-permute-start
  7.6 2.5 %collective-permute-start.1 = (f32[17,32,128]{2,1,0:T(8,128)S(1)}, f32[17,32,128]{2,1,0:T(8,128)S(1)}, u32[]{:S(2)}, u32[]{:S(2)}) collective-permute-start(f32[17,32,128]{2,1,0:T(8,128)S(1)} %get-tuple-element.28), channel_id=1, source_target_pairs={{1,2},{2,1},{3,4},{4,3},{5,6},{6,5},{9,10},{10,9},{11,12},{12,11},... | collective-permute-start | bytes 835592 | tf_op jit(solution)/shard_map/ppermute | solution.py:16
  10.1 0.0 copy-done.2
  10.2 0.0 copy-done.3
  10.2 0.0 copy-done.4
  10.2 0.7 %adjoint_first.1 = (f32[14,32,128]{2,1,0:T(8,128)S(1)}, f32[14,32,128]{2,1,0:T(8,128)S(1)}) custom-call(s32[2]{0:T(128)S(1)} %pad_add_fusion.refs_0_.meta.meta_ref, f32[3,4,32,128]{3,2,1,0:T(8,128)S(1)} %bitcast.27, f32[3,4,32,128]{3,2,1,0:T(8,128)S(1)} %bitcast.29, f32[3,4,32,128]{3,2,1,0:T(8,128)S(1)} %bitcast.31, ...), custom_call_target="tpu_custom_call" | custom-call | tf_op jit(solution)/shard_map/adjoint_first/pallas_call | solution.py:508
  10.9 1.0 %collective-permute-start.4 = (f32[14,32,128]{2,1,0:T(8,128)S(1)}, f32[14,32,128]{2,1,0:T(8,128)S(1)}, u32[]{:S(2)}, u32[]{:S(2)}) collective-permute-start(f32[14,32,128]{2,1,0:T(8,128)S(1)} %get-tuple-element.37), channel_id=1, source_target_pairs={{0,1},{1,0},{2,3},{3,2},{4,5},{5,4},{6,7},{7,6},{8,9},{9,8},{10,11... | collective-permute-start | bytes 688136 | tf_op jit(solution)/shard_map/ppermute | solution.py:16
  11.9 2.1 %collective-permute-start.5 = (f32[14,32,128]{2,1,0:T(8,128)S(1)}, f32[14,32,128]{2,1,0:T(8,128)S(1)}, u32[]{:S(2)}, u32[]{:S(2)}) collective-permute-start(f32[14,32,128]{2,1,0:T(8,128)S(1)} %get-tuple-element.38), channel_id=1, source_target_pairs={{1,2},{2,1},{3,4},{4,3},{5,6},{6,5},{9,10},{10,9},{11,12},{12,11},... | collective-permute-start | bytes 688136 | tf_op jit(solution)/shard_map/ppermute | solution.py:16
  14.0 0.0 collective-permute-done.a_ref
  14.0 2.9 %collective-permute-done.1.b_ref = f32[17,32,128]{2,1,0:T(8,128)S(1)} collective-permute-done((f32[17,32,128]{2,1,0:T(8,128)S(1)}, f32[17,32,128]{2,1,0:T(8,128)S(1)}, u32[]{:S(2)}, u32[]{:S(2)}) %collective-permute-start.1) | collective-permute-done | bytes 278560 | tf_op jit(solution)/shard_map/ppermute | solution.py:16
  16.9 1.4 %forward_one.1 = (f32[3,3,4,32,128]{4,3,2,1,0:T(8,128)S(1)}, f32[3,7,32,128]{3,2,1,0:T(8,128)S(1)}, f32[3,6,32,128]{3,2,1,0:T(8,128)S(1)}, f32[2,4,32,128]{3,2,1...) custom-call(s32[2]{0:T(128)S(1)} %pad_add_fusion.refs_0_.meta.meta_ref, ...), custom_call_target="tpu_custom_call" | custom-call | tf_op jit(solution)/shard_map/forward_one/pallas_call | solution.py:508
  18.3 0.0 copy-start.15
  18.3 0.0 copy-start.16
  18.3 3.0 %collective-permute-start.2 = (f32[8,32,128]{2,1,0:T(8,128)S(1)}, f32[8,32,128]{2,1,0:T(8,128)S(1)}, u32[]{:S(2)}, u32[]{:S(2)}) collective-permute-start(f32[8,32,128]{2,1,0:T(8,128)S(1)} %get-tuple-element.33), channel_id=1, source_target_pairs={{0,1},{1,0},{2,3},{3,2},{4,5},{5,4},{6,7},{7,6},{8,9},{9,8},{10,11... | collective-permute-start | bytes 393224 | tf_op jit(solution)/shard_map/ppermute | solution.py:16
  21.3 1.9 %collective-permute-start.3 = (f32[8,32,128]{2,1,0:T(8,128)S(1)}, f32[8,32,128]{2,1,0:T(8,128)S(1)}, u32[]{:S(2)}, u32[]{:S(2)}) collective-permute-start(f32[8,32,128]{2,1,0:T(8,128)S(1)} %get-tuple-element.34), channel_id=1, source_target_pairs={{1,2},{2,1},{3,4},{4,3},{5,6},{6,5},{9,10},{10,9},{11,12},{12,11},... | collective-permute-start | bytes 393224 | tf_op jit(solution)/shard_map/ppermute | solution.py:16
  23.2 0.0 copy-done.17
  23.2 0.0 copy-done.16
  23.2 0.0 copy-done.15
  23.3 9.3 %all-gather = f32[64,128]{1,0:T(8,128)S(1)} all-gather(f32[8,128]{1,0:T(8,128)S(1)} %pad_maximum_fusion), channel_id=2, replica_groups=mesh['shot'=4,'sub'=8] {'sub'}, dimensions={0}, use_global_device_ids=true | all-gather | bytes 36864 | tf_op jit(solution)/shard_map/all_gather | solution.py:550
  32.6 4.1 %receivers.1.maps_ref = f32[7,6,32,128]{3,2,1,0:T(8,128)S(1)} custom-call(s32[2]{0:T(128)S(1)} %pad_add_fusion.refs_0_.meta.meta_ref, f32[8,8,128]{2,1,0:T(8,128)S(1)} %bitcast.37), custom_call_target="tpu_custom_call" | custom-call | tf_op jit(solution)/shard_map/receivers/pallas_call | solution.py:508
  36.7 0.0 collective-permute-done.2.a_ref
  36.7 0.0 collective-permute-done.3.b_ref
  36.7 1.3 %forward_two.1 = (f32[3,3,4,32,128]{4,3,2,1,0:T(8,128)S(1)}, f32[4,32,128]{2,1,0:T(8,128)S(1)}, f32[2,32,128]{2,1,0:T(8,128)S(1)}, f32[2,32,128]{2,1,0:T(8,128)S(1)}) custom-call(s32[2]{0:T(128)S(1)} %pad_add_fusion.refs_0_.meta.meta_ref, f32[6]{0:T(128)S(1)} %copy-done.10, f32[3,3,4,32,128]{4,3,2,1,0:T(8,128)S(1)} %get-tuple-element.30.hist_in.hist1_ref, ...), custom_call_target="tpu_custom_call" | custom-call | tf_op jit(solution)/shard_map/forward_two/pallas_call | solution.py:508
  38.0 0.4 collective-permute-start.6
  38.4 3.1 %collective-permute-start.7 = (f32[2,32,128]{2,1,0:T(8,128)S(1)}, f32[2,32,128]{2,1,0:T(8,128)S(1)}, u32[]{:S(2)}, u32[]{:S(2)}) collective-permute-start(f32[2,32,128]{2,1,0:T(8,128)S(1)} %get-tuple-element.40), channel_id=1, source_target_pairs={{1,2},{2,1},{3,4},{4,3},{5,6},{6,5},{9,10},{10,9},{11,12},{12,11},... | collective-permute-start | bytes 98312 | tf_op jit(solution)/shard_map/ppermute | solution.py:16
  41.5 0.0 collective-permute-done.4.a_ref
  41.5 0.0 collective-permute-done.5.b_ref
  41.5 0.0 collective-permute-done.6.ra_ref
  41.5 2.1 %collective-permute-done.7.rb_ref = f32[2,32,128]{2,1,0:T(8,128)S(1)} collective-permute-done((f32[2,32,128]{2,1,0:T(8,128)S(1)}, f32[2,32,128]{2,1,0:T(8,128)S(1)}, u32[]{:S(2)}, u32[]{:S(2)}) %collective-permute-start.7) | collective-permute-done | bytes 32800 | tf_op jit(solution)/shard_map/ppermute | solution.py:16
  43.7 1.6 %adjoint_one.1 = (f32[3,4,32,128]{3,2,1,0:T(8,128)S(1)}, f32[3,7,32,128]{3,2,1,0:T(8,128)S(1)}, f32[3,6,32,128]{3,2,1,0:T(8,128)S(1)}, f32[2,4,32,128]{3,2,1,0:T...) custom-call(s32[2]{0:T(128)S(1)} %pad_add_fusion.refs_0_.meta.meta_ref, ...), custom_call_target="tpu_custom_call" | custom-call | tf_op jit(solution)/shard_map/adjoint_one/pallas_call | solution.py:508
  45.3 1.2 %collective-permute-start.8 = (f32[8,32,128]{2,1,0:T(8,128)S(1)}, f32[8,32,128]{2,1,0:T(8,128)S(1)}, u32[]{:S(2)}, u32[]{:S(2)}) collective-permute-start(f32[8,32,128]{2,1,0:T(8,128)S(1)} %get-tuple-element.46), channel_id=1, source_target_pairs={{0,1},{1,0},{2,3},{3,2},{4,5},{5,4},{6,7},{7,6},{8,9},{9,8},{10,11... | collective-permute-start | bytes 393224 | tf_op jit(solution)/shard_map/ppermute | solution.py:16
  46.4 2.1 %collective-permute-start.9 = (f32[8,32,128]{2,1,0:T(8,128)S(1)}, f32[8,32,128]{2,1,0:T(8,128)S(1)}, u32[]{:S(2)}, u32[]{:S(2)}) collective-permute-start(f32[8,32,128]{2,1,0:T(8,128)S(1)} %get-tuple-element.47), channel_id=1, source_target_pairs={{1,2},{2,1},{3,4},{4,3},{5,6},{6,5},{9,10},{10,9},{11,12},{12,11},... | collective-permute-start | bytes 393224 | tf_op jit(solution)/shard_map/ppermute | solution.py:16
  48.5 0.0 collective-permute-done.8.a_ref
  48.5 4.2 %collective-permute-done.9.b_ref = f32[8,32,128]{2,1,0:T(8,128)S(1)} collective-permute-done((f32[8,32,128]{2,1,0:T(8,128)S(1)}, f32[8,32,128]{2,1,0:T(8,128)S(1)}, u32[]{:S(2)}, u32[]{:S(2)}) %collective-permute-start.9) | collective-permute-done | bytes 131104 | tf_op jit(solution)/shard_map/ppermute | solution.py:16
  52.7 0.0 copy-done.1
  52.7 1.4 %adjoint_two.1 = f32[2,4,32,128]{3,2,1,0:T(8,128)S(1)} custom-call(s32[2]{0:T(128)S(1)} %pad_add_fusion.refs_0_.meta.meta_ref, f32[3,4,32,128]{3,2,1,0:T(8,128)S(1)} %get-tuple-element.41.e_ref, f32[3,7,32,128]{3,2,1,0:T(8,128)S(1)} %get-tuple-element.42.hs_in, f32[3,6,32,128]{3,2,1,0:T(8,128)S(1)} %get-tuple-element.43.ps_in, ...), custom_call_target="tpu_custom_call" | custom-call | tf_op jit(solution)/shard_map/adjoint_two/pallas_call | solution.py:508
  54.1 1.6 %collective-permute-start.10 = (f32[2,4,32,128]{3,2,1,0:T(8,128)S(1)}, f32[2,4,32,128]{3,2,1,0:T(8,128)S(1)}, u32[]{:S(2)}, u32[]{:S(2)}) collective-permute-start(f32[2,4,32,128]{3,2,1,0:T(8,128)S(1)} %adjoint_two.1), channel_id=1, source_target_pairs={{0,8},{8,0},{16,24},{24,16},{1,9},{9,1},{17,25},{25,17},{2,10},{10... | collective-permute-start | bytes 393224 | tf_op jit(solution)/shard_map/ppermute | solution.py:31
  55.7 4.8 %collective-permute-done.10 = f32[2,4,32,128]{3,2,1,0:T(8,128)S(1)} collective-permute-done((f32[2,4,32,128]{3,2,1,0:T(8,128)S(1)}, f32[2,4,32,128]{3,2,1,0:T(8,128)S(1)}, u32[]{:S(2)}, u32[]{:S(2)}) %collective-permute-start.10) | collective-permute-done | bytes 131104 | tf_op jit(solution)/shard_map/ppermute | solution.py:31
  60.6 0.5 collective-permute-start.11
  61.1 7.9 %collective-permute-done.11 = f32[2,4,32,128]{3,2,1,0:T(8,128)S(1)} collective-permute-done((f32[2,4,32,128]{3,2,1,0:T(8,128)S(1)}, f32[2,4,32,128]{3,2,1,0:T(8,128)S(1)}, u32[]{:S(2)}, u32[]{:S(2)}) %collective-permute-start.11) | collective-permute-done | bytes 131104 | tf_op jit(solution)/shard_map/ppermute | solution.py:31
  69.0 0.7 fusion.1
  (11 shorter events, 0.1 us)
Async XLA Ops:
  0.7 0.7 copy-start.13
  0.7 0.7 copy-start.14
  0.7 0.7 copy-start.10
  0.7 0.7 %copy-start.11 = (f32[8]{0:T(128)S(1)}, f32[8]{0:T(128)}, u32[]{:S(2)}) copy-start(f32[8]{0:T(128)} %rate_t.1) | copy-start | bytes 100
  0.7 0.7 %copy-start.12 = (f32[8]{0:T(128)S(1)}, f32[8]{0:T(128)}, u32[]{:S(2)}) copy-start(f32[8]{0:T(128)} %strength_t.1) | copy-start | bytes 100
  1.4 0.9 %copy-start = (f32[1,3,4,32,128]{4,3,2,1,0:T(8,128)S(1)}, f32[1,3,4,32,128]{4,3,2,1,0:T(8,128)}, u32[]{:S(2)}) copy-start(f32[1,3,4,32,128]{4,3,2,1,0:T(8,128)} %param.17) | copy-start | bytes 589828
  2.4 0.9 %copy-start.5 = (f32[1,3,4,32,128]{4,3,2,1,0:T(8,128)S(1)}, f32[1,3,4,32,128]{4,3,2,1,0:T(8,128)}, u32[]{:S(2)}) copy-start(f32[1,3,4,32,128]{4,3,2,1,0:T(8,128)} %param.18) | copy-start | bytes 589828
  3.3 0.9 %copy-start.6 = (f32[1,3,4,32,128]{4,3,2,1,0:T(8,128)S(1)}, f32[1,3,4,32,128]{4,3,2,1,0:T(8,128)}, u32[]{:S(2)}) copy-start(f32[1,3,4,32,128]{4,3,2,1,0:T(8,128)} %param.19) | copy-start | bytes 589828
  4.2 0.8 %copy-start.7 = (f32[4,32,128]{2,1,0:T(8,128)S(1)}, f32[4,32,128]{2,1,0:T(8,128)}, u32[]{:S(2)}) copy-start(f32[4,32,128]{2,1,0:T(8,128)} %refs_7_.1) | copy-start | bytes 196612
  5.1 0.8 %copy-start.8 = (f32[4,32,128]{2,1,0:T(8,128)S(1)}, f32[4,32,128]{2,1,0:T(8,128)}, u32[]{:S(2)}) copy-start(f32[4,32,128]{2,1,0:T(8,128)} %refs_8_.1) | copy-start | bytes 196612
  5.9 0.8 %copy-start.9 = (s32[4,32,128]{2,1,0:T(8,128)S(1)}, s32[4,32,128]{2,1,0:T(8,128)}, u32[]{:S(2)}) copy-start(s32[4,32,128]{2,1,0:T(8,128)} %refs_9_.1) | copy-start | bytes 196612
  6.7 3.4 %copy-start.2 = (f32[1,3,4,32,128]{4,3,2,1,0:T(8,128)S(1)}, f32[1,3,4,32,128]{4,3,2,1,0:T(8,128)}, u32[]{:S(2)}) copy-start(f32[1,3,4,32,128]{4,3,2,1,0:T(8,128)} %param.20) | copy-start | bytes 589828
  6.7 3.4 %copy-start.3 = (f32[1,3,4,32,128]{4,3,2,1,0:T(8,128)S(1)}, f32[1,3,4,32,128]{4,3,2,1,0:T(8,128)}, u32[]{:S(2)}) copy-start(f32[1,3,4,32,128]{4,3,2,1,0:T(8,128)} %param.21) | copy-start | bytes 589828
  6.7 3.4 %copy-start.4 = (f32[1,3,4,32,128]{4,3,2,1,0:T(8,128)S(1)}, f32[1,3,4,32,128]{4,3,2,1,0:T(8,128)}, u32[]{:S(2)}) copy-start(f32[1,3,4,32,128]{4,3,2,1,0:T(8,128)} %param.22) | copy-start | bytes 589828
  7.5 6.5 %collective-permute-start = (f32[17,32,128]{2,1,0:T(8,128)S(1)}, f32[17,32,128]{2,1,0:T(8,128)S(1)}, u32[]{:S(2)}, u32[]{:S(2)}) collective-permute-start(f32[17,32,128]{2,1,0:T(8,128)S(1)} %get-tuple-element.27), channel_id=1, source_target_pairs={{0,1},{1,0},{2,3},{3,2},{4,5},{5,4},{6,7},{7,6},{8,9},{9,8},{10,11... | collective-permute-start | bytes 835592 | tf_op jit(solution)/shard_map/ppermute | solution.py:16
  7.6 9.3 %collective-permute-start.1 = (f32[17,32,128]{2,1,0:T(8,128)S(1)}, f32[17,32,128]{2,1,0:T(8,128)S(1)}, u32[]{:S(2)}, u32[]{:S(2)}) collective-permute-start(f32[17,32,128]{2,1,0:T(8,128)S(1)} %get-tuple-element.28), channel_id=1, source_target_pairs={{1,2},{2,1},{3,4},{4,3},{5,6},{6,5},{9,10},{10,9},{11,12},{12,11},... | collective-permute-start | bytes 835592 | tf_op jit(solution)/shard_map/ppermute | solution.py:16
  10.9 30.6 %collective-permute-start.4 = (f32[14,32,128]{2,1,0:T(8,128)S(1)}, f32[14,32,128]{2,1,0:T(8,128)S(1)}, u32[]{:S(2)}, u32[]{:S(2)}) collective-permute-start(f32[14,32,128]{2,1,0:T(8,128)S(1)} %get-tuple-element.37), channel_id=1, source_target_pairs={{0,1},{1,0},{2,3},{3,2},{4,5},{5,4},{6,7},{7,6},{8,9},{9,8},{10,11... | collective-permute-start | bytes 688136 | tf_op jit(solution)/shard_map/ppermute | solution.py:16
  11.9 29.6 %collective-permute-start.5 = (f32[14,32,128]{2,1,0:T(8,128)S(1)}, f32[14,32,128]{2,1,0:T(8,128)S(1)}, u32[]{:S(2)}, u32[]{:S(2)}) collective-permute-start(f32[14,32,128]{2,1,0:T(8,128)S(1)} %get-tuple-element.38), channel_id=1, source_target_pairs={{1,2},{2,1},{3,4},{4,3},{5,6},{6,5},{9,10},{10,9},{11,12},{12,11},... | collective-permute-start | bytes 688136 | tf_op jit(solution)/shard_map/ppermute | solution.py:16
  16.9 6.3 %copy-start.17 = (s32[1,128,1]{1,2,0:T(1,128)S(1)}, s32[1,128,1]{1,2,0:T(1,128)}, u32[]{:S(2)}) copy-start(s32[1,128,1]{1,2,0:T(1,128)} %param.31) | copy-start | bytes 1540
  18.3 4.9 %copy-start.15 = (f32[1,6,128]{2,0,1:T(1,128)S(1)}, f32[1,6,128]{2,0,1:T(1,128)}, u32[]{:S(2)}) copy-start(f32[1,6,128]{2,0,1:T(1,128)} %param.33) | copy-start | bytes 9220
  18.3 4.9 %copy-start.16 = (s32[1,128]{1,0:T(1,128)S(1)}, s32[1,128]{1,0:T(1,128)}, u32[]{:S(2)}) copy-start(s32[1,128]{1,0:T(1,128)} %param.32) | copy-start | bytes 1540
  18.3 18.4 %collective-permute-start.2 = (f32[8,32,128]{2,1,0:T(8,128)S(1)}, f32[8,32,128]{2,1,0:T(8,128)S(1)}, u32[]{:S(2)}, u32[]{:S(2)}) collective-permute-start(f32[8,32,128]{2,1,0:T(8,128)S(1)} %get-tuple-element.33), channel_id=1, source_target_pairs={{0,1},{1,0},{2,3},{3,2},{4,5},{5,4},{6,7},{7,6},{8,9},{9,8},{10,11... | collective-permute-start | bytes 393224 | tf_op jit(solution)/shard_map/ppermute | solution.py:16
  21.3 15.4 %collective-permute-start.3 = (f32[8,32,128]{2,1,0:T(8,128)S(1)}, f32[8,32,128]{2,1,0:T(8,128)S(1)}, u32[]{:S(2)}, u32[]{:S(2)}) collective-permute-start(f32[8,32,128]{2,1,0:T(8,128)S(1)} %get-tuple-element.34), channel_id=1, source_target_pairs={{1,2},{2,1},{3,4},{4,3},{5,6},{6,5},{9,10},{10,9},{11,12},{12,11},... | collective-permute-start | bytes 393224 | tf_op jit(solution)/shard_map/ppermute | solution.py:16
  38.0 3.5 %collective-permute-start.6 = (f32[2,32,128]{2,1,0:T(8,128)S(1)}, f32[2,32,128]{2,1,0:T(8,128)S(1)}, u32[]{:S(2)}, u32[]{:S(2)}) collective-permute-start(f32[2,32,128]{2,1,0:T(8,128)S(1)} %get-tuple-element.39), channel_id=1, source_target_pairs={{0,1},{1,0},{2,3},{3,2},{4,5},{5,4},{6,7},{7,6},{8,9},{9,8},{10,11... | collective-permute-start | bytes 98312 | tf_op jit(solution)/shard_map/ppermute | solution.py:16
  38.4 5.2 %collective-permute-start.7 = (f32[2,32,128]{2,1,0:T(8,128)S(1)}, f32[2,32,128]{2,1,0:T(8,128)S(1)}, u32[]{:S(2)}, u32[]{:S(2)}) collective-permute-start(f32[2,32,128]{2,1,0:T(8,128)S(1)} %get-tuple-element.40), channel_id=1, source_target_pairs={{1,2},{2,1},{3,4},{4,3},{5,6},{6,5},{9,10},{10,9},{11,12},{12,11},... | collective-permute-start | bytes 98312 | tf_op jit(solution)/shard_map/ppermute | solution.py:16
  43.7 9.0 %copy-start.1 = (f32[1,3,4,32,128]{4,3,2,1,0:T(8,128)S(1)}, f32[1,3,4,32,128]{4,3,2,1,0:T(8,128)}, u32[]{:S(2)}) copy-start(f32[1,3,4,32,128]{4,3,2,1,0:T(8,128)} %param.17) | copy-start | bytes 589828
  45.3 3.2 %collective-permute-start.8 = (f32[8,32,128]{2,1,0:T(8,128)S(1)}, f32[8,32,128]{2,1,0:T(8,128)S(1)}, u32[]{:S(2)}, u32[]{:S(2)}) collective-permute-start(f32[8,32,128]{2,1,0:T(8,128)S(1)} %get-tuple-element.46), channel_id=1, source_target_pairs={{0,1},{1,0},{2,3},{3,2},{4,5},{5,4},{6,7},{7,6},{8,9},{9,8},{10,11... | collective-permute-start | bytes 393224 | tf_op jit(solution)/shard_map/ppermute | solution.py:16
  46.4 6.3 %collective-permute-start.9 = (f32[8,32,128]{2,1,0:T(8,128)S(1)}, f32[8,32,128]{2,1,0:T(8,128)S(1)}, u32[]{:S(2)}, u32[]{:S(2)}) collective-permute-start(f32[8,32,128]{2,1,0:T(8,128)S(1)} %get-tuple-element.47), channel_id=1, source_target_pairs={{1,2},{2,1},{3,4},{4,3},{5,6},{6,5},{9,10},{10,9},{11,12},{12,11},... | collective-permute-start | bytes 393224 | tf_op jit(solution)/shard_map/ppermute | solution.py:16
  54.1 6.4 %collective-permute-start.10 = (f32[2,4,32,128]{3,2,1,0:T(8,128)S(1)}, f32[2,4,32,128]{3,2,1,0:T(8,128)S(1)}, u32[]{:S(2)}, u32[]{:S(2)}) collective-permute-start(f32[2,4,32,128]{3,2,1,0:T(8,128)S(1)} %adjoint_two.1), channel_id=1, source_target_pairs={{0,8},{8,0},{16,24},{24,16},{1,9},{9,1},{17,25},{25,17},{2,10},{10... | collective-permute-start | bytes 393224 | tf_op jit(solution)/shard_map/ppermute | solution.py:31
  60.6 8.4 %collective-permute-start.11 = (f32[2,4,32,128]{3,2,1,0:T(8,128)S(1)}, f32[2,4,32,128]{3,2,1,0:T(8,128)S(1)}, u32[]{:S(2)}, u32[]{:S(2)}) collective-permute-start(f32[2,4,32,128]{3,2,1,0:T(8,128)S(1)} %add.21), channel_id=1, source_target_pairs={{0,24},{8,16},{16,8},{24,0},{1,25},{9,17},{17,9},{25,1},{2,26},{10... | collective-permute-start | bytes 393224 | tf_op jit(solution)/shard_map/ppermute | solution.py:31

commit v2 on v1

--- a/solution.py
+++ b/solution.py
@@ -182,12 +182,18 @@
     return lax.dot_general(left, right, (((1,), (1,)), ((), ())), preferred_element_type=F32)
 
 
-def first_kernel(full_x, meta, rate_t, strength_t, wavelet, e_ref, h_ref, p_ref, perm, cond, cls, cells, signs,
-                 coef_ref, src_ref, a_ref, b_ref):
+def first_kernel(full_x, meta, rate_t, strength_t, wavelet, e_in, h_in, p_in, perm_in, cond_in, cls_in, cells, signs,
+                 e_ref, h_ref, p_ref, coef_ref, src_ref, a_ref, b_ref, perm, cond, cls, sems):
     even = meta[1] == 0
     width, depth, span = perm.shape
+    moves = [(perm_in, perm), (cond_in, cond), (cls_in, cls), (e_in, e_ref), (h_in, h_ref), (p_in, p_ref)]
+    copies = [pltpu.make_async_copy(a, b, sems.at[k]) for k, (a, b) in enumerate(moves)]
+    for copy in copies:
+        copy.start()
     src = source_map(cells, signs, meta[0], width, depth, span, full_x)
     src_ref[...] = src.reshape(width + 2, depth, span)
+    for copy in copies[:3]:
+        copy.wait()
     for i in range(width):
         ratio = cond[i] / (2.0 * perm[i])
         coef_ref[0, i] = (1.0 - ratio) / (1.0 + ratio)
@@ -200,6 +206,8 @@
             gain = jnp.where(kind == k, (1.0 - rate_t[k]) * strength_t[k], gain)
         coef_ref[2, i] = rate
         coef_ref[3, i] = gain
+    for copy in copies[3:]:
+        copy.wait()
     planes = own_planes(e_ref, h_ref, p_ref)
     h1, e1 = pre_steps(planes, lambda i: [coef_ref[k, i] for k in range(4)], lambda i: src_ref[i + 1] * wavelet[0])
     emit_state(even, planes, h1, e1, a_ref, b_ref, True)
@@ -215,32 +223,35 @@
     emit_state(meta[1] == 0, planes, h1, e1, a_ref, b_ref, True)
 
 
-def receiver_kernel(meta, width, depth, got, maps_ref, acc):
+def receiver_kernel(width, depth, meta, got, maps_ref, acc):
     mine = meta[0]
     rows = (width + 2) * depth
-    span = acc.shape[2]
+    span = acc.shape[1]
     blocks, lists, n = got.shape
     steps = lists - 2
     acc[...] = jnp.zeros(acc.shape, F32)
+    first_row = ((mine * width - 1) * depth).astype(F32)
+    row_at = lax.broadcasted_iota(jnp.int32, (rows, n), 0).astype(F32)
+    y_at = lax.broadcasted_iota(jnp.int32, (span, n), 0).astype(F32)
 
     def block(b, carry):
-        row = got[b, 0:1, :] - ((mine * width - 1) * depth).astype(F32)
-        y = got[b, 1:2, :]
-        hot = lax.broadcasted_iota(jnp.int32, (rows, n), 0).astype(F32) == row
-        left = jnp.where(hot, 1.0, 0.0).astype(jnp.bfloat16)
-        left3 = jnp.concatenate([left, left, left], axis=1)
-        at_y = lax.broadcasted_iota(jnp.int32, (span, n), 0).astype(F32) == y
-        one = jnp.where(at_y, 1.0, 0.0).astype(jnp.bfloat16)
-        dims = (((1,), (1,)), ((), ()))
-        acc[0] += lax.dot_general(left, one, dims, preferred_element_type=F32)
+        hot = row_at == got[b, 0:1, :] - first_row
+        at_y = jnp.where(y_at == got[b, 1:2, :], 1.0, 0.0).astype(jnp.bfloat16)
+        zero = jnp.zeros((rows, n), jnp.bfloat16)
+        left = [jnp.concatenate([jnp.where(hot, 1.0, 0.0).astype(jnp.bfloat16), zero, zero], axis=1)]
         for s in range(steps):
             v = got[b, 2 + s:3 + s, :]
             high = v.astype(jnp.bfloat16).astype(F32)
             mid = (v - high).astype(jnp.bfloat16).astype(F32)
             low = (v - high) - mid
-            parts = [jnp.where(at_y, u, 0.0).astype(jnp.bfloat16) for u in (high, mid, low)]
-            right = jnp.concatenate(parts, axis=1)
-            acc[1 + s] += lax.dot_general(left3, right, dims, preferred_element_type=F32)
+            parts = [jnp.where(hot, u, 0.0).astype(jnp.bfloat16) for u in (high, mid, low)]
+            left.append(jnp.concatenate(parts, axis=1))
+        acc[...] += lax.dot_general(
+            jnp.concatenate(left, axis=0),
+            jnp.concatenate([at_y, at_y, at_y], axis=1),
+            (((1,), (1,)), ((), ())),
+            preferred_element_type=F32,
+        )
         return carry
 
     lax.fori_loop(0, blocks, block, 0)
@@ -502,18 +513,20 @@
                scratch_dest(es_ref, hs_ref, ps_ref), None, seen)
 
 
-def call(body, name, inputs, scalars, outs, scratch=()):
+def call(body, name, inputs, scalars, outs, scratch=(), remote=0, work=10**10):
     smem = pl.BlockSpec(memory_space=pltpu.SMEM)
     vmem = pl.BlockSpec(memory_space=pltpu.VMEM)
+    stay = pl.BlockSpec(memory_space=pltpu.HBM)
     return pl.pallas_call(
         body,
         name=name,
         out_shape=[jax.ShapeDtypeStruct(s, F32) for s in outs],
-        in_specs=[smem] * len(scalars) + [vmem] * len(inputs),
+        in_specs=[smem] * len(scalars) + [stay] * remote + [vmem] * (len(inputs) - remote),
         out_specs=[vmem] * len(outs),
-        scratch_shapes=[pltpu.VMEM(s, F32) for s in scratch],
+        scratch_shapes=[s if not isinstance(s, tuple) else pltpu.VMEM(s, F32) for s in scratch],
+        cost_estimate=pl.CostEstimate(flops=work, transcendentals=0, bytes_accessed=0),
         compiler_params=pltpu.CompilerParams(vmem_limit_bytes=48 * 1024 * 1024),
-    )(*scalars, *inputs)
+    )(*scalars, *[pltpu.with_memory_space_constraint(x, pltpu.HBM) for x in inputs[:remote]], *inputs[remote:])
 
 
 def per_device(
@@ -547,28 +560,28 @@
     rec_y, rec_z = split_index(rest, span)
     rec_row = (rec_owner[0, :, 0] * width + in_x) * depth + rec_z
     listed = jnp.concatenate([rec_row[None].astype(F32), rec_y[None].astype(F32), observed[0]], axis=0)
-    got = lax.all_gather(listed, "sub")
-
     fields = (electric[0], magnetic[0], polar[0])
     adjoint = (adj_electric[0], adj_magnetic[0], adj_polar[0])
 
-    coef, src, a1, b1 = call(
+    own = (3, width, *plane)
+    *fields, coef, src, a1, b1 = call(
         lambda *refs: first_kernel(width * nsub, *refs),
         "first",
         [*fields, permittivity, conductivity, debye_class, src_cell, src_sign],
         [meta, debye_rate, debye_strength, wavelet],
-        [(4, width, *plane), (width + 2, *plane), (17, *plane), (17, *plane)],
+        [own, own, own, (4, width, *plane), (width + 2, *plane), (17, *plane), (17, *plane)],
+        [
+            (width, *plane),
+            (width, *plane),
+            pltpu.VMEM((width, *plane), jnp.int32),
+            pltpu.SemaphoreType.DMA((6,)),
+        ],
+        remote=6,
     )
     got_a1, got_b1 = exchange(a1, b1)
-    a3, b3 = call(adjoint_first_kernel, "adjoint_first", [*adjoint, coef], [meta], [(14, *plane), (14, *plane)])
-    (maps,) = call(
-        lambda meta_ref, *refs: receiver_kernel(meta_ref, width, depth, *refs),
-        "receivers",
-        [got],
-        [meta],
-        [(steps + 1, width + 2, *plane)],
-        [(steps + 1, (width + 2) * depth, span)],
-    )
+    listed, b1 = lax.optimization_barrier((listed, b1))
+    got = lax.all_to_all(jnp.broadcast_to(listed[None], (nsub, *listed.shape)), "sub", 0, 0)
+    got, got_a1, got_b1 = lax.optimization_barrier((got, got_a1, got_b1))
     e_sh, h_sh, p_sh = (3, width + 2, *plane), (3, width + 3, *plane), (3, width + 2, *plane)
     hist1, hs, ps, coefh, ey2, a2, b2 = call(
         forward_one_kernel,
@@ -578,7 +591,18 @@
         [(ROUND, 3, width, *plane), h_sh, p_sh, (2, 4, *plane), (2, *plane), (8, *plane), (8, *plane)],
         [e_sh],
     )
+    got, a2, b2 = lax.optimization_barrier((got, a2, b2))
     got_a2, got_b2 = exchange(a2, b2)
+    (maps,) = call(
+        lambda *refs: receiver_kernel(width, depth, *refs),
+        "receivers",
+        [got],
+        [meta],
+        [(steps + 1, width + 2, *plane)],
+        [((steps + 1) * (width + 2) * depth, span)],
+    )
+    coef_later, maps = lax.optimization_barrier((coef, maps))
+    a3, b3 = call(adjoint_first_kernel, "adjoint_first", [*adjoint, coef_later], [meta], [(14, *plane), (14, *plane)])
     got_a3, got_b3 = exchange(a3, b3)
     hist2, eyh, a4, b4 = call(
         forward_two_kernel,

time: 70.1 us -> 61.8 us (0.88)
  local copies, waits for them, and re-layouts: 6.03 us -> 0.75 us
  starting transfers between devices: 19.4 us -> 17 us
  waiting for transfers between devices: 21.9 us -> 20.1 us
  Pallas kernels: 11.3 us -> 12.6 us
    all_to_all x0 -> x1, blocking collectives: none -> 9.38 us  [per_device(): lax.all_to_all(jnp.broadcast_to(listed[None], (nsub, *listed.shape)), 'su...]
    all_gather x1 -> x0, blocking collectives: 9.29 us -> none  [per_device(): got = lax.all_gather(listed, 'sub')]
    unnamed x37 -> x23, local copies, waits for them, and re-layouts: 6.03 us -> 0.74 us
    ppermute x10, starting transfers between devices: 17.3 us -> 14.8 us  [pair_swap(): return lax.ppermute(block, axis, route)]
    ppermute x10, waiting for transfers between devices: 9.19 us -> 7.52 us  [pair_swap(): return lax.ppermute(block, axis, route)]
    pallas_call x7, Pallas kernels: 11.3 us -> 12.6 us  [call(): pl.pallas_call(body, name=name, out_shape=[jax.ShapeDtypeStruct(s, F32) f...]
  transfers between devices with their start and end apart: 12 -> 12, of which waited for: 5 -> 4; matrix products, arithmetic and copies ran while one was open for 0% -> 0% of each run, Pallas kernels for 11% -> 10%
where the time goes in v2:
time: 61.8 us; the launch traced here: 61.5 us
  waiting for transfers between devices  20.1 us (33%)
  starting transfers between devices  17 us (28%)
  Pallas kernels  12.6 us (20%)
  blocking collectives  9.38 us (15%)
  between operations  0.92 us (1%)
  other arithmetic  0.79 us (1%)
  local copies, waits for them, and re-layouts  0.75 us (1%)
    ppermute x10, starting transfers between devices, pair_swap(): return lax.ppermute(block, axis, route)  14.8 us
    pallas_call x7, Pallas kernels, call(): pl.pallas_call(body, name=name, out_shape=[jax.ShapeDtypeStruct(s, F32) f...  12.6 us
    ppermute x2, waiting for transfers between devices, shot_sum(): x = x + lax.ppermute(x, 'shot', [(i, i ^ flip) for i in range(n)])  12.6 us
    all_to_all x1, blocking collectives, per_device(): lax.all_to_all(jnp.broadcast_to(listed[None], (nsub, *listed.shape)), 'su...  9.38 us
    ppermute x10, waiting for transfers between devices, pair_swap(): return lax.ppermute(block, axis, route)  7.52 us
    ppermute x2, starting transfers between devices, shot_sum(): x = x + lax.ppermute(x, 'shot', [(i, i ^ flip) for i in range(n)])  2.16 us
  transfers between devices with their start and end apart: 12, of which 4 were waited for; matrix products, arithmetic and copies ran while one was open for 0% of the time, Pallas kernels for 10%

profile of v2, /device:TPU:18, one launch (start us, length us, event | category | flops | bytes accessed | tf_op | source)
XLA Modules:
  0.0 61.5 jit_solution(14963818604800256675)
XLA Ops:
  0.6 0.1 pad_add_fusion.refs_0_.meta
  0.7 0.0 copy-start.6
  0.7 0.0 copy-start.7
  0.7 0.0 copy-start.3
  0.7 0.0 copy-start.4
  0.7 0.0 copy-start.5
  0.7 0.6 %copy-done.6 = f32[8]{0:T(128)S(1)} copy-done((f32[8]{0:T(128)S(1)}, f32[8]{0:T(128)}, u32[]{:S(2)}) %copy-start.6) | copy-done | bytes 56
  1.4 0.0 copy-done.7
  1.4 0.0 copy-done.3
  1.4 0.0 copy-done.4
  1.4 0.0 copy-done.5
  1.4 2.0 %first.1 = (f32[3,4,32,128]{3,2,1,0:T(8,128)S(1)}, f32[3,4,32,128]{3,2,1,0:T(8,128)S(1)}, f32[3,4,32,128]{3,2,1,0:T(8,128)S(1)}, f32[4,4,32,128]{3,2,1,0:T(8,128...) custom-call(s32[2]{0:T(128)S(1)} %pad_add_fusion.refs_0_.meta, ...), custom_call_target="tpu_custom_call" | custom-call | flops 10000000000 | tf_op jit(solution)/shard_map/first/pallas_call | solution.py:520
  3.5 0.0 copy-start.8
  3.5 0.1 collective-permute-start
  3.6 0.0 copy-start.9
  3.6 0.0 copy-start.10
  3.6 2.6 %collective-permute-start.1 = (f32[17,32,128]{2,1,0:T(8,128)S(1)}, f32[17,32,128]{2,1,0:T(8,128)S(1)}, u32[]{:S(2)}, u32[]{:S(2)}) collective-permute-start(f32[17,32,128]{2,1,0:T(8,128)S(1)} %get-tuple-element.42), channel_id=1, source_target_pairs={{1,2},{2,1},{3,4},{4,3},{5,6},{6,5},{9,10},{10,9},{11,12},{12,11},... | collective-permute-start | bytes 835592 | tf_op jit(solution)/shard_map/ppermute | solution.py:16
  6.2 0.0 copy-done.8
  6.2 0.0 copy-done.9
  6.3 0.0 copy-done.10
  6.3 9.4 %all_to_all.5.refs_1_ = f32[8,8,128]{2,1,0:T(8,128)S(1)} all-to-all(f32[8,8,128]{2,1,0:T(8,128)S(1)} %broadcast_in_dim.2), channel_id=1, replica_groups=mesh['shot'=4,'sub'=8] {'sub'}, dimensions={0} | all-to-all | bytes 65536 | tf_op jit(solution)/shard_map/all_to_all | solution.py:583
  15.7 0.0 collective-permute-done.a_ref
  15.7 0.0 collective-permute-done.1.b_ref
  15.7 1.4 %forward_one.1 = (f32[3,3,4,32,128]{4,3,2,1,0:T(8,128)S(1)}, f32[3,7,32,128]{3,2,1,0:T(8,128)S(1)}, f32[3,6,32,128]{3,2,1,0:T(8,128)S(1)}, f32[2,4,32,128]{3,2,1...) custom-call(s32[2]{0:T(128)S(1)} %pad_add_fusion.refs_0_.meta, ...), custom_call_target="tpu_custom_call" | custom-call | flops 10000000000 | tf_op jit(solution)/shard_map/forward_one/pallas_call | solution.py:520
  17.1 0.0 copy-start
  17.2 0.0 copy-start.1
  17.2 0.0 copy-start.2
  17.2 0.1 collective-permute-start.2
  17.3 2.4 %collective-permute-start.3 = (f32[8,32,128]{2,1,0:T(8,128)S(1)}, f32[8,32,128]{2,1,0:T(8,128)S(1)}, u32[]{:S(2)}, u32[]{:S(2)}) collective-permute-start(f32[8,32,128]{2,1,0:T(8,128)S(1)} %get-tuple-element.57), channel_id=1, source_target_pairs={{1,2},{2,1},{3,4},{4,3},{5,6},{6,5},{9,10},{10,9},{11,12},{12,11},... | collective-permute-start | bytes 393224 | tf_op jit(solution)/shard_map/ppermute | solution.py:16
  19.6 4.1 %receivers.1.maps_ref = f32[7,6,32,128]{3,2,1,0:T(8,128)S(1)} custom-call(s32[2]{0:T(128)S(1)} %pad_add_fusion.refs_0_.meta, f32[8,8,128]{2,1,0:T(8,128)S(1)} %all_to_all.5.refs_1_), custom_call_target="tpu_custom_call" | custom-call | flops 10000000000 | tf_op jit(solution)/shard_map/receivers/pallas_call | solution.py:520
  23.7 0.0 copy-done
  23.7 0.0 copy-done.1
  23.7 0.0 copy-done.2
  23.8 0.7 %adjoint_first.1 = (f32[14,32,128]{2,1,0:T(8,128)S(1)}, f32[14,32,128]{2,1,0:T(8,128)S(1)}) custom-call(s32[2]{0:T(128)S(1)} %pad_add_fusion.refs_0_.meta, f32[3,4,32,128]{3,2,1,0:T(8,128)S(1)} %bitcast.23, f32[3,4,32,128]{3,2,1,0:T(8,128)S(1)} %bitcast.25, f32[3,4,32,128]{3,2,1,0:T(8,128)S(1)} %bitcast.27, f32[4,4,32,128]{3,2,1,0:T(8,128)S(1)} %get-tuple-element.60.coef_ref), custom_call_target="tpu_custom_call" | custom-call | flops 10000000000 | tf_op jit(solution)/shard_map/adjoint_first/pallas_call | solution.py:520
  24.5 1.2 %collective-permute-start.4 = (f32[14,32,128]{2,1,0:T(8,128)S(1)}, f32[14,32,128]{2,1,0:T(8,128)S(1)}, u32[]{:S(2)}, u32[]{:S(2)}) collective-permute-start(f32[14,32,128]{2,1,0:T(8,128)S(1)} %get-tuple-element.61), channel_id=1, source_target_pairs={{0,1},{1,0},{2,3},{3,2},{4,5},{5,4},{6,7},{7,6},{8,9},{9,8},{10,11... | collective-permute-start | bytes 688136 | tf_op jit(solution)/shard_map/ppermute | solution.py:16
  25.6 2.3 %collective-permute-start.5 = (f32[14,32,128]{2,1,0:T(8,128)S(1)}, f32[14,32,128]{2,1,0:T(8,128)S(1)}, u32[]{:S(2)}, u32[]{:S(2)}) collective-permute-start(f32[14,32,128]{2,1,0:T(8,128)S(1)} %get-tuple-element.62), channel_id=1, source_target_pairs={{1,2},{2,1},{3,4},{4,3},{5,6},{6,5},{9,10},{10,9},{11,12},{12,11},... | collective-permute-start | bytes 688136 | tf_op jit(solution)/shard_map/ppermute | solution.py:16
  27.9 0.0 collective-permute-done.2.a_ref
  27.9 0.0 collective-permute-done.3.b_ref
  27.9 1.3 %forward_two.1 = (f32[3,3,4,32,128]{4,3,2,1,0:T(8,128)S(1)}, f32[4,32,128]{2,1,0:T(8,128)S(1)}, f32[2,32,128]{2,1,0:T(8,128)S(1)}, f32[2,32,128]{2,1,0:T(8,128)S(1)}) custom-call(s32[2]{0:T(128)S(1)} %pad_add_fusion.refs_0_.meta, f32[6]{0:T(128)S(1)} %copy-done.7, f32[3,3,4,32,128]{4,3,2,1,0:T(8,128)S(1)} %get-tuple-element.53.hist_in.hist1_ref, ...), custom_call_target="tpu_custom_call" | custom-call | flops 10000000000 | tf_op jit(solution)/shard_map/forward_two/pallas_call | solution.py:520
  29.2 1.3 %collective-permute-start.6 = (f32[2,32,128]{2,1,0:T(8,128)S(1)}, f32[2,32,128]{2,1,0:T(8,128)S(1)}, u32[]{:S(2)}, u32[]{:S(2)}) collective-permute-start(f32[2,32,128]{2,1,0:T(8,128)S(1)} %get-tuple-element.63), channel_id=1, source_target_pairs={{0,1},{1,0},{2,3},{3,2},{4,5},{5,4},{6,7},{7,6},{8,9},{9,8},{10,11... | collective-permute-start | bytes 98312 | tf_op jit(solution)/shard_map/ppermute | solution.py:16
  30.5 2.1 %collective-permute-start.7 = (f32[2,32,128]{2,1,0:T(8,128)S(1)}, f32[2,32,128]{2,1,0:T(8,128)S(1)}, u32[]{:S(2)}, u32[]{:S(2)}) collective-permute-start(f32[2,32,128]{2,1,0:T(8,128)S(1)} %get-tuple-element.64), channel_id=1, source_target_pairs={{1,2},{2,1},{3,4},{4,3},{5,6},{6,5},{9,10},{10,9},{11,12},{12,11},... | collective-permute-start | bytes 98312 | tf_op jit(solution)/shard_map/ppermute | solution.py:16
  32.6 0.0 collective-permute-done.6.ra_ref
  32.6 3.1 %collective-permute-done.7.rb_ref = f32[2,32,128]{2,1,0:T(8,128)S(1)} collective-permute-done((f32[2,32,128]{2,1,0:T(8,128)S(1)}, f32[2,32,128]{2,1,0:T(8,128)S(1)}, u32[]{:S(2)}, u32[]{:S(2)}) %collective-permute-start.7) | collective-permute-done | bytes 32800 | tf_op jit(solution)/shard_map/ppermute | solution.py:16
  35.8 0.0 collective-permute-done.4.a_ref
  35.8 0.0 collective-permute-done.5.b_ref
  35.8 1.6 %adjoint_one.1 = (f32[3,4,32,128]{3,2,1,0:T(8,128)S(1)}, f32[3,7,32,128]{3,2,1,0:T(8,128)S(1)}, f32[3,6,32,128]{3,2,1,0:T(8,128)S(1)}, f32[2,4,32,128]{3,2,1,0:T...) custom-call(s32[2]{0:T(128)S(1)} %pad_add_fusion.refs_0_.meta, f32[3,4,32,128]{3,2,1,0:T(8,128)S(1)} %bitcast.24, ...), custom_call_target="tpu_custom_call" | custom-call | flops 10000000000 | tf_op jit(solution)/shard_map/adjoint_one/pallas_call | solution.py:520
  37.4 1.0 %collective-permute-start.8 = (f32[8,32,128]{2,1,0:T(8,128)S(1)}, f32[8,32,128]{2,1,0:T(8,128)S(1)}, u32[]{:S(2)}, u32[]{:S(2)}) collective-permute-start(f32[8,32,128]{2,1,0:T(8,128)S(1)} %get-tuple-element.70), channel_id=1, source_target_pairs={{0,1},{1,0},{2,3},{3,2},{4,5},{5,4},{6,7},{7,6},{8,9},{9,8},{10,11... | collective-permute-start | bytes 393224 | tf_op jit(solution)/shard_map/ppermute | solution.py:16
  38.4 1.9 %collective-permute-start.9 = (f32[8,32,128]{2,1,0:T(8,128)S(1)}, f32[8,32,128]{2,1,0:T(8,128)S(1)}, u32[]{:S(2)}, u32[]{:S(2)}) collective-permute-start(f32[8,32,128]{2,1,0:T(8,128)S(1)} %get-tuple-element.71), channel_id=1, source_target_pairs={{1,2},{2,1},{3,4},{4,3},{5,6},{6,5},{9,10},{10,9},{11,12},{12,11},... | collective-permute-start | bytes 393224 | tf_op jit(solution)/shard_map/ppermute | solution.py:16
  40.3 0.0 collective-permute-done.8.a_ref
  40.3 4.3 %collective-permute-done.9.b_ref = f32[8,32,128]{2,1,0:T(8,128)S(1)} collective-permute-done((f32[8,32,128]{2,1,0:T(8,128)S(1)}, f32[8,32,128]{2,1,0:T(8,128)S(1)}, u32[]{:S(2)}, u32[]{:S(2)}) %collective-permute-start.9) | collective-permute-done | bytes 131104 | tf_op jit(solution)/shard_map/ppermute | solution.py:16
  44.7 1.4 %adjoint_two.1 = f32[2,4,32,128]{3,2,1,0:T(8,128)S(1)} custom-call(s32[2]{0:T(128)S(1)} %pad_add_fusion.refs_0_.meta, f32[3,4,32,128]{3,2,1,0:T(8,128)S(1)} %get-tuple-element.65.e_ref, f32[3,7,32,128]{3,2,1,0:T(8,128)S(1)} %get-tuple-element.66.hs_in, f32[3,6,32,128]{3,2,1,0:T(8,128)S(1)} %get-tuple-element.67.ps_in, ...), custom_call_target="tpu_custom_call" | custom-call | flops 10000000000 | tf_op jit(solution)/shard_map/adjoint_two/pallas_call | solution.py:520
  46.1 1.6 %collective-permute-start.10 = (f32[2,4,32,128]{3,2,1,0:T(8,128)S(1)}, f32[2,4,32,128]{3,2,1,0:T(8,128)S(1)}, u32[]{:S(2)}, u32[]{:S(2)}) collective-permute-start(f32[2,4,32,128]{3,2,1,0:T(8,128)S(1)} %adjoint_two.1), channel_id=1, source_target_pairs={{0,8},{8,0},{16,24},{24,16},{1,9},{9,1},{17,25},{25,17},{2,10},{10... | collective-permute-start | bytes 393224 | tf_op jit(solution)/shard_map/ppermute | solution.py:31
  47.8 4.7 %collective-permute-done.10 = f32[2,4,32,128]{3,2,1,0:T(8,128)S(1)} collective-permute-done((f32[2,4,32,128]{3,2,1,0:T(8,128)S(1)}, f32[2,4,32,128]{3,2,1,0:T(8,128)S(1)}, u32[]{:S(2)}, u32[]{:S(2)}) %collective-permute-start.10) | collective-permute-done | bytes 131104 | tf_op jit(solution)/shard_map/ppermute | solution.py:31
  52.5 0.5 collective-permute-start.11
  53.0 7.8 %collective-permute-done.11 = f32[2,4,32,128]{3,2,1,0:T(8,128)S(1)} collective-permute-done((f32[2,4,32,128]{3,2,1,0:T(8,128)S(1)}, f32[2,4,32,128]{3,2,1,0:T(8,128)S(1)}, u32[]{:S(2)}, u32[]{:S(2)}) %collective-permute-start.11) | collective-permute-done | bytes 131104 | tf_op jit(solution)/shard_map/ppermute | solution.py:31
  60.9 0.7 %fusion.1 = (f32[4,32,128]{2,1,0:T(8,128)}, f32[4,32,128]{2,1,0:T(8,128)}) fusion(f32[2,4,32,128]{3,2,1,0:T(8,128)S(1)} %add.22), kind=kLoop, calls=%fused_computation.2 | loop fusion | flops 65536 | bytes 262144 | tf_op jit(solution)/shard_map/neg | solution.py:634
  (6 shorter events, 0.1 us)
Async XLA Ops:
  0.7 0.7 %copy-start.6 = (f32[8]{0:T(128)S(1)}, f32[8]{0:T(128)}, u32[]{:S(2)}) copy-start(f32[8]{0:T(128)} %strength_t.1) | copy-start | bytes 100
  0.7 0.7 %copy-start.7 = (f32[6]{0:T(128)S(1)}, f32[6]{0:T(128)}, u32[]{:S(2)}) copy-start(f32[6]{0:T(128)} %wavelet.3) | copy-start | bytes 76
  0.7 0.7 %copy-start.3 = (s32[1,64]{1,0:T(1,128)S(1)}, s32[1,64]{1,0:T(1,128)}, u32[]{:S(2)}) copy-start(s32[1,64]{1,0:T(1,128)} %refs_10_.1) | copy-start | bytes 772
  0.7 0.7 %copy-start.4 = (s32[1,64]{1,0:T(1,128)S(1)}, s32[1,64]{1,0:T(1,128)}, u32[]{:S(2)}) copy-start(s32[1,64]{1,0:T(1,128)} %refs_11_.1) | copy-start | bytes 772
  0.7 0.7 %copy-start.5 = (f32[8]{0:T(128)S(1)}, f32[8]{0:T(128)}, u32[]{:S(2)}) copy-start(f32[8]{0:T(128)} %rate_t.1) | copy-start | bytes 100
  3.5 2.8 %copy-start.8 = (f32[1,6,128]{2,0,1:T(1,128)S(1)}, f32[1,6,128]{2,0,1:T(1,128)}, u32[]{:S(2)}) copy-start(f32[1,6,128]{2,0,1:T(1,128)} %param.33) | copy-start | bytes 9220
  3.5 12.2 %collective-permute-start = (f32[17,32,128]{2,1,0:T(8,128)S(1)}, f32[17,32,128]{2,1,0:T(8,128)S(1)}, u32[]{:S(2)}, u32[]{:S(2)}) collective-permute-start(f32[17,32,128]{2,1,0:T(8,128)S(1)} %get-tuple-element.44), channel_id=1, source_target_pairs={{0,1},{1,0},{2,3},{3,2},{4,5},{5,4},{6,7},{7,6},{8,9},{9,8},{10,11... | collective-permute-start | bytes 835592 | tf_op jit(solution)/shard_map/ppermute | solution.py:16
  3.6 2.7 %copy-start.9 = (s32[1,128]{1,0:T(1,128)S(1)}, s32[1,128]{1,0:T(1,128)}, u32[]{:S(2)}) copy-start(s32[1,128]{1,0:T(1,128)} %param.32) | copy-start | bytes 1540
  3.6 2.7 %copy-start.10 = (s32[1,128,1]{1,2,0:T(1,128)S(1)}, s32[1,128,1]{1,2,0:T(1,128)}, u32[]{:S(2)}) copy-start(s32[1,128,1]{1,2,0:T(1,128)} %param.31) | copy-start | bytes 1540
  3.6 12.1 %collective-permute-start.1 = (f32[17,32,128]{2,1,0:T(8,128)S(1)}, f32[17,32,128]{2,1,0:T(8,128)S(1)}, u32[]{:S(2)}, u32[]{:S(2)}) collective-permute-start(f32[17,32,128]{2,1,0:T(8,128)S(1)} %get-tuple-element.42), channel_id=1, source_target_pairs={{1,2},{2,1},{3,4},{4,3},{5,6},{6,5},{9,10},{10,9},{11,12},{12,11},... | collective-permute-start | bytes 835592 | tf_op jit(solution)/shard_map/ppermute | solution.py:16
  17.1 6.6 %copy-start = (f32[1,3,4,32,128]{4,3,2,1,0:T(8,128)S(1)}, f32[1,3,4,32,128]{4,3,2,1,0:T(8,128)}, u32[]{:S(2)}) copy-start(f32[1,3,4,32,128]{4,3,2,1,0:T(8,128)} %param.20) | copy-start | bytes 589828
  17.2 6.6 %copy-start.1 = (f32[1,3,4,32,128]{4,3,2,1,0:T(8,128)S(1)}, f32[1,3,4,32,128]{4,3,2,1,0:T(8,128)}, u32[]{:S(2)}) copy-start(f32[1,3,4,32,128]{4,3,2,1,0:T(8,128)} %param.21) | copy-start | bytes 589828
  17.2 6.6 %copy-start.2 = (f32[1,3,4,32,128]{4,3,2,1,0:T(8,128)S(1)}, f32[1,3,4,32,128]{4,3,2,1,0:T(8,128)}, u32[]{:S(2)}) copy-start(f32[1,3,4,32,128]{4,3,2,1,0:T(8,128)} %param.22) | copy-start | bytes 589828
  17.2 10.7 %collective-permute-start.2 = (f32[8,32,128]{2,1,0:T(8,128)S(1)}, f32[8,32,128]{2,1,0:T(8,128)S(1)}, u32[]{:S(2)}, u32[]{:S(2)}) collective-permute-start(f32[8,32,128]{2,1,0:T(8,128)S(1)} %get-tuple-element.56), channel_id=1, source_target_pairs={{0,1},{1,0},{2,3},{3,2},{4,5},{5,4},{6,7},{7,6},{8,9},{9,8},{10,11... | collective-permute-start | bytes 393224 | tf_op jit(solution)/shard_map/ppermute | solution.py:16
  17.3 10.7 %collective-permute-start.3 = (f32[8,32,128]{2,1,0:T(8,128)S(1)}, f32[8,32,128]{2,1,0:T(8,128)S(1)}, u32[]{:S(2)}, u32[]{:S(2)}) collective-permute-start(f32[8,32,128]{2,1,0:T(8,128)S(1)} %get-tuple-element.57), channel_id=1, source_target_pairs={{1,2},{2,1},{3,4},{4,3},{5,6},{6,5},{9,10},{10,9},{11,12},{12,11},... | collective-permute-start | bytes 393224 | tf_op jit(solution)/shard_map/ppermute | solution.py:16
  24.5 11.3 %collective-permute-start.4 = (f32[14,32,128]{2,1,0:T(8,128)S(1)}, f32[14,32,128]{2,1,0:T(8,128)S(1)}, u32[]{:S(2)}, u32[]{:S(2)}) collective-permute-start(f32[14,32,128]{2,1,0:T(8,128)S(1)} %get-tuple-element.61), channel_id=1, source_target_pairs={{0,1},{1,0},{2,3},{3,2},{4,5},{5,4},{6,7},{7,6},{8,9},{9,8},{10,11... | collective-permute-start | bytes 688136 | tf_op jit(solution)/shard_map/ppermute | solution.py:16
  25.6 10.1 %collective-permute-start.5 = (f32[14,32,128]{2,1,0:T(8,128)S(1)}, f32[14,32,128]{2,1,0:T(8,128)S(1)}, u32[]{:S(2)}, u32[]{:S(2)}) collective-permute-start(f32[14,32,128]{2,1,0:T(8,128)S(1)} %get-tuple-element.62), channel_id=1, source_target_pairs={{1,2},{2,1},{3,4},{4,3},{5,6},{6,5},{9,10},{10,9},{11,12},{12,11},... | collective-permute-start | bytes 688136 | tf_op jit(solution)/shard_map/ppermute | solution.py:16
  29.2 3.4 %collective-permute-start.6 = (f32[2,32,128]{2,1,0:T(8,128)S(1)}, f32[2,32,128]{2,1,0:T(8,128)S(1)}, u32[]{:S(2)}, u32[]{:S(2)}) collective-permute-start(f32[2,32,128]{2,1,0:T(8,128)S(1)} %get-tuple-element.63), channel_id=1, source_target_pairs={{0,1},{1,0},{2,3},{3,2},{4,5},{5,4},{6,7},{7,6},{8,9},{9,8},{10,11... | collective-permute-start | bytes 98312 | tf_op jit(solution)/shard_map/ppermute | solution.py:16
  30.5 5.2 %collective-permute-start.7 = (f32[2,32,128]{2,1,0:T(8,128)S(1)}, f32[2,32,128]{2,1,0:T(8,128)S(1)}, u32[]{:S(2)}, u32[]{:S(2)}) collective-permute-start(f32[2,32,128]{2,1,0:T(8,128)S(1)} %get-tuple-element.64), channel_id=1, source_target_pairs={{1,2},{2,1},{3,4},{4,3},{5,6},{6,5},{9,10},{10,9},{11,12},{12,11},... | collective-permute-start | bytes 98312 | tf_op jit(solution)/shard_map/ppermute | solution.py:16
  37.4 2.9 %collective-permute-start.8 = (f32[8,32,128]{2,1,0:T(8,128)S(1)}, f32[8,32,128]{2,1,0:T(8,128)S(1)}, u32[]{:S(2)}, u32[]{:S(2)}) collective-permute-start(f32[8,32,128]{2,1,0:T(8,128)S(1)} %get-tuple-element.70), channel_id=1, source_target_pairs={{0,1},{1,0},{2,3},{3,2},{4,5},{5,4},{6,7},{7,6},{8,9},{9,8},{10,11... | collective-permute-start | bytes 393224 | tf_op jit(solution)/shard_map/ppermute | solution.py:16
  38.4 6.3 %collective-permute-start.9 = (f32[8,32,128]{2,1,0:T(8,128)S(1)}, f32[8,32,128]{2,1,0:T(8,128)S(1)}, u32[]{:S(2)}, u32[]{:S(2)}) collective-permute-start(f32[8,32,128]{2,1,0:T(8,128)S(1)} %get-tuple-element.71), channel_id=1, source_target_pairs={{1,2},{2,1},{3,4},{4,3},{5,6},{6,5},{9,10},{10,9},{11,12},{12,11},... | collective-permute-start | bytes 393224 | tf_op jit(solution)/shard_map/ppermute | solution.py:16
  46.1 6.4 %collective-permute-start.10 = (f32[2,4,32,128]{3,2,1,0:T(8,128)S(1)}, f32[2,4,32,128]{3,2,1,0:T(8,128)S(1)}, u32[]{:S(2)}, u32[]{:S(2)}) collective-permute-start(f32[2,4,32,128]{3,2,1,0:T(8,128)S(1)} %adjoint_two.1), channel_id=1, source_target_pairs={{0,8},{8,0},{16,24},{24,16},{1,9},{9,1},{17,25},{25,17},{2,10},{10... | collective-permute-start | bytes 393224 | tf_op jit(solution)/shard_map/ppermute | solution.py:31
  52.5 8.3 %collective-permute-start.11 = (f32[2,4,32,128]{3,2,1,0:T(8,128)S(1)}, f32[2,4,32,128]{3,2,1,0:T(8,128)S(1)}, u32[]{:S(2)}, u32[]{:S(2)}) collective-permute-start(f32[2,4,32,128]{3,2,1,0:T(8,128)S(1)} %add.21), channel_id=1, source_target_pairs={{0,24},{8,16},{16,8},{24,0},{1,25},{9,17},{17,9},{25,1},{2,26},{10... | collective-permute-start | bytes 393224 | tf_op jit(solution)/shard_map/ppermute | solution.py:31

commit v3 on v2

--- a/solution.py
+++ b/solution.py
@@ -182,17 +182,26 @@
     return lax.dot_general(left, right, (((1,), (1,)), ((), ())), preferred_element_type=F32)
 
 
-def first_kernel(full_x, meta, rate_t, strength_t, wavelet, e_in, h_in, p_in, perm_in, cond_in, cls_in, cells, signs,
-                 e_ref, h_ref, p_ref, coef_ref, src_ref, a_ref, b_ref, perm, cond, cls, sems):
+def first_kernel(full_x, meta, e_in, h_in, p_in, perm_in, cond_in, cls_in, cells_in, signs_in, rate_in, strength_in,
+                 wavelet_in, e_ref, h_ref, p_ref, coef_ref, src_ref, tab_ref, a_ref, b_ref, perm, cond, cls, cells, signs,
+                 rate_t, strength_t, wavelet, sems):
     even = meta[1] == 0
     width, depth, span = perm.shape
-    moves = [(perm_in, perm), (cond_in, cond), (cls_in, cls), (e_in, e_ref), (h_in, h_ref), (p_in, p_ref)]
+    moves = [(cells_in, cells), (signs_in, signs), (wavelet_in, wavelet), (rate_in, rate_t), (strength_in, strength_t)]
+    moves += [(perm_in, perm), (cond_in, cond), (cls_in, cls), (e_in, e_ref), (h_in, h_ref), (p_in, p_ref)]
     copies = [pltpu.make_async_copy(a, b, sems.at[k]) for k, (a, b) in enumerate(moves)]
     for copy in copies:
         copy.start()
+    for copy in copies[:5]:
+        copy.wait()
+    listed = [rate_t[k] for k in range(rate_t.shape[0])]
+    listed += [(1.0 - rate_t[k]) * strength_t[k] for k in range(rate_t.shape[0])]
+    listed += [wavelet[k] for k in range(wavelet.shape[0])]
+    for k, value in enumerate(listed):
+        tab_ref[k:k + 1, :] = jnp.full((1, span), value, F32)
     src = source_map(cells, signs, meta[0], width, depth, span, full_x)
     src_ref[...] = src.reshape(width + 2, depth, span)
-    for copy in copies[:3]:
+    for copy in copies[5:8]:
         copy.wait()
     for i in range(width):
         ratio = cond[i] / (2.0 * perm[i])
@@ -206,7 +215,7 @@
             gain = jnp.where(kind == k, (1.0 - rate_t[k]) * strength_t[k], gain)
         coef_ref[2, i] = rate
         coef_ref[3, i] = gain
-    for copy in copies[3:]:
+    for copy in copies[8:]:
         copy.wait()
     planes = own_planes(e_ref, h_ref, p_ref)
     h1, e1 = pre_steps(planes, lambda i: [coef_ref[k, i] for k in range(4)], lambda i: src_ref[i + 1] * wavelet[0])
@@ -223,38 +232,44 @@
     emit_state(meta[1] == 0, planes, h1, e1, a_ref, b_ref, True)
 
 
-def receiver_kernel(width, depth, meta, got, maps_ref, acc):
+def receiver_kernel(width, depth, which, meta, got, maps_ref, acc):
     mine = meta[0]
-    rows = (width + 2) * depth
+    rows = (width + 4) * depth
     span = acc.shape[1]
-    blocks, lists, n = got.shape
-    steps = lists - 2
+    blocks, _, n = got.shape
     acc[...] = jnp.zeros(acc.shape, F32)
-    first_row = ((mine * width - 1) * depth).astype(F32)
+    first_row = ((mine * width - 2) * depth).astype(F32)
     row_at = lax.broadcasted_iota(jnp.int32, (rows, n), 0).astype(F32)
     y_at = lax.broadcasted_iota(jnp.int32, (span, n), 0).astype(F32)
-
-    def block(b, carry):
-        hot = row_at == got[b, 0:1, :] - first_row
-        at_y = jnp.where(y_at == got[b, 1:2, :], 1.0, 0.0).astype(jnp.bfloat16)
-        zero = jnp.zeros((rows, n), jnp.bfloat16)
-        left = [jnp.concatenate([jnp.where(hot, 1.0, 0.0).astype(jnp.bfloat16), zero, zero], axis=1)]
-        for s in range(steps):
-            v = got[b, 2 + s:3 + s, :]
-            high = v.astype(jnp.bfloat16).astype(F32)
-            mid = (v - high).astype(jnp.bfloat16).astype(F32)
-            low = (v - high) - mid
-            parts = [jnp.where(hot, u, 0.0).astype(jnp.bfloat16) for u in (high, mid, low)]
-            left.append(jnp.concatenate(parts, axis=1))
+    group = max(g for g in (1, 2, 4, 8) if blocks % g == 0)
+    zero = jnp.zeros((rows, n), jnp.bfloat16)
+
+    def block(k, carry):
+        left = [[] for _ in which]
+        right = []
+        for b in range(group):
+            at = k * group + b
+            hot = row_at == got[at, 0:1, :] - first_row
+            at_y = jnp.where(y_at == got[at, 1:2, :], 1.0, 0.0).astype(jnp.bfloat16)
+            right += [at_y] * 3
+            for part, s in zip(left, which):
+                if s == 0:
+                    part += [jnp.where(hot, 1.0, 0.0).astype(jnp.bfloat16), zero, zero]
+                    continue
+                v = got[at, 1 + s:2 + s, :]
+                high = v.astype(jnp.bfloat16).astype(F32)
+                mid = (v - high).astype(jnp.bfloat16).astype(F32)
+                low = (v - high) - mid
+                part += [jnp.where(hot, u, 0.0).astype(jnp.bfloat16) for u in (high, mid, low)]
         acc[...] += lax.dot_general(
-            jnp.concatenate(left, axis=0),
-            jnp.concatenate([at_y, at_y, at_y], axis=1),
+            jnp.concatenate([jnp.concatenate(part, axis=1) for part in left], axis=0) if len(left) > 1 else jnp.concatenate(left[0], axis=1),
+            jnp.concatenate(right, axis=1),
             (((1,), (1,)), ((), ())),
             preferred_element_type=F32,
         )
         return carry
 
-    lax.fori_loop(0, blocks, block, 0)
+    lax.fori_loop(0, blocks // group, block, 0)
     maps_ref[...] = acc[...].reshape(maps_ref.shape)
 
 
@@ -363,19 +378,21 @@
     return dest
 
 
-def forward_one_kernel(meta, rate_t, strength_t, wavelet, e_ref, h_ref, p_ref, coef_ref, src_ref, a_ref, b_ref,
+def forward_one_kernel(meta, tab_ref, e_ref, h_ref, p_ref, coef_ref, src_ref, b_ref, a_ref,
                        hist_ref, hs_ref, ps_ref, coefh_ref, eyh_ref, oa_ref, ob_ref, es_ref):
     even = meta[1] == 0
     width = e_ref.shape[1]
+    classes = (tab_ref.shape[0] - 2 * ROUND) // 2
+    wavelet = 2 * classes
     for side in (0, 1):
         coefh_ref[side, 0] = pick(even, a_ref, b_ref, 14, side == 0)
         coefh_ref[side, 1] = pick(even, a_ref, b_ref, 15, side == 0)
         kind = pick(even, a_ref, b_ref, 16, side == 0)
         rate = jnp.zeros(kind.shape, F32)
         gain = jnp.zeros(kind.shape, F32)
-        for k in range(rate_t.shape[0]):
-            rate = jnp.where(kind == float(k), rate_t[k], rate)
-            gain = jnp.where(kind == float(k), (1.0 - rate_t[k]) * strength_t[k], gain)
+        for k in range(classes):
+            rate = jnp.where(kind == float(k), tab_ref[k:k + 1, :], rate)
+            gain = jnp.where(kind == float(k), tab_ref[classes + k:classes + k + 1, :], gain)
         coefh_ref[side, 2] = rate
         coefh_ref[side, 3] = gain
     planes = own_planes(e_ref, h_ref, p_ref)
@@ -385,7 +402,7 @@
             eyh_ref[0 if i < 0 else 1] = e[1]
 
     round_body(planes, meta, coef_ref, coefh_ref, a_ref, b_ref, True,
-               lambda level, i: src_ref[i + 1] * wavelet[level - 1], None,
+               lambda level, i: src_ref[i + 1] * tab_ref[wavelet + level - 1:wavelet + level, :], None,
                scratch_dest(es_ref, hs_ref, ps_ref, hist_ref, width), (oa_ref, ob_ref), seen)
 
 
@@ -406,10 +423,11 @@
     return planes
 
 
-def forward_two_kernel(meta, wavelet, hist_in, hs_in, ps_in, coef_ref, coefh_ref, src_ref, maps_ref, a_ref, b_ref,
+def forward_two_kernel(meta, tab_ref, hist_in, hs_in, ps_in, coef_ref, coefh_ref, src_ref, b_ref, a_ref,
                        hist_ref, eyh_ref, oa_ref, ob_ref, es_ref, hs_ref, ps_ref):
     even = meta[1] == 0
     width = hist_in.shape[2]
+    wavelet = tab_ref.shape[0] - ROUND
     planes = state_planes(hist_in, hs_in, ps_in, 2)
     eyh_ref[0] = pick(even, a_ref, b_ref, 1, True)
     eyh_ref[1] = pick(even, a_ref, b_ref, 1, False)
@@ -419,16 +437,11 @@
             eyh_ref[2 if i < 0 else 3] = e[1]
 
     round_body(planes, meta, coef_ref, coefh_ref, a_ref, b_ref, False,
-               lambda level, i: src_ref[i + 1] * wavelet[ROUND + level - 1], None,
+               lambda level, i: src_ref[i + 1] * tab_ref[wavelet + level - 1:wavelet + level, :], None,
                scratch_dest(es_ref, hs_ref, ps_ref, hist_ref, width), None, seen)
-    steps = 2 * ROUND
-
-    def resid(i):
-        return maps_ref[0, i + 1] * hist_ref[2, 1, i] - maps_ref[steps, i + 1]
-
     last = width - 1
-    emit(even, oa_ref, ob_ref, 0, resid(last), resid(0))
-    emit(even, oa_ref, ob_ref, 1, resid(last - 1), resid(1))
+    emit(even, oa_ref, ob_ref, 0, hist_ref[2, 1, last], hist_ref[2, 1, 0])
+    emit(even, oa_ref, ob_ref, 1, hist_ref[2, 1, last - 1], hist_ref[2, 1, 1])
 
 
 def correlate(corr_ref, i, b, now, prev, add):
@@ -440,8 +453,8 @@
     corr_ref[1, i] = sig
 
 
-def adjoint_one_kernel(meta, e_ref, h_ref, p_ref, coef_ref, coefh_ref, maps_ref, hist1_ref, hist2_ref, eyh_ref,
-                       a_ref, b_ref, ra_ref, rb_ref, e_out, hs_ref, ps_ref, corr_ref, oa_ref, ob_ref, es_ref):
+def adjoint_one_kernel(meta, e_ref, h_ref, p_ref, coef_ref, coefh_ref, maps6_ref, maps5_ref, hist1_ref, hist2_ref, eyh_ref,
+                       b_ref, a_ref, rb_ref, ra_ref, e_out, hs_ref, ps_ref, corr_ref, oa_ref, ob_ref, es_ref):
     even = meta[1] == 0
     width = e_ref.shape[1]
     steps = 2 * ROUND
@@ -455,14 +468,17 @@
 
     def extra(i):
         if i < 0:
-            return pick(even, ra_ref, rb_ref, -1 - i, True)
-        return pick(even, ra_ref, rb_ref, i - width, False)
+            ey_last = pick(even, ra_ref, rb_ref, -1 - i, True)
+        else:
+            ey_last = pick(even, ra_ref, rb_ref, i - width, False)
+        return maps6_ref[0, i + 2] * ey_last - maps6_ref[1, i + 2]
 
     def inject(level, i):
         n = steps + 1 - level
         if n == steps and not 0 <= i < width:
             return extra(i)
-        return maps_ref[0, i + 1] * ey(n, i) - maps_ref[n, i + 1]
+        seen_at = maps6_ref[1, i + 2] if n == steps else maps5_ref[steps - 1 - n, i + 2]
+        return maps6_ref[0, i + 2] * ey(n, i) - seen_at
 
     def seen(level, i, e):
         if not 0 <= i < width:
@@ -484,8 +500,8 @@
     round_body(planes, meta, coef_ref, coefh_ref, a_ref, b_ref, True, inject, extra, dest, (oa_ref, ob_ref), seen)
 
 
-def adjoint_two_kernel(meta, e_ref, hs_in, ps_in, coef_ref, coefh_ref, maps_ref, e0_ref, hist1_ref, ey2_ref, eyh_ref,
-                       corr_in, a_ref, b_ref, corr_ref, es_ref, hs_ref, ps_ref):
+def adjoint_two_kernel(meta, e_ref, hs_in, ps_in, coef_ref, coefh_ref, maps6_ref, maps5_ref, maps2_ref, e0_ref, hist1_ref, ey2_ref, eyh_ref,
+                       corr_in, b_ref, a_ref, corr_ref, es_ref, hs_ref, ps_ref):
     width = e_ref.shape[1]
     steps = 2 * ROUND
     planes = state_planes(e_ref, hs_in, ps_in)
@@ -499,7 +515,8 @@
 
     def inject(level, i):
         n = steps + 1 - ROUND - level
-        return maps_ref[0, i + 1] * ey(n, i) - maps_ref[n, i + 1]
+        seen_at = maps5_ref[ROUND - 1, i + 2] if n == ROUND else maps2_ref[ROUND - 1 - n, i + 2]
+        return maps6_ref[0, i + 2] * ey(n, i) - seen_at
 
     def seen(level, i, e):
         if not 0 <= i < width:
@@ -564,19 +581,26 @@
     adjoint = (adj_electric[0], adj_magnetic[0], adj_polar[0])
 
     own = (3, width, *plane)
-    *fields, coef, src, a1, b1 = call(
+    classes = debye_rate.shape[0]
+    tab_rows = 2 * classes + steps
+    *fields, coef, src, tab, a1, b1 = call(
         lambda *refs: first_kernel(width * nsub, *refs),
         "first",
-        [*fields, permittivity, conductivity, debye_class, src_cell, src_sign],
-        [meta, debye_rate, debye_strength, wavelet],
-        [own, own, own, (4, width, *plane), (width + 2, *plane), (17, *plane), (17, *plane)],
+        [*fields, permittivity, conductivity, debye_class, src_cell, src_sign, debye_rate, debye_strength, wavelet],
+        [meta],
+        [own, own, own, (4, width, *plane), (width + 2, *plane), (tab_rows, span), (17, *plane), (17, *plane)],
         [
             (width, *plane),
             (width, *plane),
             pltpu.VMEM((width, *plane), jnp.int32),
-            pltpu.SemaphoreType.DMA((6,)),
+            pltpu.VMEM(src_cell.shape, jnp.int32),
+            pltpu.VMEM(src_sign.shape, jnp.int32),
+            pltpu.SMEM(debye_rate.shape, F32),
+            pltpu.SMEM(debye_strength.shape, F32),
+            pltpu.SMEM(wavelet.shape, F32),
+            pltpu.SemaphoreType.DMA((11,)),
         ],
-        remote=6,
+        remote=11,
     )
     got_a1, got_b1 = exchange(a1, b1)
     listed, b1 = lax.optimization_barrier((listed, b1))
@@ -586,46 +610,54 @@
     hist1, hs, ps, coefh, ey2, a2, b2 = call(
         forward_one_kernel,
         "forward_one",
-        [*fields, coef, src, got_a1, got_b1],
-        [meta, debye_rate, debye_strength, wavelet],
+        [tab, *fields, coef, src, got_b1, got_a1],
+        [meta],
         [(ROUND, 3, width, *plane), h_sh, p_sh, (2, 4, *plane), (2, *plane), (8, *plane), (8, *plane)],
         [e_sh],
     )
-    got, a2, b2 = lax.optimization_barrier((got, a2, b2))
+    got, coef, a2, b2 = lax.optimization_barrier((got, coef, a2, b2))
     got_a2, got_b2 = exchange(a2, b2)
-    (maps,) = call(
-        lambda *refs: receiver_kernel(width, depth, *refs),
-        "receivers",
-        [got],
-        [meta],
-        [(steps + 1, width + 2, *plane)],
-        [((steps + 1) * (width + 2) * depth, span)],
-    )
-    coef_later, maps = lax.optimization_barrier((coef, maps))
-    a3, b3 = call(adjoint_first_kernel, "adjoint_first", [*adjoint, coef_later], [meta], [(14, *plane), (14, *plane)])
+    a3, b3 = call(adjoint_first_kernel, "adjoint_first", [*adjoint, coef], [meta], [(14, *plane), (14, *plane)])
     got_a3, got_b3 = exchange(a3, b3)
+
+    def receivers(name, which):
+        (maps,) = call(
+            lambda *refs: receiver_kernel(width, depth, which, *refs),
+            name,
+            [got],
+            [meta],
+            [(len(which), width + 4, *plane)],
+            [(len(which) * (width + 4) * depth, span)],
+        )
+        return maps
+
+    maps6 = receivers("receivers_last", (0, steps))
     hist2, eyh, a4, b4 = call(
         forward_two_kernel,
         "forward_two",
-        [hist1, hs, ps, coef, coefh, src, maps, got_a2, got_b2],
-        [meta, wavelet],
+        [tab, hist1, hs, ps, coef, coefh, src, got_b2, got_a2],
+        [meta],
         [(ROUND, 3, width, *plane), (4, *plane), (2, *plane), (2, *plane)],
         [e_sh, h_sh, p_sh],
     )
+    got, a4, b4 = lax.optimization_barrier((got, a4, b4))
     got_a4, got_b4 = exchange(a4, b4)
+    maps5 = receivers("receivers_middle", tuple(range(steps - 1, ROUND - 1, -1)))
     e_adj, hs, ps, corr, a5, b5 = call(
         adjoint_one_kernel,
         "adjoint_one",
-        [*adjoint, coef, coefh, maps, hist1, hist2, eyh, got_a3, got_b3, got_a4, got_b4],
+        [*adjoint, coef, coefh, maps6, maps5, hist1, hist2, eyh, got_b3, got_a3, got_b4, got_a4],
         [meta],
         [(3, width, *plane), h_sh, p_sh, (2, width, *plane), (8, *plane), (8, *plane)],
         [e_sh],
     )
+    got, a5, b5 = lax.optimization_barrier((got, a5, b5))
     got_a5, got_b5 = exchange(a5, b5)
+    maps2 = receivers("receivers_first", tuple(range(ROUND - 1, 0, -1)))
     (corr,) = call(
         adjoint_two_kernel,
         "adjoint_two",
-        [e_adj, hs, ps, coef, coefh, maps, fields[0], hist1, ey2, eyh, corr, got_a5, got_b5],
+        [e_adj, hs, ps, coef, coefh, maps6, maps5, maps2, fields[0], hist1, ey2, eyh, corr, got_b5, got_a5],
         [meta],
         [(2, width, *plane)],
         [e_sh, h_sh, p_sh],

time: 61.8 us -> 56.9 us (0.921)
  the two profiles are of different devices: /device:TPU:18 before, /device:TPU:4 now
where the time goes in v3:
time: 56.9 us; the launch traced here: 56.4 us
  starting transfers between devices  21.8 us (38%)
  Pallas kernels  13.4 us (24%)
  waiting for transfers between devices  11.9 us (21%)
  blocking collectives  7.56 us (13%)
  between operations  0.92 us (2%)
  other arithmetic  0.79 us (1%)
    ppermute x10, starting transfers between devices, pair_swap(): return lax.ppermute(block, axis, route)  16.7 us
    pallas_call x9, Pallas kernels, call(): pl.pallas_call(body, name=name, out_shape=[jax.ShapeDtypeStruct(s, F32) f...  13.4 us
    all_to_all x1, blocking collectives, per_device(): lax.all_to_all(jnp.broadcast_to(listed[None], (nsub, *listed.shape)), 'su...  7.56 us
    ppermute x2, waiting for transfers between devices, shot_sum(): x = x + lax.ppermute(x, 'shot', [(i, i ^ flip) for i in range(n)])  6.87 us
    ppermute x2, starting transfers between devices, shot_sum(): x = x + lax.ppermute(x, 'shot', [(i, i ^ flip) for i in range(n)])  5.1 us
    ppermute x10, waiting for transfers between devices, pair_swap(): return lax.ppermute(block, axis, route)  5.03 us
  transfers between devices with their start and end apart: 12, of which 4 were waited for; matrix products, arithmetic and copies ran while one was open for 0% of the time, Pallas kernels for 12%

profile of v3, /device:TPU:4, one launch (start us, length us, event | category | flops | bytes accessed | tf_op | source)
XLA Modules:
  0.0 56.4 jit_solution(13264977445426290840)
XLA Ops:
  0.6 0.1 pad_add_fusion.refs_0_.meta
  0.7 2.1 %first.1 = (f32[3,4,32,128]{3,2,1,0:T(8,128)S(1)}, f32[3,4,32,128]{3,2,1,0:T(8,128)S(1)}, f32[3,4,32,128]{3,2,1,0:T(8,128)S(1)}, f32[4,4,32,128]{3,2,1,0:T(8,128...) custom-call(s32[2]{0:T(128)S(1)} %pad_add_fusion.refs_0_.meta, ...), custom_call_target="tpu_custom_call" | custom-call | flops 10000000000 | tf_op jit(solution)/shard_map/first/pallas_call | solution.py:537
  2.8 0.0 copy-start.3
  2.8 0.1 collective-permute-start
  2.9 0.0 copy-start.4
  2.9 0.0 copy-start.5
  2.9 3.5 %collective-permute-start.1 = (f32[17,32,128]{2,1,0:T(8,128)S(1)}, f32[17,32,128]{2,1,0:T(8,128)S(1)}, u32[]{:S(2)}, u32[]{:S(2)}) collective-permute-start(f32[17,32,128]{2,1,0:T(8,128)S(1)} %get-tuple-element.43), channel_id=1, source_target_pairs={{1,2},{2,1},{3,4},{4,3},{5,6},{6,5},{9,10},{10,9},{11,12},{12,11},... | collective-permute-start | bytes 835592 | tf_op jit(solution)/shard_map/ppermute | solution.py:16
  6.5 0.0 copy-done.3
  6.5 0.0 copy-done.4
  6.5 0.0 copy-done.5
  6.5 7.6 %all_to_all.5.refs_1_ = f32[8,8,128]{2,1,0:T(8,128)S(1)} all-to-all(f32[8,8,128]{2,1,0:T(8,128)S(1)} %broadcast_in_dim.2), channel_id=1, replica_groups=mesh['shot'=4,'sub'=8] {'sub'}, dimensions={0} | all-to-all | bytes 65536 | tf_op jit(solution)/shard_map/all_to_all | solution.py:607
  14.1 0.0 collective-permute-done.a_ref
  14.1 0.0 collective-permute-done.1.b_ref
  14.1 1.3 %forward_one.1 = (f32[3,3,4,32,128]{4,3,2,1,0:T(8,128)S(1)}, f32[3,7,32,128]{3,2,1,0:T(8,128)S(1)}, f32[3,6,32,128]{3,2,1,0:T(8,128)S(1)}, f32[2,4,32,128]{3,2,1...) custom-call(s32[2]{0:T(128)S(1)} %pad_add_fusion.refs_0_.meta, ...), custom_call_target="tpu_custom_call" | custom-call | flops 10000000000 | tf_op jit(solution)/shard_map/forward_one/pallas_call | solution.py:537
  15.4 0.0 copy-start
  15.5 0.0 copy-start.1
  15.5 0.0 copy-start.2
  15.5 3.7 %collective-permute-start.2 = (f32[8,32,128]{2,1,0:T(8,128)S(1)}, f32[8,32,128]{2,1,0:T(8,128)S(1)}, u32[]{:S(2)}, u32[]{:S(2)}) collective-permute-start(f32[8,32,128]{2,1,0:T(8,128)S(1)} %get-tuple-element.63), channel_id=1, source_target_pairs={{1,2},{2,1},{3,4},{4,3},{5,6},{6,5},{9,10},{10,9},{11,12},{12,11},... | collective-permute-start | bytes 393224 | tf_op jit(solution)/shard_map/ppermute | solution.py:16
  19.2 0.1 collective-permute-start.3
  19.3 1.5 %receivers_last.1.maps6_ref = f32[2,8,32,128]{3,2,1,0:T(8,128)S(1)} custom-call(s32[2]{0:T(128)S(1)} %pad_add_fusion.refs_0_.meta, f32[8,8,128]{2,1,0:T(8,128)S(1)} %all_to_all.5.refs_1_), custom_call_target="tpu_custom_call" | custom-call | flops 10000000000 | tf_op jit(solution)/shard_map/receivers_last/pallas_call | solution.py:537
  20.8 0.0 copy-done
  20.8 0.0 copy-done.1
  20.8 0.0 copy-done.2
  20.9 0.7 %adjoint_first.1 = (f32[14,32,128]{2,1,0:T(8,128)S(1)}, f32[14,32,128]{2,1,0:T(8,128)S(1)}) custom-call(s32[2]{0:T(128)S(1)} %pad_add_fusion.refs_0_.meta, f32[3,4,32,128]{3,2,1,0:T(8,128)S(1)} %bitcast.23, f32[3,4,32,128]{3,2,1,0:T(8,128)S(1)} %bitcast.25, f32[3,4,32,128]{3,2,1,0:T(8,128)S(1)} %bitcast.27, f32[4,4,32,128]{3,2,1,0:T(8,128)S(1)} %get-tuple-element.57.coef_ref), custom_call_target="tpu_custom_call" | custom-call | flops 10000000000 | tf_op jit(solution)/shard_map/adjoint_first/pallas_call | solution.py:537
  21.6 2.9 %collective-permute-start.4 = (f32[14,32,128]{2,1,0:T(8,128)S(1)}, f32[14,32,128]{2,1,0:T(8,128)S(1)}, u32[]{:S(2)}, u32[]{:S(2)}) collective-permute-start(f32[14,32,128]{2,1,0:T(8,128)S(1)} %get-tuple-element.70), channel_id=1, source_target_pairs={{1,2},{2,1},{3,4},{4,3},{5,6},{6,5},{9,10},{10,9},{11,12},{12,11},... | collective-permute-start | bytes 688136 | tf_op jit(solution)/shard_map/ppermute | solution.py:16
  24.4 0.1 collective-permute-start.5
  24.5 0.0 collective-permute-done.2.b_ref
  24.5 0.0 collective-permute-done.3.a_ref
  24.5 1.3 %forward_two.1 = (f32[3,3,4,32,128]{4,3,2,1,0:T(8,128)S(1)}, f32[4,32,128]{2,1,0:T(8,128)S(1)}, f32[2,32,128]{2,1,0:T(8,128)S(1)}, f32[2,32,128]{2,1,0:T(8,128)S(1)}) custom-call(s32[2]{0:T(128)S(1)} %pad_add_fusion.refs_0_.meta, f32[22,128]{1,0:T(8,128)S(1)} %get-tuple-element.48.tab_ref, f32[3,3,4,32,128]{4,3,2,1,0:T(8,128)S(1)} %get-tuple-element.60.hist_in.hist1_ref, ...), custom_call_target="tpu_custom_call" | custom-call | flops 10000000000 | tf_op jit(solution)/shard_map/forward_two/pallas_call | solution.py:537
  25.8 3.6 %collective-permute-start.6 = (f32[2,32,128]{2,1,0:T(8,128)S(1)}, f32[2,32,128]{2,1,0:T(8,128)S(1)}, u32[]{:S(2)}, u32[]{:S(2)}) collective-permute-start(f32[2,32,128]{2,1,0:T(8,128)S(1)} %get-tuple-element.72), channel_id=1, source_target_pairs={{1,2},{2,1},{3,4},{4,3},{5,6},{6,5},{9,10},{10,9},{11,12},{12,11},... | collective-permute-start | bytes 98312 | tf_op jit(solution)/shard_map/ppermute | solution.py:16
  29.4 0.1 collective-permute-start.7
  29.5 1.9 %receivers_middle.1.maps5_ref = f32[3,8,32,128]{3,2,1,0:T(8,128)S(1)} custom-call(s32[2]{0:T(128)S(1)} %pad_add_fusion.refs_0_.meta, f32[8,8,128]{2,1,0:T(8,128)S(1)} %all_to_all.5.refs_1_), custom_call_target="tpu_custom_call" | custom-call | flops 10000000000 | tf_op jit(solution)/shard_map/receivers_middle/pallas_call | solution.py:537
  31.4 1.5 %collective-permute-done.6.rb_ref = f32[2,32,128]{2,1,0:T(8,128)S(1)} collective-permute-done((f32[2,32,128]{2,1,0:T(8,128)S(1)}, f32[2,32,128]{2,1,0:T(8,128)S(1)}, u32[]{:S(2)}, u32[]{:S(2)}) %collective-permute-start.6) | collective-permute-done | bytes 32800 | tf_op jit(solution)/shard_map/ppermute | solution.py:16
  32.9 0.0 collective-permute-done.7.ra_ref
  32.9 0.0 collective-permute-done.4.b_ref
  32.9 0.0 collective-permute-done.5.a_ref
  32.9 1.6 %adjoint_one.1 = (f32[3,4,32,128]{3,2,1,0:T(8,128)S(1)}, f32[3,7,32,128]{3,2,1,0:T(8,128)S(1)}, f32[3,6,32,128]{3,2,1,0:T(8,128)S(1)}, f32[2,4,32,128]{3,2,1,0:T...) custom-call(s32[2]{0:T(128)S(1)} %pad_add_fusion.refs_0_.meta, f32[3,4,32,128]{3,2,1,0:T(8,128)S(1)} %bitcast.24, ...), custom_call_target="tpu_custom_call" | custom-call | flops 10000000000 | tf_op jit(solution)/shard_map/adjoint_one/pallas_call | solution.py:537
  34.6 2.6 %collective-permute-start.8 = (f32[8,32,128]{2,1,0:T(8,128)S(1)}, f32[8,32,128]{2,1,0:T(8,128)S(1)}, u32[]{:S(2)}, u32[]{:S(2)}) collective-permute-start(f32[8,32,128]{2,1,0:T(8,128)S(1)} %get-tuple-element.82), channel_id=1, source_target_pairs={{1,2},{2,1},{3,4},{4,3},{5,6},{6,5},{9,10},{10,9},{11,12},{12,11},... | collective-permute-start | bytes 393224 | tf_op jit(solution)/shard_map/ppermute | solution.py:16
  37.2 0.1 collective-permute-start.9
  37.3 1.5 %receivers_first.1.maps2_ref = f32[2,8,32,128]{3,2,1,0:T(8,128)S(1)} custom-call(s32[2]{0:T(128)S(1)} %pad_add_fusion.refs_0_.meta, f32[8,8,128]{2,1,0:T(8,128)S(1)} %all_to_all.5.refs_1_), custom_call_target="tpu_custom_call" | custom-call | flops 10000000000 | tf_op jit(solution)/shard_map/receivers_first/pallas_call | solution.py:537
  38.8 3.5 %collective-permute-done.8.b_ref = f32[8,32,128]{2,1,0:T(8,128)S(1)} collective-permute-done((f32[8,32,128]{2,1,0:T(8,128)S(1)}, f32[8,32,128]{2,1,0:T(8,128)S(1)}, u32[]{:S(2)}, u32[]{:S(2)}) %collective-permute-start.8) | collective-permute-done | bytes 131104 | tf_op jit(solution)/shard_map/ppermute | solution.py:16
  42.3 0.0 collective-permute-done.9.a_ref
  42.3 1.4 %adjoint_two.1 = f32[2,4,32,128]{3,2,1,0:T(8,128)S(1)} custom-call(s32[2]{0:T(128)S(1)} %pad_add_fusion.refs_0_.meta, f32[3,4,32,128]{3,2,1,0:T(8,128)S(1)} %get-tuple-element.74.e_ref, f32[3,7,32,128]{3,2,1,0:T(8,128)S(1)} %get-tuple-element.75.hs_in, f32[3,6,32,128]{3,2,1,0:T(8,128)S(1)} %get-tuple-element.76.ps_in, ...), custom_call_target="tpu_custom_call" | custom-call | flops 10000000000 | tf_op jit(solution)/shard_map/adjoint_two/pallas_call | solution.py:537
  43.7 1.5 %collective-permute-start.10 = (f32[2,4,32,128]{3,2,1,0:T(8,128)S(1)}, f32[2,4,32,128]{3,2,1,0:T(8,128)S(1)}, u32[]{:S(2)}, u32[]{:S(2)}) collective-permute-start(f32[2,4,32,128]{3,2,1,0:T(8,128)S(1)} %adjoint_two.1), channel_id=1, source_target_pairs={{0,8},{8,0},{16,24},{24,16},{1,9},{9,1},{17,25},{25,17},{2,10},{10... | collective-permute-start | bytes 393224 | tf_op jit(solution)/shard_map/ppermute | solution.py:31
  45.3 3.5 %collective-permute-done.10 = f32[2,4,32,128]{3,2,1,0:T(8,128)S(1)} collective-permute-done((f32[2,4,32,128]{3,2,1,0:T(8,128)S(1)}, f32[2,4,32,128]{3,2,1,0:T(8,128)S(1)}, u32[]{:S(2)}, u32[]{:S(2)}) %collective-permute-start.10) | collective-permute-done | bytes 131104 | tf_op jit(solution)/shard_map/ppermute | solution.py:31
  48.8 3.6 %collective-permute-start.11 = (f32[2,4,32,128]{3,2,1,0:T(8,128)S(1)}, f32[2,4,32,128]{3,2,1,0:T(8,128)S(1)}, u32[]{:S(2)}, u32[]{:S(2)}) collective-permute-start(f32[2,4,32,128]{3,2,1,0:T(8,128)S(1)} %add.21), channel_id=1, source_target_pairs={{0,24},{8,16},{16,8},{24,0},{1,25},{9,17},{17,9},{25,1},{2,26},{10... | collective-permute-start | bytes 393224 | tf_op jit(solution)/shard_map/ppermute | solution.py:31
  52.3 3.4 %collective-permute-done.11 = f32[2,4,32,128]{3,2,1,0:T(8,128)S(1)} collective-permute-done((f32[2,4,32,128]{3,2,1,0:T(8,128)S(1)}, f32[2,4,32,128]{3,2,1,0:T(8,128)S(1)}, u32[]{:S(2)}, u32[]{:S(2)}) %collective-permute-start.11) | collective-permute-done | bytes 131104 | tf_op jit(solution)/shard_map/ppermute | solution.py:31
  55.7 0.7 %fusion.1 = (f32[4,32,128]{2,1,0:T(8,128)}, f32[4,32,128]{2,1,0:T(8,128)}) fusion(f32[2,4,32,128]{3,2,1,0:T(8,128)S(1)} %add.22), kind=kLoop, calls=%fused_computation.2 | loop fusion | flops 65536 | bytes 262144 | tf_op jit(solution)/shard_map/neg | solution.py:666
  (6 shorter events, 0.1 us)
Async XLA Ops:
  2.8 3.7 %copy-start.3 = (f32[1,6,128]{2,0,1:T(1,128)S(1)}, f32[1,6,128]{2,0,1:T(1,128)}, u32[]{:S(2)}) copy-start(f32[1,6,128]{2,0,1:T(1,128)} %param.33) | copy-start | bytes 9220
  2.8 11.3 %collective-permute-start = (f32[17,32,128]{2,1,0:T(8,128)S(1)}, f32[17,32,128]{2,1,0:T(8,128)S(1)}, u32[]{:S(2)}, u32[]{:S(2)}) collective-permute-start(f32[17,32,128]{2,1,0:T(8,128)S(1)} %get-tuple-element.45), channel_id=1, source_target_pairs={{0,1},{1,0},{2,3},{3,2},{4,5},{5,4},{6,7},{7,6},{8,9},{9,8},{10,11... | collective-permute-start | bytes 835592 | tf_op jit(solution)/shard_map/ppermute | solution.py:16
  2.9 3.6 %copy-start.4 = (s32[1,128]{1,0:T(1,128)S(1)}, s32[1,128]{1,0:T(1,128)}, u32[]{:S(2)}) copy-start(s32[1,128]{1,0:T(1,128)} %param.32) | copy-start | bytes 1540
  2.9 3.6 %copy-start.5 = (s32[1,128,1]{1,2,0:T(1,128)S(1)}, s32[1,128,1]{1,2,0:T(1,128)}, u32[]{:S(2)}) copy-start(s32[1,128,1]{1,2,0:T(1,128)} %param.31) | copy-start | bytes 1540
  2.9 11.2 %collective-permute-start.1 = (f32[17,32,128]{2,1,0:T(8,128)S(1)}, f32[17,32,128]{2,1,0:T(8,128)S(1)}, u32[]{:S(2)}, u32[]{:S(2)}) collective-permute-start(f32[17,32,128]{2,1,0:T(8,128)S(1)} %get-tuple-element.43), channel_id=1, source_target_pairs={{1,2},{2,1},{3,4},{4,3},{5,6},{6,5},{9,10},{10,9},{11,12},{12,11},... | collective-permute-start | bytes 835592 | tf_op jit(solution)/shard_map/ppermute | solution.py:16
  15.4 5.4 %copy-start = (f32[1,3,4,32,128]{4,3,2,1,0:T(8,128)S(1)}, f32[1,3,4,32,128]{4,3,2,1,0:T(8,128)}, u32[]{:S(2)}) copy-start(f32[1,3,4,32,128]{4,3,2,1,0:T(8,128)} %param.20) | copy-start | bytes 589828
  15.5 5.4 %copy-start.1 = (f32[1,3,4,32,128]{4,3,2,1,0:T(8,128)S(1)}, f32[1,3,4,32,128]{4,3,2,1,0:T(8,128)}, u32[]{:S(2)}) copy-start(f32[1,3,4,32,128]{4,3,2,1,0:T(8,128)} %param.21) | copy-start | bytes 589828
  15.5 5.4 %copy-start.2 = (f32[1,3,4,32,128]{4,3,2,1,0:T(8,128)S(1)}, f32[1,3,4,32,128]{4,3,2,1,0:T(8,128)}, u32[]{:S(2)}) copy-start(f32[1,3,4,32,128]{4,3,2,1,0:T(8,128)} %param.22) | copy-start | bytes 589828
  15.5 9.0 %collective-permute-start.2 = (f32[8,32,128]{2,1,0:T(8,128)S(1)}, f32[8,32,128]{2,1,0:T(8,128)S(1)}, u32[]{:S(2)}, u32[]{:S(2)}) collective-permute-start(f32[8,32,128]{2,1,0:T(8,128)S(1)} %get-tuple-element.63), channel_id=1, source_target_pairs={{1,2},{2,1},{3,4},{4,3},{5,6},{6,5},{9,10},{10,9},{11,12},{12,11},... | collective-permute-start | bytes 393224 | tf_op jit(solution)/shard_map/ppermute | solution.py:16
  19.2 5.3 %collective-permute-start.3 = (f32[8,32,128]{2,1,0:T(8,128)S(1)}, f32[8,32,128]{2,1,0:T(8,128)S(1)}, u32[]{:S(2)}, u32[]{:S(2)}) collective-permute-start(f32[8,32,128]{2,1,0:T(8,128)S(1)} %get-tuple-element.64), channel_id=1, source_target_pairs={{0,1},{1,0},{2,3},{3,2},{4,5},{5,4},{6,7},{7,6},{8,9},{9,8},{10,11... | collective-permute-start | bytes 393224 | tf_op jit(solution)/shard_map/ppermute | solution.py:16
  21.6 11.3 %collective-permute-start.4 = (f32[14,32,128]{2,1,0:T(8,128)S(1)}, f32[14,32,128]{2,1,0:T(8,128)S(1)}, u32[]{:S(2)}, u32[]{:S(2)}) collective-permute-start(f32[14,32,128]{2,1,0:T(8,128)S(1)} %get-tuple-element.70), channel_id=1, source_target_pairs={{1,2},{2,1},{3,4},{4,3},{5,6},{6,5},{9,10},{10,9},{11,12},{12,11},... | collective-permute-start | bytes 688136 | tf_op jit(solution)/shard_map/ppermute | solution.py:16
  24.4 8.5 %collective-permute-start.5 = (f32[14,32,128]{2,1,0:T(8,128)S(1)}, f32[14,32,128]{2,1,0:T(8,128)S(1)}, u32[]{:S(2)}, u32[]{:S(2)}) collective-permute-start(f32[14,32,128]{2,1,0:T(8,128)S(1)} %get-tuple-element.71), channel_id=1, source_target_pairs={{0,1},{1,0},{2,3},{3,2},{4,5},{5,4},{6,7},{7,6},{8,9},{9,8},{10,11... | collective-permute-start | bytes 688136 | tf_op jit(solution)/shard_map/ppermute | solution.py:16
  25.8 7.1 %collective-permute-start.6 = (f32[2,32,128]{2,1,0:T(8,128)S(1)}, f32[2,32,128]{2,1,0:T(8,128)S(1)}, u32[]{:S(2)}, u32[]{:S(2)}) collective-permute-start(f32[2,32,128]{2,1,0:T(8,128)S(1)} %get-tuple-element.72), channel_id=1, source_target_pairs={{1,2},{2,1},{3,4},{4,3},{5,6},{6,5},{9,10},{10,9},{11,12},{12,11},... | collective-permute-start | bytes 98312 | tf_op jit(solution)/shard_map/ppermute | solution.py:16
  29.4 3.5 %collective-permute-start.7 = (f32[2,32,128]{2,1,0:T(8,128)S(1)}, f32[2,32,128]{2,1,0:T(8,128)S(1)}, u32[]{:S(2)}, u32[]{:S(2)}) collective-permute-start(f32[2,32,128]{2,1,0:T(8,128)S(1)} %get-tuple-element.73), channel_id=1, source_target_pairs={{0,1},{1,0},{2,3},{3,2},{4,5},{5,4},{6,7},{7,6},{8,9},{9,8},{10,11... | collective-permute-start | bytes 98312 | tf_op jit(solution)/shard_map/ppermute | solution.py:16
  34.6 7.8 %collective-permute-start.8 = (f32[8,32,128]{2,1,0:T(8,128)S(1)}, f32[8,32,128]{2,1,0:T(8,128)S(1)}, u32[]{:S(2)}, u32[]{:S(2)}) collective-permute-start(f32[8,32,128]{2,1,0:T(8,128)S(1)} %get-tuple-element.82), channel_id=1, source_target_pairs={{1,2},{2,1},{3,4},{4,3},{5,6},{6,5},{9,10},{10,9},{11,12},{12,11},... | collective-permute-start | bytes 393224 | tf_op jit(solution)/shard_map/ppermute | solution.py:16
  37.2 5.1 %collective-permute-start.9 = (f32[8,32,128]{2,1,0:T(8,128)S(1)}, f32[8,32,128]{2,1,0:T(8,128)S(1)}, u32[]{:S(2)}, u32[]{:S(2)}) collective-permute-start(f32[8,32,128]{2,1,0:T(8,128)S(1)} %get-tuple-element.83), channel_id=1, source_target_pairs={{0,1},{1,0},{2,3},{3,2},{4,5},{5,4},{6,7},{7,6},{8,9},{9,8},{10,11... | collective-permute-start | bytes 393224 | tf_op jit(solution)/shard_map/ppermute | solution.py:16
  43.7 5.0 %collective-permute-start.10 = (f32[2,4,32,128]{3,2,1,0:T(8,128)S(1)}, f32[2,4,32,128]{3,2,1,0:T(8,128)S(1)}, u32[]{:S(2)}, u32[]{:S(2)}) collective-permute-start(f32[2,4,32,128]{3,2,1,0:T(8,128)S(1)} %adjoint_two.1), channel_id=1, source_target_pairs={{0,8},{8,0},{16,24},{24,16},{1,9},{9,1},{17,25},{25,17},{2,10},{10... | collective-permute-start | bytes 393224 | tf_op jit(solution)/shard_map/ppermute | solution.py:31
  48.8 6.9 %collective-permute-start.11 = (f32[2,4,32,128]{3,2,1,0:T(8,128)S(1)}, f32[2,4,32,128]{3,2,1,0:T(8,128)S(1)}, u32[]{:S(2)}, u32[]{:S(2)}) collective-permute-start(f32[2,4,32,128]{3,2,1,0:T(8,128)S(1)} %add.21), channel_id=1, source_target_pairs={{0,24},{8,16},{16,8},{24,0},{1,25},{9,17},{17,9},{25,1},{2,26},{10... | collective-permute-start | bytes 393224 | tf_op jit(solution)/shard_map/ppermute | solution.py:31

commit v4 on v3

--- a/solution.py
+++ b/solution.py
@@ -114,6 +114,10 @@
         return {c: self.get(kind, c, i) for c in parts}
 
 
+def is_even(meta, shape):
+    return jnp.broadcast_to(meta[1:2, :], shape) > 0.5
+
+
 def pick(even, a_ref, b_ref, k, low):
     a, b = a_ref[k], b_ref[k]
     return jnp.where(even, b, a) if low else jnp.where(even, a, b)
@@ -171,9 +175,9 @@
     flat = cell_ref[...]
     x, rest = split_index(flat, full_x)
     y, z = split_index(rest, span)
-    row = (x - (mine * width - 1)) * depth + z
+    n = flat.shape[1]
+    row = (x - (jnp.broadcast_to(mine, (1, n)) * width - 1)) * depth + z
     rows = (width + 2) * depth
-    n = flat.shape[1]
     hot = lax.broadcasted_iota(jnp.int32, (rows, n), 0) == row
     amp = (2 * sign_ref[...] - 1).astype(F32)
     where_y = lax.broadcasted_iota(jnp.int32, (span, n), 0) == y
@@ -185,8 +189,8 @@
 def first_kernel(full_x, meta, e_in, h_in, p_in, perm_in, cond_in, cls_in, cells_in, signs_in, rate_in, strength_in,
                  wavelet_in, e_ref, h_ref, p_ref, coef_ref, src_ref, tab_ref, a_ref, b_ref, perm, cond, cls, cells, signs,
                  rate_t, strength_t, wavelet, sems):
-    even = meta[1] == 0
     width, depth, span = perm.shape
+    even = is_even(meta, (depth, span))
     moves = [(cells_in, cells), (signs_in, signs), (wavelet_in, wavelet), (rate_in, rate_t), (strength_in, strength_t)]
     moves += [(perm_in, perm), (cond_in, cond), (cls_in, cls), (e_in, e_ref), (h_in, h_ref), (p_in, p_ref)]
     copies = [pltpu.make_async_copy(a, b, sems.at[k]) for k, (a, b) in enumerate(moves)]
@@ -199,7 +203,7 @@
     listed += [wavelet[k] for k in range(wavelet.shape[0])]
     for k, value in enumerate(listed):
         tab_ref[k:k + 1, :] = jnp.full((1, span), value, F32)
-    src = source_map(cells, signs, meta[0], width, depth, span, full_x)
+    src = source_map(cells, signs, meta[0:1, 0:1].astype(jnp.int32), width, depth, span, full_x)
     src_ref[...] = src.reshape(width + 2, depth, span)
     for copy in copies[5:8]:
         copy.wait()
@@ -229,16 +233,15 @@
 def adjoint_first_kernel(meta, e_ref, h_ref, p_ref, coef_ref, a_ref, b_ref):
     planes = own_planes(e_ref, h_ref, p_ref)
     h1, e1 = pre_steps(planes, lambda i: [coef_ref[k, i] for k in range(4)], lambda i: 0.0)
-    emit_state(meta[1] == 0, planes, h1, e1, a_ref, b_ref, True)
+    emit_state(is_even(meta, e_ref.shape[2:]), planes, h1, e1, a_ref, b_ref, True)
 
 
 def receiver_kernel(width, depth, which, meta, got, maps_ref, acc):
-    mine = meta[0]
     rows = (width + 4) * depth
     span = acc.shape[1]
     blocks, _, n = got.shape
     acc[...] = jnp.zeros(acc.shape, F32)
-    first_row = ((mine * width - 2) * depth).astype(F32)
+    first_row = (meta[0:1, :] * width - 2.0) * depth
     row_at = lax.broadcasted_iota(jnp.int32, (rows, n), 0).astype(F32)
     y_at = lax.broadcasted_iota(jnp.int32, (span, n), 0).astype(F32)
     group = max(g for g in (1, 2, 4, 8) if blocks % g == 0)
@@ -249,7 +252,7 @@
         right = []
         for b in range(group):
             at = k * group + b
-            hot = row_at == got[at, 0:1, :] - first_row
+            hot = row_at == got[at, 0:1, :] - first_row[:, :n]
             at_y = jnp.where(y_at == got[at, 1:2, :], 1.0, 0.0).astype(jnp.bfloat16)
             right += [at_y] * 3
             for part, s in zip(left, which):
@@ -274,8 +277,8 @@
 
 
 def round_body(planes, meta, coef_ref, coefh_ref, a_ref, b_ref, full, inject, first_extra, dest, prestep, seen):
-    even = meta[1] == 0
-    keep = jnp.where(meta[0] > 0, 1.0, 0.0).astype(F32)
+    even = is_even(meta, coef_ref.shape[2:])
+    keep = meta[2:3, :]
     last = planes.last
     w = last + 1
 
@@ -380,7 +383,7 @@
 
 def forward_one_kernel(meta, tab_ref, e_ref, h_ref, p_ref, coef_ref, src_ref, b_ref, a_ref,
                        hist_ref, hs_ref, ps_ref, coefh_ref, eyh_ref, oa_ref, ob_ref, es_ref):
-    even = meta[1] == 0
+    even = is_even(meta, e_ref.shape[2:])
     width = e_ref.shape[1]
     classes = (tab_ref.shape[0] - 2 * ROUND) // 2
     wavelet = 2 * classes
@@ -425,7 +428,7 @@
 
 def forward_two_kernel(meta, tab_ref, hist_in, hs_in, ps_in, coef_ref, coefh_ref, src_ref, b_ref, a_ref,
                        hist_ref, eyh_ref, oa_ref, ob_ref, es_ref, hs_ref, ps_ref):
-    even = meta[1] == 0
+    even = is_even(meta, hist_in.shape[3:])
     width = hist_in.shape[2]
     wavelet = tab_ref.shape[0] - ROUND
     planes = state_planes(hist_in, hs_in, ps_in, 2)
@@ -453,9 +456,9 @@
     corr_ref[1, i] = sig
 
 
-def adjoint_one_kernel(meta, e_ref, h_ref, p_ref, coef_ref, coefh_ref, maps6_ref, maps5_ref, hist1_ref, hist2_ref, eyh_ref,
+def adjoint_one_kernel(meta, e_ref, h_ref, p_ref, coef_ref, coefh_ref, maps_ref, hist1_ref, hist2_ref, eyh_ref,
                        b_ref, a_ref, rb_ref, ra_ref, e_out, hs_ref, ps_ref, corr_ref, oa_ref, ob_ref, es_ref):
-    even = meta[1] == 0
+    even = is_even(meta, e_ref.shape[2:])
     width = e_ref.shape[1]
     steps = 2 * ROUND
     planes = own_planes(e_ref, h_ref, p_ref)
@@ -471,14 +474,13 @@
             ey_last = pick(even, ra_ref, rb_ref, -1 - i, True)
         else:
             ey_last = pick(even, ra_ref, rb_ref, i - width, False)
-        return maps6_ref[0, i + 2] * ey_last - maps6_ref[1, i + 2]
+        return maps_ref[0, i + 2] * ey_last - maps_ref[1, i + 2]
 
     def inject(level, i):
         n = steps + 1 - level
         if n == steps and not 0 <= i < width:
             return extra(i)
-        seen_at = maps6_ref[1, i + 2] if n == steps else maps5_ref[steps - 1 - n, i + 2]
-        return maps6_ref[0, i + 2] * ey(n, i) - seen_at
+        return maps_ref[0, i + 2] * ey(n, i) - maps_ref[steps + 1 - n, i + 2]
 
     def seen(level, i, e):
         if not 0 <= i < width:
@@ -500,7 +502,7 @@
     round_body(planes, meta, coef_ref, coefh_ref, a_ref, b_ref, True, inject, extra, dest, (oa_ref, ob_ref), seen)
 
 
-def adjoint_two_kernel(meta, e_ref, hs_in, ps_in, coef_ref, coefh_ref, maps6_ref, maps5_ref, maps2_ref, e0_ref, hist1_ref, ey2_ref, eyh_ref,
+def adjoint_two_kernel(meta, e_ref, hs_in, ps_in, coef_ref, coefh_ref, maps_ref, maps2_ref, e0_ref, hist1_ref, ey2_ref, eyh_ref,
                        corr_in, b_ref, a_ref, corr_ref, es_ref, hs_ref, ps_ref):
     width = e_ref.shape[1]
     steps = 2 * ROUND
@@ -515,8 +517,8 @@
 
     def inject(level, i):
         n = steps + 1 - ROUND - level
-        seen_at = maps5_ref[ROUND - 1, i + 2] if n == ROUND else maps2_ref[ROUND - 1 - n, i + 2]
-        return maps6_ref[0, i + 2] * ey(n, i) - seen_at
+        seen_at = maps_ref[ROUND + 1, i + 2] if n == ROUND else maps2_ref[ROUND - 1 - n, i + 2]
+        return maps_ref[0, i + 2] * ey(n, i) - seen_at
 
     def seen(level, i, e):
         if not 0 <= i < width:
@@ -530,20 +532,19 @@
                scratch_dest(es_ref, hs_ref, ps_ref), None, seen)
 
 
-def call(body, name, inputs, scalars, outs, scratch=(), remote=0, work=10**10):
-    smem = pl.BlockSpec(memory_space=pltpu.SMEM)
+def call(body, name, inputs, outs, scratch=(), remote=(), work=10**10):
     vmem = pl.BlockSpec(memory_space=pltpu.VMEM)
     stay = pl.BlockSpec(memory_space=pltpu.HBM)
     return pl.pallas_call(
         body,
         name=name,
         out_shape=[jax.ShapeDtypeStruct(s, F32) for s in outs],
-        in_specs=[smem] * len(scalars) + [stay] * remote + [vmem] * (len(inputs) - remote),
+        in_specs=[vmem] * len(inputs) + [stay] * len(remote),
         out_specs=[vmem] * len(outs),
         scratch_shapes=[s if not isinstance(s, tuple) else pltpu.VMEM(s, F32) for s in scratch],
         cost_estimate=pl.CostEstimate(flops=work, transcendentals=0, bytes_accessed=0),
         compiler_params=pltpu.CompilerParams(vmem_limit_bytes=48 * 1024 * 1024),
-    )(*scalars, *[pltpu.with_memory_space_constraint(x, pltpu.HBM) for x in inputs[:remote]], *inputs[remote:])
+    )(*inputs, *[pltpu.with_memory_space_constraint(x, pltpu.HBM) for x in remote])
 
 
 def per_device(
@@ -570,13 +571,24 @@
     nsub = lax.axis_size("sub")
     nshot = lax.axis_size("shot")
     mine = lax.axis_index("sub")
-    meta = jnp.stack([mine, mine % 2]).astype(jnp.int32)
+    facts = jnp.stack([mine, 1 - mine % 2, jnp.minimum(mine, 1)]).astype(F32)
+    meta = jnp.broadcast_to(jnp.pad(facts, (0, 5))[:, None], (8, 128))
     plane = (depth, span)
 
     in_x, rest = split_index(rec_pos[0], width)
     rec_y, rec_z = split_index(rest, span)
     rec_row = (rec_owner[0, :, 0] * width + in_x) * depth + rec_z
     listed = jnp.concatenate([rec_row[None].astype(F32), rec_y[None].astype(F32), observed[0]], axis=0)
+    def receivers(name, which):
+        (maps,) = call(
+            lambda *refs: receiver_kernel(width, depth, which, *refs),
+            name,
+            [meta, got],
+            [(len(which), width + 4, *plane)],
+            [(len(which) * (width + 4) * depth, span)],
+        )
+        return maps
+
     fields = (electric[0], magnetic[0], polar[0])
     adjoint = (adj_electric[0], adj_magnetic[0], adj_polar[0])
 
@@ -586,7 +598,6 @@
     *fields, coef, src, tab, a1, b1 = call(
         lambda *refs: first_kernel(width * nsub, *refs),
         "first",
-        [*fields, permittivity, conductivity, debye_class, src_cell, src_sign, debye_rate, debye_strength, wavelet],
         [meta],
         [own, own, own, (4, width, *plane), (width + 2, *plane), (tab_rows, span), (17, *plane), (17, *plane)],
         [
@@ -600,7 +611,7 @@
             pltpu.SMEM(wavelet.shape, F32),
             pltpu.SemaphoreType.DMA((11,)),
         ],
-        remote=11,
+        [*fields, permittivity, conductivity, debye_class, src_cell, src_sign, debye_rate, debye_strength, wavelet],
     )
     got_a1, got_b1 = exchange(a1, b1)
     listed, b1 = lax.optimization_barrier((listed, b1))
@@ -610,55 +621,38 @@
     hist1, hs, ps, coefh, ey2, a2, b2 = call(
         forward_one_kernel,
         "forward_one",
-        [tab, *fields, coef, src, got_b1, got_a1],
-        [meta],
+        [meta, tab, *fields, coef, src, got_b1, got_a1],
         [(ROUND, 3, width, *plane), h_sh, p_sh, (2, 4, *plane), (2, *plane), (8, *plane), (8, *plane)],
         [e_sh],
     )
     got, coef, a2, b2 = lax.optimization_barrier((got, coef, a2, b2))
     got_a2, got_b2 = exchange(a2, b2)
-    a3, b3 = call(adjoint_first_kernel, "adjoint_first", [*adjoint, coef], [meta], [(14, *plane), (14, *plane)])
+    a3, b3 = call(adjoint_first_kernel, "adjoint_first", [meta, *adjoint, coef], [(14, *plane), (14, *plane)])
     got_a3, got_b3 = exchange(a3, b3)
-
-    def receivers(name, which):
-        (maps,) = call(
-            lambda *refs: receiver_kernel(width, depth, which, *refs),
-            name,
-            [got],
-            [meta],
-            [(len(which), width + 4, *plane)],
-            [(len(which) * (width + 4) * depth, span)],
-        )
-        return maps
-
-    maps6 = receivers("receivers_last", (0, steps))
     hist2, eyh, a4, b4 = call(
         forward_two_kernel,
         "forward_two",
-        [tab, hist1, hs, ps, coef, coefh, src, got_b2, got_a2],
-        [meta],
+        [meta, tab, hist1, hs, ps, coef, coefh, src, got_b2, got_a2],
         [(ROUND, 3, width, *plane), (4, *plane), (2, *plane), (2, *plane)],
         [e_sh, h_sh, p_sh],
     )
     got, a4, b4 = lax.optimization_barrier((got, a4, b4))
     got_a4, got_b4 = exchange(a4, b4)
-    maps5 = receivers("receivers_middle", tuple(range(steps - 1, ROUND - 1, -1)))
+    maps = receivers("receivers_late", (0, *range(steps, ROUND - 1, -1)))
     e_adj, hs, ps, corr, a5, b5 = call(
         adjoint_one_kernel,
         "adjoint_one",
-        [*adjoint, coef, coefh, maps6, maps5, hist1, hist2, eyh, got_b3, got_a3, got_b4, got_a4],
-        [meta],
+        [meta, *adjoint, coef, coefh, maps, hist1, hist2, eyh, got_b3, got_a3, got_b4, got_a4],
         [(3, width, *plane), h_sh, p_sh, (2, width, *plane), (8, *plane), (8, *plane)],
         [e_sh],
     )
     got, a5, b5 = lax.optimization_barrier((got, a5, b5))
     got_a5, got_b5 = exchange(a5, b5)
-    maps2 = receivers("receivers_first", tuple(range(ROUND - 1, 0, -1)))
+    maps2 = receivers("receivers_early", tuple(range(ROUND - 1, 0, -1)))
     (corr,) = call(
         adjoint_two_kernel,
         "adjoint_two",
-        [e_adj, hs, ps, coef, coefh, maps6, maps5, maps2, fields[0], hist1, ey2, eyh, corr, got_b5, got_a5],
-        [meta],
+        [meta, e_adj, hs, ps, coef, coefh, maps, maps2, fields[0], hist1, ey2, eyh, corr, got_b5, got_a5],
         [(2, width, *plane)],
         [e_sh, h_sh, p_sh],
     )

time: 56.9 us -> 53.6 us (0.942)
  the two profiles are of different devices: /device:TPU:4 before, /device:TPU:10 now
where the time goes in v4:
time: 53.6 us; the launch traced here: 53.3 us
  starting transfers between devices  19.8 us (37%)
  waiting for transfers between devices  14 us (26%)
  blocking collectives  9.38 us (18%)
  Pallas kernels  8.27 us (15%)
  between operations  0.88 us (2%)
  other arithmetic  0.79 us (1%)
    ppermute x10, starting transfers between devices, pair_swap(): return lax.ppermute(block, axis, route)  17.7 us
    ppermute x2, waiting for transfers between devices, shot_sum(): x = x + lax.ppermute(x, 'shot', [(i, i ^ flip) for i in range(n)])  12.6 us
    all_to_all x1, blocking collectives, per_device(): lax.all_to_all(jnp.broadcast_to(listed[None], (nsub, *listed.shape)), 'su...  9.38 us
    pallas_call x8, Pallas kernels, call(): pl.pallas_call(body, name=name, out_shape=[jax.ShapeDtypeStruct(s, F32) f...  8.27 us
    ppermute x2, starting transfers between devices, shot_sum(): x = x + lax.ppermute(x, 'shot', [(i, i ^ flip) for i in range(n)])  2.12 us
    ppermute x10, waiting for transfers between devices, pair_swap(): return lax.ppermute(block, axis, route)  1.43 us
  transfers between devices with their start and end apart: 12, of which 3 were waited for; matrix products, arithmetic and copies ran while one was open for 0% of the time, Pallas kernels for 8%

profile of v4, /device:TPU:10, one launch (start us, length us, event | category | flops | bytes accessed | tf_op | source)
XLA Modules:
  0.0 53.3 jit_solution(16226499137713607182)
XLA Ops:
  0.6 0.1 add_convert_fusion
  0.7 0.1 broadcast_in_dim.4.refs_0_.meta
  0.8 1.5 %first.1 = (f32[3,4,32,128]{3,2,1,0:T(8,128)S(1)}, f32[3,4,32,128]{3,2,1,0:T(8,128)S(1)}, f32[3,4,32,128]{3,2,1,0:T(8,128)S(1)}, f32[4,4,32,128]{3,2,1,0:T(8,128...) custom-call(f32[8,128]{1,0:T(8,128)S(1)} %broadcast_in_dim.4.refs_0_, ...), custom_call_target="tpu_custom_call" | custom-call | flops 10000000000 | tf_op jit(solution)/shard_map/first/pallas_call | solution.py:538
  2.3 0.0 copy-start.3
  2.4 0.1 collective-permute-start
  2.4 0.0 copy-start.4
  2.5 0.0 copy-start.5
  2.5 2.6 %collective-permute-start.1 = (f32[17,32,128]{2,1,0:T(8,128)S(1)}, f32[17,32,128]{2,1,0:T(8,128)S(1)}, u32[]{:S(2)}, u32[]{:S(2)}) collective-permute-start(f32[17,32,128]{2,1,0:T(8,128)S(1)} %get-tuple-element.43), channel_id=1, source_target_pairs={{1,2},{2,1},{3,4},{4,3},{5,6},{6,5},{9,10},{10,9},{11,12},{12,11},... | collective-permute-start | bytes 835592 | tf_op jit(solution)/shard_map/ppermute | solution.py:16
  5.1 0.0 copy-done.3
  5.1 0.0 copy-done.4
  5.1 0.0 copy-done.5
  5.2 9.4 %all_to_all.5.refs_1_ = f32[8,8,128]{2,1,0:T(8,128)S(1)} all-to-all(f32[8,8,128]{2,1,0:T(8,128)S(1)} %broadcast_in_dim.5), channel_id=1, replica_groups=mesh['shot'=4,'sub'=8] {'sub'}, dimensions={0} | all-to-all | bytes 65536 | tf_op jit(solution)/shard_map/all_to_all | solution.py:618
  14.6 0.0 collective-permute-done.a_ref
  14.6 0.0 collective-permute-done.1.b_ref
  14.6 0.0 copy-start
  14.6 0.0 copy-start.1
  14.6 0.0 copy-start.2
  14.6 0.8 %forward_one.1 = (f32[3,3,4,32,128]{4,3,2,1,0:T(8,128)S(1)}, f32[3,7,32,128]{3,2,1,0:T(8,128)S(1)}, f32[3,6,32,128]{3,2,1,0:T(8,128)S(1)}, f32[2,4,32,128]{3,2,1...) custom-call(f32[8,128]{1,0:T(8,128)S(1)} %broadcast_in_dim.4.refs_0_.meta, ...), custom_call_target="tpu_custom_call" | custom-call | flops 10000000000 | tf_op jit(solution)/shard_map/forward_one/pallas_call | solution.py:538
  15.4 1.9 %collective-permute-start.2 = (f32[8,32,128]{2,1,0:T(8,128)S(1)}, f32[8,32,128]{2,1,0:T(8,128)S(1)}, u32[]{:S(2)}, u32[]{:S(2)}) collective-permute-start(f32[8,32,128]{2,1,0:T(8,128)S(1)} %get-tuple-element.63), channel_id=1, source_target_pairs={{1,2},{2,1},{3,4},{4,3},{5,6},{6,5},{9,10},{10,9},{11,12},{12,11},... | collective-permute-start | bytes 393224 | tf_op jit(solution)/shard_map/ppermute | solution.py:16
  17.3 1.5 %collective-permute-start.3 = (f32[8,32,128]{2,1,0:T(8,128)S(1)}, f32[8,32,128]{2,1,0:T(8,128)S(1)}, u32[]{:S(2)}, u32[]{:S(2)}) collective-permute-start(f32[8,32,128]{2,1,0:T(8,128)S(1)} %get-tuple-element.64), channel_id=1, source_target_pairs={{0,1},{1,0},{2,3},{3,2},{4,5},{5,4},{6,7},{7,6},{8,9},{9,8},{10,11... | collective-permute-start | bytes 393224 | tf_op jit(solution)/shard_map/ppermute | solution.py:16
  18.8 0.0 copy-done
  18.8 0.0 copy-done.1
  18.8 0.0 copy-done.2
  18.8 0.2 adjoint_first.1
  19.0 2.3 %collective-permute-start.4 = (f32[14,32,128]{2,1,0:T(8,128)S(1)}, f32[14,32,128]{2,1,0:T(8,128)S(1)}, u32[]{:S(2)}, u32[]{:S(2)}) collective-permute-start(f32[14,32,128]{2,1,0:T(8,128)S(1)} %get-tuple-element.70), channel_id=1, source_target_pairs={{1,2},{2,1},{3,4},{4,3},{5,6},{6,5},{9,10},{10,9},{11,12},{12,11},... | collective-permute-start | bytes 688136 | tf_op jit(solution)/shard_map/ppermute | solution.py:16
  21.3 0.7 %collective-permute-start.5 = (f32[14,32,128]{2,1,0:T(8,128)S(1)}, f32[14,32,128]{2,1,0:T(8,128)S(1)}, u32[]{:S(2)}, u32[]{:S(2)}) collective-permute-start(f32[14,32,128]{2,1,0:T(8,128)S(1)} %get-tuple-element.71), channel_id=1, source_target_pairs={{0,1},{1,0},{2,3},{3,2},{4,5},{5,4},{6,7},{7,6},{8,9},{9,8},{10,11... | collective-permute-start | bytes 688136 | tf_op jit(solution)/shard_map/ppermute | solution.py:16
  22.0 0.0 collective-permute-done.2.b_ref
  22.0 0.0 collective-permute-done.3.a_ref
  22.0 0.7 %forward_two.1 = (f32[3,3,4,32,128]{4,3,2,1,0:T(8,128)S(1)}, f32[4,32,128]{2,1,0:T(8,128)S(1)}, f32[2,32,128]{2,1,0:T(8,128)S(1)}, f32[2,32,128]{2,1,0:T(8,128)S(1)}) custom-call(f32[8,128]{1,0:T(8,128)S(1)} %broadcast_in_dim.4.refs_0_.meta, f32[22,128]{1,0:T(8,128)S(1)} %get-tuple-element.48.tab_ref, ...), custom_call_target="tpu_custom_call" | custom-call | flops 10000000000 | tf_op jit(solution)/shard_map/forward_two/pallas_call | solution.py:538
  22.7 2.7 %collective-permute-start.6 = (f32[2,32,128]{2,1,0:T(8,128)S(1)}, f32[2,32,128]{2,1,0:T(8,128)S(1)}, u32[]{:S(2)}, u32[]{:S(2)}) collective-permute-start(f32[2,32,128]{2,1,0:T(8,128)S(1)} %get-tuple-element.72), channel_id=1, source_target_pairs={{1,2},{2,1},{3,4},{4,3},{5,6},{6,5},{9,10},{10,9},{11,12},{12,11},... | collective-permute-start | bytes 98312 | tf_op jit(solution)/shard_map/ppermute | solution.py:16
  25.4 2.0 %collective-permute-start.7 = (f32[2,32,128]{2,1,0:T(8,128)S(1)}, f32[2,32,128]{2,1,0:T(8,128)S(1)}, u32[]{:S(2)}, u32[]{:S(2)}) collective-permute-start(f32[2,32,128]{2,1,0:T(8,128)S(1)} %get-tuple-element.73), channel_id=1, source_target_pairs={{0,1},{1,0},{2,3},{3,2},{4,5},{5,4},{6,7},{7,6},{8,9},{9,8},{10,11... | collective-permute-start | bytes 98312 | tf_op jit(solution)/shard_map/ppermute | solution.py:16
  27.4 2.2 %receivers_late.1.maps_ref = f32[5,8,32,128]{3,2,1,0:T(8,128)S(1)} custom-call(f32[8,128]{1,0:T(8,128)S(1)} %broadcast_in_dim.4.refs_0_.meta, f32[8,8,128]{2,1,0:T(8,128)S(1)} %all_to_all.5.refs_1_), custom_call_target="tpu_custom_call" | custom-call | flops 10000000000 | tf_op jit(solution)/shard_map/receivers_late/pallas_call | solution.py:538
  29.6 0.0 collective-permute-done.6.rb_ref
  29.6 0.0 collective-permute-done.7.ra_ref
  29.6 0.0 collective-permute-done.4.b_ref
  29.6 0.0 collective-permute-done.5.a_ref
  29.6 1.1 %adjoint_one.1 = (f32[3,4,32,128]{3,2,1,0:T(8,128)S(1)}, f32[3,7,32,128]{3,2,1,0:T(8,128)S(1)}, f32[3,6,32,128]{3,2,1,0:T(8,128)S(1)}, f32[2,4,32,128]{3,2,1,0:T...) custom-call(f32[8,128]{1,0:T(8,128)S(1)} %broadcast_in_dim.4.refs_0_.meta, ...), custom_call_target="tpu_custom_call" | custom-call | flops 10000000000 | tf_op jit(solution)/shard_map/adjoint_one/pallas_call | solution.py:538
  30.7 1.9 %collective-permute-start.8 = (f32[8,32,128]{2,1,0:T(8,128)S(1)}, f32[8,32,128]{2,1,0:T(8,128)S(1)}, u32[]{:S(2)}, u32[]{:S(2)}) collective-permute-start(f32[8,32,128]{2,1,0:T(8,128)S(1)} %get-tuple-element.82), channel_id=1, source_target_pairs={{1,2},{2,1},{3,4},{4,3},{5,6},{6,5},{9,10},{10,9},{11,12},{12,11},... | collective-permute-start | bytes 393224 | tf_op jit(solution)/shard_map/ppermute | solution.py:16
  32.6 2.0 %collective-permute-start.9 = (f32[8,32,128]{2,1,0:T(8,128)S(1)}, f32[8,32,128]{2,1,0:T(8,128)S(1)}, u32[]{:S(2)}, u32[]{:S(2)}) collective-permute-start(f32[8,32,128]{2,1,0:T(8,128)S(1)} %get-tuple-element.83), channel_id=1, source_target_pairs={{0,1},{1,0},{2,3},{3,2},{4,5},{5,4},{6,7},{7,6},{8,9},{9,8},{10,11... | collective-permute-start | bytes 393224 | tf_op jit(solution)/shard_map/ppermute | solution.py:16
  34.6 1.0 %receivers_early.1.maps2_ref = f32[2,8,32,128]{3,2,1,0:T(8,128)S(1)} custom-call(f32[8,128]{1,0:T(8,128)S(1)} %broadcast_in_dim.4.refs_0_.meta, f32[8,8,128]{2,1,0:T(8,128)S(1)} %all_to_all.5.refs_1_), custom_call_target="tpu_custom_call" | custom-call | flops 10000000000 | tf_op jit(solution)/shard_map/receivers_early/pallas_call | solution.py:538
  35.6 1.4 %collective-permute-done.8.b_ref = f32[8,32,128]{2,1,0:T(8,128)S(1)} collective-permute-done((f32[8,32,128]{2,1,0:T(8,128)S(1)}, f32[8,32,128]{2,1,0:T(8,128)S(1)}, u32[]{:S(2)}, u32[]{:S(2)}) %collective-permute-start.8) | collective-permute-done | bytes 131104 | tf_op jit(solution)/shard_map/ppermute | solution.py:16
  37.0 0.0 collective-permute-done.9.a_ref
  37.0 0.8 %adjoint_two.1 = f32[2,4,32,128]{3,2,1,0:T(8,128)S(1)} custom-call(f32[8,128]{1,0:T(8,128)S(1)} %broadcast_in_dim.4.refs_0_.meta, f32[3,4,32,128]{3,2,1,0:T(8,128)S(1)} %get-tuple-element.74.e_ref, f32[3,7,32,128]{3,2,1,0:T(8,128)S(1)} %get-tuple-element.75.hs_in, f32[3,6,32,128]{3,2,1,0:T(8,128)S(1)} %get-tuple-element.76.ps_in, ...), custom_call_target="tpu_custom_call" | custom-call | flops 10000000000 | tf_op jit(solution)/shard_map/adjoint_two/pallas_call | solution.py:538
  37.8 0.5 collective-permute-start.10
  38.3 5.9 %collective-permute-done.10 = f32[2,4,32,128]{3,2,1,0:T(8,128)S(1)} collective-permute-done((f32[2,4,32,128]{3,2,1,0:T(8,128)S(1)}, f32[2,4,32,128]{3,2,1,0:T(8,128)S(1)}, u32[]{:S(2)}, u32[]{:S(2)}) %collective-permute-start.10) | collective-permute-done | bytes 131104 | tf_op jit(solution)/shard_map/ppermute | solution.py:31
  44.2 1.6 %collective-permute-start.11 = (f32[2,4,32,128]{3,2,1,0:T(8,128)S(1)}, f32[2,4,32,128]{3,2,1,0:T(8,128)S(1)}, u32[]{:S(2)}, u32[]{:S(2)}) collective-permute-start(f32[2,4,32,128]{3,2,1,0:T(8,128)S(1)} %add.23), channel_id=1, source_target_pairs={{0,24},{8,16},{16,8},{24,0},{1,25},{9,17},{17,9},{25,1},{2,26},{10... | collective-permute-start | bytes 393224 | tf_op jit(solution)/shard_map/ppermute | solution.py:31
  45.8 6.7 %collective-permute-done.11 = f32[2,4,32,128]{3,2,1,0:T(8,128)S(1)} collective-permute-done((f32[2,4,32,128]{3,2,1,0:T(8,128)S(1)}, f32[2,4,32,128]{3,2,1,0:T(8,128)S(1)}, u32[]{:S(2)}, u32[]{:S(2)}) %collective-permute-start.11) | collective-permute-done | bytes 131104 | tf_op jit(solution)/shard_map/ppermute | solution.py:31
  52.6 0.7 %fusion.1 = (f32[4,32,128]{2,1,0:T(8,128)}, f32[4,32,128]{2,1,0:T(8,128)}) fusion(f32[2,4,32,128]{3,2,1,0:T(8,128)S(1)} %add.24), kind=kLoop, calls=%fused_computation.2 | loop fusion | flops 65536 | bytes 262144 | tf_op jit(solution)/shard_map/neg | solution.py:660
  (7 shorter events, 0.1 us)
Async XLA Ops:
  2.3 2.8 %copy-start.3 = (f32[1,6,128]{2,0,1:T(1,128)S(1)}, f32[1,6,128]{2,0,1:T(1,128)}, u32[]{:S(2)}) copy-start(f32[1,6,128]{2,0,1:T(1,128)} %param.33) | copy-start | bytes 9220
  2.4 12.2 %collective-permute-start = (f32[17,32,128]{2,1,0:T(8,128)S(1)}, f32[17,32,128]{2,1,0:T(8,128)S(1)}, u32[]{:S(2)}, u32[]{:S(2)}) collective-permute-start(f32[17,32,128]{2,1,0:T(8,128)S(1)} %get-tuple-element.45), channel_id=1, source_target_pairs={{0,1},{1,0},{2,3},{3,2},{4,5},{5,4},{6,7},{7,6},{8,9},{9,8},{10,11... | collective-permute-start | bytes 835592 | tf_op jit(solution)/shard_map/ppermute | solution.py:16
  2.4 2.7 %copy-start.4 = (s32[1,128]{1,0:T(1,128)S(1)}, s32[1,128]{1,0:T(1,128)}, u32[]{:S(2)}) copy-start(s32[1,128]{1,0:T(1,128)} %param.32) | copy-start | bytes 1540
  2.5 2.7 %copy-start.5 = (s32[1,128,1]{1,2,0:T(1,128)S(1)}, s32[1,128,1]{1,2,0:T(1,128)}, u32[]{:S(2)}) copy-start(s32[1,128,1]{1,2,0:T(1,128)} %param.31) | copy-start | bytes 1540
  2.5 12.1 %collective-permute-start.1 = (f32[17,32,128]{2,1,0:T(8,128)S(1)}, f32[17,32,128]{2,1,0:T(8,128)S(1)}, u32[]{:S(2)}, u32[]{:S(2)}) collective-permute-start(f32[17,32,128]{2,1,0:T(8,128)S(1)} %get-tuple-element.43), channel_id=1, source_target_pairs={{1,2},{2,1},{3,4},{4,3},{5,6},{6,5},{9,10},{10,9},{11,12},{12,11},... | collective-permute-start | bytes 835592 | tf_op jit(solution)/shard_map/ppermute | solution.py:16
  14.6 4.2 %copy-start = (f32[1,3,4,32,128]{4,3,2,1,0:T(8,128)S(1)}, f32[1,3,4,32,128]{4,3,2,1,0:T(8,128)}, u32[]{:S(2)}) copy-start(f32[1,3,4,32,128]{4,3,2,1,0:T(8,128)} %param.20) | copy-start | bytes 589828
  14.6 4.2 %copy-start.1 = (f32[1,3,4,32,128]{4,3,2,1,0:T(8,128)S(1)}, f32[1,3,4,32,128]{4,3,2,1,0:T(8,128)}, u32[]{:S(2)}) copy-start(f32[1,3,4,32,128]{4,3,2,1,0:T(8,128)} %param.21) | copy-start | bytes 589828
  14.6 4.2 %copy-start.2 = (f32[1,3,4,32,128]{4,3,2,1,0:T(8,128)S(1)}, f32[1,3,4,32,128]{4,3,2,1,0:T(8,128)}, u32[]{:S(2)}) copy-start(f32[1,3,4,32,128]{4,3,2,1,0:T(8,128)} %param.22) | copy-start | bytes 589828
  15.4 6.6 %collective-permute-start.2 = (f32[8,32,128]{2,1,0:T(8,128)S(1)}, f32[8,32,128]{2,1,0:T(8,128)S(1)}, u32[]{:S(2)}, u32[]{:S(2)}) collective-permute-start(f32[8,32,128]{2,1,0:T(8,128)S(1)} %get-tuple-element.63), channel_id=1, source_target_pairs={{1,2},{2,1},{3,4},{4,3},{5,6},{6,5},{9,10},{10,9},{11,12},{12,11},... | collective-permute-start | bytes 393224 | tf_op jit(solution)/shard_map/ppermute | solution.py:16
  17.3 4.6 %collective-permute-start.3 = (f32[8,32,128]{2,1,0:T(8,128)S(1)}, f32[8,32,128]{2,1,0:T(8,128)S(1)}, u32[]{:S(2)}, u32[]{:S(2)}) collective-permute-start(f32[8,32,128]{2,1,0:T(8,128)S(1)} %get-tuple-element.64), channel_id=1, source_target_pairs={{0,1},{1,0},{2,3},{3,2},{4,5},{5,4},{6,7},{7,6},{8,9},{9,8},{10,11... | collective-permute-start | bytes 393224 | tf_op jit(solution)/shard_map/ppermute | solution.py:16
  19.0 10.6 %collective-permute-start.4 = (f32[14,32,128]{2,1,0:T(8,128)S(1)}, f32[14,32,128]{2,1,0:T(8,128)S(1)}, u32[]{:S(2)}, u32[]{:S(2)}) collective-permute-start(f32[14,32,128]{2,1,0:T(8,128)S(1)} %get-tuple-element.70), channel_id=1, source_target_pairs={{1,2},{2,1},{3,4},{4,3},{5,6},{6,5},{9,10},{10,9},{11,12},{12,11},... | collective-permute-start | bytes 688136 | tf_op jit(solution)/shard_map/ppermute | solution.py:16
  21.3 8.4 %collective-permute-start.5 = (f32[14,32,128]{2,1,0:T(8,128)S(1)}, f32[14,32,128]{2,1,0:T(8,128)S(1)}, u32[]{:S(2)}, u32[]{:S(2)}) collective-permute-start(f32[14,32,128]{2,1,0:T(8,128)S(1)} %get-tuple-element.71), channel_id=1, source_target_pairs={{0,1},{1,0},{2,3},{3,2},{4,5},{5,4},{6,7},{7,6},{8,9},{9,8},{10,11... | collective-permute-start | bytes 688136 | tf_op jit(solution)/shard_map/ppermute | solution.py:16
  22.7 6.9 %collective-permute-start.6 = (f32[2,32,128]{2,1,0:T(8,128)S(1)}, f32[2,32,128]{2,1,0:T(8,128)S(1)}, u32[]{:S(2)}, u32[]{:S(2)}) collective-permute-start(f32[2,32,128]{2,1,0:T(8,128)S(1)} %get-tuple-element.72), channel_id=1, source_target_pairs={{1,2},{2,1},{3,4},{4,3},{5,6},{6,5},{9,10},{10,9},{11,12},{12,11},... | collective-permute-start | bytes 98312 | tf_op jit(solution)/shard_map/ppermute | solution.py:16
  25.4 4.2 %collective-permute-start.7 = (f32[2,32,128]{2,1,0:T(8,128)S(1)}, f32[2,32,128]{2,1,0:T(8,128)S(1)}, u32[]{:S(2)}, u32[]{:S(2)}) collective-permute-start(f32[2,32,128]{2,1,0:T(8,128)S(1)} %get-tuple-element.73), channel_id=1, source_target_pairs={{0,1},{1,0},{2,3},{3,2},{4,5},{5,4},{6,7},{7,6},{8,9},{9,8},{10,11... | collective-permute-start | bytes 98312 | tf_op jit(solution)/shard_map/ppermute | solution.py:16
  30.7 6.3 %collective-permute-start.8 = (f32[8,32,128]{2,1,0:T(8,128)S(1)}, f32[8,32,128]{2,1,0:T(8,128)S(1)}, u32[]{:S(2)}, u32[]{:S(2)}) collective-permute-start(f32[8,32,128]{2,1,0:T(8,128)S(1)} %get-tuple-element.82), channel_id=1, source_target_pairs={{1,2},{2,1},{3,4},{4,3},{5,6},{6,5},{9,10},{10,9},{11,12},{12,11},... | collective-permute-start | bytes 393224 | tf_op jit(solution)/shard_map/ppermute | solution.py:16
  32.6 4.4 %collective-permute-start.9 = (f32[8,32,128]{2,1,0:T(8,128)S(1)}, f32[8,32,128]{2,1,0:T(8,128)S(1)}, u32[]{:S(2)}, u32[]{:S(2)}) collective-permute-start(f32[8,32,128]{2,1,0:T(8,128)S(1)} %get-tuple-element.83), channel_id=1, source_target_pairs={{0,1},{1,0},{2,3},{3,2},{4,5},{5,4},{6,7},{7,6},{8,9},{9,8},{10,11... | collective-permute-start | bytes 393224 | tf_op jit(solution)/shard_map/ppermute | solution.py:16
  37.8 6.3 %collective-permute-start.10 = (f32[2,4,32,128]{3,2,1,0:T(8,128)S(1)}, f32[2,4,32,128]{3,2,1,0:T(8,128)S(1)}, u32[]{:S(2)}, u32[]{:S(2)}) collective-permute-start(f32[2,4,32,128]{3,2,1,0:T(8,128)S(1)} %adjoint_two.1), channel_id=1, source_target_pairs={{0,8},{8,0},{16,24},{24,16},{1,9},{9,1},{17,25},{25,17},{2,10},{10... | collective-permute-start | bytes 393224 | tf_op jit(solution)/shard_map/ppermute | solution.py:31
  44.2 8.4 %collective-permute-start.11 = (f32[2,4,32,128]{3,2,1,0:T(8,128)S(1)}, f32[2,4,32,128]{3,2,1,0:T(8,128)S(1)}, u32[]{:S(2)}, u32[]{:S(2)}) collective-permute-start(f32[2,4,32,128]{3,2,1,0:T(8,128)S(1)} %add.23), channel_id=1, source_target_pairs={{0,24},{8,16},{16,8},{24,0},{1,25},{9,17},{17,9},{25,1},{2,26},{10... | collective-permute-start | bytes 393224 | tf_op jit(solution)/shard_map/ppermute | solution.py:31

commit v5 on v4

v5 whole, which is shorter than its diff:
```python
import jax
import jax.numpy as jnp
from jax import lax
from jax.experimental import pallas as pl
from jax.experimental.pallas import tpu as pltpu
from jax.sharding import PartitionSpec as P

ROUND = 3
F32 = jnp.float32


def pair_swap(block, axis, first):
    route = []
    for i in range(first, lax.axis_size(axis) - 1, 2):
        route += [(i, i + 1), (i + 1, i)]
    return lax.ppermute(block, axis, route)


def exchange(inner, outer):
    got_outer = pair_swap(outer, "sub", 1)
    got_inner = pair_swap(inner, "sub", 0)
    return got_inner, got_outer


def shot_sum(x):
    n = lax.axis_size("shot")
    if n & (n - 1):
        return lax.psum(x, "shot")
    flip = 1
    while flip < n:
        x = x + lax.ppermute(x, "shot", [(i, i ^ flip) for i in range(n)])
        flip = 2 * flip + 1
    return x


def split_index(v, n):
    if n & (n - 1) == 0:
        return v & (n - 1), v >> (n.bit_length() - 1)
    return v % n, v // n


def ahead(u, axis):
    n = u.shape[axis]
    edge = lax.broadcasted_iota(jnp.int32, u.shape, axis) == n - 1
    return jnp.where(edge, 0.0, pltpu.roll(u, n - 1, axis))


def behind(u, axis):
    edge = lax.broadcasted_iota(jnp.int32, u.shape, axis) == 0
    return jnp.where(edge, 0.0, pltpu.roll(u, 1, axis))


def dfy(u):
    return ahead(u, 1) - u


def dfz(u):
    return ahead(u, 0) - u


def dby(u):
    return u - behind(u, 1)


def dbz(u):
    return u - behind(u, 0)


def h_step(h, e, e_next, keep=None, parts=(0, 1, 2)):
    ex, ey, ez = e[0], e[1], e[2]
    new = {}
    if 0 in parts:
        new[0] = h[0] - 0.5 * (dfy(ez) - dfz(ey))
    if 1 in parts:
        ahead_z = -ez if e_next is None else (e_next[2] if keep is None else e_next[2] * keep) - ez
        new[1] = h[1] - 0.5 * (dfz(ex) - ahead_z)
    if 2 in parts:
        ahead_y = -ey if e_next is None else (e_next[1] if keep is None else e_next[1] * keep) - ey
        new[2] = h[2] - 0.5 * (ahead_y - dfy(ex))
    return new


def e_step(e, h, h_prev, p, coef, inject, parts=(0, 1, 2)):
    ca, cb = coef[0], coef[1]
    new = {}
    for c in parts:
        if c == 0:
            curl = dby(h[2]) - dbz(h[1])
        elif c == 1:
            curl = dbz(h[0]) - (h[2] if h_prev is None else h[2] - h_prev[2])
        else:
            curl = (h[1] if h_prev is None else h[1] - h_prev[1]) - dby(h[0])
        new[c] = ca * e[c] + cb * (curl - p[c])
        if c == 1:
            new[c] = new[c] + inject
    return new


def p_step(p, e_new, coef):
    return {c: coef[2] * p[c] + coef[3] * e_new[c] for c in e_new}


class Planes:
    def __init__(self):
        self.at = {}

    def put(self, key, ref, *idx):
        self.at[key] = (ref, idx)

    def get(self, kind, c, i):
        ref, idx = self.at[kind, c, i]
        return ref[idx]

    def triple(self, kind, i, parts=(0, 1, 2)):
        return {c: self.get(kind, c, i) for c in parts}


def is_even(meta, shape):
    return jnp.broadcast_to(meta[1:2, :], shape) > 0.5


def pick(even, a_ref, b_ref, k, low):
    a, b = a_ref[k], b_ref[k]
    return jnp.where(even, b, a) if low else jnp.where(even, a, b)


def emit(even, a_ref, b_ref, k, right, left):
    a_ref[k] = jnp.where(even, right, left)
    b_ref[k] = jnp.where(even, left, right)


def edge_values(planes, coef_of, inject):
    last = planes.last
    lo = last - ROUND + 1
    e, h, p = ({i: planes.triple(kind, i) for i in range(lo, last + 1)} for kind in "EHP")
    right = []
    for step in range(1, ROUND + 1):
        parts = (1, 2) if step == ROUND else (0, 1, 2)
        for i in range(lo + step - 1, last + 1):
            h[i].update(h_step(h[i], e[i], e[i + 1] if i < last else None, parts=parts))
        right += [h[last][1], h[last][2]]
        if step < ROUND:
            for i in range(lo + step, last + 1):
                e[i] = e_step(e[i], h[i], h[i - 1], p[i], coef_of(i), inject(step, i))
                p[i] = p_step(p[i], e[i], coef_of(i))
    e, h, p = ({i: planes.triple(kind, i) for i in range(ROUND)} for kind in "EHP")
    left = [e[0][1], e[0][2]]
    for step in range(1, ROUND):
        for i in range(ROUND - step):
            h[i] = h_step(h[i], e[i], e[i + 1])
        for i in range(ROUND - step):
            parts = (0, 1, 2) if i < ROUND - step - 1 else (1, 2)
            e[i] = e_step(e[i], h[i], h[i - 1] if i > 0 else None, p[i], coef_of(i), inject(step, i), parts)
            p[i] = p_step(p[i], e[i], coef_of(i))
        left += [e[0][1], e[0][2]]
    return right, left


def emit_all(even, a_ref, b_ref, right, left, first=0):
    for k, (r, l) in enumerate(zip(right, left)):
        emit(even, a_ref, b_ref, first + k, r, l)


def own_planes(e_ref, h_ref, p_ref, level=None):
    planes = Planes()
    width = h_ref.shape[1]
    planes.last = width - 1
    for i in range(width):
        for c in range(3):
            planes.put(("E", c, i), e_ref, *((c, i) if level is None else (level, c, i)))
            planes.put(("H", c, i), h_ref, c, i)
            planes.put(("P", c, i), p_ref, c, i)
    return planes


def source_map(cell_ref, sign_ref, mine, width, depth, span, full_x):
    flat = cell_ref[...]
    x, rest = split_index(flat, full_x)
    y, z = split_index(rest, span)
    n = flat.shape[1]
    row = (x - jnp.broadcast_to(mine, (1, n)) * width) * depth + z
    rows = width * depth
    hot = lax.broadcasted_iota(jnp.int32, (rows, n), 0) == row
    amp = (2 * sign_ref[...] - 1).astype(F32)
    where_y = lax.broadcasted_iota(jnp.int32, (span, n), 0) == y
    left = jnp.where(hot, 1.0, 0.0).astype(jnp.bfloat16)
    right = jnp.where(where_y, amp, 0.0).astype(jnp.bfloat16)
    return lax.dot_general(left, right, (((1,), (1,)), ((), ())), preferred_element_type=F32)


def first_kernel(full_x, meta, e_in, h_in, p_in, perm_in, cond_in, cls_in, cells_in, signs_in, rate_in, strength_in,
                 wavelet_in, e_ref, h_ref, p_ref, coef_ref, src_ref, tab_ref, a_ref, b_ref, perm, cond, cls, cells, signs,
                 rate_t, strength_t, wavelet, sems):
    width, depth, span = perm.shape
    even = is_even(meta, (depth, span))
    moves = [(cells_in, cells), (signs_in, signs), (wavelet_in, wavelet), (rate_in, rate_t), (strength_in, strength_t)]
    moves += [(perm_in, perm), (cond_in, cond), (cls_in, cls), (e_in, e_ref), (h_in, h_ref), (p_in, p_ref)]
    copies = [pltpu.make_async_copy(a, b, sems.at[k]) for k, (a, b) in enumerate(moves)]
    for copy in copies:
        copy.start()
    for copy in copies[:5]:
        copy.wait()
    listed = [rate_t[k] for k in range(rate_t.shape[0])]
    listed += [(1.0 - rate_t[k]) * strength_t[k] for k in range(rate_t.shape[0])]
    listed += [wavelet[k] for k in range(wavelet.shape[0])]
    for k, value in enumerate(listed):
        tab_ref[k:k + 1, :] = jnp.full((1, span), value, F32)
    src = source_map(cells, signs, meta[0:1, 0:1].astype(jnp.int32), width, depth, span, full_x)
    src_ref[...] = src.reshape(width, depth, span)
    for copy in copies[5:8]:
        copy.wait()
    for i in range(width):
        ratio = cond[i] / (2.0 * perm[i])
        coef_ref[0, i] = (1.0 - ratio) / (1.0 + ratio)
        coef_ref[1, i] = 0.5 / (perm[i] * (1.0 + ratio))
        kind = cls[i]
        rate = jnp.zeros((depth, span), F32)
        gain = jnp.zeros((depth, span), F32)
        for k in range(rate_t.shape[0]):
            rate = jnp.where(kind == k, rate_t[k], rate)
            gain = jnp.where(kind == k, (1.0 - rate_t[k]) * strength_t[k], gain)
        coef_ref[2, i] = rate
        coef_ref[3, i] = gain
    for copy in copies[8:]:
        copy.wait()
    planes = own_planes(e_ref, h_ref, p_ref)
    right, left = edge_values(planes, lambda i: [coef_ref[k, i] for k in range(4)],
                              lambda step, i: src_ref[i] * wavelet[step - 1])
    last = width - 1
    right += [coef_ref[0, last], coef_ref[1, last], cls[last].astype(F32)]
    left += [coef_ref[0, 0], coef_ref[1, 0], cls[0].astype(F32)]
    emit_all(even, a_ref, b_ref, right, left)


def receiver_kernel(width, depth, which, meta, got, maps_ref, acc):
    rows = width * depth
    span = acc.shape[1]
    blocks, _, n = got.shape
    acc[...] = jnp.zeros(acc.shape, F32)
    first_row = meta[0:1, :] * (width * depth)
    row_at = lax.broadcasted_iota(jnp.int32, (rows, n), 0).astype(F32)
    y_at = lax.broadcasted_iota(jnp.int32, (span, n), 0).astype(F32)
    group = max(g for g in (1, 2, 4, 8) if blocks % g == 0)
    zero = jnp.zeros((rows, n), jnp.bfloat16)

    def block(k, carry):
        left = [[] for _ in which]
        right = []
        for b in range(group):
            at = k * group + b
            hot = row_at == got[at, 0:1, :] - first_row[:, :n]
            at_y = jnp.where(y_at == got[at, 1:2, :], 1.0, 0.0).astype(jnp.bfloat16)
            right += [at_y] * 3
            for part, s in zip(left, which):
                if s == 0:
                    part += [jnp.where(hot, 1.0, 0.0).astype(jnp.bfloat16), zero, zero]
                    continue
                v = got[at, 1 + s:2 + s, :]
                high = v.astype(jnp.bfloat16).astype(F32)
                mid = (v - high).astype(jnp.bfloat16).astype(F32)
                low = (v - high) - mid
                part += [jnp.where(hot, u, 0.0).astype(jnp.bfloat16) for u in (high, mid, low)]
        acc[...] += lax.dot_general(
            jnp.concatenate([jnp.concatenate(part, axis=1) for part in left], axis=0) if len(left) > 1 else jnp.concatenate(left[0], axis=1),
            jnp.concatenate(right, axis=1),
            (((1,), (1,)), ((), ())),
            preferred_element_type=F32,
        )
        return carry

    lax.fori_loop(0, blocks // group, block, 0)
    maps_ref[...] = acc[...].reshape(maps_ref.shape)


def round_body(planes, meta, coef_ref, coefh_ref, a_ref, b_ref, inject, dest, seen=None):
    even = is_even(meta, coef_ref.shape[2:])
    keep = meta[2:3, :]
    last = planes.last

    def coef_of(i):
        return [coef_ref[k, i] for k in range(4)]

    before, after = ([coefh_ref[side, k] for k in range(4)] for side in (0, 1))
    zero = jnp.zeros(coef_ref.shape[2:], F32)
    none = {c: zero for c in range(3)}

    def store(kind, c, i, level, value):
        ref, idx = dest(kind, c, i, level)
        ref[idx] = value
        planes.put((kind, c, i), ref, *idx)

    low_e = low_h = low_p = high_e = high_p = None
    for level in range(1, ROUND + 1):
        sent = 2 * (level - 1)
        edge = {c: planes.get("E", c, 0) * keep for c in (1, 2)}
        if level == 1:
            low_h = {0: zero, 1: 0.5 * edge[2], 2: -0.5 * edge[1]}
            far = None
        else:
            far = {1: 0.5 * low_e[2], 2: -0.5 * low_e[1]}
            low_h.update(h_step(low_h, low_e, edge, parts=(0, 1, 2) if level < ROUND else (1, 2)))
        if level == 1:
            low_e = {0: before[1] * (dby(low_h[2]) - dbz(low_h[1])), 1: -(before[1] * low_h[2]), 2: before[1] * low_h[1]}
            low_p = {c: before[3] * low_e[c] for c in range(3)}
        elif level < ROUND:
            low_e = e_step(low_e, low_h, far, low_p, before, 0.0)
            low_p = p_step(low_p, low_e, before)
        h_prev = {c: low_h[c] + pick(even, a_ref, b_ref, sent + c - 1, True) for c in (1, 2)}
        for i in range(last + 1):
            e = planes.triple("E", i)
            if i < last:
                e_next = planes.triple("E", i + 1, (1, 2))
            else:
                e_next = {c: pick(even, a_ref, b_ref, sent + c - 1, False) for c in (1, 2)}
                if level > 1:
                    e_next = {c: e_next[c] + high_e[c] for c in (1, 2)}
            h = h_step(planes.triple("H", i), e, e_next)
            cf = coef_of(i)
            new = e_step(e, h, h_prev, planes.triple("P", i), cf, inject(level, i))
            pn = p_step(planes.triple("P", i), new, cf)
            for c in range(3):
                store("H", c, i, level, h[c])
                store("E", c, i, level, new[c])
                store("P", c, i, level, pn[c])
            if seen is not None:
                seen(level, i, new)
            h_prev = h
        if level == 1:
            high_e = {0: zero, 1: after[1] * h_prev[2], 2: -(after[1] * h_prev[1])}
            high_p = {c: after[3] * high_e[c] for c in range(3)}
            high_h = none
        elif level < ROUND:
            high_h = h_step(high_h, high_e, None)
            high_e = e_step(high_e, high_h, h_prev, high_p, after, 0.0)
            high_p = p_step(high_p, high_e, after)


def store_in(e_ref, h_ref, p_ref, by_level=False):
    refs = {"E": e_ref, "H": h_ref, "P": p_ref}

    def dest(kind, c, i, level):
        return refs[kind], ((level - 1, c, i) if kind == "E" and by_level else (c, i))

    return dest


def forward_one_kernel(meta, tab_ref, e_ref, h_ref, p_ref, coef_ref, src_ref, b_ref, a_ref,
                       hist_ref, hs_ref, ps_ref, coefh_ref, oa_ref, ob_ref):
    even = is_even(meta, e_ref.shape[2:])
    classes = (tab_ref.shape[0] - 2 * ROUND) // 2
    wavelet = 2 * classes
    for side in (0, 1):
        coefh_ref[side, 0] = pick(even, a_ref, b_ref, 2 * ROUND, side == 0)
        coefh_ref[side, 1] = pick(even, a_ref, b_ref, 2 * ROUND + 1, side == 0)
        kind = pick(even, a_ref, b_ref, 2 * ROUND + 2, side == 0)
        rate = jnp.zeros(kind.shape, F32)
        gain = jnp.zeros(kind.shape, F32)
        for k in range(classes):
            rate = jnp.where(kind == float(k), tab_ref[k:k + 1, :], rate)
            gain = jnp.where(kind == float(k), tab_ref[classes + k:classes + k + 1, :], gain)
        coefh_ref[side, 2] = rate
        coefh_ref[side, 3] = gain
    planes = own_planes(e_ref, h_ref, p_ref)

    def inject(level, i):
        return src_ref[i] * tab_ref[wavelet + level - 1:wavelet + level, :]

    round_body(planes, meta, coef_ref, coefh_ref, a_ref, b_ref, inject, store_in(hist_ref, hs_ref, ps_ref, True))
    right, left = edge_values(planes, lambda i: [coef_ref[k, i] for k in range(4)], lambda step, i: inject(ROUND + step, i))
    emit_all(even, oa_ref, ob_ref, right, left)


def forward_two_kernel(meta, tab_ref, hist_in, hs_in, ps_in, coef_ref, coefh_ref, src_ref, maps_ref, e_ref, h_ref, p_ref,
                       b_ref, a_ref, hist_ref, oa_ref, ob_ref, hs_ref, ps_ref):
    wavelet = tab_ref.shape[0] - ROUND
    round_body(own_planes(hist_in, hs_in, ps_in, ROUND - 1), meta, coef_ref, coefh_ref, a_ref, b_ref,
               lambda level, i: src_ref[i] * tab_ref[wavelet + level - 1:wavelet + level, :],
               store_in(hist_ref, hs_ref, ps_ref, True))

    def inject(step, i):
        return maps_ref[0, i] * hist_ref[ROUND - step, 1, i] - maps_ref[step, i]

    right, left = edge_values(own_planes(e_ref, h_ref, p_ref), lambda i: [coef_ref[k, i] for k in range(4)], inject)
    emit_all(is_even(meta, e_ref.shape[2:]), oa_ref, ob_ref, right, left)


def correlate(corr_ref, i, b, now, prev, add):
    eps = b[0] * (now[0] - prev[0]) + b[1] * (now[1] - prev[1]) + b[2] * (now[2] - prev[2])
    sig = b[0] * now[0] + b[1] * now[1] + b[2] * now[2]
    if add is not None:
        eps, sig = eps + add[0, i], sig + add[1, i]
    corr_ref[0, i] = eps
    corr_ref[1, i] = sig


def adjoint_one_kernel(meta, e_ref, h_ref, p_ref, coef_ref, coefh_ref, maps_ref, maps2_ref, hist1_ref, hist2_ref,
                       b_ref, a_ref, e_out, hs_ref, ps_ref, corr_ref, oa_ref, ob_ref):
    planes = own_planes(e_ref, h_ref, p_ref)

    def seen(level, i, e):
        n = ROUND - level
        now = [hist2_ref[n, c, i] for c in range(3)]
        prev = [hist2_ref[n - 1, c, i] if n > 0 else hist1_ref[ROUND - 1, c, i] for c in range(3)]
        correlate(corr_ref, i, e, now, prev, corr_ref if level > 1 else None)

    def inject(level, i):
        return maps_ref[0, i] * hist2_ref[ROUND - level, 1, i] - maps_ref[level, i]

    def inject_next(step, i):
        return maps_ref[0, i] * hist1_ref[ROUND - step, 1, i] - maps2_ref[step - 1, i]

    round_body(planes, meta, coef_ref, coefh_ref, a_ref, b_ref, inject, store_in(e_out, hs_ref, ps_ref), seen)
    right, left = edge_values(planes, lambda i: [coef_ref[k, i] for k in range(4)], inject_next)
    emit_all(is_even(meta, e_ref.shape[2:]), oa_ref, ob_ref, right, left)


def adjoint_two_kernel(meta, e_ref, hs_in, ps_in, coef_ref, coefh_ref, maps_ref, maps2_ref, e0_ref, hist1_ref,
                       corr_in, b_ref, a_ref, corr_ref, es_ref, hs_ref, ps_ref):
    def seen(level, i, e):
        n = ROUND - level
        now = [hist1_ref[n, c, i] for c in range(3)]
        prev = [hist1_ref[n - 1, c, i] if n > 0 else e0_ref[c, i] for c in range(3)]
        correlate(corr_ref, i, e, now, prev, corr_ref if level > 1 else corr_in)

    def inject(level, i):
        return maps_ref[0, i] * hist1_ref[ROUND - level, 1, i] - maps2_ref[level - 1, i]

    round_body(own_planes(e_ref, hs_in, ps_in), meta, coef_ref, coefh_ref, a_ref, b_ref, inject,
               store_in(es_ref, hs_ref, ps_ref), seen)


def call(body, name, inputs, outs, scratch=(), remote=(), work=10**10):
    vmem = pl.BlockSpec(memory_space=pltpu.VMEM)
    stay = pl.BlockSpec(memory_space=pltpu.HBM)
    return pl.pallas_call(
        body,
        name=name,
        out_shape=[jax.ShapeDtypeStruct(s, F32) for s in outs],
        in_specs=[vmem] * len(inputs) + [stay] * len(remote),
        out_specs=[vmem] * len(outs),
        scratch_shapes=[s if not isinstance(s, tuple) else pltpu.VMEM(s, F32) for s in scratch],
        cost_estimate=pl.CostEstimate(flops=work, transcendentals=0, bytes_accessed=0),
        compiler_params=pltpu.CompilerParams(vmem_limit_bytes=48 * 1024 * 1024),
    )(*inputs, *[pltpu.with_memory_space_constraint(x, pltpu.HBM) for x in remote])


def per_device(
    electric,
    magnetic,
    polar,
    adj_electric,
    adj_magnetic,
    adj_polar,
    permittivity,
    conductivity,
    debye_class,
    debye_rate,
    debye_strength,
    wavelet,
    src_cell,
    src_sign,
    rec_owner,
    rec_pos,
    observed,
):
    width, depth, span = permittivity.shape
    steps = wavelet.shape[0]
    nsub = lax.axis_size("sub")
    nshot = lax.axis_size("shot")
    mine = lax.axis_index("sub")
    facts = jnp.stack([mine, 1 - mine % 2, jnp.minimum(mine, 1)]).astype(F32)
    meta = jnp.broadcast_to(jnp.pad(facts, (0, 5))[:, None], (8, 128))
    plane = (depth, span)

    in_x, rest = split_index(rec_pos[0], width)
    rec_y, rec_z = split_index(rest, span)
    rec_row = (rec_owner[0, :, 0] * width + in_x) * depth + rec_z
    listed = jnp.concatenate([rec_row[None].astype(F32), rec_y[None].astype(F32), observed[0]], axis=0)
    def receivers(name, which):
        (maps,) = call(
            lambda *refs: receiver_kernel(width, depth, which, *refs),
            name,
            [meta, got],
            [(len(which), width, *plane)],
            [(len(which) * width * depth, span)],
            work=10**9,
        )
        return maps

    fields = (electric[0], magnetic[0], polar[0])
    adjoint = (adj_electric[0], adj_magnetic[0], adj_polar[0])

    own = (3, width, *plane)
    classes = debye_rate.shape[0]
    tab_rows = 2 * classes + steps
    *fields, coef, src, tab, a1, b1 = call(
        lambda *refs: first_kernel(width * nsub, *refs),
        "first",
        [meta],
        [own, own, own, (4, width, *plane), (width, *plane), (tab_rows, span), *[(2 * ROUND + 3, *plane)] * 2],
        [
            (width, *plane),
            (width, *plane),
            pltpu.VMEM((width, *plane), jnp.int32),
            pltpu.VMEM(src_cell.shape, jnp.int32),
            pltpu.VMEM(src_sign.shape, jnp.int32),
            pltpu.SMEM(debye_rate.shape, F32),
            pltpu.SMEM(debye_strength.shape, F32),
            pltpu.SMEM(wavelet.shape, F32),
            pltpu.SemaphoreType.DMA((11,)),
        ],
        [*fields, permittivity, conductivity, debye_class, src_cell, src_sign, debye_rate, debye_strength, wavelet],
    )
    got_a1, got_b1 = exchange(a1, b1)
    listed, b1 = lax.optimization_barrier((listed, b1))
    got = lax.all_to_all(jnp.broadcast_to(listed[None], (nsub, *listed.shape)), "sub", 0, 0)
    edges = [(2 * ROUND, *plane)] * 2
    hist1, hs, ps, coefh, a2, b2 = call(
        forward_one_kernel,
        "forward_one",
        [meta, tab, *fields, coef, src, got_b1, got_a1],
        [(ROUND, *own), own, own, (2, 4, *plane), *edges],
    )
    got, hs = lax.optimization_barrier((got, hs))
    got_a2, got_b2 = exchange(a2, b2)
    maps = receivers("receivers_late", (0, *range(steps, ROUND, -1)))
    hist2, a3, b3 = call(
        forward_two_kernel,
        "forward_two",
        [meta, tab, hist1, hs, ps, coef, coefh, src, maps, *adjoint, got_b2, got_a2],
        [(ROUND, *own), *edges],
        [own, own],
    )
    got, hist2 = lax.optimization_barrier((got, hist2))
    got_a3, got_b3 = exchange(a3, b3)
    maps2 = receivers("receivers_early", tuple(range(ROUND, 0, -1)))
    e_adj, hs, ps, corr, a4, b4 = call(
        adjoint_one_kernel,
        "adjoint_one",
        [meta, *adjoint, coef, coefh, maps, maps2, hist1, hist2, got_b3, got_a3],
        [own, own, own, (2, width, *plane), *edges],
    )
    got_a4, got_b4 = exchange(a4, b4)
    (corr,) = call(
        adjoint_two_kernel,
        "adjoint_two",
        [meta, e_adj, hs, ps, coef, coefh, maps, maps2, fields[0], hist1, corr, got_b4, got_a4],
        [(2, width, *plane)],
        [own, own, own],
    )
    total = shot_sum(corr)
    return (-(total[0] / (steps * nshot)), -(total[1] / (steps * nshot)))


def solution(mesh):
    in_specs = (
        P("shot", None, "sub", None, None),
        P("shot", None, "sub", None, None),
        P("shot", None, "sub", None, None),
        P("shot", None, "sub", None, None),
        P("shot", None, "sub", None, None),
        P("shot", None, "sub", None, None),
        P("sub", None, None),
        P("sub", None, None),
        P("sub", None, None),
        P(),
        P(),
        P(),
        P("shot", None),
        P("shot", None),
        P("shot", "sub", None),
        P("shot", "sub"),
        P("shot", None, "sub"),
    )
    out_specs = (P("sub", None, None), P("sub", None, None))
    return jax.shard_map(
        per_device, mesh=mesh, in_specs=in_specs, out_specs=out_specs, check_vma=False
    )
```

time: 53.6 us -> 49.1 us (0.916)
  the two profiles are of different devices: /device:TPU:10 before, /device:TPU:4 now
where the time goes in v5:
time: 49.1 us; the launch traced here: 48.2 us
  starting transfers between devices  24.6 us (50%)
  waiting for transfers between devices  13.8 us (28%)
  Pallas kernels  7.39 us (15%)
  between operations  0.87 us (2%)
  other arithmetic  0.79 us (2%)
  local copies, waits for them, and re-layouts  0.73 us (1%)
    ppermute x8, starting transfers between devices, pair_swap(): return lax.ppermute(block, axis, route)  14.9 us
    ppermute x8, waiting for transfers between devices, pair_swap(): return lax.ppermute(block, axis, route)  7.83 us
    pallas_call x7, Pallas kernels, call(): pl.pallas_call(body, name=name, out_shape=[jax.ShapeDtypeStruct(s, F32) f...  7.39 us
    ppermute x2, starting transfers between devices, shot_sum(): x = x + lax.ppermute(x, 'shot', [(i, i ^ flip) for i in range(n)])  6.36 us
    ppermute x2, waiting for transfers between devices, shot_sum(): x = x + lax.ppermute(x, 'shot', [(i, i ^ flip) for i in range(n)])  6 us
    all_to_all x1, starting transfers between devices, per_device(): lax.all_to_all(jnp.broadcast_to(listed[None], (nsub, *listed.shape)), 'su...  3.33 us
  transfers between devices with their start and end apart: 11, of which 6 were waited for; matrix products, arithmetic and copies ran while one was open for 1% of the time, Pallas kernels for 6%

profile of v5, /device:TPU:4, one launch (start us, length us, event | category | flops | bytes accessed | tf_op | source)
XLA Modules:
  0.0 48.2 jit_solution(2673573559103483773)
XLA Ops:
  0.6 0.1 add_convert_fusion
  0.7 0.1 broadcast_in_dim.4.refs_0_.meta
  0.8 0.0 copy-start.5
  0.8 1.7 %first.1 = (f32[3,4,32,128]{3,2,1,0:T(8,128)S(1)}, f32[3,4,32,128]{3,2,1,0:T(8,128)S(1)}, f32[3,4,32,128]{3,2,1,0:T(8,128)S(1)}, f32[4,4,32,128]{3,2,1,0:T(8,128...) custom-call(f32[8,128]{1,0:T(8,128)S(1)} %broadcast_in_dim.4.refs_0_, ...), custom_call_target="tpu_custom_call" | custom-call | flops 10000000000 | tf_op jit(solution)/shard_map/first/pallas_call | solution.py:435
  2.5 0.0 copy-start.3
  2.6 0.0 copy-start.4
  2.6 0.1 collective-permute-start.1
  2.7 3.4 %collective-permute-start = (f32[9,32,128]{2,1,0:T(8,128)S(1)}, f32[9,32,128]{2,1,0:T(8,128)S(1)}, u32[]{:S(2)}, u32[]{:S(2)}) collective-permute-start(f32[9,32,128]{2,1,0:T(8,128)S(1)} %get-tuple-element.36), channel_id=1, source_target_pairs={{1,2},{2,1},{3,4},{4,3},{5,6},{6,5},{9,10},{10,9},{11,12},{12,11},... | collective-permute-start | bytes 442376 | tf_op jit(solution)/shard_map/ppermute | solution.py:16
  6.1 0.0 copy-done.5
  6.1 0.0 copy-done.4
  6.1 0.0 copy-done.3
  6.2 0.6 %broadcast_in_dim.5 = f32[8,8,128]{2,1,0:T(8,128)} broadcast(f32[8,128]{1,0:T(8,128)S(1)} %pad_maximum_fusion), dimensions={1,2} | broadcast | bytes 36864 | tf_op jit(solution)/shard_map/broadcast_in_dim | solution.py:516
  6.8 3.3 %all-to-all-start = ((f32[8,8,128]{2,1,0:T(8,128)}), f32[8,8,128]{2,1,0:T(8,128)S(1)}, u32[]{:S(2)}, u32[]{:S(2)}) async-start(f32[8,8,128]{2,1,0:T(8,128)} %broadcast_in_dim.5), calls=%async_computation | async-start | bytes 65536 | tf_op jit(solution)/shard_map/all_to_all | solution.py:516
  10.1 0.0 collective-permute-done.1.a_ref
  10.1 0.6 %collective-permute-done.b_ref = f32[9,32,128]{2,1,0:T(8,128)S(1)} collective-permute-done((f32[9,32,128]{2,1,0:T(8,128)S(1)}, f32[9,32,128]{2,1,0:T(8,128)S(1)}, u32[]{:S(2)}, u32[]{:S(2)}) %collective-permute-start) | collective-permute-done | bytes 147488 | tf_op jit(solution)/shard_map/ppermute | solution.py:16
  10.7 1.0 %forward_one.1 = (f32[3,3,4,32,128]{4,3,2,1,0:T(8,128)S(1)}, f32[3,4,32,128]{3,2,1,0:T(8,128)S(1)}, f32[3,4,32,128]{3,2,1,0:T(8,128)S(1)}, f32[2,4,32,128]{3,2,1...) custom-call(f32[8,128]{1,0:T(8,128)S(1)} %broadcast_in_dim.4.refs_0_.meta, ...), custom_call_target="tpu_custom_call" | custom-call | flops 10000000000 | tf_op jit(solution)/shard_map/forward_one/pallas_call | solution.py:435
  11.7 3.7 %collective-permute-start.2 = (f32[6,32,128]{2,1,0:T(8,128)S(1)}, f32[6,32,128]{2,1,0:T(8,128)S(1)}, u32[]{:S(2)}, u32[]{:S(2)}) collective-permute-start(f32[6,32,128]{2,1,0:T(8,128)S(1)} %get-tuple-element.45), channel_id=1, source_target_pairs={{1,2},{2,1},{3,4},{4,3},{5,6},{6,5},{9,10},{10,9},{11,12},{12,11},... | collective-permute-start | bytes 294920 | tf_op jit(solution)/shard_map/ppermute | solution.py:16
  15.4 0.1 collective-permute-start.3
  15.5 0.0 all-to-all-done.refs_1_
  15.5 0.0 copy-start
  15.5 0.0 copy-start.1
  15.6 0.0 copy-start.2
  15.6 1.0 %receivers_late.1.maps_ref = f32[4,4,32,128]{3,2,1,0:T(8,128)S(1)} custom-call(f32[8,128]{1,0:T(8,128)S(1)} %broadcast_in_dim.4.refs_0_.meta, f32[8,8,128]{2,1,0:T(8,128)S(1)} %all-to-all-done.refs_1_), custom_call_target="tpu_custom_call" | custom-call | flops 1000000000 | tf_op jit(solution)/shard_map/receivers_late/pallas_call | solution.py:435
  16.6 2.0 %collective-permute-done.2.b_ref = f32[6,32,128]{2,1,0:T(8,128)S(1)} collective-permute-done((f32[6,32,128]{2,1,0:T(8,128)S(1)}, f32[6,32,128]{2,1,0:T(8,128)S(1)}, u32[]{:S(2)}, u32[]{:S(2)}) %collective-permute-start.2) | collective-permute-done | bytes 98336 | tf_op jit(solution)/shard_map/ppermute | solution.py:16
  18.5 0.0 collective-permute-done.3.a_ref
  18.5 0.0 copy-done
  18.5 0.0 copy-done.1
  18.6 0.0 copy-done.2
  18.6 1.0 %forward_two.1 = (f32[3,3,4,32,128]{4,3,2,1,0:T(8,128)S(1)}, f32[6,32,128]{2,1,0:T(8,128)S(1)}, f32[6,32,128]{2,1,0:T(8,128)S(1)}) custom-call(f32[8,128]{1,0:T(8,128)S(1)} %broadcast_in_dim.4.refs_0_.meta, f32[22,128]{1,0:T(8,128)S(1)} %get-tuple-element.31.tab_ref, f32[3,3,4,32,128]{4,3,2,1,0:T(8,128)S(1)} %get-tuple-element.42.hist_in.hist1_ref, ...), custom_call_target="tpu_custom_call" | custom-call | flops 10000000000 | tf_op jit(solution)/shard_map/forward_two/pallas_call | solution.py:435
  19.6 3.7 %collective-permute-start.4 = (f32[6,32,128]{2,1,0:T(8,128)S(1)}, f32[6,32,128]{2,1,0:T(8,128)S(1)}, u32[]{:S(2)}, u32[]{:S(2)}) collective-permute-start(f32[6,32,128]{2,1,0:T(8,128)S(1)} %get-tuple-element.50), channel_id=1, source_target_pairs={{1,2},{2,1},{3,4},{4,3},{5,6},{6,5},{9,10},{10,9},{11,12},{12,11},... | collective-permute-start | bytes 294920 | tf_op jit(solution)/shard_map/ppermute | solution.py:16
  23.3 0.1 collective-permute-start.5
  23.4 0.8 %receivers_early.1.maps2_ref = f32[3,4,32,128]{3,2,1,0:T(8,128)S(1)} custom-call(f32[8,128]{1,0:T(8,128)S(1)} %broadcast_in_dim.4.refs_0_.meta, f32[8,8,128]{2,1,0:T(8,128)S(1)} %all-to-all-done.refs_1_), custom_call_target="tpu_custom_call" | custom-call | flops 1000000000 | tf_op jit(solution)/shard_map/receivers_early/pallas_call | solution.py:435
  24.1 2.2 %collective-permute-done.4.b_ref = f32[6,32,128]{2,1,0:T(8,128)S(1)} collective-permute-done((f32[6,32,128]{2,1,0:T(8,128)S(1)}, f32[6,32,128]{2,1,0:T(8,128)S(1)}, u32[]{:S(2)}, u32[]{:S(2)}) %collective-permute-start.4) | collective-permute-done | bytes 98336 | tf_op jit(solution)/shard_map/ppermute | solution.py:16
  26.4 0.0 collective-permute-done.5.a_ref
  26.4 1.1 %adjoint_one.1 = (f32[3,4,32,128]{3,2,1,0:T(8,128)S(1)}, f32[3,4,32,128]{3,2,1,0:T(8,128)S(1)}, f32[3,4,32,128]{3,2,1,0:T(8,128)S(1)}, f32[2,4,32,128]{3,2,1,0:T...) custom-call(f32[8,128]{1,0:T(8,128)S(1)} %broadcast_in_dim.4.refs_0_.meta, ...), custom_call_target="tpu_custom_call" | custom-call | flops 10000000000 | tf_op jit(solution)/shard_map/adjoint_one/pallas_call | solution.py:435
  27.5 3.7 %collective-permute-start.6 = (f32[6,32,128]{2,1,0:T(8,128)S(1)}, f32[6,32,128]{2,1,0:T(8,128)S(1)}, u32[]{:S(2)}, u32[]{:S(2)}) collective-permute-start(f32[6,32,128]{2,1,0:T(8,128)S(1)} %get-tuple-element.56), channel_id=1, source_target_pairs={{1,2},{2,1},{3,4},{4,3},{5,6},{6,5},{9,10},{10,9},{11,12},{12,11},... | collective-permute-start | bytes 294920 | tf_op jit(solution)/shard_map/ppermute | solution.py:16
  31.3 0.1 collective-permute-start.7
  31.4 3.0 %collective-permute-done.6.b_ref = f32[6,32,128]{2,1,0:T(8,128)S(1)} collective-permute-done((f32[6,32,128]{2,1,0:T(8,128)S(1)}, f32[6,32,128]{2,1,0:T(8,128)S(1)}, u32[]{:S(2)}, u32[]{:S(2)}) %collective-permute-start.6) | collective-permute-done | bytes 98336 | tf_op jit(solution)/shard_map/ppermute | solution.py:16
  34.4 0.0 collective-permute-done.7.a_ref
  34.4 0.8 %adjoint_two.1 = f32[2,4,32,128]{3,2,1,0:T(8,128)S(1)} custom-call(f32[8,128]{1,0:T(8,128)S(1)} %broadcast_in_dim.4.refs_0_.meta, f32[3,4,32,128]{3,2,1,0:T(8,128)S(1)} %get-tuple-element.52.e_ref, f32[3,4,32,128]{3,2,1,0:T(8,128)S(1)} %get-tuple-element.53.hs_in, f32[3,4,32,128]{3,2,1,0:T(8,128)S(1)} %get-tuple-element.54.ps_in, ...), custom_call_target="tpu_custom_call" | custom-call | flops 10000000000 | tf_op jit(solution)/shard_map/adjoint_two/pallas_call | solution.py:435
  35.1 2.3 %collective-permute-start.8 = (f32[2,4,32,128]{3,2,1,0:T(8,128)S(1)}, f32[2,4,32,128]{3,2,1,0:T(8,128)S(1)}, u32[]{:S(2)}, u32[]{:S(2)}) collective-permute-start(f32[2,4,32,128]{3,2,1,0:T(8,128)S(1)} %adjoint_two.1), channel_id=1, source_target_pairs={{0,8},{8,0},{16,24},{24,16},{1,9},{9,1},{17,25},{25,17},{2,10},{10... | collective-permute-start | bytes 393224 | tf_op jit(solution)/shard_map/ppermute | solution.py:31
  37.4 2.9 %collective-permute-done.8 = f32[2,4,32,128]{3,2,1,0:T(8,128)S(1)} collective-permute-done((f32[2,4,32,128]{3,2,1,0:T(8,128)S(1)}, f32[2,4,32,128]{3,2,1,0:T(8,128)S(1)}, u32[]{:S(2)}, u32[]{:S(2)}) %collective-permute-start.8) | collective-permute-done | bytes 131104 | tf_op jit(solution)/shard_map/ppermute | solution.py:31
  40.4 4.1 %collective-permute-start.9 = (f32[2,4,32,128]{3,2,1,0:T(8,128)S(1)}, f32[2,4,32,128]{3,2,1,0:T(8,128)S(1)}, u32[]{:S(2)}, u32[]{:S(2)}) collective-permute-start(f32[2,4,32,128]{3,2,1,0:T(8,128)S(1)} %add.23), channel_id=1, source_target_pairs={{0,24},{8,16},{16,8},{24,0},{1,25},{9,17},{17,9},{25,1},{2,26},{10... | collective-permute-start | bytes 393224 | tf_op jit(solution)/shard_map/ppermute | solution.py:31
  44.5 3.1 %collective-permute-done.9 = f32[2,4,32,128]{3,2,1,0:T(8,128)S(1)} collective-permute-done((f32[2,4,32,128]{3,2,1,0:T(8,128)S(1)}, f32[2,4,32,128]{3,2,1,0:T(8,128)S(1)}, u32[]{:S(2)}, u32[]{:S(2)}) %collective-permute-start.9) | collective-permute-done | bytes 131104 | tf_op jit(solution)/shard_map/ppermute | solution.py:31
  47.6 0.7 %fusion.1 = (f32[4,32,128]{2,1,0:T(8,128)}, f32[4,32,128]{2,1,0:T(8,128)}) fusion(f32[2,4,32,128]{3,2,1,0:T(8,128)S(1)} %add.24), kind=kLoop, calls=%fused_computation.2 | loop fusion | flops 65536 | bytes 262144 | tf_op jit(solution)/shard_map/neg | solution.py:552
  (6 shorter events, 0.1 us)
Async XLA Ops:
  0.8 5.3 %copy-start.5 = (s32[1,128,1]{1,2,0:T(1,128)S(1)}, s32[1,128,1]{1,2,0:T(1,128)}, u32[]{:S(2)}) copy-start(s32[1,128,1]{1,2,0:T(1,128)} %param.31) | copy-start | bytes 1540
  2.5 3.6 %copy-start.3 = (f32[1,6,128]{2,0,1:T(1,128)S(1)}, f32[1,6,128]{2,0,1:T(1,128)}, u32[]{:S(2)}) copy-start(f32[1,6,128]{2,0,1:T(1,128)} %param.33) | copy-start | bytes 9220
  2.6 3.5 %copy-start.4 = (s32[1,128]{1,0:T(1,128)S(1)}, s32[1,128]{1,0:T(1,128)}, u32[]{:S(2)}) copy-start(s32[1,128]{1,0:T(1,128)} %param.32) | copy-start | bytes 1540
  2.6 7.5 %collective-permute-start.1 = (f32[9,32,128]{2,1,0:T(8,128)S(1)}, f32[9,32,128]{2,1,0:T(8,128)S(1)}, u32[]{:S(2)}, u32[]{:S(2)}) collective-permute-start(f32[9,32,128]{2,1,0:T(8,128)S(1)} %get-tuple-element.37), channel_id=1, source_target_pairs={{0,1},{1,0},{2,3},{3,2},{4,5},{5,4},{6,7},{7,6},{8,9},{9,8},{10,11... | collective-permute-start | bytes 442376 | tf_op jit(solution)/shard_map/ppermute | solution.py:16
  2.7 8.0 %collective-permute-start = (f32[9,32,128]{2,1,0:T(8,128)S(1)}, f32[9,32,128]{2,1,0:T(8,128)S(1)}, u32[]{:S(2)}, u32[]{:S(2)}) collective-permute-start(f32[9,32,128]{2,1,0:T(8,128)S(1)} %get-tuple-element.36), channel_id=1, source_target_pairs={{1,2},{2,1},{3,4},{4,3},{5,6},{6,5},{9,10},{10,9},{11,12},{12,11},... | collective-permute-start | bytes 442376 | tf_op jit(solution)/shard_map/ppermute | solution.py:16
  6.8 8.7 %all-to-all-start = ((f32[8,8,128]{2,1,0:T(8,128)}), f32[8,8,128]{2,1,0:T(8,128)S(1)}, u32[]{:S(2)}, u32[]{:S(2)}) async-start(f32[8,8,128]{2,1,0:T(8,128)} %broadcast_in_dim.5), calls=%async_computation | async-start | bytes 65536 | tf_op jit(solution)/shard_map/all_to_all | solution.py:516
  11.7 6.8 %collective-permute-start.2 = (f32[6,32,128]{2,1,0:T(8,128)S(1)}, f32[6,32,128]{2,1,0:T(8,128)S(1)}, u32[]{:S(2)}, u32[]{:S(2)}) collective-permute-start(f32[6,32,128]{2,1,0:T(8,128)S(1)} %get-tuple-element.45), channel_id=1, source_target_pairs={{1,2},{2,1},{3,4},{4,3},{5,6},{6,5},{9,10},{10,9},{11,12},{12,11},... | collective-permute-start | bytes 294920 | tf_op jit(solution)/shard_map/ppermute | solution.py:16
  15.4 3.1 %collective-permute-start.3 = (f32[6,32,128]{2,1,0:T(8,128)S(1)}, f32[6,32,128]{2,1,0:T(8,128)S(1)}, u32[]{:S(2)}, u32[]{:S(2)}) collective-permute-start(f32[6,32,128]{2,1,0:T(8,128)S(1)} %get-tuple-element.46), channel_id=1, source_target_pairs={{0,1},{1,0},{2,3},{3,2},{4,5},{5,4},{6,7},{7,6},{8,9},{9,8},{10,11... | collective-permute-start | bytes 294920 | tf_op jit(solution)/shard_map/ppermute | solution.py:16
  15.5 3.0 %copy-start = (f32[1,3,4,32,128]{4,3,2,1,0:T(8,128)S(1)}, f32[1,3,4,32,128]{4,3,2,1,0:T(8,128)}, u32[]{:S(2)}) copy-start(f32[1,3,4,32,128]{4,3,2,1,0:T(8,128)} %param.20) | copy-start | bytes 589828
  15.5 3.0 %copy-start.1 = (f32[1,3,4,32,128]{4,3,2,1,0:T(8,128)S(1)}, f32[1,3,4,32,128]{4,3,2,1,0:T(8,128)}, u32[]{:S(2)}) copy-start(f32[1,3,4,32,128]{4,3,2,1,0:T(8,128)} %param.21) | copy-start | bytes 589828
  15.6 3.0 %copy-start.2 = (f32[1,3,4,32,128]{4,3,2,1,0:T(8,128)S(1)}, f32[1,3,4,32,128]{4,3,2,1,0:T(8,128)}, u32[]{:S(2)}) copy-start(f32[1,3,4,32,128]{4,3,2,1,0:T(8,128)} %param.22) | copy-start | bytes 589828
  19.6 6.8 %collective-permute-start.4 = (f32[6,32,128]{2,1,0:T(8,128)S(1)}, f32[6,32,128]{2,1,0:T(8,128)S(1)}, u32[]{:S(2)}, u32[]{:S(2)}) collective-permute-start(f32[6,32,128]{2,1,0:T(8,128)S(1)} %get-tuple-element.50), channel_id=1, source_target_pairs={{1,2},{2,1},{3,4},{4,3},{5,6},{6,5},{9,10},{10,9},{11,12},{12,11},... | collective-permute-start | bytes 294920 | tf_op jit(solution)/shard_map/ppermute | solution.py:16
  23.3 3.1 %collective-permute-start.5 = (f32[6,32,128]{2,1,0:T(8,128)S(1)}, f32[6,32,128]{2,1,0:T(8,128)S(1)}, u32[]{:S(2)}, u32[]{:S(2)}) collective-permute-start(f32[6,32,128]{2,1,0:T(8,128)S(1)} %get-tuple-element.51), channel_id=1, source_target_pairs={{0,1},{1,0},{2,3},{3,2},{4,5},{5,4},{6,7},{7,6},{8,9},{9,8},{10,11... | collective-permute-start | bytes 294920 | tf_op jit(solution)/shard_map/ppermute | solution.py:16
  27.5 6.8 %collective-permute-start.6 = (f32[6,32,128]{2,1,0:T(8,128)S(1)}, f32[6,32,128]{2,1,0:T(8,128)S(1)}, u32[]{:S(2)}, u32[]{:S(2)}) collective-permute-start(f32[6,32,128]{2,1,0:T(8,128)S(1)} %get-tuple-element.56), channel_id=1, source_target_pairs={{1,2},{2,1},{3,4},{4,3},{5,6},{6,5},{9,10},{10,9},{11,12},{12,11},... | collective-permute-start | bytes 294920 | tf_op jit(solution)/shard_map/ppermute | solution.py:16
  31.3 3.1 %collective-permute-start.7 = (f32[6,32,128]{2,1,0:T(8,128)S(1)}, f32[6,32,128]{2,1,0:T(8,128)S(1)}, u32[]{:S(2)}, u32[]{:S(2)}) collective-permute-start(f32[6,32,128]{2,1,0:T(8,128)S(1)} %get-tuple-element.57), channel_id=1, source_target_pairs={{0,1},{1,0},{2,3},{3,2},{4,5},{5,4},{6,7},{7,6},{8,9},{9,8},{10,11... | collective-permute-start | bytes 294920 | tf_op jit(solution)/shard_map/ppermute | solution.py:16
  35.1 5.2 %collective-permute-start.8 = (f32[2,4,32,128]{3,2,1,0:T(8,128)S(1)}, f32[2,4,32,128]{3,2,1,0:T(8,128)S(1)}, u32[]{:S(2)}, u32[]{:S(2)}) collective-permute-start(f32[2,4,32,128]{3,2,1,0:T(8,128)S(1)} %adjoint_two.1), channel_id=1, source_target_pairs={{0,8},{8,0},{16,24},{24,16},{1,9},{9,1},{17,25},{25,17},{2,10},{10... | collective-permute-start | bytes 393224 | tf_op jit(solution)/shard_map/ppermute | solution.py:31
  40.4 7.2 %collective-permute-start.9 = (f32[2,4,32,128]{3,2,1,0:T(8,128)S(1)}, f32[2,4,32,128]{3,2,1,0:T(8,128)S(1)}, u32[]{:S(2)}, u32[]{:S(2)}) collective-permute-start(f32[2,4,32,128]{3,2,1,0:T(8,128)S(1)} %add.23), channel_id=1, source_target_pairs={{0,24},{8,16},{16,8},{24,0},{1,25},{9,17},{17,9},{25,1},{2,26},{10... | collective-permute-start | bytes 393224 | tf_op jit(solution)/shard_map/ppermute | solution.py:31

commit v6 on v5

--- a/solution.py
+++ b/solution.py
@@ -129,25 +129,35 @@
     b_ref[k] = jnp.where(even, left, right)
 
 
-def edge_values(planes, coef_of, inject):
+def edge_values(planes, coef_of, inject, h_out):
     last = planes.last
     lo = last - ROUND + 1
-    e, h, p = ({i: planes.triple(kind, i) for i in range(lo, last + 1)} for kind in "EHP")
+    e0 = {i: planes.triple("E", i) for i in range(last + 1)}
+    h1 = {i: h_step(planes.triple("H", i), e0[i], e0[i + 1] if i < last else None) for i in range(last + 1)}
+    p0 = {i: planes.triple("P", i) for i in range(last + 1)}
+    raw = planes.triple("H", last)
+    for c in range(3):
+        for i in range(last):
+            h_out[c, i] = h1[i][c]
+        h_out[c, last] = raw[c]
+    e, h, p = dict(e0), dict(h1), dict(p0)
     right = []
     for step in range(1, ROUND + 1):
-        parts = (1, 2) if step == ROUND else (0, 1, 2)
-        for i in range(lo + step - 1, last + 1):
-            h[i].update(h_step(h[i], e[i], e[i + 1] if i < last else None, parts=parts))
+        if step > 1:
+            parts = (1, 2) if step == ROUND else (0, 1, 2)
+            for i in range(lo + step - 1, last + 1):
+                h[i] = {**h[i], **h_step(h[i], e[i], e[i + 1] if i < last else None, parts=parts)}
         right += [h[last][1], h[last][2]]
         if step < ROUND:
             for i in range(lo + step, last + 1):
                 e[i] = e_step(e[i], h[i], h[i - 1], p[i], coef_of(i), inject(step, i))
                 p[i] = p_step(p[i], e[i], coef_of(i))
-    e, h, p = ({i: planes.triple(kind, i) for i in range(ROUND)} for kind in "EHP")
+    e, h, p = dict(e0), dict(h1), dict(p0)
     left = [e[0][1], e[0][2]]
     for step in range(1, ROUND):
-        for i in range(ROUND - step):
-            h[i] = h_step(h[i], e[i], e[i + 1])
+        if step > 1:
+            for i in range(ROUND - step):
+                h[i] = h_step(h[i], e[i], e[i + 1])
         for i in range(ROUND - step):
             parts = (0, 1, 2) if i < ROUND - step - 1 else (1, 2)
             e[i] = e_step(e[i], h[i], h[i - 1] if i > 0 else None, p[i], coef_of(i), inject(step, i), parts)
@@ -200,11 +210,8 @@
         copy.start()
     for copy in copies[:5]:
         copy.wait()
-    listed = [rate_t[k] for k in range(rate_t.shape[0])]
-    listed += [(1.0 - rate_t[k]) * strength_t[k] for k in range(rate_t.shape[0])]
-    listed += [wavelet[k] for k in range(wavelet.shape[0])]
-    for k, value in enumerate(listed):
-        tab_ref[k:k + 1, :] = jnp.full((1, span), value, F32)
+    for k in range(wavelet.shape[0]):
+        tab_ref[k:k + 1, :] = jnp.full((1, span), wavelet[k], F32)
     src = source_map(cells, signs, meta[0:1, 0:1].astype(jnp.int32), width, depth, span, full_x)
     src_ref[...] = src.reshape(width, depth, span)
     for copy in copies[5:8]:
@@ -225,10 +232,10 @@
         copy.wait()
     planes = own_planes(e_ref, h_ref, p_ref)
     right, left = edge_values(planes, lambda i: [coef_ref[k, i] for k in range(4)],
-                              lambda step, i: src_ref[i] * wavelet[step - 1])
+                              lambda step, i: src_ref[i] * wavelet[step - 1], h_ref)
     last = width - 1
-    right += [coef_ref[0, last], coef_ref[1, last], cls[last].astype(F32)]
-    left += [coef_ref[0, 0], coef_ref[1, 0], cls[0].astype(F32)]
+    right += [coef_ref[k, last] for k in (0, 1, 3)]
+    left += [coef_ref[k, 0] for k in (0, 1, 3)]
     emit_all(even, a_ref, b_ref, right, left)
 
 
@@ -280,7 +287,7 @@
     def coef_of(i):
         return [coef_ref[k, i] for k in range(4)]
 
-    before, after = ([coefh_ref[side, k] for k in range(4)] for side in (0, 1))
+    before, after = ([coefh_ref[side, k] for k in range(3)] for side in (0, 1))
     zero = jnp.zeros(coef_ref.shape[2:], F32)
     none = {c: zero for c in range(3)}
 
@@ -301,10 +308,9 @@
             low_h.update(h_step(low_h, low_e, edge, parts=(0, 1, 2) if level < ROUND else (1, 2)))
         if level == 1:
             low_e = {0: before[1] * (dby(low_h[2]) - dbz(low_h[1])), 1: -(before[1] * low_h[2]), 2: before[1] * low_h[1]}
-            low_p = {c: before[3] * low_e[c] for c in range(3)}
+            low_p = {c: before[2] * low_e[c] for c in range(3)}
         elif level < ROUND:
             low_e = e_step(low_e, low_h, far, low_p, before, 0.0)
-            low_p = p_step(low_p, low_e, before)
         h_prev = {c: low_h[c] + pick(even, a_ref, b_ref, sent + c - 1, True) for c in (1, 2)}
         for i in range(last + 1):
             e = planes.triple("E", i)
@@ -314,12 +320,15 @@
                 e_next = {c: pick(even, a_ref, b_ref, sent + c - 1, False) for c in (1, 2)}
                 if level > 1:
                     e_next = {c: e_next[c] + high_e[c] for c in (1, 2)}
-            h = h_step(planes.triple("H", i), e, e_next)
+            h = planes.triple("H", i)
+            if level > 1 or i == last:
+                h = h_step(h, e, e_next)
             cf = coef_of(i)
             new = e_step(e, h, h_prev, planes.triple("P", i), cf, inject(level, i))
             pn = p_step(planes.triple("P", i), new, cf)
             for c in range(3):
-                store("H", c, i, level, h[c])
+                if level > 1 or i == last:
+                    store("H", c, i, level, h[c])
                 store("E", c, i, level, new[c])
                 store("P", c, i, level, pn[c])
             if seen is not None:
@@ -327,12 +336,11 @@
             h_prev = h
         if level == 1:
             high_e = {0: zero, 1: after[1] * h_prev[2], 2: -(after[1] * h_prev[1])}
-            high_p = {c: after[3] * high_e[c] for c in range(3)}
+            high_p = {c: after[2] * high_e[c] for c in range(3)}
             high_h = none
         elif level < ROUND:
             high_h = h_step(high_h, high_e, None)
             high_e = e_step(high_e, high_h, h_prev, high_p, after, 0.0)
-            high_p = p_step(high_p, high_e, after)
 
 
 def store_in(e_ref, h_ref, p_ref, by_level=False):
@@ -347,32 +355,23 @@
 def forward_one_kernel(meta, tab_ref, e_ref, h_ref, p_ref, coef_ref, src_ref, b_ref, a_ref,
                        hist_ref, hs_ref, ps_ref, coefh_ref, oa_ref, ob_ref):
     even = is_even(meta, e_ref.shape[2:])
-    classes = (tab_ref.shape[0] - 2 * ROUND) // 2
-    wavelet = 2 * classes
+    wavelet = 0
     for side in (0, 1):
-        coefh_ref[side, 0] = pick(even, a_ref, b_ref, 2 * ROUND, side == 0)
-        coefh_ref[side, 1] = pick(even, a_ref, b_ref, 2 * ROUND + 1, side == 0)
-        kind = pick(even, a_ref, b_ref, 2 * ROUND + 2, side == 0)
-        rate = jnp.zeros(kind.shape, F32)
-        gain = jnp.zeros(kind.shape, F32)
-        for k in range(classes):
-            rate = jnp.where(kind == float(k), tab_ref[k:k + 1, :], rate)
-            gain = jnp.where(kind == float(k), tab_ref[classes + k:classes + k + 1, :], gain)
-        coefh_ref[side, 2] = rate
-        coefh_ref[side, 3] = gain
+        for k in range(3):
+            coefh_ref[side, k] = pick(even, a_ref, b_ref, 2 * ROUND + k, side == 0)
     planes = own_planes(e_ref, h_ref, p_ref)
 
     def inject(level, i):
         return src_ref[i] * tab_ref[wavelet + level - 1:wavelet + level, :]
 
     round_body(planes, meta, coef_ref, coefh_ref, a_ref, b_ref, inject, store_in(hist_ref, hs_ref, ps_ref, True))
-    right, left = edge_values(planes, lambda i: [coef_ref[k, i] for k in range(4)], lambda step, i: inject(ROUND + step, i))
+    right, left = edge_values(planes, lambda i: [coef_ref[k, i] for k in range(4)], lambda step, i: inject(ROUND + step, i), hs_ref)
     emit_all(even, oa_ref, ob_ref, right, left)
 
 
 def forward_two_kernel(meta, tab_ref, hist_in, hs_in, ps_in, coef_ref, coefh_ref, src_ref, maps_ref, e_ref, h_ref, p_ref,
-                       b_ref, a_ref, hist_ref, oa_ref, ob_ref, hs_ref, ps_ref):
-    wavelet = tab_ref.shape[0] - ROUND
+                       b_ref, a_ref, hist_ref, h_out, oa_ref, ob_ref, hs_ref, ps_ref):
+    wavelet = ROUND
     round_body(own_planes(hist_in, hs_in, ps_in, ROUND - 1), meta, coef_ref, coefh_ref, a_ref, b_ref,
                lambda level, i: src_ref[i] * tab_ref[wavelet + level - 1:wavelet + level, :],
                store_in(hist_ref, hs_ref, ps_ref, True))
@@ -380,7 +379,7 @@
     def inject(step, i):
         return maps_ref[0, i] * hist_ref[ROUND - step, 1, i] - maps_ref[step, i]
 
-    right, left = edge_values(own_planes(e_ref, h_ref, p_ref), lambda i: [coef_ref[k, i] for k in range(4)], inject)
+    right, left = edge_values(own_planes(e_ref, h_ref, p_ref), lambda i: [coef_ref[k, i] for k in range(4)], inject, h_out)
     emit_all(is_even(meta, e_ref.shape[2:]), oa_ref, ob_ref, right, left)
 
 
@@ -394,14 +393,8 @@
 
 
 def adjoint_one_kernel(meta, e_ref, h_ref, p_ref, coef_ref, coefh_ref, maps_ref, maps2_ref, hist1_ref, hist2_ref,
-                       b_ref, a_ref, e_out, hs_ref, ps_ref, corr_ref, oa_ref, ob_ref):
+                       b_ref, a_ref, e_out, hs_ref, ps_ref, oa_ref, ob_ref):
     planes = own_planes(e_ref, h_ref, p_ref)
-
-    def seen(level, i, e):
-        n = ROUND - level
-        now = [hist2_ref[n, c, i] for c in range(3)]
-        prev = [hist2_ref[n - 1, c, i] if n > 0 else hist1_ref[ROUND - 1, c, i] for c in range(3)]
-        correlate(corr_ref, i, e, now, prev, corr_ref if level > 1 else None)
 
     def inject(level, i):
         return maps_ref[0, i] * hist2_ref[ROUND - level, 1, i] - maps_ref[level, i]
@@ -409,9 +402,19 @@
     def inject_next(step, i):
         return maps_ref[0, i] * hist1_ref[ROUND - step, 1, i] - maps2_ref[step - 1, i]
 
-    round_body(planes, meta, coef_ref, coefh_ref, a_ref, b_ref, inject, store_in(e_out, hs_ref, ps_ref), seen)
-    right, left = edge_values(planes, lambda i: [coef_ref[k, i] for k in range(4)], inject_next)
+    round_body(planes, meta, coef_ref, coefh_ref, a_ref, b_ref, inject, store_in(e_out, hs_ref, ps_ref, True))
+    right, left = edge_values(planes, lambda i: [coef_ref[k, i] for k in range(4)], inject_next, hs_ref)
     emit_all(is_even(meta, e_ref.shape[2:]), oa_ref, ob_ref, right, left)
+
+
+def correlation_kernel(adj_ref, hist1_ref, hist2_ref, corr_ref):
+    for i in range(corr_ref.shape[1]):
+        for level in range(1, ROUND + 1):
+            n = ROUND - level
+            e = [adj_ref[level - 1, c, i] for c in range(3)]
+            now = [hist2_ref[n, c, i] for c in range(3)]
+            prev = [hist2_ref[n - 1, c, i] if n > 0 else hist1_ref[ROUND - 1, c, i] for c in range(3)]
+            correlate(corr_ref, i, e, now, prev, corr_ref if level > 1 else None)
 
 
 def adjoint_two_kernel(meta, e_ref, hs_in, ps_in, coef_ref, coefh_ref, maps_ref, maps2_ref, e0_ref, hist1_ref,
@@ -425,7 +428,7 @@
     def inject(level, i):
         return maps_ref[0, i] * hist1_ref[ROUND - level, 1, i] - maps2_ref[level - 1, i]
 
-    round_body(own_planes(e_ref, hs_in, ps_in), meta, coef_ref, coefh_ref, a_ref, b_ref, inject,
+    round_body(own_planes(e_ref, hs_in, ps_in, ROUND - 1), meta, coef_ref, coefh_ref, a_ref, b_ref, inject,
                store_in(es_ref, hs_ref, ps_ref), seen)
 
 
@@ -491,13 +494,11 @@
     adjoint = (adj_electric[0], adj_magnetic[0], adj_polar[0])
 
     own = (3, width, *plane)
-    classes = debye_rate.shape[0]
-    tab_rows = 2 * classes + steps
     *fields, coef, src, tab, a1, b1 = call(
         lambda *refs: first_kernel(width * nsub, *refs),
         "first",
         [meta],
-        [own, own, own, (4, width, *plane), (width, *plane), (tab_rows, span), *[(2 * ROUND + 3, *plane)] * 2],
+        [own, own, own, (4, width, *plane), (width, *plane), (steps, span), *[(2 * ROUND + 3, *plane)] * 2],
         [
             (width, *plane),
             (width, *plane),
@@ -519,32 +520,33 @@
         forward_one_kernel,
         "forward_one",
         [meta, tab, *fields, coef, src, got_b1, got_a1],
-        [(ROUND, *own), own, own, (2, 4, *plane), *edges],
+        [(ROUND, *own), own, own, (2, 3, *plane), *edges],
     )
     got, hs = lax.optimization_barrier((got, hs))
     got_a2, got_b2 = exchange(a2, b2)
     maps = receivers("receivers_late", (0, *range(steps, ROUND, -1)))
-    hist2, a3, b3 = call(
+    hist2, adj_h, a3, b3 = call(
         forward_two_kernel,
         "forward_two",
         [meta, tab, hist1, hs, ps, coef, coefh, src, maps, *adjoint, got_b2, got_a2],
-        [(ROUND, *own), *edges],
+        [(ROUND, *own), own, *edges],
         [own, own],
     )
     got, hist2 = lax.optimization_barrier((got, hist2))
     got_a3, got_b3 = exchange(a3, b3)
     maps2 = receivers("receivers_early", tuple(range(ROUND, 0, -1)))
-    e_adj, hs, ps, corr, a4, b4 = call(
+    adj, hs, ps, a4, b4 = call(
         adjoint_one_kernel,
         "adjoint_one",
-        [meta, *adjoint, coef, coefh, maps, maps2, hist1, hist2, got_b3, got_a3],
-        [own, own, own, (2, width, *plane), *edges],
+        [meta, adjoint[0], adj_h, adjoint[2], coef, coefh, maps, maps2, hist1, hist2, got_b3, got_a3],
+        [(ROUND, *own), own, own, *edges],
     )
     got_a4, got_b4 = exchange(a4, b4)
+    (corr,) = call(correlation_kernel, "correlation", [adj, hist1, hist2], [(2, width, *plane)], work=10**9)
     (corr,) = call(
         adjoint_two_kernel,
         "adjoint_two",
-        [meta, e_adj, hs, ps, coef, coefh, maps, maps2, fields[0], hist1, corr, got_b4, got_a4],
+        [meta, adj, hs, ps, coef, coefh, maps, maps2, fields[0], hist1, corr, got_b4, got_a4],
         [(2, width, *plane)],
         [own, own, own],
     )

time: 49.1 us -> 48.8 us (level)
    pallas_call x7 -> x8, Pallas kernels: 7.39 us -> 7.22 us  [call(): pl.pallas_call(body, name=name, out_shape=[jax.ShapeDtypeStruct(s, F32) f...]
where the time goes in v6:
time: 48.8 us; the launch traced here: 47.9 us
  starting transfers between devices  24.6 us (50%)
  waiting for transfers between devices  13.7 us (28%)
  Pallas kernels  7.22 us (15%)
  between operations  0.87 us (2%)
  other arithmetic  0.79 us (2%)
  local copies, waits for them, and re-layouts  0.73 us (1%)
    ppermute x8, starting transfers between devices, pair_swap(): return lax.ppermute(block, axis, route)  14.9 us
    ppermute x8, waiting for transfers between devices, pair_swap(): return lax.ppermute(block, axis, route)  7.73 us
    pallas_call x8, Pallas kernels, call(): pl.pallas_call(body, name=name, out_shape=[jax.ShapeDtypeStruct(s, F32) f...  7.22 us
    ppermute x2, starting transfers between devices, shot_sum(): x = x + lax.ppermute(x, 'shot', [(i, i ^ flip) for i in range(n)])  6.36 us
    ppermute x2, waiting for transfers between devices, shot_sum(): x = x + lax.ppermute(x, 'shot', [(i, i ^ flip) for i in range(n)])  6 us
    all_to_all x1, starting transfers between devices, per_device(): lax.all_to_all(jnp.broadcast_to(listed[None], (nsub, *listed.shape)), 'su...  3.33 us
  transfers between devices with their start and end apart: 11, of which 6 were waited for; matrix products, arithmetic and copies ran while one was open for 1% of the time, Pallas kernels for 6%

profile of v6, /device:TPU:4, one launch (start us, length us, event | category | flops | bytes accessed | tf_op | source)
XLA Modules:
  0.0 47.9 jit_solution(13625228736152227030)
XLA Ops:
  0.6 0.1 add_convert_fusion
  0.7 0.1 broadcast_in_dim.4.refs_0_.meta
  0.8 0.0 copy-start.5
  0.8 1.7 %first.1 = (f32[3,4,32,128]{3,2,1,0:T(8,128)S(1)}, f32[3,4,32,128]{3,2,1,0:T(8,128)S(1)}, f32[3,4,32,128]{3,2,1,0:T(8,128)S(1)}, f32[4,4,32,128]{3,2,1,0:T(8,128...) custom-call(f32[8,128]{1,0:T(8,128)S(1)} %broadcast_in_dim.4.refs_0_, ...), custom_call_target="tpu_custom_call" | custom-call | flops 10000000000 | tf_op jit(solution)/shard_map/first/pallas_call | solution.py:438
  2.5 0.0 copy-start.3
  2.6 0.0 copy-start.4
  2.6 0.1 collective-permute-start.1
  2.6 3.4 %collective-permute-start = (f32[9,32,128]{2,1,0:T(8,128)S(1)}, f32[9,32,128]{2,1,0:T(8,128)S(1)}, u32[]{:S(2)}, u32[]{:S(2)}) collective-permute-start(f32[9,32,128]{2,1,0:T(8,128)S(1)} %get-tuple-element.36), channel_id=1, source_target_pairs={{1,2},{2,1},{3,4},{4,3},{5,6},{6,5},{9,10},{10,9},{11,12},{12,11},... | collective-permute-start | bytes 442376 | tf_op jit(solution)/shard_map/ppermute | solution.py:16
  6.1 0.0 copy-done.5
  6.1 0.0 copy-done.4
  6.1 0.0 copy-done.3
  6.2 0.6 %broadcast_in_dim.5 = f32[8,8,128]{2,1,0:T(8,128)} broadcast(f32[8,128]{1,0:T(8,128)S(1)} %pad_maximum_fusion), dimensions={1,2} | broadcast | bytes 36864 | tf_op jit(solution)/shard_map/broadcast_in_dim | solution.py:517
  6.8 3.3 %all-to-all-start = ((f32[8,8,128]{2,1,0:T(8,128)}), f32[8,8,128]{2,1,0:T(8,128)S(1)}, u32[]{:S(2)}, u32[]{:S(2)}) async-start(f32[8,8,128]{2,1,0:T(8,128)} %broadcast_in_dim.5), calls=%async_computation | async-start | bytes 65536 | tf_op jit(solution)/shard_map/all_to_all | solution.py:517
  10.1 0.0 collective-permute-done.1.a_ref
  10.1 0.6 %collective-permute-done.b_ref = f32[9,32,128]{2,1,0:T(8,128)S(1)} collective-permute-done((f32[9,32,128]{2,1,0:T(8,128)S(1)}, f32[9,32,128]{2,1,0:T(8,128)S(1)}, u32[]{:S(2)}, u32[]{:S(2)}) %collective-permute-start) | collective-permute-done | bytes 147488 | tf_op jit(solution)/shard_map/ppermute | solution.py:16
  10.7 1.0 %forward_one.1 = (f32[3,3,4,32,128]{4,3,2,1,0:T(8,128)S(1)}, f32[3,4,32,128]{3,2,1,0:T(8,128)S(1)}, f32[3,4,32,128]{3,2,1,0:T(8,128)S(1)}, f32[2,3,32,128]{3,2,1...) custom-call(f32[8,128]{1,0:T(8,128)S(1)} %broadcast_in_dim.4.refs_0_.meta, ...), custom_call_target="tpu_custom_call" | custom-call | flops 10000000000 | tf_op jit(solution)/shard_map/forward_one/pallas_call | solution.py:438
  11.7 3.7 %collective-permute-start.2 = (f32[6,32,128]{2,1,0:T(8,128)S(1)}, f32[6,32,128]{2,1,0:T(8,128)S(1)}, u32[]{:S(2)}, u32[]{:S(2)}) collective-permute-start(f32[6,32,128]{2,1,0:T(8,128)S(1)} %get-tuple-element.45), channel_id=1, source_target_pairs={{1,2},{2,1},{3,4},{4,3},{5,6},{6,5},{9,10},{10,9},{11,12},{12,11},... | collective-permute-start | bytes 294920 | tf_op jit(solution)/shard_map/ppermute | solution.py:16
  15.4 0.1 collective-permute-start.3
  15.5 0.0 all-to-all-done.refs_1_
  15.5 0.0 copy-start
  15.5 0.0 copy-start.1
  15.5 0.0 copy-start.2
  15.5 1.0 %receivers_late.1.maps_ref = f32[4,4,32,128]{3,2,1,0:T(8,128)S(1)} custom-call(f32[8,128]{1,0:T(8,128)S(1)} %broadcast_in_dim.4.refs_0_.meta, f32[8,8,128]{2,1,0:T(8,128)S(1)} %all-to-all-done.refs_1_), custom_call_target="tpu_custom_call" | custom-call | flops 1000000000 | tf_op jit(solution)/shard_map/receivers_late/pallas_call | solution.py:438
  16.5 2.0 %collective-permute-done.2.b_ref = f32[6,32,128]{2,1,0:T(8,128)S(1)} collective-permute-done((f32[6,32,128]{2,1,0:T(8,128)S(1)}, f32[6,32,128]{2,1,0:T(8,128)S(1)}, u32[]{:S(2)}, u32[]{:S(2)}) %collective-permute-start.2) | collective-permute-done | bytes 98336 | tf_op jit(solution)/shard_map/ppermute | solution.py:16
  18.5 0.0 collective-permute-done.3.a_ref
  18.5 0.0 copy-done
  18.5 0.0 copy-done.1
  18.5 0.0 copy-done.2
  18.5 0.9 %forward_two.1 = (f32[3,3,4,32,128]{4,3,2,1,0:T(8,128)S(1)}, f32[3,4,32,128]{3,2,1,0:T(8,128)S(1)}, f32[6,32,128]{2,1,0:T(8,128)S(1)}, f32[6,32,128]{2,1,0:T(8,128)S(1)}) custom-call(f32[8,128]{1,0:T(8,128)S(1)} %broadcast_in_dim.4.refs_0_.meta, f32[6,128]{1,0:T(8,128)S(1)} %get-tuple-element.30.tab_ref, ...), custom_call_target="tpu_custom_call" | custom-call | flops 10000000000 | tf_op jit(solution)/shard_map/forward_two/pallas_call | solution.py:438
  19.5 3.7 %collective-permute-start.4 = (f32[6,32,128]{2,1,0:T(8,128)S(1)}, f32[6,32,128]{2,1,0:T(8,128)S(1)}, u32[]{:S(2)}, u32[]{:S(2)}) collective-permute-start(f32[6,32,128]{2,1,0:T(8,128)S(1)} %get-tuple-element.51), channel_id=1, source_target_pairs={{1,2},{2,1},{3,4},{4,3},{5,6},{6,5},{9,10},{10,9},{11,12},{12,11},... | collective-permute-start | bytes 294920 | tf_op jit(solution)/shard_map/ppermute | solution.py:16
  23.2 0.1 collective-permute-start.5
  23.3 0.8 %receivers_early.1.maps2_ref = f32[3,4,32,128]{3,2,1,0:T(8,128)S(1)} custom-call(f32[8,128]{1,0:T(8,128)S(1)} %broadcast_in_dim.4.refs_0_.meta, f32[8,8,128]{2,1,0:T(8,128)S(1)} %all-to-all-done.refs_1_), custom_call_target="tpu_custom_call" | custom-call | flops 1000000000 | tf_op jit(solution)/shard_map/receivers_early/pallas_call | solution.py:438
  24.1 2.2 %collective-permute-done.4.b_ref = f32[6,32,128]{2,1,0:T(8,128)S(1)} collective-permute-done((f32[6,32,128]{2,1,0:T(8,128)S(1)}, f32[6,32,128]{2,1,0:T(8,128)S(1)}, u32[]{:S(2)}, u32[]{:S(2)}) %collective-permute-start.4) | collective-permute-done | bytes 98336 | tf_op jit(solution)/shard_map/ppermute | solution.py:16
  26.3 0.0 collective-permute-done.5.a_ref
  26.3 1.0 %adjoint_one.1 = (f32[3,3,4,32,128]{4,3,2,1,0:T(8,128)S(1)}, f32[3,4,32,128]{3,2,1,0:T(8,128)S(1)}, f32[3,4,32,128]{3,2,1,0:T(8,128)S(1)}, f32[6,32,128]{2,1,0:T(8,128)S(1)}, f32[6,32,128]{2,1,0:T(8,128)S(1)}) custom-call(f32[8,128]{1,0:T(8,128)S(1)} %broadcast_in_dim.4.refs_0_.meta, f32[3,4,32,128]{3,2,1,0:T(8,128)S(1)} %bitcast.26, ...), custom_call_target="tpu_custom_call" | custom-call | flops 10000000000 | tf_op jit(solution)/shard_map/adjoint_one/pallas_call | solution.py:438
  27.3 3.7 %collective-permute-start.6 = (f32[6,32,128]{2,1,0:T(8,128)S(1)}, f32[6,32,128]{2,1,0:T(8,128)S(1)}, u32[]{:S(2)}, u32[]{:S(2)}) collective-permute-start(f32[6,32,128]{2,1,0:T(8,128)S(1)} %get-tuple-element.56), channel_id=1, source_target_pairs={{1,2},{2,1},{3,4},{4,3},{5,6},{6,5},{9,10},{10,9},{11,12},{12,11},... | collective-permute-start | bytes 294920 | tf_op jit(solution)/shard_map/ppermute | solution.py:16
  31.0 0.1 collective-permute-start.7
  31.1 0.1 correlation.1.corr_in
  31.2 2.9 %collective-permute-done.6.b_ref = f32[6,32,128]{2,1,0:T(8,128)S(1)} collective-permute-done((f32[6,32,128]{2,1,0:T(8,128)S(1)}, f32[6,32,128]{2,1,0:T(8,128)S(1)}, u32[]{:S(2)}, u32[]{:S(2)}) %collective-permute-start.6) | collective-permute-done | bytes 98336 | tf_op jit(solution)/shard_map/ppermute | solution.py:16
  34.1 0.0 collective-permute-done.7.a_ref
  34.2 0.7 %adjoint_two.1 = f32[2,4,32,128]{3,2,1,0:T(8,128)S(1)} custom-call(f32[8,128]{1,0:T(8,128)S(1)} %broadcast_in_dim.4.refs_0_.meta, f32[3,3,4,32,128]{4,3,2,1,0:T(8,128)S(1)} %get-tuple-element.53.adj_ref.e_ref, f32[3,4,32,128]{3,2,1,0:T(8,128)S(1)} %get-tuple-element.54.hs_in, f32[3,4,32,128]{3,2,1,0:T(8,128)S(1)} %get-tuple-element.55.ps_in, ...), custom_call_target="tpu_custom_call" | custom-call | flops 10000000000 | tf_op jit(solution)/shard_map/adjoint_two/pallas_call | solution.py:438
  34.9 2.3 %collective-permute-start.8 = (f32[2,4,32,128]{3,2,1,0:T(8,128)S(1)}, f32[2,4,32,128]{3,2,1,0:T(8,128)S(1)}, u32[]{:S(2)}, u32[]{:S(2)}) collective-permute-start(f32[2,4,32,128]{3,2,1,0:T(8,128)S(1)} %adjoint_two.1), channel_id=1, source_target_pairs={{0,8},{8,0},{16,24},{24,16},{1,9},{9,1},{17,25},{25,17},{2,10},{10... | collective-permute-start | bytes 393224 | tf_op jit(solution)/shard_map/ppermute | solution.py:31
  37.1 2.9 %collective-permute-done.8 = f32[2,4,32,128]{3,2,1,0:T(8,128)S(1)} collective-permute-done((f32[2,4,32,128]{3,2,1,0:T(8,128)S(1)}, f32[2,4,32,128]{3,2,1,0:T(8,128)S(1)}, u32[]{:S(2)}, u32[]{:S(2)}) %collective-permute-start.8) | collective-permute-done | bytes 131104 | tf_op jit(solution)/shard_map/ppermute | solution.py:31
  40.1 4.1 %collective-permute-start.9 = (f32[2,4,32,128]{3,2,1,0:T(8,128)S(1)}, f32[2,4,32,128]{3,2,1,0:T(8,128)S(1)}, u32[]{:S(2)}, u32[]{:S(2)}) collective-permute-start(f32[2,4,32,128]{3,2,1,0:T(8,128)S(1)} %add.23), channel_id=1, source_target_pairs={{0,24},{8,16},{16,8},{24,0},{1,25},{9,17},{17,9},{25,1},{2,26},{10... | collective-permute-start | bytes 393224 | tf_op jit(solution)/shard_map/ppermute | solution.py:31
  44.2 3.1 %collective-permute-done.9 = f32[2,4,32,128]{3,2,1,0:T(8,128)S(1)} collective-permute-done((f32[2,4,32,128]{3,2,1,0:T(8,128)S(1)}, f32[2,4,32,128]{3,2,1,0:T(8,128)S(1)}, u32[]{:S(2)}, u32[]{:S(2)}) %collective-permute-start.9) | collective-permute-done | bytes 131104 | tf_op jit(solution)/shard_map/ppermute | solution.py:31
  47.3 0.7 %fusion.1 = (f32[4,32,128]{2,1,0:T(8,128)}, f32[4,32,128]{2,1,0:T(8,128)}) fusion(f32[2,4,32,128]{3,2,1,0:T(8,128)S(1)} %add.24), kind=kLoop, calls=%fused_computation.2 | loop fusion | flops 65536 | bytes 262144 | tf_op jit(solution)/shard_map/neg | solution.py:554
  (6 shorter events, 0.1 us)
Async XLA Ops:
  0.8 5.3 %copy-start.5 = (s32[1,128,1]{1,2,0:T(1,128)S(1)}, s32[1,128,1]{1,2,0:T(1,128)}, u32[]{:S(2)}) copy-start(s32[1,128,1]{1,2,0:T(1,128)} %param.31) | copy-start | bytes 1540
  2.5 3.6 %copy-start.3 = (f32[1,6,128]{2,0,1:T(1,128)S(1)}, f32[1,6,128]{2,0,1:T(1,128)}, u32[]{:S(2)}) copy-start(f32[1,6,128]{2,0,1:T(1,128)} %param.33) | copy-start | bytes 9220
  2.6 3.5 %copy-start.4 = (s32[1,128]{1,0:T(1,128)S(1)}, s32[1,128]{1,0:T(1,128)}, u32[]{:S(2)}) copy-start(s32[1,128]{1,0:T(1,128)} %param.32) | copy-start | bytes 1540
  2.6 7.5 %collective-permute-start.1 = (f32[9,32,128]{2,1,0:T(8,128)S(1)}, f32[9,32,128]{2,1,0:T(8,128)S(1)}, u32[]{:S(2)}, u32[]{:S(2)}) collective-permute-start(f32[9,32,128]{2,1,0:T(8,128)S(1)} %get-tuple-element.37), channel_id=1, source_target_pairs={{0,1},{1,0},{2,3},{3,2},{4,5},{5,4},{6,7},{7,6},{8,9},{9,8},{10,11... | collective-permute-start | bytes 442376 | tf_op jit(solution)/shard_map/ppermute | solution.py:16
  2.6 8.0 %collective-permute-start = (f32[9,32,128]{2,1,0:T(8,128)S(1)}, f32[9,32,128]{2,1,0:T(8,128)S(1)}, u32[]{:S(2)}, u32[]{:S(2)}) collective-permute-start(f32[9,32,128]{2,1,0:T(8,128)S(1)} %get-tuple-element.36), channel_id=1, source_target_pairs={{1,2},{2,1},{3,4},{4,3},{5,6},{6,5},{9,10},{10,9},{11,12},{12,11},... | collective-permute-start | bytes 442376 | tf_op jit(solution)/shard_map/ppermute | solution.py:16
  6.8 8.7 %all-to-all-start = ((f32[8,8,128]{2,1,0:T(8,128)}), f32[8,8,128]{2,1,0:T(8,128)S(1)}, u32[]{:S(2)}, u32[]{:S(2)}) async-start(f32[8,8,128]{2,1,0:T(8,128)} %broadcast_in_dim.5), calls=%async_computation | async-start | bytes 65536 | tf_op jit(solution)/shard_map/all_to_all | solution.py:517
  11.7 6.8 %collective-permute-start.2 = (f32[6,32,128]{2,1,0:T(8,128)S(1)}, f32[6,32,128]{2,1,0:T(8,128)S(1)}, u32[]{:S(2)}, u32[]{:S(2)}) collective-permute-start(f32[6,32,128]{2,1,0:T(8,128)S(1)} %get-tuple-element.45), channel_id=1, source_target_pairs={{1,2},{2,1},{3,4},{4,3},{5,6},{6,5},{9,10},{10,9},{11,12},{12,11},... | collective-permute-start | bytes 294920 | tf_op jit(solution)/shard_map/ppermute | solution.py:16
  15.4 3.1 %collective-permute-start.3 = (f32[6,32,128]{2,1,0:T(8,128)S(1)}, f32[6,32,128]{2,1,0:T(8,128)S(1)}, u32[]{:S(2)}, u32[]{:S(2)}) collective-permute-start(f32[6,32,128]{2,1,0:T(8,128)S(1)} %get-tuple-element.46), channel_id=1, source_target_pairs={{0,1},{1,0},{2,3},{3,2},{4,5},{5,4},{6,7},{7,6},{8,9},{9,8},{10,11... | collective-permute-start | bytes 294920 | tf_op jit(solution)/shard_map/ppermute | solution.py:16
  15.5 3.0 %copy-start = (f32[1,3,4,32,128]{4,3,2,1,0:T(8,128)S(1)}, f32[1,3,4,32,128]{4,3,2,1,0:T(8,128)}, u32[]{:S(2)}) copy-start(f32[1,3,4,32,128]{4,3,2,1,0:T(8,128)} %param.21) | copy-start | bytes 589828
  15.5 3.0 %copy-start.1 = (f32[1,3,4,32,128]{4,3,2,1,0:T(8,128)S(1)}, f32[1,3,4,32,128]{4,3,2,1,0:T(8,128)}, u32[]{:S(2)}) copy-start(f32[1,3,4,32,128]{4,3,2,1,0:T(8,128)} %param.20) | copy-start | bytes 589828
  15.5 3.0 %copy-start.2 = (f32[1,3,4,32,128]{4,3,2,1,0:T(8,128)S(1)}, f32[1,3,4,32,128]{4,3,2,1,0:T(8,128)}, u32[]{:S(2)}) copy-start(f32[1,3,4,32,128]{4,3,2,1,0:T(8,128)} %param.22) | copy-start | bytes 589828
  19.5 6.8 %collective-permute-start.4 = (f32[6,32,128]{2,1,0:T(8,128)S(1)}, f32[6,32,128]{2,1,0:T(8,128)S(1)}, u32[]{:S(2)}, u32[]{:S(2)}) collective-permute-start(f32[6,32,128]{2,1,0:T(8,128)S(1)} %get-tuple-element.51), channel_id=1, source_target_pairs={{1,2},{2,1},{3,4},{4,3},{5,6},{6,5},{9,10},{10,9},{11,12},{12,11},... | collective-permute-start | bytes 294920 | tf_op jit(solution)/shard_map/ppermute | solution.py:16
  23.2 3.1 %collective-permute-start.5 = (f32[6,32,128]{2,1,0:T(8,128)S(1)}, f32[6,32,128]{2,1,0:T(8,128)S(1)}, u32[]{:S(2)}, u32[]{:S(2)}) collective-permute-start(f32[6,32,128]{2,1,0:T(8,128)S(1)} %get-tuple-element.52), channel_id=1, source_target_pairs={{0,1},{1,0},{2,3},{3,2},{4,5},{5,4},{6,7},{7,6},{8,9},{9,8},{10,11... | collective-permute-start | bytes 294920 | tf_op jit(solution)/shard_map/ppermute | solution.py:16
  27.3 6.8 %collective-permute-start.6 = (f32[6,32,128]{2,1,0:T(8,128)S(1)}, f32[6,32,128]{2,1,0:T(8,128)S(1)}, u32[]{:S(2)}, u32[]{:S(2)}) collective-permute-start(f32[6,32,128]{2,1,0:T(8,128)S(1)} %get-tuple-element.56), channel_id=1, source_target_pairs={{1,2},{2,1},{3,4},{4,3},{5,6},{6,5},{9,10},{10,9},{11,12},{12,11},... | collective-permute-start | bytes 294920 | tf_op jit(solution)/shard_map/ppermute | solution.py:16
  31.0 3.1 %collective-permute-start.7 = (f32[6,32,128]{2,1,0:T(8,128)S(1)}, f32[6,32,128]{2,1,0:T(8,128)S(1)}, u32[]{:S(2)}, u32[]{:S(2)}) collective-permute-start(f32[6,32,128]{2,1,0:T(8,128)S(1)} %get-tuple-element.57), channel_id=1, source_target_pairs={{0,1},{1,0},{2,3},{3,2},{4,5},{5,4},{6,7},{7,6},{8,9},{9,8},{10,11... | collective-permute-start | bytes 294920 | tf_op jit(solution)/shard_map/ppermute | solution.py:16
  34.9 5.2 %collective-permute-start.8 = (f32[2,4,32,128]{3,2,1,0:T(8,128)S(1)}, f32[2,4,32,128]{3,2,1,0:T(8,128)S(1)}, u32[]{:S(2)}, u32[]{:S(2)}) collective-permute-start(f32[2,4,32,128]{3,2,1,0:T(8,128)S(1)} %adjoint_two.1), channel_id=1, source_target_pairs={{0,8},{8,0},{16,24},{24,16},{1,9},{9,1},{17,25},{25,17},{2,10},{10... | collective-permute-start | bytes 393224 | tf_op jit(solution)/shard_map/ppermute | solution.py:31
  40.1 7.2 %collective-permute-start.9 = (f32[2,4,32,128]{3,2,1,0:T(8,128)S(1)}, f32[2,4,32,128]{3,2,1,0:T(8,128)S(1)}, u32[]{:S(2)}, u32[]{:S(2)}) collective-permute-start(f32[2,4,32,128]{3,2,1,0:T(8,128)S(1)} %add.23), channel_id=1, source_target_pairs={{0,24},{8,16},{16,8},{24,0},{1,25},{9,17},{17,9},{25,1},{2,26},{10... | collective-permute-start | bytes 393224 | tf_op jit(solution)/shard_map/ppermute | solution.py:31

commit v7 on v6

--- a/solution.py
+++ b/solution.py
@@ -312,23 +312,26 @@
         elif level < ROUND:
             low_e = e_step(low_e, low_h, far, low_p, before, 0.0)
         h_prev = {c: low_h[c] + pick(even, a_ref, b_ref, sent + c - 1, True) for c in (1, 2)}
+        now_h = {}
         for i in range(last + 1):
-            e = planes.triple("E", i)
-            if i < last:
-                e_next = planes.triple("E", i + 1, (1, 2))
-            else:
-                e_next = {c: pick(even, a_ref, b_ref, sent + c - 1, False) for c in (1, 2)}
-                if level > 1:
-                    e_next = {c: e_next[c] + high_e[c] for c in (1, 2)}
             h = planes.triple("H", i)
             if level > 1 or i == last:
-                h = h_step(h, e, e_next)
+                if i < last:
+                    e_next = planes.triple("E", i + 1, (1, 2))
+                else:
+                    e_next = {c: pick(even, a_ref, b_ref, sent + c - 1, False) for c in (1, 2)}
+                    if level > 1:
+                        e_next = {c: e_next[c] + high_e[c] for c in (1, 2)}
+                h = h_step(h, planes.triple("E", i), e_next)
+                for c in range(3):
+                    store("H", c, i, level, h[c])
+            now_h[i] = h
+        for i in range(last + 1):
+            h = now_h[i]
             cf = coef_of(i)
-            new = e_step(e, h, h_prev, planes.triple("P", i), cf, inject(level, i))
+            new = e_step(planes.triple("E", i), h, h_prev, planes.triple("P", i), cf, inject(level, i))
             pn = p_step(planes.triple("P", i), new, cf)
             for c in range(3):
-                if level > 1 or i == last:
-                    store("H", c, i, level, h[c])
                 store("E", c, i, level, new[c])
                 store("P", c, i, level, pn[c])
             if seen is not None:
@@ -513,7 +516,7 @@
         [*fields, permittivity, conductivity, debye_class, src_cell, src_sign, debye_rate, debye_strength, wavelet],
     )
     got_a1, got_b1 = exchange(a1, b1)
-    listed, b1 = lax.optimization_barrier((listed, b1))
+    listed, a1 = lax.optimization_barrier((listed, a1))
     got = lax.all_to_all(jnp.broadcast_to(listed[None], (nsub, *listed.shape)), "sub", 0, 0)
     edges = [(2 * ROUND, *plane)] * 2
     hist1, hs, ps, coefh, a2, b2 = call(

time: 48.8 us -> 48 us (0.984); the launches traced: 47.9 us -> 47.7 us
  starting transfers between devices: 24.6 us -> 23.7 us
  waiting for transfers between devices: 13.7 us -> 14.4 us
    ppermute x2, starting transfers between devices: 6.36 us -> 5.31 us  [shot_sum(): x = x + lax.ppermute(x, 'shot', [(i, i ^ flip) for i in range(n)])]
    ppermute x2, waiting for transfers between devices: 6 us -> 6.66 us  [shot_sum(): x = x + lax.ppermute(x, 'shot', [(i, i ^ flip) for i in range(n)])]
  transfers between devices with their start and end apart: 11 -> 11, of which waited for: 6 -> 5; matrix products, arithmetic and copies ran while one was open for 1% -> 1% of each run, Pallas kernels for 6% -> 6%
where the time goes in v7:
time: 48 us; the launch traced here: 47.7 us
  starting transfers between devices  23.7 us (49%)
  waiting for transfers between devices  14.4 us (30%)
  Pallas kernels  7.22 us (15%)
  between operations  0.84 us (2%)
  other arithmetic  0.79 us (2%)
  local copies, waits for them, and re-layouts  0.73 us (2%)
    ppermute x8, starting transfers between devices, pair_swap(): return lax.ppermute(block, axis, route)  14.6 us
    ppermute x8, waiting for transfers between devices, pair_swap(): return lax.ppermute(block, axis, route)  7.75 us
    pallas_call x8, Pallas kernels, call(): pl.pallas_call(body, name=name, out_shape=[jax.ShapeDtypeStruct(s, F32) f...  7.22 us
    ppermute x2, waiting for transfers between devices, shot_sum(): x = x + lax.ppermute(x, 'shot', [(i, i ^ flip) for i in range(n)])  6.66 us
    ppermute x2, starting transfers between devices, shot_sum(): x = x + lax.ppermute(x, 'shot', [(i, i ^ flip) for i in range(n)])  5.31 us
    all_to_all x1, starting transfers between devices, per_device(): lax.all_to_all(jnp.broadcast_to(listed[None], (nsub, *listed.shape)), 'su...  3.77 us
  transfers between devices with their start and end apart: 11, of which 5 were waited for; matrix products, arithmetic and copies ran while one was open for 1% of the time, Pallas kernels for 6%

profile of v7, /device:TPU:4, one launch (start us, length us, event | category | flops | bytes accessed | tf_op | source)
XLA Modules:
  0.0 47.7 jit_solution(8666752877285996850)
XLA Ops:
  0.6 0.1 add_convert_fusion
  0.7 0.1 broadcast_in_dim.4.refs_0_.meta
  0.8 0.0 copy-start.5
  0.8 1.7 %first.1 = (f32[3,4,32,128]{3,2,1,0:T(8,128)S(1)}, f32[3,4,32,128]{3,2,1,0:T(8,128)S(1)}, f32[3,4,32,128]{3,2,1,0:T(8,128)S(1)}, f32[4,4,32,128]{3,2,1,0:T(8,128...) custom-call(f32[8,128]{1,0:T(8,128)S(1)} %broadcast_in_dim.4.refs_0_, ...), custom_call_target="tpu_custom_call" | custom-call | flops 10000000000 | tf_op jit(solution)/shard_map/first/pallas_call | solution.py:441
  2.5 0.0 copy-start.3
  2.6 0.0 copy-start.4
  2.6 2.8 %collective-permute-start = (f32[9,32,128]{2,1,0:T(8,128)S(1)}, f32[9,32,128]{2,1,0:T(8,128)S(1)}, u32[]{:S(2)}, u32[]{:S(2)}) collective-permute-start(f32[9,32,128]{2,1,0:T(8,128)S(1)} %get-tuple-element.36), channel_id=1, source_target_pairs={{1,2},{2,1},{3,4},{4,3},{5,6},{6,5},{9,10},{10,9},{11,12},{12,11},... | collective-permute-start | bytes 442376 | tf_op jit(solution)/shard_map/ppermute | solution.py:16
  5.4 0.8 %collective-permute-start.1 = (f32[9,32,128]{2,1,0:T(8,128)S(1)}, f32[9,32,128]{2,1,0:T(8,128)S(1)}, u32[]{:S(2)}, u32[]{:S(2)}) collective-permute-start(f32[9,32,128]{2,1,0:T(8,128)S(1)} %get-tuple-element.37), channel_id=1, source_target_pairs={{0,1},{1,0},{2,3},{3,2},{4,5},{5,4},{6,7},{7,6},{8,9},{9,8},{10,11... | collective-permute-start | bytes 442376 | tf_op jit(solution)/shard_map/ppermute | solution.py:16
  6.2 0.0 copy-done.5
  6.2 0.0 copy-done.4
  6.2 0.0 copy-done.3
  6.2 0.6 %broadcast_in_dim.5 = f32[8,8,128]{2,1,0:T(8,128)} broadcast(f32[8,128]{1,0:T(8,128)S(1)} %pad_maximum_fusion), dimensions={1,2} | broadcast | bytes 36864 | tf_op jit(solution)/shard_map/broadcast_in_dim | solution.py:520
  6.8 3.8 %all-to-all-start = ((f32[8,8,128]{2,1,0:T(8,128)}), f32[8,8,128]{2,1,0:T(8,128)S(1)}, u32[]{:S(2)}, u32[]{:S(2)}) async-start(f32[8,8,128]{2,1,0:T(8,128)} %broadcast_in_dim.5), calls=%async_computation | async-start | bytes 65536 | tf_op jit(solution)/shard_map/all_to_all | solution.py:520
  10.6 0.0 collective-permute-done.b_ref
  10.6 0.0 collective-permute-done.1.a_ref
  10.6 1.0 %forward_one.1 = (f32[3,3,4,32,128]{4,3,2,1,0:T(8,128)S(1)}, f32[3,4,32,128]{3,2,1,0:T(8,128)S(1)}, f32[3,4,32,128]{3,2,1,0:T(8,128)S(1)}, f32[2,3,32,128]{3,2,1...) custom-call(f32[8,128]{1,0:T(8,128)S(1)} %broadcast_in_dim.4.refs_0_.meta, ...), custom_call_target="tpu_custom_call" | custom-call | flops 10000000000 | tf_op jit(solution)/shard_map/forward_one/pallas_call | solution.py:441
  11.6 3.6 %collective-permute-start.2 = (f32[6,32,128]{2,1,0:T(8,128)S(1)}, f32[6,32,128]{2,1,0:T(8,128)S(1)}, u32[]{:S(2)}, u32[]{:S(2)}) collective-permute-start(f32[6,32,128]{2,1,0:T(8,128)S(1)} %get-tuple-element.45), channel_id=1, source_target_pairs={{1,2},{2,1},{3,4},{4,3},{5,6},{6,5},{9,10},{10,9},{11,12},{12,11},... | collective-permute-start | bytes 294920 | tf_op jit(solution)/shard_map/ppermute | solution.py:16
  15.3 0.1 collective-permute-start.3
  15.3 0.0 all-to-all-done.refs_1_
  15.3 0.0 copy-start
  15.4 0.0 copy-start.1
  15.4 0.0 copy-start.2
  15.4 1.0 %receivers_late.1.maps_ref = f32[4,4,32,128]{3,2,1,0:T(8,128)S(1)} custom-call(f32[8,128]{1,0:T(8,128)S(1)} %broadcast_in_dim.4.refs_0_.meta, f32[8,8,128]{2,1,0:T(8,128)S(1)} %all-to-all-done.refs_1_), custom_call_target="tpu_custom_call" | custom-call | flops 1000000000 | tf_op jit(solution)/shard_map/receivers_late/pallas_call | solution.py:441
  16.4 2.3 %collective-permute-done.2.b_ref = f32[6,32,128]{2,1,0:T(8,128)S(1)} collective-permute-done((f32[6,32,128]{2,1,0:T(8,128)S(1)}, f32[6,32,128]{2,1,0:T(8,128)S(1)}, u32[]{:S(2)}, u32[]{:S(2)}) %collective-permute-start.2) | collective-permute-done | bytes 98336 | tf_op jit(solution)/shard_map/ppermute | solution.py:16
  18.7 0.0 collective-permute-done.3.a_ref
  18.7 0.0 copy-done
  18.7 0.0 copy-done.1
  18.7 0.0 copy-done.2
  18.7 0.9 %forward_two.1 = (f32[3,3,4,32,128]{4,3,2,1,0:T(8,128)S(1)}, f32[3,4,32,128]{3,2,1,0:T(8,128)S(1)}, f32[6,32,128]{2,1,0:T(8,128)S(1)}, f32[6,32,128]{2,1,0:T(8,128)S(1)}) custom-call(f32[8,128]{1,0:T(8,128)S(1)} %broadcast_in_dim.4.refs_0_.meta, f32[6,128]{1,0:T(8,128)S(1)} %get-tuple-element.30.tab_ref, ...), custom_call_target="tpu_custom_call" | custom-call | flops 10000000000 | tf_op jit(solution)/shard_map/forward_two/pallas_call | solution.py:441
  19.7 3.6 %collective-permute-start.4 = (f32[6,32,128]{2,1,0:T(8,128)S(1)}, f32[6,32,128]{2,1,0:T(8,128)S(1)}, u32[]{:S(2)}, u32[]{:S(2)}) collective-permute-start(f32[6,32,128]{2,1,0:T(8,128)S(1)} %get-tuple-element.51), channel_id=1, source_target_pairs={{1,2},{2,1},{3,4},{4,3},{5,6},{6,5},{9,10},{10,9},{11,12},{12,11},... | collective-permute-start | bytes 294920 | tf_op jit(solution)/shard_map/ppermute | solution.py:16
  23.3 0.1 collective-permute-start.5
  23.4 0.8 %receivers_early.1.maps2_ref = f32[3,4,32,128]{3,2,1,0:T(8,128)S(1)} custom-call(f32[8,128]{1,0:T(8,128)S(1)} %broadcast_in_dim.4.refs_0_.meta, f32[8,8,128]{2,1,0:T(8,128)S(1)} %all-to-all-done.refs_1_), custom_call_target="tpu_custom_call" | custom-call | flops 1000000000 | tf_op jit(solution)/shard_map/receivers_early/pallas_call | solution.py:441
  24.1 2.4 %collective-permute-done.4.b_ref = f32[6,32,128]{2,1,0:T(8,128)S(1)} collective-permute-done((f32[6,32,128]{2,1,0:T(8,128)S(1)}, f32[6,32,128]{2,1,0:T(8,128)S(1)}, u32[]{:S(2)}, u32[]{:S(2)}) %collective-permute-start.4) | collective-permute-done | bytes 98336 | tf_op jit(solution)/shard_map/ppermute | solution.py:16
  26.5 0.0 collective-permute-done.5.a_ref
  26.5 1.0 %adjoint_one.1 = (f32[3,3,4,32,128]{4,3,2,1,0:T(8,128)S(1)}, f32[3,4,32,128]{3,2,1,0:T(8,128)S(1)}, f32[3,4,32,128]{3,2,1,0:T(8,128)S(1)}, f32[6,32,128]{2,1,0:T(8,128)S(1)}, f32[6,32,128]{2,1,0:T(8,128)S(1)}) custom-call(f32[8,128]{1,0:T(8,128)S(1)} %broadcast_in_dim.4.refs_0_.meta, f32[3,4,32,128]{3,2,1,0:T(8,128)S(1)} %bitcast.26, ...), custom_call_target="tpu_custom_call" | custom-call | flops 10000000000 | tf_op jit(solution)/shard_map/adjoint_one/pallas_call | solution.py:441
  27.5 3.6 %collective-permute-start.6 = (f32[6,32,128]{2,1,0:T(8,128)S(1)}, f32[6,32,128]{2,1,0:T(8,128)S(1)}, u32[]{:S(2)}, u32[]{:S(2)}) collective-permute-start(f32[6,32,128]{2,1,0:T(8,128)S(1)} %get-tuple-element.56), channel_id=1, source_target_pairs={{1,2},{2,1},{3,4},{4,3},{5,6},{6,5},{9,10},{10,9},{11,12},{12,11},... | collective-permute-start | bytes 294920 | tf_op jit(solution)/shard_map/ppermute | solution.py:16
  31.1 0.1 collective-permute-start.7
  31.2 0.1 correlation.1.corr_in
  31.3 3.0 %collective-permute-done.6.b_ref = f32[6,32,128]{2,1,0:T(8,128)S(1)} collective-permute-done((f32[6,32,128]{2,1,0:T(8,128)S(1)}, f32[6,32,128]{2,1,0:T(8,128)S(1)}, u32[]{:S(2)}, u32[]{:S(2)}) %collective-permute-start.6) | collective-permute-done | bytes 98336 | tf_op jit(solution)/shard_map/ppermute | solution.py:16
  34.3 0.0 collective-permute-done.7.a_ref
  34.3 0.7 %adjoint_two.1 = f32[2,4,32,128]{3,2,1,0:T(8,128)S(1)} custom-call(f32[8,128]{1,0:T(8,128)S(1)} %broadcast_in_dim.4.refs_0_.meta, f32[3,3,4,32,128]{4,3,2,1,0:T(8,128)S(1)} %get-tuple-element.53.adj_ref.e_ref, f32[3,4,32,128]{3,2,1,0:T(8,128)S(1)} %get-tuple-element.54.hs_in, f32[3,4,32,128]{3,2,1,0:T(8,128)S(1)} %get-tuple-element.55.ps_in, ...), custom_call_target="tpu_custom_call" | custom-call | flops 10000000000 | tf_op jit(solution)/shard_map/adjoint_two/pallas_call | solution.py:441
  35.1 1.6 %collective-permute-start.8 = (f32[2,4,32,128]{3,2,1,0:T(8,128)S(1)}, f32[2,4,32,128]{3,2,1,0:T(8,128)S(1)}, u32[]{:S(2)}, u32[]{:S(2)}) collective-permute-start(f32[2,4,32,128]{3,2,1,0:T(8,128)S(1)} %adjoint_two.1), channel_id=1, source_target_pairs={{0,8},{8,0},{16,24},{24,16},{1,9},{9,1},{17,25},{25,17},{2,10},{10... | collective-permute-start | bytes 393224 | tf_op jit(solution)/shard_map/ppermute | solution.py:31
  36.7 3.4 %collective-permute-done.8 = f32[2,4,32,128]{3,2,1,0:T(8,128)S(1)} collective-permute-done((f32[2,4,32,128]{3,2,1,0:T(8,128)S(1)}, f32[2,4,32,128]{3,2,1,0:T(8,128)S(1)}, u32[]{:S(2)}, u32[]{:S(2)}) %collective-permute-start.8) | collective-permute-done | bytes 131104 | tf_op jit(solution)/shard_map/ppermute | solution.py:31
  40.1 3.7 %collective-permute-start.9 = (f32[2,4,32,128]{3,2,1,0:T(8,128)S(1)}, f32[2,4,32,128]{3,2,1,0:T(8,128)S(1)}, u32[]{:S(2)}, u32[]{:S(2)}) collective-permute-start(f32[2,4,32,128]{3,2,1,0:T(8,128)S(1)} %add.23), channel_id=1, source_target_pairs={{0,24},{8,16},{16,8},{24,0},{1,25},{9,17},{17,9},{25,1},{2,26},{10... | collective-permute-start | bytes 393224 | tf_op jit(solution)/shard_map/ppermute | solution.py:31
  43.8 3.3 %collective-permute-done.9 = f32[2,4,32,128]{3,2,1,0:T(8,128)S(1)} collective-permute-done((f32[2,4,32,128]{3,2,1,0:T(8,128)S(1)}, f32[2,4,32,128]{3,2,1,0:T(8,128)S(1)}, u32[]{:S(2)}, u32[]{:S(2)}) %collective-permute-start.9) | collective-permute-done | bytes 131104 | tf_op jit(solution)/shard_map/ppermute | solution.py:31
  47.1 0.7 %fusion.1 = (f32[4,32,128]{2,1,0:T(8,128)}, f32[4,32,128]{2,1,0:T(8,128)}) fusion(f32[2,4,32,128]{3,2,1,0:T(8,128)S(1)} %add.24), kind=kLoop, calls=%fused_computation.2 | loop fusion | flops 65536 | bytes 262144 | tf_op jit(solution)/shard_map/neg | solution.py:557
  (6 shorter events, 0.1 us)
Async XLA Ops:
  0.8 5.4 %copy-start.5 = (s32[1,128,1]{1,2,0:T(1,128)S(1)}, s32[1,128,1]{1,2,0:T(1,128)}, u32[]{:S(2)}) copy-start(s32[1,128,1]{1,2,0:T(1,128)} %param.31) | copy-start | bytes 1540
  2.5 3.6 %copy-start.3 = (f32[1,6,128]{2,0,1:T(1,128)S(1)}, f32[1,6,128]{2,0,1:T(1,128)}, u32[]{:S(2)}) copy-start(f32[1,6,128]{2,0,1:T(1,128)} %param.33) | copy-start | bytes 9220
  2.6 3.6 %copy-start.4 = (s32[1,128]{1,0:T(1,128)S(1)}, s32[1,128]{1,0:T(1,128)}, u32[]{:S(2)}) copy-start(s32[1,128]{1,0:T(1,128)} %param.32) | copy-start | bytes 1540
  2.6 8.0 %collective-permute-start = (f32[9,32,128]{2,1,0:T(8,128)S(1)}, f32[9,32,128]{2,1,0:T(8,128)S(1)}, u32[]{:S(2)}, u32[]{:S(2)}) collective-permute-start(f32[9,32,128]{2,1,0:T(8,128)S(1)} %get-tuple-element.36), channel_id=1, source_target_pairs={{1,2},{2,1},{3,4},{4,3},{5,6},{6,5},{9,10},{10,9},{11,12},{12,11},... | collective-permute-start | bytes 442376 | tf_op jit(solution)/shard_map/ppermute | solution.py:16
  5.4 5.3 %collective-permute-start.1 = (f32[9,32,128]{2,1,0:T(8,128)S(1)}, f32[9,32,128]{2,1,0:T(8,128)S(1)}, u32[]{:S(2)}, u32[]{:S(2)}) collective-permute-start(f32[9,32,128]{2,1,0:T(8,128)S(1)} %get-tuple-element.37), channel_id=1, source_target_pairs={{0,1},{1,0},{2,3},{3,2},{4,5},{5,4},{6,7},{7,6},{8,9},{9,8},{10,11... | collective-permute-start | bytes 442376 | tf_op jit(solution)/shard_map/ppermute | solution.py:16
  6.8 8.5 %all-to-all-start = ((f32[8,8,128]{2,1,0:T(8,128)}), f32[8,8,128]{2,1,0:T(8,128)S(1)}, u32[]{:S(2)}, u32[]{:S(2)}) async-start(f32[8,8,128]{2,1,0:T(8,128)} %broadcast_in_dim.5), calls=%async_computation | async-start | bytes 65536 | tf_op jit(solution)/shard_map/all_to_all | solution.py:520
  11.6 7.1 %collective-permute-start.2 = (f32[6,32,128]{2,1,0:T(8,128)S(1)}, f32[6,32,128]{2,1,0:T(8,128)S(1)}, u32[]{:S(2)}, u32[]{:S(2)}) collective-permute-start(f32[6,32,128]{2,1,0:T(8,128)S(1)} %get-tuple-element.45), channel_id=1, source_target_pairs={{1,2},{2,1},{3,4},{4,3},{5,6},{6,5},{9,10},{10,9},{11,12},{12,11},... | collective-permute-start | bytes 294920 | tf_op jit(solution)/shard_map/ppermute | solution.py:16
  15.3 3.4 %collective-permute-start.3 = (f32[6,32,128]{2,1,0:T(8,128)S(1)}, f32[6,32,128]{2,1,0:T(8,128)S(1)}, u32[]{:S(2)}, u32[]{:S(2)}) collective-permute-start(f32[6,32,128]{2,1,0:T(8,128)S(1)} %get-tuple-element.46), channel_id=1, source_target_pairs={{0,1},{1,0},{2,3},{3,2},{4,5},{5,4},{6,7},{7,6},{8,9},{9,8},{10,11... | collective-permute-start | bytes 294920 | tf_op jit(solution)/shard_map/ppermute | solution.py:16
  15.3 3.4 %copy-start = (f32[1,3,4,32,128]{4,3,2,1,0:T(8,128)S(1)}, f32[1,3,4,32,128]{4,3,2,1,0:T(8,128)}, u32[]{:S(2)}) copy-start(f32[1,3,4,32,128]{4,3,2,1,0:T(8,128)} %param.21) | copy-start | bytes 589828
  15.4 3.4 %copy-start.1 = (f32[1,3,4,32,128]{4,3,2,1,0:T(8,128)S(1)}, f32[1,3,4,32,128]{4,3,2,1,0:T(8,128)}, u32[]{:S(2)}) copy-start(f32[1,3,4,32,128]{4,3,2,1,0:T(8,128)} %param.20) | copy-start | bytes 589828
  15.4 3.3 %copy-start.2 = (f32[1,3,4,32,128]{4,3,2,1,0:T(8,128)S(1)}, f32[1,3,4,32,128]{4,3,2,1,0:T(8,128)}, u32[]{:S(2)}) copy-start(f32[1,3,4,32,128]{4,3,2,1,0:T(8,128)} %param.22) | copy-start | bytes 589828
  19.7 6.8 %collective-permute-start.4 = (f32[6,32,128]{2,1,0:T(8,128)S(1)}, f32[6,32,128]{2,1,0:T(8,128)S(1)}, u32[]{:S(2)}, u32[]{:S(2)}) collective-permute-start(f32[6,32,128]{2,1,0:T(8,128)S(1)} %get-tuple-element.51), channel_id=1, source_target_pairs={{1,2},{2,1},{3,4},{4,3},{5,6},{6,5},{9,10},{10,9},{11,12},{12,11},... | collective-permute-start | bytes 294920 | tf_op jit(solution)/shard_map/ppermute | solution.py:16
  23.3 3.2 %collective-permute-start.5 = (f32[6,32,128]{2,1,0:T(8,128)S(1)}, f32[6,32,128]{2,1,0:T(8,128)S(1)}, u32[]{:S(2)}, u32[]{:S(2)}) collective-permute-start(f32[6,32,128]{2,1,0:T(8,128)S(1)} %get-tuple-element.52), channel_id=1, source_target_pairs={{0,1},{1,0},{2,3},{3,2},{4,5},{5,4},{6,7},{7,6},{8,9},{9,8},{10,11... | collective-permute-start | bytes 294920 | tf_op jit(solution)/shard_map/ppermute | solution.py:16
  27.5 6.8 %collective-permute-start.6 = (f32[6,32,128]{2,1,0:T(8,128)S(1)}, f32[6,32,128]{2,1,0:T(8,128)S(1)}, u32[]{:S(2)}, u32[]{:S(2)}) collective-permute-start(f32[6,32,128]{2,1,0:T(8,128)S(1)} %get-tuple-element.56), channel_id=1, source_target_pairs={{1,2},{2,1},{3,4},{4,3},{5,6},{6,5},{9,10},{10,9},{11,12},{12,11},... | collective-permute-start | bytes 294920 | tf_op jit(solution)/shard_map/ppermute | solution.py:16
  31.1 3.2 %collective-permute-start.7 = (f32[6,32,128]{2,1,0:T(8,128)S(1)}, f32[6,32,128]{2,1,0:T(8,128)S(1)}, u32[]{:S(2)}, u32[]{:S(2)}) collective-permute-start(f32[6,32,128]{2,1,0:T(8,128)S(1)} %get-tuple-element.57), channel_id=1, source_target_pairs={{0,1},{1,0},{2,3},{3,2},{4,5},{5,4},{6,7},{7,6},{8,9},{9,8},{10,11... | collective-permute-start | bytes 294920 | tf_op jit(solution)/shard_map/ppermute | solution.py:16
  35.1 5.0 %collective-permute-start.8 = (f32[2,4,32,128]{3,2,1,0:T(8,128)S(1)}, f32[2,4,32,128]{3,2,1,0:T(8,128)S(1)}, u32[]{:S(2)}, u32[]{:S(2)}) collective-permute-start(f32[2,4,32,128]{3,2,1,0:T(8,128)S(1)} %adjoint_two.1), channel_id=1, source_target_pairs={{0,8},{8,0},{16,24},{24,16},{1,9},{9,1},{17,25},{25,17},{2,10},{10... | collective-permute-start | bytes 393224 | tf_op jit(solution)/shard_map/ppermute | solution.py:31
  40.1 6.9 %collective-permute-start.9 = (f32[2,4,32,128]{3,2,1,0:T(8,128)S(1)}, f32[2,4,32,128]{3,2,1,0:T(8,128)S(1)}, u32[]{:S(2)}, u32[]{:S(2)}) collective-permute-start(f32[2,4,32,128]{3,2,1,0:T(8,128)S(1)} %add.23), channel_id=1, source_target_pairs={{0,24},{8,16},{16,8},{24,0},{1,25},{9,17},{17,9},{25,1},{2,26},{10... | collective-permute-start | bytes 393224 | tf_op jit(solution)/shard_map/ppermute | solution.py:31

commit v8 on v7

--- a/solution.py
+++ b/solution.py
@@ -217,9 +217,10 @@
     for copy in copies[5:8]:
         copy.wait()
     for i in range(width):
-        ratio = cond[i] / (2.0 * perm[i])
-        coef_ref[0, i] = (1.0 - ratio) / (1.0 + ratio)
-        coef_ref[1, i] = 0.5 / (perm[i] * (1.0 + ratio))
+        double = 2.0 * perm[i]
+        share = 1.0 / (double + cond[i])
+        coef_ref[0, i] = (double - cond[i]) * share
+        coef_ref[1, i] = share
         kind = cls[i]
         rate = jnp.zeros((depth, span), F32)
         gain = jnp.zeros((depth, span), F32)
@@ -234,8 +235,8 @@
     right, left = edge_values(planes, lambda i: [coef_ref[k, i] for k in range(4)],
                               lambda step, i: src_ref[i] * wavelet[step - 1], h_ref)
     last = width - 1
-    right += [coef_ref[k, last] for k in (0, 1, 3)]
-    left += [coef_ref[k, 0] for k in (0, 1, 3)]
+    right += [coef_ref[0, last] - coef_ref[1, last] * coef_ref[3, last], coef_ref[1, last]]
+    left += [coef_ref[0, 0] - coef_ref[1, 0] * coef_ref[3, 0], coef_ref[1, 0]]
     emit_all(even, a_ref, b_ref, right, left)
 
 
@@ -287,7 +288,8 @@
     def coef_of(i):
         return [coef_ref[k, i] for k in range(4)]
 
-    before, after = ([coefh_ref[side, k] for k in range(3)] for side in (0, 1))
+    before, after = ([coefh_ref[side, k] for k in range(2)] for side in (0, 1))
+    rest = {c: 0.0 for c in range(3)}
     zero = jnp.zeros(coef_ref.shape[2:], F32)
     none = {c: zero for c in range(3)}
 
@@ -296,7 +298,7 @@
         ref[idx] = value
         planes.put((kind, c, i), ref, *idx)
 
-    low_e = low_h = low_p = high_e = high_p = None
+    low_e = low_h = high_e = high_h = None
     for level in range(1, ROUND + 1):
         sent = 2 * (level - 1)
         edge = {c: planes.get("E", c, 0) * keep for c in (1, 2)}
@@ -308,9 +310,8 @@
             low_h.update(h_step(low_h, low_e, edge, parts=(0, 1, 2) if level < ROUND else (1, 2)))
         if level == 1:
             low_e = {0: before[1] * (dby(low_h[2]) - dbz(low_h[1])), 1: -(before[1] * low_h[2]), 2: before[1] * low_h[1]}
-            low_p = {c: before[2] * low_e[c] for c in range(3)}
         elif level < ROUND:
-            low_e = e_step(low_e, low_h, far, low_p, before, 0.0)
+            low_e = e_step(low_e, low_h, far, rest, before, 0.0)
         h_prev = {c: low_h[c] + pick(even, a_ref, b_ref, sent + c - 1, True) for c in (1, 2)}
         now_h = {}
         for i in range(last + 1):
@@ -339,11 +340,10 @@
             h_prev = h
         if level == 1:
             high_e = {0: zero, 1: after[1] * h_prev[2], 2: -(after[1] * h_prev[1])}
-            high_p = {c: after[2] * high_e[c] for c in range(3)}
             high_h = none
         elif level < ROUND:
             high_h = h_step(high_h, high_e, None)
-            high_e = e_step(high_e, high_h, h_prev, high_p, after, 0.0)
+            high_e = e_step(high_e, high_h, h_prev, rest, after, 0.0)
 
 
 def store_in(e_ref, h_ref, p_ref, by_level=False):
@@ -360,7 +360,7 @@
     even = is_even(meta, e_ref.shape[2:])
     wavelet = 0
     for side in (0, 1):
-        for k in range(3):
+        for k in range(2):
             coefh_ref[side, k] = pick(even, a_ref, b_ref, 2 * ROUND + k, side == 0)
     planes = own_planes(e_ref, h_ref, p_ref)
 
@@ -501,7 +501,7 @@
         lambda *refs: first_kernel(width * nsub, *refs),
         "first",
         [meta],
-        [own, own, own, (4, width, *plane), (width, *plane), (steps, span), *[(2 * ROUND + 3, *plane)] * 2],
+        [own, own, own, (4, width, *plane), (width, *plane), (steps, span), *[(2 * ROUND + 2, *plane)] * 2],
         [
             (width, *plane),
             (width, *plane),
@@ -523,7 +523,7 @@
         forward_one_kernel,
         "forward_one",
         [meta, tab, *fields, coef, src, got_b1, got_a1],
-        [(ROUND, *own), own, own, (2, 3, *plane), *edges],
+        [(ROUND, *own), own, own, (2, 2, *plane), *edges],
     )
     got, hs = lax.optimization_barrier((got, hs))
     got_a2, got_b2 = exchange(a2, b2)

time: 48 us -> 47.9 us (level)
  no operation moved by 1% of the time
where the time goes in v8:
time: 47.9 us; the launch traced here: 47.7 us
  starting transfers between devices  23.6 us (49%)
  waiting for transfers between devices  14.6 us (30%)
  Pallas kernels  7.15 us (15%)
  between operations  0.82 us (2%)
  other arithmetic  0.79 us (2%)
  local copies, waits for them, and re-layouts  0.73 us (2%)
    ppermute x8, starting transfers between devices, pair_swap(): return lax.ppermute(block, axis, route)  14.5 us
    ppermute x8, waiting for transfers between devices, pair_swap(): return lax.ppermute(block, axis, route)  7.94 us
    pallas_call x8, Pallas kernels, call(): pl.pallas_call(body, name=name, out_shape=[jax.ShapeDtypeStruct(s, F32) f...  7.15 us
    ppermute x2, waiting for transfers between devices, shot_sum(): x = x + lax.ppermute(x, 'shot', [(i, i ^ flip) for i in range(n)])  6.66 us
    ppermute x2, starting transfers between devices, shot_sum(): x = x + lax.ppermute(x, 'shot', [(i, i ^ flip) for i in range(n)])  5.31 us
    all_to_all x1, starting transfers between devices, per_device(): lax.all_to_all(jnp.broadcast_to(listed[None], (nsub, *listed.shape)), 'su...  3.77 us
  transfers between devices with their start and end apart: 11, of which 5 were waited for; matrix products, arithmetic and copies ran while one was open for 1% of the time, Pallas kernels for 6%

profile of v8, /device:TPU:4, one launch (start us, length us, event | category | flops | bytes accessed | tf_op | source)
XLA Modules:
  0.0 47.7 jit_solution(1506638805954297529)
XLA Ops:
  0.6 0.1 add_convert_fusion
  0.7 0.1 broadcast_in_dim.4.refs_0_.meta
  0.8 0.0 copy-start.5
  0.8 1.7 %first.1 = (f32[3,4,32,128]{3,2,1,0:T(8,128)S(1)}, f32[3,4,32,128]{3,2,1,0:T(8,128)S(1)}, f32[3,4,32,128]{3,2,1,0:T(8,128)S(1)}, f32[4,4,32,128]{3,2,1,0:T(8,128...) custom-call(f32[8,128]{1,0:T(8,128)S(1)} %broadcast_in_dim.4.refs_0_, ...), custom_call_target="tpu_custom_call" | custom-call | flops 10000000000 | tf_op jit(solution)/shard_map/first/pallas_call | solution.py:441
  2.5 0.0 copy-start.3
  2.6 0.0 copy-start.4
  2.6 2.8 %collective-permute-start = (f32[8,32,128]{2,1,0:T(8,128)S(1)}, f32[8,32,128]{2,1,0:T(8,128)S(1)}, u32[]{:S(2)}, u32[]{:S(2)}) collective-permute-start(f32[8,32,128]{2,1,0:T(8,128)S(1)} %get-tuple-element.36), channel_id=1, source_target_pairs={{1,2},{2,1},{3,4},{4,3},{5,6},{6,5},{9,10},{10,9},{11,12},{12,11},... | collective-permute-start | bytes 393224 | tf_op jit(solution)/shard_map/ppermute | solution.py:16
  5.4 0.8 %collective-permute-start.1 = (f32[8,32,128]{2,1,0:T(8,128)S(1)}, f32[8,32,128]{2,1,0:T(8,128)S(1)}, u32[]{:S(2)}, u32[]{:S(2)}) collective-permute-start(f32[8,32,128]{2,1,0:T(8,128)S(1)} %get-tuple-element.37), channel_id=1, source_target_pairs={{0,1},{1,0},{2,3},{3,2},{4,5},{5,4},{6,7},{7,6},{8,9},{9,8},{10,11... | collective-permute-start | bytes 393224 | tf_op jit(solution)/shard_map/ppermute | solution.py:16
  6.2 0.0 copy-done.5
  6.2 0.0 copy-done.4
  6.2 0.0 copy-done.3
  6.2 0.6 %broadcast_in_dim.5 = f32[8,8,128]{2,1,0:T(8,128)} broadcast(f32[8,128]{1,0:T(8,128)S(1)} %pad_maximum_fusion), dimensions={1,2} | broadcast | bytes 36864 | tf_op jit(solution)/shard_map/broadcast_in_dim | solution.py:520
  6.8 3.8 %all-to-all-start = ((f32[8,8,128]{2,1,0:T(8,128)}), f32[8,8,128]{2,1,0:T(8,128)S(1)}, u32[]{:S(2)}, u32[]{:S(2)}) async-start(f32[8,8,128]{2,1,0:T(8,128)} %broadcast_in_dim.5), calls=%async_computation | async-start | bytes 65536 | tf_op jit(solution)/shard_map/all_to_all | solution.py:520
  10.6 0.0 collective-permute-done.b_ref
  10.6 0.0 collective-permute-done.1.a_ref
  10.6 1.0 %forward_one.1 = (f32[3,3,4,32,128]{4,3,2,1,0:T(8,128)S(1)}, f32[3,4,32,128]{3,2,1,0:T(8,128)S(1)}, f32[3,4,32,128]{3,2,1,0:T(8,128)S(1)}, f32[2,2,32,128]{3,2,1...) custom-call(f32[8,128]{1,0:T(8,128)S(1)} %broadcast_in_dim.4.refs_0_.meta, ...), custom_call_target="tpu_custom_call" | custom-call | flops 10000000000 | tf_op jit(solution)/shard_map/forward_one/pallas_call | solution.py:441
  11.6 3.3 %collective-permute-start.2 = (f32[6,32,128]{2,1,0:T(8,128)S(1)}, f32[6,32,128]{2,1,0:T(8,128)S(1)}, u32[]{:S(2)}, u32[]{:S(2)}) collective-permute-start(f32[6,32,128]{2,1,0:T(8,128)S(1)} %get-tuple-element.45), channel_id=1, source_target_pairs={{1,2},{2,1},{3,4},{4,3},{5,6},{6,5},{9,10},{10,9},{11,12},{12,11},... | collective-permute-start | bytes 294920 | tf_op jit(solution)/shard_map/ppermute | solution.py:16
  14.9 0.3 collective-permute-start.3
  15.1 0.0 all-to-all-done.refs_1_
  15.2 0.0 copy-start
  15.2 0.0 copy-start.1
  15.2 0.0 copy-start.2
  15.2 1.0 %receivers_late.1.maps_ref = f32[4,4,32,128]{3,2,1,0:T(8,128)S(1)} custom-call(f32[8,128]{1,0:T(8,128)S(1)} %broadcast_in_dim.4.refs_0_.meta, f32[8,8,128]{2,1,0:T(8,128)S(1)} %all-to-all-done.refs_1_), custom_call_target="tpu_custom_call" | custom-call | flops 1000000000 | tf_op jit(solution)/shard_map/receivers_late/pallas_call | solution.py:441
  16.1 2.5 %collective-permute-done.2.b_ref = f32[6,32,128]{2,1,0:T(8,128)S(1)} collective-permute-done((f32[6,32,128]{2,1,0:T(8,128)S(1)}, f32[6,32,128]{2,1,0:T(8,128)S(1)}, u32[]{:S(2)}, u32[]{:S(2)}) %collective-permute-start.2) | collective-permute-done | bytes 98336 | tf_op jit(solution)/shard_map/ppermute | solution.py:16
  18.7 0.0 collective-permute-done.3.a_ref
  18.7 0.0 copy-done
  18.7 0.0 copy-done.1
  18.7 0.0 copy-done.2
  18.7 0.9 %forward_two.1 = (f32[3,3,4,32,128]{4,3,2,1,0:T(8,128)S(1)}, f32[3,4,32,128]{3,2,1,0:T(8,128)S(1)}, f32[6,32,128]{2,1,0:T(8,128)S(1)}, f32[6,32,128]{2,1,0:T(8,128)S(1)}) custom-call(f32[8,128]{1,0:T(8,128)S(1)} %broadcast_in_dim.4.refs_0_.meta, f32[6,128]{1,0:T(8,128)S(1)} %get-tuple-element.30.tab_ref, ...), custom_call_target="tpu_custom_call" | custom-call | flops 10000000000 | tf_op jit(solution)/shard_map/forward_two/pallas_call | solution.py:441
  19.6 3.6 %collective-permute-start.4 = (f32[6,32,128]{2,1,0:T(8,128)S(1)}, f32[6,32,128]{2,1,0:T(8,128)S(1)}, u32[]{:S(2)}, u32[]{:S(2)}) collective-permute-start(f32[6,32,128]{2,1,0:T(8,128)S(1)} %get-tuple-element.51), channel_id=1, source_target_pairs={{1,2},{2,1},{3,4},{4,3},{5,6},{6,5},{9,10},{10,9},{11,12},{12,11},... | collective-permute-start | bytes 294920 | tf_op jit(solution)/shard_map/ppermute | solution.py:16
  23.2 0.1 collective-permute-start.5
  23.3 0.8 %receivers_early.1.maps2_ref = f32[3,4,32,128]{3,2,1,0:T(8,128)S(1)} custom-call(f32[8,128]{1,0:T(8,128)S(1)} %broadcast_in_dim.4.refs_0_.meta, f32[8,8,128]{2,1,0:T(8,128)S(1)} %all-to-all-done.refs_1_), custom_call_target="tpu_custom_call" | custom-call | flops 1000000000 | tf_op jit(solution)/shard_map/receivers_early/pallas_call | solution.py:441
  24.1 2.4 %collective-permute-done.4.b_ref = f32[6,32,128]{2,1,0:T(8,128)S(1)} collective-permute-done((f32[6,32,128]{2,1,0:T(8,128)S(1)}, f32[6,32,128]{2,1,0:T(8,128)S(1)}, u32[]{:S(2)}, u32[]{:S(2)}) %collective-permute-start.4) | collective-permute-done | bytes 98336 | tf_op jit(solution)/shard_map/ppermute | solution.py:16
  26.5 0.0 collective-permute-done.5.a_ref
  26.5 1.0 %adjoint_one.1 = (f32[3,3,4,32,128]{4,3,2,1,0:T(8,128)S(1)}, f32[3,4,32,128]{3,2,1,0:T(8,128)S(1)}, f32[3,4,32,128]{3,2,1,0:T(8,128)S(1)}, f32[6,32,128]{2,1,0:T(8,128)S(1)}, f32[6,32,128]{2,1,0:T(8,128)S(1)}) custom-call(f32[8,128]{1,0:T(8,128)S(1)} %broadcast_in_dim.4.refs_0_.meta, f32[3,4,32,128]{3,2,1,0:T(8,128)S(1)} %bitcast.26, ...), custom_call_target="tpu_custom_call" | custom-call | flops 10000000000 | tf_op jit(solution)/shard_map/adjoint_one/pallas_call | solution.py:441
  27.4 3.6 %collective-permute-start.6 = (f32[6,32,128]{2,1,0:T(8,128)S(1)}, f32[6,32,128]{2,1,0:T(8,128)S(1)}, u32[]{:S(2)}, u32[]{:S(2)}) collective-permute-start(f32[6,32,128]{2,1,0:T(8,128)S(1)} %get-tuple-element.56), channel_id=1, source_target_pairs={{1,2},{2,1},{3,4},{4,3},{5,6},{6,5},{9,10},{10,9},{11,12},{12,11},... | collective-permute-start | bytes 294920 | tf_op jit(solution)/shard_map/ppermute | solution.py:16
  31.1 0.1 collective-permute-start.7
  31.1 0.1 correlation.1.corr_in
  31.2 3.0 %collective-permute-done.6.b_ref = f32[6,32,128]{2,1,0:T(8,128)S(1)} collective-permute-done((f32[6,32,128]{2,1,0:T(8,128)S(1)}, f32[6,32,128]{2,1,0:T(8,128)S(1)}, u32[]{:S(2)}, u32[]{:S(2)}) %collective-permute-start.6) | collective-permute-done | bytes 98336 | tf_op jit(solution)/shard_map/ppermute | solution.py:16
  34.3 0.0 collective-permute-done.7.a_ref
  34.3 0.7 %adjoint_two.1 = f32[2,4,32,128]{3,2,1,0:T(8,128)S(1)} custom-call(f32[8,128]{1,0:T(8,128)S(1)} %broadcast_in_dim.4.refs_0_.meta, f32[3,3,4,32,128]{4,3,2,1,0:T(8,128)S(1)} %get-tuple-element.53.adj_ref.e_ref, f32[3,4,32,128]{3,2,1,0:T(8,128)S(1)} %get-tuple-element.54.hs_in, f32[3,4,32,128]{3,2,1,0:T(8,128)S(1)} %get-tuple-element.55.ps_in, ...), custom_call_target="tpu_custom_call" | custom-call | flops 10000000000 | tf_op jit(solution)/shard_map/adjoint_two/pallas_call | solution.py:441
  35.0 1.6 %collective-permute-start.8 = (f32[2,4,32,128]{3,2,1,0:T(8,128)S(1)}, f32[2,4,32,128]{3,2,1,0:T(8,128)S(1)}, u32[]{:S(2)}, u32[]{:S(2)}) collective-permute-start(f32[2,4,32,128]{3,2,1,0:T(8,128)S(1)} %adjoint_two.1), channel_id=1, source_target_pairs={{0,8},{8,0},{16,24},{24,16},{1,9},{9,1},{17,25},{25,17},{2,10},{10... | collective-permute-start | bytes 393224 | tf_op jit(solution)/shard_map/ppermute | solution.py:31
  36.6 3.4 %collective-permute-done.8 = f32[2,4,32,128]{3,2,1,0:T(8,128)S(1)} collective-permute-done((f32[2,4,32,128]{3,2,1,0:T(8,128)S(1)}, f32[2,4,32,128]{3,2,1,0:T(8,128)S(1)}, u32[]{:S(2)}, u32[]{:S(2)}) %collective-permute-start.8) | collective-permute-done | bytes 131104 | tf_op jit(solution)/shard_map/ppermute | solution.py:31
  40.0 3.7 %collective-permute-start.9 = (f32[2,4,32,128]{3,2,1,0:T(8,128)S(1)}, f32[2,4,32,128]{3,2,1,0:T(8,128)S(1)}, u32[]{:S(2)}, u32[]{:S(2)}) collective-permute-start(f32[2,4,32,128]{3,2,1,0:T(8,128)S(1)} %add.23), channel_id=1, source_target_pairs={{0,24},{8,16},{16,8},{24,0},{1,25},{9,17},{17,9},{25,1},{2,26},{10... | collective-permute-start | bytes 393224 | tf_op jit(solution)/shard_map/ppermute | solution.py:31
  43.7 3.3 %collective-permute-done.9 = f32[2,4,32,128]{3,2,1,0:T(8,128)S(1)} collective-permute-done((f32[2,4,32,128]{3,2,1,0:T(8,128)S(1)}, f32[2,4,32,128]{3,2,1,0:T(8,128)S(1)}, u32[]{:S(2)}, u32[]{:S(2)}) %collective-permute-start.9) | collective-permute-done | bytes 131104 | tf_op jit(solution)/shard_map/ppermute | solution.py:31
  47.0 0.7 %fusion.1 = (f32[4,32,128]{2,1,0:T(8,128)}, f32[4,32,128]{2,1,0:T(8,128)}) fusion(f32[2,4,32,128]{3,2,1,0:T(8,128)S(1)} %add.24), kind=kLoop, calls=%fused_computation.2 | loop fusion | flops 65536 | bytes 262144 | tf_op jit(solution)/shard_map/neg | solution.py:557
  (6 shorter events, 0.1 us)
Async XLA Ops:
  0.8 5.4 %copy-start.5 = (s32[1,128,1]{1,2,0:T(1,128)S(1)}, s32[1,128,1]{1,2,0:T(1,128)}, u32[]{:S(2)}) copy-start(s32[1,128,1]{1,2,0:T(1,128)} %param.31) | copy-start | bytes 1540
  2.5 3.6 %copy-start.3 = (f32[1,6,128]{2,0,1:T(1,128)S(1)}, f32[1,6,128]{2,0,1:T(1,128)}, u32[]{:S(2)}) copy-start(f32[1,6,128]{2,0,1:T(1,128)} %param.33) | copy-start | bytes 9220
  2.6 3.6 %copy-start.4 = (s32[1,128]{1,0:T(1,128)S(1)}, s32[1,128]{1,0:T(1,128)}, u32[]{:S(2)}) copy-start(s32[1,128]{1,0:T(1,128)} %param.32) | copy-start | bytes 1540
  2.6 8.0 %collective-permute-start = (f32[8,32,128]{2,1,0:T(8,128)S(1)}, f32[8,32,128]{2,1,0:T(8,128)S(1)}, u32[]{:S(2)}, u32[]{:S(2)}) collective-permute-start(f32[8,32,128]{2,1,0:T(8,128)S(1)} %get-tuple-element.36), channel_id=1, source_target_pairs={{1,2},{2,1},{3,4},{4,3},{5,6},{6,5},{9,10},{10,9},{11,12},{12,11},... | collective-permute-start | bytes 393224 | tf_op jit(solution)/shard_map/ppermute | solution.py:16
  5.4 5.2 %collective-permute-start.1 = (f32[8,32,128]{2,1,0:T(8,128)S(1)}, f32[8,32,128]{2,1,0:T(8,128)S(1)}, u32[]{:S(2)}, u32[]{:S(2)}) collective-permute-start(f32[8,32,128]{2,1,0:T(8,128)S(1)} %get-tuple-element.37), channel_id=1, source_target_pairs={{0,1},{1,0},{2,3},{3,2},{4,5},{5,4},{6,7},{7,6},{8,9},{9,8},{10,11... | collective-permute-start | bytes 393224 | tf_op jit(solution)/shard_map/ppermute | solution.py:16
  6.8 8.3 %all-to-all-start = ((f32[8,8,128]{2,1,0:T(8,128)}), f32[8,8,128]{2,1,0:T(8,128)S(1)}, u32[]{:S(2)}, u32[]{:S(2)}) async-start(f32[8,8,128]{2,1,0:T(8,128)} %broadcast_in_dim.5), calls=%async_computation | async-start | bytes 65536 | tf_op jit(solution)/shard_map/all_to_all | solution.py:520
  11.6 7.1 %collective-permute-start.2 = (f32[6,32,128]{2,1,0:T(8,128)S(1)}, f32[6,32,128]{2,1,0:T(8,128)S(1)}, u32[]{:S(2)}, u32[]{:S(2)}) collective-permute-start(f32[6,32,128]{2,1,0:T(8,128)S(1)} %get-tuple-element.45), channel_id=1, source_target_pairs={{1,2},{2,1},{3,4},{4,3},{5,6},{6,5},{9,10},{10,9},{11,12},{12,11},... | collective-permute-start | bytes 294920 | tf_op jit(solution)/shard_map/ppermute | solution.py:16
  14.9 3.8 %collective-permute-start.3 = (f32[6,32,128]{2,1,0:T(8,128)S(1)}, f32[6,32,128]{2,1,0:T(8,128)S(1)}, u32[]{:S(2)}, u32[]{:S(2)}) collective-permute-start(f32[6,32,128]{2,1,0:T(8,128)S(1)} %get-tuple-element.46), channel_id=1, source_target_pairs={{0,1},{1,0},{2,3},{3,2},{4,5},{5,4},{6,7},{7,6},{8,9},{9,8},{10,11... | collective-permute-start | bytes 294920 | tf_op jit(solution)/shard_map/ppermute | solution.py:16
  15.2 3.5 %copy-start = (f32[1,3,4,32,128]{4,3,2,1,0:T(8,128)S(1)}, f32[1,3,4,32,128]{4,3,2,1,0:T(8,128)}, u32[]{:S(2)}) copy-start(f32[1,3,4,32,128]{4,3,2,1,0:T(8,128)} %param.21) | copy-start | bytes 589828
  15.2 3.5 %copy-start.1 = (f32[1,3,4,32,128]{4,3,2,1,0:T(8,128)S(1)}, f32[1,3,4,32,128]{4,3,2,1,0:T(8,128)}, u32[]{:S(2)}) copy-start(f32[1,3,4,32,128]{4,3,2,1,0:T(8,128)} %param.20) | copy-start | bytes 589828
  15.2 3.5 %copy-start.2 = (f32[1,3,4,32,128]{4,3,2,1,0:T(8,128)S(1)}, f32[1,3,4,32,128]{4,3,2,1,0:T(8,128)}, u32[]{:S(2)}) copy-start(f32[1,3,4,32,128]{4,3,2,1,0:T(8,128)} %param.22) | copy-start | bytes 589828
  19.6 6.8 %collective-permute-start.4 = (f32[6,32,128]{2,1,0:T(8,128)S(1)}, f32[6,32,128]{2,1,0:T(8,128)S(1)}, u32[]{:S(2)}, u32[]{:S(2)}) collective-permute-start(f32[6,32,128]{2,1,0:T(8,128)S(1)} %get-tuple-element.51), channel_id=1, source_target_pairs={{1,2},{2,1},{3,4},{4,3},{5,6},{6,5},{9,10},{10,9},{11,12},{12,11},... | collective-permute-start | bytes 294920 | tf_op jit(solution)/shard_map/ppermute | solution.py:16
  23.2 3.2 %collective-permute-start.5 = (f32[6,32,128]{2,1,0:T(8,128)S(1)}, f32[6,32,128]{2,1,0:T(8,128)S(1)}, u32[]{:S(2)}, u32[]{:S(2)}) collective-permute-start(f32[6,32,128]{2,1,0:T(8,128)S(1)} %get-tuple-element.52), channel_id=1, source_target_pairs={{0,1},{1,0},{2,3},{3,2},{4,5},{5,4},{6,7},{7,6},{8,9},{9,8},{10,11... | collective-permute-start | bytes 294920 | tf_op jit(solution)/shard_map/ppermute | solution.py:16
  27.4 6.8 %collective-permute-start.6 = (f32[6,32,128]{2,1,0:T(8,128)S(1)}, f32[6,32,128]{2,1,0:T(8,128)S(1)}, u32[]{:S(2)}, u32[]{:S(2)}) collective-permute-start(f32[6,32,128]{2,1,0:T(8,128)S(1)} %get-tuple-element.56), channel_id=1, source_target_pairs={{1,2},{2,1},{3,4},{4,3},{5,6},{6,5},{9,10},{10,9},{11,12},{12,11},... | collective-permute-start | bytes 294920 | tf_op jit(solution)/shard_map/ppermute | solution.py:16
  31.1 3.2 %collective-permute-start.7 = (f32[6,32,128]{2,1,0:T(8,128)S(1)}, f32[6,32,128]{2,1,0:T(8,128)S(1)}, u32[]{:S(2)}, u32[]{:S(2)}) collective-permute-start(f32[6,32,128]{2,1,0:T(8,128)S(1)} %get-tuple-element.57), channel_id=1, source_target_pairs={{0,1},{1,0},{2,3},{3,2},{4,5},{5,4},{6,7},{7,6},{8,9},{9,8},{10,11... | collective-permute-start | bytes 294920 | tf_op jit(solution)/shard_map/ppermute | solution.py:16
  35.0 5.0 %collective-permute-start.8 = (f32[2,4,32,128]{3,2,1,0:T(8,128)S(1)}, f32[2,4,32,128]{3,2,1,0:T(8,128)S(1)}, u32[]{:S(2)}, u32[]{:S(2)}) collective-permute-start(f32[2,4,32,128]{3,2,1,0:T(8,128)S(1)} %adjoint_two.1), channel_id=1, source_target_pairs={{0,8},{8,0},{16,24},{24,16},{1,9},{9,1},{17,25},{25,17},{2,10},{10... | collective-permute-start | bytes 393224 | tf_op jit(solution)/shard_map/ppermute | solution.py:31
  40.0 6.9 %collective-permute-start.9 = (f32[2,4,32,128]{3,2,1,0:T(8,128)S(1)}, f32[2,4,32,128]{3,2,1,0:T(8,128)S(1)}, u32[]{:S(2)}, u32[]{:S(2)}) collective-permute-start(f32[2,4,32,128]{3,2,1,0:T(8,128)S(1)} %add.23), channel_id=1, source_target_pairs={{0,24},{8,16},{16,8},{24,0},{1,25},{9,17},{17,9},{25,1},{2,26},{10... | collective-permute-start | bytes 393224 | tf_op jit(solution)/shard_map/ppermute | solution.py:31

commit v9 on v8

--- a/solution.py
+++ b/solution.py
@@ -199,22 +199,31 @@
 
 
 def first_kernel(full_x, meta, e_in, h_in, p_in, perm_in, cond_in, cls_in, cells_in, signs_in, rate_in, strength_in,
-                 wavelet_in, e_ref, h_ref, p_ref, coef_ref, src_ref, tab_ref, a_ref, b_ref, perm, cond, cls, cells, signs,
-                 rate_t, strength_t, wavelet, sems):
+                 wavelet_in, pos_in, owner_in, seen_in, e_ref, h_ref, p_ref, coef_ref, src_ref, tab_ref, list_out, a_ref,
+                 b_ref, perm, cond, cls, cells, signs, rate_t, strength_t, wavelet, pos, owner, seen, listed, sems):
     width, depth, span = perm.shape
     even = is_even(meta, (depth, span))
     moves = [(cells_in, cells), (signs_in, signs), (wavelet_in, wavelet), (rate_in, rate_t), (strength_in, strength_t)]
+    moves += [(pos_in, pos), (owner_in, owner), (seen_in, seen)]
     moves += [(perm_in, perm), (cond_in, cond), (cls_in, cls), (e_in, e_ref), (h_in, h_ref), (p_in, p_ref)]
     copies = [pltpu.make_async_copy(a, b, sems.at[k]) for k, (a, b) in enumerate(moves)]
     for copy in copies:
         copy.start()
-    for copy in copies[:5]:
+    for copy in copies[:8]:
         copy.wait()
+    in_x, rest = split_index(pos[...], width)
+    rec_y, rec_z = split_index(rest, span)
+    lines = [((owner[...] * width + in_x) * depth + rec_z).astype(F32), rec_y.astype(F32)]
+    lines = jnp.concatenate(lines + [seen[k] for k in range(seen.shape[0])], axis=0)
+    for slab in range(listed.shape[0]):
+        listed[slab] = lines
+    leave = pltpu.make_async_copy(listed, list_out, sems.at[len(moves)])
+    leave.start()
     for k in range(wavelet.shape[0]):
         tab_ref[k:k + 1, :] = jnp.full((1, span), wavelet[k], F32)
     src = source_map(cells, signs, meta[0:1, 0:1].astype(jnp.int32), width, depth, span, full_x)
     src_ref[...] = src.reshape(width, depth, span)
-    for copy in copies[5:8]:
+    for copy in copies[8:11]:
         copy.wait()
     for i in range(width):
         double = 2.0 * perm[i]
@@ -229,7 +238,7 @@
             gain = jnp.where(kind == k, (1.0 - rate_t[k]) * strength_t[k], gain)
         coef_ref[2, i] = rate
         coef_ref[3, i] = gain
-    for copy in copies[8:]:
+    for copy in copies[11:]:
         copy.wait()
     planes = own_planes(e_ref, h_ref, p_ref)
     right, left = edge_values(planes, lambda i: [coef_ref[k, i] for k in range(4)],
@@ -238,6 +247,7 @@
     right += [coef_ref[0, last] - coef_ref[1, last] * coef_ref[3, last], coef_ref[1, last]]
     left += [coef_ref[0, 0] - coef_ref[1, 0] * coef_ref[3, 0], coef_ref[1, 0]]
     emit_all(even, a_ref, b_ref, right, left)
+    leave.wait()
 
 
 def receiver_kernel(width, depth, which, meta, got, maps_ref, acc):
@@ -280,7 +290,7 @@
     maps_ref[...] = acc[...].reshape(maps_ref.shape)
 
 
-def round_body(planes, meta, coef_ref, coefh_ref, a_ref, b_ref, inject, dest, seen=None):
+def round_body(planes, meta, coef_ref, coefh_ref, a_ref, b_ref, inject, dest, seen=None, final=False):
     even = is_even(meta, coef_ref.shape[2:])
     keep = meta[2:3, :]
     last = planes.last
@@ -325,16 +335,19 @@
                         e_next = {c: e_next[c] + high_e[c] for c in (1, 2)}
                 h = h_step(h, planes.triple("E", i), e_next)
                 for c in range(3):
-                    store("H", c, i, level, h[c])
+                    if not (final and level == ROUND):
+                        store("H", c, i, level, h[c])
             now_h[i] = h
         for i in range(last + 1):
             h = now_h[i]
             cf = coef_of(i)
             new = e_step(planes.triple("E", i), h, h_prev, planes.triple("P", i), cf, inject(level, i))
-            pn = p_step(planes.triple("P", i), new, cf)
             for c in range(3):
                 store("E", c, i, level, new[c])
-                store("P", c, i, level, pn[c])
+            if not (final and level == ROUND):
+                pn = p_step(planes.triple("P", i), new, cf)
+                for c in range(3):
+                    store("P", c, i, level, pn[c])
             if seen is not None:
                 seen(level, i, new)
             h_prev = h
@@ -377,7 +390,7 @@
     wavelet = ROUND
     round_body(own_planes(hist_in, hs_in, ps_in, ROUND - 1), meta, coef_ref, coefh_ref, a_ref, b_ref,
                lambda level, i: src_ref[i] * tab_ref[wavelet + level - 1:wavelet + level, :],
-               store_in(hist_ref, hs_ref, ps_ref, True))
+               store_in(hist_ref, hs_ref, ps_ref, True), final=True)
 
     def inject(step, i):
         return maps_ref[0, i] * hist_ref[ROUND - step, 1, i] - maps_ref[step, i]
@@ -432,10 +445,10 @@
         return maps_ref[0, i] * hist1_ref[ROUND - level, 1, i] - maps2_ref[level - 1, i]
 
     round_body(own_planes(e_ref, hs_in, ps_in, ROUND - 1), meta, coef_ref, coefh_ref, a_ref, b_ref, inject,
-               store_in(es_ref, hs_ref, ps_ref), seen)
-
-
-def call(body, name, inputs, outs, scratch=(), remote=(), work=10**10):
+               store_in(es_ref, hs_ref, ps_ref), seen, final=True)
+
+
+def call(body, name, inputs, outs, scratch=(), remote=(), work=10**10, stay_out=()):
     vmem = pl.BlockSpec(memory_space=pltpu.VMEM)
     stay = pl.BlockSpec(memory_space=pltpu.HBM)
     return pl.pallas_call(
@@ -443,7 +456,7 @@
         name=name,
         out_shape=[jax.ShapeDtypeStruct(s, F32) for s in outs],
         in_specs=[vmem] * len(inputs) + [stay] * len(remote),
-        out_specs=[vmem] * len(outs),
+        out_specs=[stay if k in stay_out else vmem for k in range(len(outs))],
         scratch_shapes=[s if not isinstance(s, tuple) else pltpu.VMEM(s, F32) for s in scratch],
         cost_estimate=pl.CostEstimate(flops=work, transcendentals=0, bytes_accessed=0),
         compiler_params=pltpu.CompilerParams(vmem_limit_bytes=48 * 1024 * 1024),
@@ -474,14 +487,10 @@
     nsub = lax.axis_size("sub")
     nshot = lax.axis_size("shot")
     mine = lax.axis_index("sub")
-    facts = jnp.stack([mine, 1 - mine % 2, jnp.minimum(mine, 1)]).astype(F32)
-    meta = jnp.broadcast_to(jnp.pad(facts, (0, 5))[:, None], (8, 128))
+    line = lax.broadcasted_iota(jnp.int32, (8, 128), 0)
+    meta = jnp.where(line == 0, mine, jnp.where(line == 1, 1 - mine % 2, jnp.minimum(mine, 1))).astype(F32)
     plane = (depth, span)
 
-    in_x, rest = split_index(rec_pos[0], width)
-    rec_y, rec_z = split_index(rest, span)
-    rec_row = (rec_owner[0, :, 0] * width + in_x) * depth + rec_z
-    listed = jnp.concatenate([rec_row[None].astype(F32), rec_y[None].astype(F32), observed[0]], axis=0)
     def receivers(name, which):
         (maps,) = call(
             lambda *refs: receiver_kernel(width, depth, which, *refs),
@@ -497,11 +506,12 @@
     adjoint = (adj_electric[0], adj_magnetic[0], adj_polar[0])
 
     own = (3, width, *plane)
-    *fields, coef, src, tab, a1, b1 = call(
+    list_shape = (nsub, steps + 2, rec_pos.shape[1])
+    *fields, coef, src, tab, listed, a1, b1 = call(
         lambda *refs: first_kernel(width * nsub, *refs),
         "first",
         [meta],
-        [own, own, own, (4, width, *plane), (width, *plane), (steps, span), *[(2 * ROUND + 2, *plane)] * 2],
+        [own, own, own, (4, width, *plane), (width, *plane), (steps, span), list_shape, *[(2 * ROUND + 2, *plane)] * 2],
         [
             (width, *plane),
             (width, *plane),
@@ -511,13 +521,21 @@
             pltpu.SMEM(debye_rate.shape, F32),
             pltpu.SMEM(debye_strength.shape, F32),
             pltpu.SMEM(wavelet.shape, F32),
-            pltpu.SemaphoreType.DMA((11,)),
+            pltpu.VMEM(rec_pos.shape, jnp.int32),
+            pltpu.VMEM(rec_pos.shape, jnp.int32),
+            (steps, *rec_pos.shape),
+            list_shape,
+            pltpu.SemaphoreType.DMA((15,)),
         ],
-        [*fields, permittivity, conductivity, debye_class, src_cell, src_sign, debye_rate, debye_strength, wavelet],
+        [
+            *fields, permittivity, conductivity, debye_class, src_cell, src_sign, debye_rate, debye_strength, wavelet,
+            rec_pos, rec_owner[:, :, 0], jnp.swapaxes(observed, 0, 1),
+        ],
+        stay_out=(6,),
     )
     got_a1, got_b1 = exchange(a1, b1)
     listed, a1 = lax.optimization_barrier((listed, a1))
-    got = lax.all_to_all(jnp.broadcast_to(listed[None], (nsub, *listed.shape)), "sub", 0, 0)
+    got = lax.all_to_all(listed, "sub", 0, 0)
     edges = [(2 * ROUND, *plane)] * 2
     hist1, hs, ps, coefh, a2, b2 = call(
         forward_one_kernel,

time: 47.9 us -> 47.3 us (0.987)
  local copies, waits for them, and re-layouts: 0.73 us -> 0.02 us
  waiting for transfers between devices: 14.6 us -> 14 us
  starting transfers between devices: 23.6 us -> 24.2 us
    broadcast_in_dim x2 -> x0, local copies, waits for them, and re-layouts: 0.69 us -> none  [the longest x1 0.62 us: per_device(): jnp.broadcast_to(listed[None], (nsub, *listed.shape))]
    ppermute x8, starting transfers between devices: 14.5 us -> 15.1 us  [pair_swap(): return lax.ppermute(block, axis, route)]
    ppermute x8, waiting for transfers between devices: 7.94 us -> 7.34 us  [pair_swap(): return lax.ppermute(block, axis, route)]
  transfers between devices with their start and end apart: 11 -> 11, of which waited for: 5 -> 6; matrix products, arithmetic and copies ran while one was open for 1% -> 0% of each run, Pallas kernels for 6% -> 6%
where the time goes in v9:
time: 47.3 us; the launch traced here: 47 us
  starting transfers between devices  24.2 us (51%)
  waiting for transfers between devices  14 us (30%)
  Pallas kernels  7.2 us (15%)
  between operations  0.83 us (2%)
  other arithmetic  0.78 us (2%)
    ppermute x8, starting transfers between devices, pair_swap(): return lax.ppermute(block, axis, route)  15.1 us
    ppermute x8, waiting for transfers between devices, pair_swap(): return lax.ppermute(block, axis, route)  7.34 us
    pallas_call x8, Pallas kernels, call(): pl.pallas_call(body, name=name, out_shape=[jax.ShapeDtypeStruct(s, F32) f...  7.2 us
    ppermute x2, waiting for transfers between devices, shot_sum(): x = x + lax.ppermute(x, 'shot', [(i, i ^ flip) for i in range(n)])  6.66 us
    ppermute x2, starting transfers between devices, shot_sum(): x = x + lax.ppermute(x, 'shot', [(i, i ^ flip) for i in range(n)])  5.31 us
    all_to_all x1, starting transfers between devices, per_device(): got = lax.all_to_all(listed, 'sub', 0, 0)  3.77 us
  transfers between devices with their start and end apart: 11, of which 6 were waited for; matrix products, arithmetic and copies ran while one was open for 0% of the time, Pallas kernels for 6%

profile of v9, /device:TPU:4, one launch (start us, length us, event | category | flops | bytes accessed | tf_op | source)
XLA Modules:
  0.0 47.0 jit_solution(10627567523962662759)
XLA Ops:
  0.7 0.1 select_convert_fusion.refs_0_.meta
  0.7 1.8 %first.1 = (f32[3,4,32,128]{3,2,1,0:T(8,128)S(1)}, f32[3,4,32,128]{3,2,1,0:T(8,128)S(1)}, f32[3,4,32,128]{3,2,1,0:T(8,128)S(1)}, f32[4,4,32,128]{3,2,1,0:T(8,128...) custom-call(f32[8,128]{1,0:T(8,128)S(1)} %select_convert_fusion.refs, ...), custom_call_target="tpu_custom_call" | custom-call | flops 10000000000 | tf_op jit(solution)/shard_map/first/pallas_call | solution.py:454
  2.6 2.8 %collective-permute-start = (f32[8,32,128]{2,1,0:T(8,128)S(1)}, f32[8,32,128]{2,1,0:T(8,128)S(1)}, u32[]{:S(2)}, u32[]{:S(2)}) collective-permute-start(f32[8,32,128]{2,1,0:T(8,128)S(1)} %get-tuple-element.37), channel_id=1, source_target_pairs={{1,2},{2,1},{3,4},{4,3},{5,6},{6,5},{9,10},{10,9},{11,12},{12,11},... | collective-permute-start | bytes 393224 | tf_op jit(solution)/shard_map/ppermute | solution.py:16
  5.4 0.8 %collective-permute-start.1 = (f32[8,32,128]{2,1,0:T(8,128)S(1)}, f32[8,32,128]{2,1,0:T(8,128)S(1)}, u32[]{:S(2)}, u32[]{:S(2)}) collective-permute-start(f32[8,32,128]{2,1,0:T(8,128)S(1)} %get-tuple-element.38), channel_id=1, source_target_pairs={{0,1},{1,0},{2,3},{3,2},{4,5},{5,4},{6,7},{7,6},{8,9},{9,8},{10,11... | collective-permute-start | bytes 393224 | tf_op jit(solution)/shard_map/ppermute | solution.py:16
  6.2 3.8 %all-to-all-start = ((f32[8,8,128]{2,1,0:T(8,128)}), f32[8,8,128]{2,1,0:T(8,128)S(1)}, u32[]{:S(2)}, u32[]{:S(2)}) async-start(f32[8,8,128]{2,1,0:T(8,128)} %get-tuple-element.41), calls=%async_computation | async-start | bytes 65536 | tf_op jit(solution)/shard_map/all_to_all | solution.py:538
  9.9 0.3 collective-permute-done.b_ref
  10.3 0.0 collective-permute-done.1.a_ref
  10.3 1.0 %forward_one.1 = (f32[3,3,4,32,128]{4,3,2,1,0:T(8,128)S(1)}, f32[3,4,32,128]{3,2,1,0:T(8,128)S(1)}, f32[3,4,32,128]{3,2,1,0:T(8,128)S(1)}, f32[2,2,32,128]{3,2,1...) custom-call(f32[8,128]{1,0:T(8,128)S(1)} %select_convert_fusion.refs_0_.meta, ...), custom_call_target="tpu_custom_call" | custom-call | flops 10000000000 | tf_op jit(solution)/shard_map/forward_one/pallas_call | solution.py:454
  11.2 3.6 %collective-permute-start.2 = (f32[6,32,128]{2,1,0:T(8,128)S(1)}, f32[6,32,128]{2,1,0:T(8,128)S(1)}, u32[]{:S(2)}, u32[]{:S(2)}) collective-permute-start(f32[6,32,128]{2,1,0:T(8,128)S(1)} %get-tuple-element.47), channel_id=1, source_target_pairs={{1,2},{2,1},{3,4},{4,3},{5,6},{6,5},{9,10},{10,9},{11,12},{12,11},... | collective-permute-start | bytes 294920 | tf_op jit(solution)/shard_map/ppermute | solution.py:16
  14.9 0.1 collective-permute-start.3
  14.9 0.0 all-to-all-done.refs_1_
  15.0 0.0 copy-start
  15.0 0.0 copy-start.1
  15.0 0.0 copy-start.2
  15.0 1.0 %receivers_late.1.maps_ref = f32[4,4,32,128]{3,2,1,0:T(8,128)S(1)} custom-call(f32[8,128]{1,0:T(8,128)S(1)} %select_convert_fusion.refs_0_.meta, f32[8,8,128]{2,1,0:T(8,128)S(1)} %all-to-all-done.refs_1_), custom_call_target="tpu_custom_call" | custom-call | flops 1000000000 | tf_op jit(solution)/shard_map/receivers_late/pallas_call | solution.py:454
  16.0 2.1 %collective-permute-done.2.b_ref = f32[6,32,128]{2,1,0:T(8,128)S(1)} collective-permute-done((f32[6,32,128]{2,1,0:T(8,128)S(1)}, f32[6,32,128]{2,1,0:T(8,128)S(1)}, u32[]{:S(2)}, u32[]{:S(2)}) %collective-permute-start.2) | collective-permute-done | bytes 98336 | tf_op jit(solution)/shard_map/ppermute | solution.py:16
  18.1 0.0 collective-permute-done.3.a_ref
  18.1 0.0 copy-done
  18.1 0.0 copy-done.1
  18.1 0.0 copy-done.2
  18.1 0.9 %forward_two.1 = (f32[3,3,4,32,128]{4,3,2,1,0:T(8,128)S(1)}, f32[3,4,32,128]{3,2,1,0:T(8,128)S(1)}, f32[6,32,128]{2,1,0:T(8,128)S(1)}, f32[6,32,128]{2,1,0:T(8,128)S(1)}) custom-call(f32[8,128]{1,0:T(8,128)S(1)} %select_convert_fusion.refs_0_.meta, f32[6,128]{1,0:T(8,128)S(1)} %get-tuple-element.31.tab_ref, ...), custom_call_target="tpu_custom_call" | custom-call | flops 10000000000 | tf_op jit(solution)/shard_map/forward_two/pallas_call | solution.py:454
  19.0 3.8 %collective-permute-start.4 = (f32[6,32,128]{2,1,0:T(8,128)S(1)}, f32[6,32,128]{2,1,0:T(8,128)S(1)}, u32[]{:S(2)}, u32[]{:S(2)}) collective-permute-start(f32[6,32,128]{2,1,0:T(8,128)S(1)} %get-tuple-element.53), channel_id=1, source_target_pairs={{1,2},{2,1},{3,4},{4,3},{5,6},{6,5},{9,10},{10,9},{11,12},{12,11},... | collective-permute-start | bytes 294920 | tf_op jit(solution)/shard_map/ppermute | solution.py:16
  22.8 0.1 collective-permute-start.5
  22.9 0.8 %receivers_early.1.maps2_ref = f32[3,4,32,128]{3,2,1,0:T(8,128)S(1)} custom-call(f32[8,128]{1,0:T(8,128)S(1)} %select_convert_fusion.refs_0_.meta, f32[8,8,128]{2,1,0:T(8,128)S(1)} %all-to-all-done.refs_1_), custom_call_target="tpu_custom_call" | custom-call | flops 1000000000 | tf_op jit(solution)/shard_map/receivers_early/pallas_call | solution.py:454
  23.7 2.1 %collective-permute-done.4.b_ref = f32[6,32,128]{2,1,0:T(8,128)S(1)} collective-permute-done((f32[6,32,128]{2,1,0:T(8,128)S(1)}, f32[6,32,128]{2,1,0:T(8,128)S(1)}, u32[]{:S(2)}, u32[]{:S(2)}) %collective-permute-start.4) | collective-permute-done | bytes 98336 | tf_op jit(solution)/shard_map/ppermute | solution.py:16
  25.8 0.0 collective-permute-done.5.a_ref
  25.8 1.0 %adjoint_one.1 = (f32[3,3,4,32,128]{4,3,2,1,0:T(8,128)S(1)}, f32[3,4,32,128]{3,2,1,0:T(8,128)S(1)}, f32[3,4,32,128]{3,2,1,0:T(8,128)S(1)}, f32[6,32,128]{2,1,0:T(8,128)S(1)}, f32[6,32,128]{2,1,0:T(8,128)S(1)}) custom-call(f32[8,128]{1,0:T(8,128)S(1)} %select_convert_fusion.refs_0_.meta, f32[3,4,32,128]{3,2,1,0:T(8,128)S(1)} %bitcast.14, ...), custom_call_target="tpu_custom_call" | custom-call | flops 10000000000 | tf_op jit(solution)/shard_map/adjoint_one/pallas_call | solution.py:454
  26.8 3.8 %collective-permute-start.6 = (f32[6,32,128]{2,1,0:T(8,128)S(1)}, f32[6,32,128]{2,1,0:T(8,128)S(1)}, u32[]{:S(2)}, u32[]{:S(2)}) collective-permute-start(f32[6,32,128]{2,1,0:T(8,128)S(1)} %get-tuple-element.58), channel_id=1, source_target_pairs={{1,2},{2,1},{3,4},{4,3},{5,6},{6,5},{9,10},{10,9},{11,12},{12,11},... | collective-permute-start | bytes 294920 | tf_op jit(solution)/shard_map/ppermute | solution.py:16
  30.7 0.1 collective-permute-start.7
  30.7 0.1 correlation.1.corr_in
  30.8 2.8 %collective-permute-done.6.b_ref = f32[6,32,128]{2,1,0:T(8,128)S(1)} collective-permute-done((f32[6,32,128]{2,1,0:T(8,128)S(1)}, f32[6,32,128]{2,1,0:T(8,128)S(1)}, u32[]{:S(2)}, u32[]{:S(2)}) %collective-permute-start.6) | collective-permute-done | bytes 98336 | tf_op jit(solution)/shard_map/ppermute | solution.py:16
  33.6 0.0 collective-permute-done.7.a_ref
  33.6 0.7 %adjoint_two.1 = f32[2,4,32,128]{3,2,1,0:T(8,128)S(1)} custom-call(f32[8,128]{1,0:T(8,128)S(1)} %select_convert_fusion.refs_0_.meta, f32[3,3,4,32,128]{4,3,2,1,0:T(8,128)S(1)} %get-tuple-element.55.adj_ref.e_ref, f32[3,4,32,128]{3,2,1,0:T(8,128)S(1)} %get-tuple-element.56.hs_in, f32[3,4,32,128]{3,2,1,0:T(8,128)S(1)} %get-tuple-element.57.ps_in, ...), custom_call_target="tpu_custom_call" | custom-call | flops 10000000000 | tf_op jit(solution)/shard_map/adjoint_two/pallas_call | solution.py:454
  34.3 1.6 %collective-permute-start.8 = (f32[2,4,32,128]{3,2,1,0:T(8,128)S(1)}, f32[2,4,32,128]{3,2,1,0:T(8,128)S(1)}, u32[]{:S(2)}, u32[]{:S(2)}) collective-permute-start(f32[2,4,32,128]{3,2,1,0:T(8,128)S(1)} %adjoint_two.1), channel_id=1, source_target_pairs={{0,8},{8,0},{16,24},{24,16},{1,9},{9,1},{17,25},{25,17},{2,10},{10... | collective-permute-start | bytes 393224 | tf_op jit(solution)/shard_map/ppermute | solution.py:31
  36.0 3.4 %collective-permute-done.8 = f32[2,4,32,128]{3,2,1,0:T(8,128)S(1)} collective-permute-done((f32[2,4,32,128]{3,2,1,0:T(8,128)S(1)}, f32[2,4,32,128]{3,2,1,0:T(8,128)S(1)}, u32[]{:S(2)}, u32[]{:S(2)}) %collective-permute-start.8) | collective-permute-done | bytes 131104 | tf_op jit(solution)/shard_map/ppermute | solution.py:31
  39.4 3.7 %collective-permute-start.9 = (f32[2,4,32,128]{3,2,1,0:T(8,128)S(1)}, f32[2,4,32,128]{3,2,1,0:T(8,128)S(1)}, u32[]{:S(2)}, u32[]{:S(2)}) collective-permute-start(f32[2,4,32,128]{3,2,1,0:T(8,128)S(1)} %add.11), channel_id=1, source_target_pairs={{0,24},{8,16},{16,8},{24,0},{1,25},{9,17},{17,9},{25,1},{2,26},{10... | collective-permute-start | bytes 393224 | tf_op jit(solution)/shard_map/ppermute | solution.py:31
  43.1 3.3 %collective-permute-done.9 = f32[2,4,32,128]{3,2,1,0:T(8,128)S(1)} collective-permute-done((f32[2,4,32,128]{3,2,1,0:T(8,128)S(1)}, f32[2,4,32,128]{3,2,1,0:T(8,128)S(1)}, u32[]{:S(2)}, u32[]{:S(2)}) %collective-permute-start.9) | collective-permute-done | bytes 131104 | tf_op jit(solution)/shard_map/ppermute | solution.py:31
  46.4 0.7 %fusion.1 = (f32[4,32,128]{2,1,0:T(8,128)}, f32[4,32,128]{2,1,0:T(8,128)}) fusion(f32[2,4,32,128]{3,2,1,0:T(8,128)S(1)} %add.12), kind=kLoop, calls=%fused_computation.2 | loop fusion | flops 65536 | bytes 262144 | tf_op jit(solution)/shard_map/neg | solution.py:575
  (4 shorter events, 0.0 us)
Async XLA Ops:
  2.6 7.7 %collective-permute-start = (f32[8,32,128]{2,1,0:T(8,128)S(1)}, f32[8,32,128]{2,1,0:T(8,128)S(1)}, u32[]{:S(2)}, u32[]{:S(2)}) collective-permute-start(f32[8,32,128]{2,1,0:T(8,128)S(1)} %get-tuple-element.37), channel_id=1, source_target_pairs={{1,2},{2,1},{3,4},{4,3},{5,6},{6,5},{9,10},{10,9},{11,12},{12,11},... | collective-permute-start | bytes 393224 | tf_op jit(solution)/shard_map/ppermute | solution.py:16
  5.4 4.9 %collective-permute-start.1 = (f32[8,32,128]{2,1,0:T(8,128)S(1)}, f32[8,32,128]{2,1,0:T(8,128)S(1)}, u32[]{:S(2)}, u32[]{:S(2)}) collective-permute-start(f32[8,32,128]{2,1,0:T(8,128)S(1)} %get-tuple-element.38), channel_id=1, source_target_pairs={{0,1},{1,0},{2,3},{3,2},{4,5},{5,4},{6,7},{7,6},{8,9},{9,8},{10,11... | collective-permute-start | bytes 393224 | tf_op jit(solution)/shard_map/ppermute | solution.py:16
  6.2 8.8 %all-to-all-start = ((f32[8,8,128]{2,1,0:T(8,128)}), f32[8,8,128]{2,1,0:T(8,128)S(1)}, u32[]{:S(2)}, u32[]{:S(2)}) async-start(f32[8,8,128]{2,1,0:T(8,128)} %get-tuple-element.41), calls=%async_computation | async-start | bytes 65536 | tf_op jit(solution)/shard_map/all_to_all | solution.py:538
  11.2 6.8 %collective-permute-start.2 = (f32[6,32,128]{2,1,0:T(8,128)S(1)}, f32[6,32,128]{2,1,0:T(8,128)S(1)}, u32[]{:S(2)}, u32[]{:S(2)}) collective-permute-start(f32[6,32,128]{2,1,0:T(8,128)S(1)} %get-tuple-element.47), channel_id=1, source_target_pairs={{1,2},{2,1},{3,4},{4,3},{5,6},{6,5},{9,10},{10,9},{11,12},{12,11},... | collective-permute-start | bytes 294920 | tf_op jit(solution)/shard_map/ppermute | solution.py:16
  14.9 3.2 %collective-permute-start.3 = (f32[6,32,128]{2,1,0:T(8,128)S(1)}, f32[6,32,128]{2,1,0:T(8,128)S(1)}, u32[]{:S(2)}, u32[]{:S(2)}) collective-permute-start(f32[6,32,128]{2,1,0:T(8,128)S(1)} %get-tuple-element.48), channel_id=1, source_target_pairs={{0,1},{1,0},{2,3},{3,2},{4,5},{5,4},{6,7},{7,6},{8,9},{9,8},{10,11... | collective-permute-start | bytes 294920 | tf_op jit(solution)/shard_map/ppermute | solution.py:16
  15.0 3.1 %copy-start = (f32[1,3,4,32,128]{4,3,2,1,0:T(8,128)S(1)}, f32[1,3,4,32,128]{4,3,2,1,0:T(8,128)}, u32[]{:S(2)}) copy-start(f32[1,3,4,32,128]{4,3,2,1,0:T(8,128)} %param.21) | copy-start | bytes 589828
  15.0 3.1 %copy-start.1 = (f32[1,3,4,32,128]{4,3,2,1,0:T(8,128)S(1)}, f32[1,3,4,32,128]{4,3,2,1,0:T(8,128)}, u32[]{:S(2)}) copy-start(f32[1,3,4,32,128]{4,3,2,1,0:T(8,128)} %param.20) | copy-start | bytes 589828
  15.0 3.1 %copy-start.2 = (f32[1,3,4,32,128]{4,3,2,1,0:T(8,128)S(1)}, f32[1,3,4,32,128]{4,3,2,1,0:T(8,128)}, u32[]{:S(2)}) copy-start(f32[1,3,4,32,128]{4,3,2,1,0:T(8,128)} %param.22) | copy-start | bytes 589828
  19.0 6.8 %collective-permute-start.4 = (f32[6,32,128]{2,1,0:T(8,128)S(1)}, f32[6,32,128]{2,1,0:T(8,128)S(1)}, u32[]{:S(2)}, u32[]{:S(2)}) collective-permute-start(f32[6,32,128]{2,1,0:T(8,128)S(1)} %get-tuple-element.53), channel_id=1, source_target_pairs={{1,2},{2,1},{3,4},{4,3},{5,6},{6,5},{9,10},{10,9},{11,12},{12,11},... | collective-permute-start | bytes 294920 | tf_op jit(solution)/shard_map/ppermute | solution.py:16
  22.8 3.0 %collective-permute-start.5 = (f32[6,32,128]{2,1,0:T(8,128)S(1)}, f32[6,32,128]{2,1,0:T(8,128)S(1)}, u32[]{:S(2)}, u32[]{:S(2)}) collective-permute-start(f32[6,32,128]{2,1,0:T(8,128)S(1)} %get-tuple-element.54), channel_id=1, source_target_pairs={{0,1},{1,0},{2,3},{3,2},{4,5},{5,4},{6,7},{7,6},{8,9},{9,8},{10,11... | collective-permute-start | bytes 294920 | tf_op jit(solution)/shard_map/ppermute | solution.py:16
  26.8 6.8 %collective-permute-start.6 = (f32[6,32,128]{2,1,0:T(8,128)S(1)}, f32[6,32,128]{2,1,0:T(8,128)S(1)}, u32[]{:S(2)}, u32[]{:S(2)}) collective-permute-start(f32[6,32,128]{2,1,0:T(8,128)S(1)} %get-tuple-element.58), channel_id=1, source_target_pairs={{1,2},{2,1},{3,4},{4,3},{5,6},{6,5},{9,10},{10,9},{11,12},{12,11},... | collective-permute-start | bytes 294920 | tf_op jit(solution)/shard_map/ppermute | solution.py:16
  30.7 3.0 %collective-permute-start.7 = (f32[6,32,128]{2,1,0:T(8,128)S(1)}, f32[6,32,128]{2,1,0:T(8,128)S(1)}, u32[]{:S(2)}, u32[]{:S(2)}) collective-permute-start(f32[6,32,128]{2,1,0:T(8,128)S(1)} %get-tuple-element.59), channel_id=1, source_target_pairs={{0,1},{1,0},{2,3},{3,2},{4,5},{5,4},{6,7},{7,6},{8,9},{9,8},{10,11... | collective-permute-start | bytes 294920 | tf_op jit(solution)/shard_map/ppermute | solution.py:16
  34.3 5.0 %collective-permute-start.8 = (f32[2,4,32,128]{3,2,1,0:T(8,128)S(1)}, f32[2,4,32,128]{3,2,1,0:T(8,128)S(1)}, u32[]{:S(2)}, u32[]{:S(2)}) collective-permute-start(f32[2,4,32,128]{3,2,1,0:T(8,128)S(1)} %adjoint_two.1), channel_id=1, source_target_pairs={{0,8},{8,0},{16,24},{24,16},{1,9},{9,1},{17,25},{25,17},{2,10},{10... | collective-permute-start | bytes 393224 | tf_op jit(solution)/shard_map/ppermute | solution.py:31
  39.4 6.9 %collective-permute-start.9 = (f32[2,4,32,128]{3,2,1,0:T(8,128)S(1)}, f32[2,4,32,128]{3,2,1,0:T(8,128)S(1)}, u32[]{:S(2)}, u32[]{:S(2)}) collective-permute-start(f32[2,4,32,128]{3,2,1,0:T(8,128)S(1)} %add.11), channel_id=1, source_target_pairs={{0,24},{8,16},{16,8},{24,0},{1,25},{9,17},{17,9},{25,1},{2,26},{10... | collective-permute-start | bytes 393224 | tf_op jit(solution)/shard_map/ppermute | solution.py:31

commit v10 on v9

--- a/solution.py
+++ b/solution.py
@@ -342,8 +342,9 @@
             h = now_h[i]
             cf = coef_of(i)
             new = e_step(planes.triple("E", i), h, h_prev, planes.triple("P", i), cf, inject(level, i))
-            for c in range(3):
-                store("E", c, i, level, new[c])
+            if not (final and level == ROUND and seen is not None):
+                for c in range(3):
+                    store("E", c, i, level, new[c])
             if not (final and level == ROUND):
                 pn = p_step(planes.triple("P", i), new, cf)
                 for c in range(3):
@@ -534,7 +535,6 @@
         stay_out=(6,),
     )
     got_a1, got_b1 = exchange(a1, b1)
-    listed, a1 = lax.optimization_barrier((listed, a1))
     got = lax.all_to_all(listed, "sub", 0, 0)
     edges = [(2 * ROUND, *plane)] * 2
     hist1, hs, ps, coefh, a2, b2 = call(

time: 47.3 us -> 47.3 us (level)
  no operation moved by 1% of the time
where the time goes in v10:
time: 47.3 us; the launch traced here: 47 us
  starting transfers between devices  24.2 us (51%)
  waiting for transfers between devices  14 us (30%)
  Pallas kernels  7.2 us (15%)
  between operations  0.83 us (2%)
  other arithmetic  0.78 us (2%)
    ppermute x8, starting transfers between devices, pair_swap(): return lax.ppermute(block, axis, route)  15.1 us
    ppermute x8, waiting for transfers between devices, pair_swap(): return lax.ppermute(block, axis, route)  7.34 us
    pallas_call x8, Pallas kernels, call(): pl.pallas_call(body, name=name, out_shape=[jax.ShapeDtypeStruct(s, F32) f...  7.2 us
    ppermute x2, waiting for transfers between devices, shot_sum(): x = x + lax.ppermute(x, 'shot', [(i, i ^ flip) for i in range(n)])  6.66 us
    ppermute x2, starting transfers between devices, shot_sum(): x = x + lax.ppermute(x, 'shot', [(i, i ^ flip) for i in range(n)])  5.31 us
    all_to_all x1, starting transfers between devices, per_device(): got = lax.all_to_all(listed, 'sub', 0, 0)  3.77 us
  transfers between devices with their start and end apart: 11, of which 6 were waited for; matrix products, arithmetic and copies ran while one was open for 0% of the time, Pallas kernels for 6%

profile of v10, /device:TPU:4, one launch (start us, length us, event | category | flops | bytes accessed | tf_op | source)
XLA Modules:
  0.0 47.0 jit_solution(10627567523962662759)
XLA Ops:
  0.7 0.1 select_convert_fusion.refs_0_.meta
  0.7 1.8 %first.1 = (f32[3,4,32,128]{3,2,1,0:T(8,128)S(1)}, f32[3,4,32,128]{3,2,1,0:T(8,128)S(1)}, f32[3,4,32,128]{3,2,1,0:T(8,128)S(1)}, f32[4,4,32,128]{3,2,1,0:T(8,128...) custom-call(f32[8,128]{1,0:T(8,128)S(1)} %select_convert_fusion.refs, ...), custom_call_target="tpu_custom_call" | custom-call | flops 10000000000 | tf_op jit(solution)/shard_map/first/pallas_call | solution.py:455
  2.6 2.8 %collective-permute-start = (f32[8,32,128]{2,1,0:T(8,128)S(1)}, f32[8,32,128]{2,1,0:T(8,128)S(1)}, u32[]{:S(2)}, u32[]{:S(2)}) collective-permute-start(f32[8,32,128]{2,1,0:T(8,128)S(1)} %get-tuple-element.36), channel_id=1, source_target_pairs={{1,2},{2,1},{3,4},{4,3},{5,6},{6,5},{9,10},{10,9},{11,12},{12,11},... | collective-permute-start | bytes 393224 | tf_op jit(solution)/shard_map/ppermute | solution.py:16
  5.4 0.8 %collective-permute-start.1 = (f32[8,32,128]{2,1,0:T(8,128)S(1)}, f32[8,32,128]{2,1,0:T(8,128)S(1)}, u32[]{:S(2)}, u32[]{:S(2)}) collective-permute-start(f32[8,32,128]{2,1,0:T(8,128)S(1)} %get-tuple-element.37), channel_id=1, source_target_pairs={{0,1},{1,0},{2,3},{3,2},{4,5},{5,4},{6,7},{7,6},{8,9},{9,8},{10,11... | collective-permute-start | bytes 393224 | tf_op jit(solution)/shard_map/ppermute | solution.py:16
  6.2 3.8 %all-to-all-start = ((f32[8,8,128]{2,1,0:T(8,128)}), f32[8,8,128]{2,1,0:T(8,128)S(1)}, u32[]{:S(2)}, u32[]{:S(2)}) async-start(f32[8,8,128]{2,1,0:T(8,128)} %get-tuple-element.39), calls=%async_computation | async-start | bytes 65536 | tf_op jit(solution)/shard_map/all_to_all | solution.py:538
  9.9 0.3 collective-permute-done.b_ref
  10.3 0.0 collective-permute-done.1.a_ref
  10.3 1.0 %forward_one.1 = (f32[3,3,4,32,128]{4,3,2,1,0:T(8,128)S(1)}, f32[3,4,32,128]{3,2,1,0:T(8,128)S(1)}, f32[3,4,32,128]{3,2,1,0:T(8,128)S(1)}, f32[2,2,32,128]{3,2,1...) custom-call(f32[8,128]{1,0:T(8,128)S(1)} %select_convert_fusion.refs_0_.meta, ...), custom_call_target="tpu_custom_call" | custom-call | flops 10000000000 | tf_op jit(solution)/shard_map/forward_one/pallas_call | solution.py:455
  11.2 3.6 %collective-permute-start.2 = (f32[6,32,128]{2,1,0:T(8,128)S(1)}, f32[6,32,128]{2,1,0:T(8,128)S(1)}, u32[]{:S(2)}, u32[]{:S(2)}) collective-permute-start(f32[6,32,128]{2,1,0:T(8,128)S(1)} %get-tuple-element.45), channel_id=1, source_target_pairs={{1,2},{2,1},{3,4},{4,3},{5,6},{6,5},{9,10},{10,9},{11,12},{12,11},... | collective-permute-start | bytes 294920 | tf_op jit(solution)/shard_map/ppermute | solution.py:16
  14.9 0.1 collective-permute-start.3
  14.9 0.0 all-to-all-done.refs_1_
  15.0 0.0 copy-start
  15.0 0.0 copy-start.1
  15.0 0.0 copy-start.2
  15.0 1.0 %receivers_late.1.maps_ref = f32[4,4,32,128]{3,2,1,0:T(8,128)S(1)} custom-call(f32[8,128]{1,0:T(8,128)S(1)} %select_convert_fusion.refs_0_.meta, f32[8,8,128]{2,1,0:T(8,128)S(1)} %all-to-all-done.refs_1_), custom_call_target="tpu_custom_call" | custom-call | flops 1000000000 | tf_op jit(solution)/shard_map/receivers_late/pallas_call | solution.py:455
  16.0 2.1 %collective-permute-done.2.b_ref = f32[6,32,128]{2,1,0:T(8,128)S(1)} collective-permute-done((f32[6,32,128]{2,1,0:T(8,128)S(1)}, f32[6,32,128]{2,1,0:T(8,128)S(1)}, u32[]{:S(2)}, u32[]{:S(2)}) %collective-permute-start.2) | collective-permute-done | bytes 98336 | tf_op jit(solution)/shard_map/ppermute | solution.py:16
  18.1 0.0 collective-permute-done.3.a_ref
  18.1 0.0 copy-done
  18.1 0.0 copy-done.1
  18.1 0.0 copy-done.2
  18.1 0.9 %forward_two.1 = (f32[3,3,4,32,128]{4,3,2,1,0:T(8,128)S(1)}, f32[3,4,32,128]{3,2,1,0:T(8,128)S(1)}, f32[6,32,128]{2,1,0:T(8,128)S(1)}, f32[6,32,128]{2,1,0:T(8,128)S(1)}) custom-call(f32[8,128]{1,0:T(8,128)S(1)} %select_convert_fusion.refs_0_.meta, f32[6,128]{1,0:T(8,128)S(1)} %get-tuple-element.30.tab_ref, ...), custom_call_target="tpu_custom_call" | custom-call | flops 10000000000 | tf_op jit(solution)/shard_map/forward_two/pallas_call | solution.py:455
  19.0 3.8 %collective-permute-start.4 = (f32[6,32,128]{2,1,0:T(8,128)S(1)}, f32[6,32,128]{2,1,0:T(8,128)S(1)}, u32[]{:S(2)}, u32[]{:S(2)}) collective-permute-start(f32[6,32,128]{2,1,0:T(8,128)S(1)} %get-tuple-element.51), channel_id=1, source_target_pairs={{1,2},{2,1},{3,4},{4,3},{5,6},{6,5},{9,10},{10,9},{11,12},{12,11},... | collective-permute-start | bytes 294920 | tf_op jit(solution)/shard_map/ppermute | solution.py:16
  22.8 0.1 collective-permute-start.5
  22.9 0.8 %receivers_early.1.maps2_ref = f32[3,4,32,128]{3,2,1,0:T(8,128)S(1)} custom-call(f32[8,128]{1,0:T(8,128)S(1)} %select_convert_fusion.refs_0_.meta, f32[8,8,128]{2,1,0:T(8,128)S(1)} %all-to-all-done.refs_1_), custom_call_target="tpu_custom_call" | custom-call | flops 1000000000 | tf_op jit(solution)/shard_map/receivers_early/pallas_call | solution.py:455
  23.7 2.1 %collective-permute-done.4.b_ref = f32[6,32,128]{2,1,0:T(8,128)S(1)} collective-permute-done((f32[6,32,128]{2,1,0:T(8,128)S(1)}, f32[6,32,128]{2,1,0:T(8,128)S(1)}, u32[]{:S(2)}, u32[]{:S(2)}) %collective-permute-start.4) | collective-permute-done | bytes 98336 | tf_op jit(solution)/shard_map/ppermute | solution.py:16
  25.8 0.0 collective-permute-done.5.a_ref
  25.8 1.0 %adjoint_one.1 = (f32[3,3,4,32,128]{4,3,2,1,0:T(8,128)S(1)}, f32[3,4,32,128]{3,2,1,0:T(8,128)S(1)}, f32[3,4,32,128]{3,2,1,0:T(8,128)S(1)}, f32[6,32,128]{2,1,0:T(8,128)S(1)}, f32[6,32,128]{2,1,0:T(8,128)S(1)}) custom-call(f32[8,128]{1,0:T(8,128)S(1)} %select_convert_fusion.refs_0_.meta, f32[3,4,32,128]{3,2,1,0:T(8,128)S(1)} %bitcast.14, ...), custom_call_target="tpu_custom_call" | custom-call | flops 10000000000 | tf_op jit(solution)/shard_map/adjoint_one/pallas_call | solution.py:455
  26.8 3.8 %collective-permute-start.6 = (f32[6,32,128]{2,1,0:T(8,128)S(1)}, f32[6,32,128]{2,1,0:T(8,128)S(1)}, u32[]{:S(2)}, u32[]{:S(2)}) collective-permute-start(f32[6,32,128]{2,1,0:T(8,128)S(1)} %get-tuple-element.56), channel_id=1, source_target_pairs={{1,2},{2,1},{3,4},{4,3},{5,6},{6,5},{9,10},{10,9},{11,12},{12,11},... | collective-permute-start | bytes 294920 | tf_op jit(solution)/shard_map/ppermute | solution.py:16
  30.7 0.1 collective-permute-start.7
  30.7 0.1 correlation.1.corr_in
  30.8 2.8 %collective-permute-done.6.b_ref = f32[6,32,128]{2,1,0:T(8,128)S(1)} collective-permute-done((f32[6,32,128]{2,1,0:T(8,128)S(1)}, f32[6,32,128]{2,1,0:T(8,128)S(1)}, u32[]{:S(2)}, u32[]{:S(2)}) %collective-permute-start.6) | collective-permute-done | bytes 98336 | tf_op jit(solution)/shard_map/ppermute | solution.py:16
  33.6 0.0 collective-permute-done.7.a_ref
  33.6 0.7 %adjoint_two.1 = f32[2,4,32,128]{3,2,1,0:T(8,128)S(1)} custom-call(f32[8,128]{1,0:T(8,128)S(1)} %select_convert_fusion.refs_0_.meta, f32[3,3,4,32,128]{4,3,2,1,0:T(8,128)S(1)} %get-tuple-element.53.adj_ref.e_ref, f32[3,4,32,128]{3,2,1,0:T(8,128)S(1)} %get-tuple-element.54.hs_in, f32[3,4,32,128]{3,2,1,0:T(8,128)S(1)} %get-tuple-element.55.ps_in, ...), custom_call_target="tpu_custom_call" | custom-call | flops 10000000000 | tf_op jit(solution)/shard_map/adjoint_two/pallas_call | solution.py:455
  34.3 1.6 %collective-permute-start.8 = (f32[2,4,32,128]{3,2,1,0:T(8,128)S(1)}, f32[2,4,32,128]{3,2,1,0:T(8,128)S(1)}, u32[]{:S(2)}, u32[]{:S(2)}) collective-permute-start(f32[2,4,32,128]{3,2,1,0:T(8,128)S(1)} %adjoint_two.1), channel_id=1, source_target_pairs={{0,8},{8,0},{16,24},{24,16},{1,9},{9,1},{17,25},{25,17},{2,10},{10... | collective-permute-start | bytes 393224 | tf_op jit(solution)/shard_map/ppermute | solution.py:31
  36.0 3.4 %collective-permute-done.8 = f32[2,4,32,128]{3,2,1,0:T(8,128)S(1)} collective-permute-done((f32[2,4,32,128]{3,2,1,0:T(8,128)S(1)}, f32[2,4,32,128]{3,2,1,0:T(8,128)S(1)}, u32[]{:S(2)}, u32[]{:S(2)}) %collective-permute-start.8) | collective-permute-done | bytes 131104 | tf_op jit(solution)/shard_map/ppermute | solution.py:31
  39.4 3.7 %collective-permute-start.9 = (f32[2,4,32,128]{3,2,1,0:T(8,128)S(1)}, f32[2,4,32,128]{3,2,1,0:T(8,128)S(1)}, u32[]{:S(2)}, u32[]{:S(2)}) collective-permute-start(f32[2,4,32,128]{3,2,1,0:T(8,128)S(1)} %add.11), channel_id=1, source_target_pairs={{0,24},{8,16},{16,8},{24,0},{1,25},{9,17},{17,9},{25,1},{2,26},{10... | collective-permute-start | bytes 393224 | tf_op jit(solution)/shard_map/ppermute | solution.py:31
  43.1 3.3 %collective-permute-done.9 = f32[2,4,32,128]{3,2,1,0:T(8,128)S(1)} collective-permute-done((f32[2,4,32,128]{3,2,1,0:T(8,128)S(1)}, f32[2,4,32,128]{3,2,1,0:T(8,128)S(1)}, u32[]{:S(2)}, u32[]{:S(2)}) %collective-permute-start.9) | collective-permute-done | bytes 131104 | tf_op jit(solution)/shard_map/ppermute | solution.py:31
  46.4 0.7 %fusion.1 = (f32[4,32,128]{2,1,0:T(8,128)}, f32[4,32,128]{2,1,0:T(8,128)}) fusion(f32[2,4,32,128]{3,2,1,0:T(8,128)S(1)} %add.12), kind=kLoop, calls=%fused_computation.2 | loop fusion | flops 65536 | bytes 262144 | tf_op jit(solution)/shard_map/neg | solution.py:575
  (4 shorter events, 0.0 us)
Async XLA Ops:
  2.6 7.7 %collective-permute-start = (f32[8,32,128]{2,1,0:T(8,128)S(1)}, f32[8,32,128]{2,1,0:T(8,128)S(1)}, u32[]{:S(2)}, u32[]{:S(2)}) collective-permute-start(f32[8,32,128]{2,1,0:T(8,128)S(1)} %get-tuple-element.36), channel_id=1, source_target_pairs={{1,2},{2,1},{3,4},{4,3},{5,6},{6,5},{9,10},{10,9},{11,12},{12,11},... | collective-permute-start | bytes 393224 | tf_op jit(solution)/shard_map/ppermute | solution.py:16
  5.4 4.9 %collective-permute-start.1 = (f32[8,32,128]{2,1,0:T(8,128)S(1)}, f32[8,32,128]{2,1,0:T(8,128)S(1)}, u32[]{:S(2)}, u32[]{:S(2)}) collective-permute-start(f32[8,32,128]{2,1,0:T(8,128)S(1)} %get-tuple-element.37), channel_id=1, source_target_pairs={{0,1},{1,0},{2,3},{3,2},{4,5},{5,4},{6,7},{7,6},{8,9},{9,8},{10,11... | collective-permute-start | bytes 393224 | tf_op jit(solution)/shard_map/ppermute | solution.py:16
  6.2 8.8 %all-to-all-start = ((f32[8,8,128]{2,1,0:T(8,128)}), f32[8,8,128]{2,1,0:T(8,128)S(1)}, u32[]{:S(2)}, u32[]{:S(2)}) async-start(f32[8,8,128]{2,1,0:T(8,128)} %get-tuple-element.39), calls=%async_computation | async-start | bytes 65536 | tf_op jit(solution)/shard_map/all_to_all | solution.py:538
  11.2 6.8 %collective-permute-start.2 = (f32[6,32,128]{2,1,0:T(8,128)S(1)}, f32[6,32,128]{2,1,0:T(8,128)S(1)}, u32[]{:S(2)}, u32[]{:S(2)}) collective-permute-start(f32[6,32,128]{2,1,0:T(8,128)S(1)} %get-tuple-element.45), channel_id=1, source_target_pairs={{1,2},{2,1},{3,4},{4,3},{5,6},{6,5},{9,10},{10,9},{11,12},{12,11},... | collective-permute-start | bytes 294920 | tf_op jit(solution)/shard_map/ppermute | solution.py:16
  14.9 3.2 %collective-permute-start.3 = (f32[6,32,128]{2,1,0:T(8,128)S(1)}, f32[6,32,128]{2,1,0:T(8,128)S(1)}, u32[]{:S(2)}, u32[]{:S(2)}) collective-permute-start(f32[6,32,128]{2,1,0:T(8,128)S(1)} %get-tuple-element.46), channel_id=1, source_target_pairs={{0,1},{1,0},{2,3},{3,2},{4,5},{5,4},{6,7},{7,6},{8,9},{9,8},{10,11... | collective-permute-start | bytes 294920 | tf_op jit(solution)/shard_map/ppermute | solution.py:16
  15.0 3.1 %copy-start = (f32[1,3,4,32,128]{4,3,2,1,0:T(8,128)S(1)}, f32[1,3,4,32,128]{4,3,2,1,0:T(8,128)}, u32[]{:S(2)}) copy-start(f32[1,3,4,32,128]{4,3,2,1,0:T(8,128)} %param.21) | copy-start | bytes 589828
  15.0 3.1 %copy-start.1 = (f32[1,3,4,32,128]{4,3,2,1,0:T(8,128)S(1)}, f32[1,3,4,32,128]{4,3,2,1,0:T(8,128)}, u32[]{:S(2)}) copy-start(f32[1,3,4,32,128]{4,3,2,1,0:T(8,128)} %param.20) | copy-start | bytes 589828
  15.0 3.1 %copy-start.2 = (f32[1,3,4,32,128]{4,3,2,1,0:T(8,128)S(1)}, f32[1,3,4,32,128]{4,3,2,1,0:T(8,128)}, u32[]{:S(2)}) copy-start(f32[1,3,4,32,128]{4,3,2,1,0:T(8,128)} %param.22) | copy-start | bytes 589828
  19.0 6.8 %collective-permute-start.4 = (f32[6,32,128]{2,1,0:T(8,128)S(1)}, f32[6,32,128]{2,1,0:T(8,128)S(1)}, u32[]{:S(2)}, u32[]{:S(2)}) collective-permute-start(f32[6,32,128]{2,1,0:T(8,128)S(1)} %get-tuple-element.51), channel_id=1, source_target_pairs={{1,2},{2,1},{3,4},{4,3},{5,6},{6,5},{9,10},{10,9},{11,12},{12,11},... | collective-permute-start | bytes 294920 | tf_op jit(solution)/shard_map/ppermute | solution.py:16
  22.8 3.0 %collective-permute-start.5 = (f32[6,32,128]{2,1,0:T(8,128)S(1)}, f32[6,32,128]{2,1,0:T(8,128)S(1)}, u32[]{:S(2)}, u32[]{:S(2)}) collective-permute-start(f32[6,32,128]{2,1,0:T(8,128)S(1)} %get-tuple-element.52), channel_id=1, source_target_pairs={{0,1},{1,0},{2,3},{3,2},{4,5},{5,4},{6,7},{7,6},{8,9},{9,8},{10,11... | collective-permute-start | bytes 294920 | tf_op jit(solution)/shard_map/ppermute | solution.py:16
  26.8 6.8 %collective-permute-start.6 = (f32[6,32,128]{2,1,0:T(8,128)S(1)}, f32[6,32,128]{2,1,0:T(8,128)S(1)}, u32[]{:S(2)}, u32[]{:S(2)}) collective-permute-start(f32[6,32,128]{2,1,0:T(8,128)S(1)} %get-tuple-element.56), channel_id=1, source_target_pairs={{1,2},{2,1},{3,4},{4,3},{5,6},{6,5},{9,10},{10,9},{11,12},{12,11},... | collective-permute-start | bytes 294920 | tf_op jit(solution)/shard_map/ppermute | solution.py:16
  30.7 3.0 %collective-permute-start.7 = (f32[6,32,128]{2,1,0:T(8,128)S(1)}, f32[6,32,128]{2,1,0:T(8,128)S(1)}, u32[]{:S(2)}, u32[]{:S(2)}) collective-permute-start(f32[6,32,128]{2,1,0:T(8,128)S(1)} %get-tuple-element.57), channel_id=1, source_target_pairs={{0,1},{1,0},{2,3},{3,2},{4,5},{5,4},{6,7},{7,6},{8,9},{9,8},{10,11... | collective-permute-start | bytes 294920 | tf_op jit(solution)/shard_map/ppermute | solution.py:16
  34.3 5.0 %collective-permute-start.8 = (f32[2,4,32,128]{3,2,1,0:T(8,128)S(1)}, f32[2,4,32,128]{3,2,1,0:T(8,128)S(1)}, u32[]{:S(2)}, u32[]{:S(2)}) collective-permute-start(f32[2,4,32,128]{3,2,1,0:T(8,128)S(1)} %adjoint_two.1), channel_id=1, source_target_pairs={{0,8},{8,0},{16,24},{24,16},{1,9},{9,1},{17,25},{25,17},{2,10},{10... | collective-permute-start | bytes 393224 | tf_op jit(solution)/shard_map/ppermute | solution.py:31
  39.4 6.9 %collective-permute-start.9 = (f32[2,4,32,128]{3,2,1,0:T(8,128)S(1)}, f32[2,4,32,128]{3,2,1,0:T(8,128)S(1)}, u32[]{:S(2)}, u32[]{:S(2)}) collective-permute-start(f32[2,4,32,128]{3,2,1,0:T(8,128)S(1)} %add.11), channel_id=1, source_target_pairs={{0,24},{8,16},{16,8},{24,0},{1,25},{9,17},{17,9},{25,1},{2,26},{10... | collective-permute-start | bytes 393224 | tf_op jit(solution)/shard_map/ppermute | solution.py:31
